TPU v7x, 32 devices: a whole 2x2x4 slice. The times are simulated.
32 devices in a mesh: row: 4 (over z), col: 4 (over x, core), dp: 2 (over y).
Axes of the slice: x: 2, y: 2, z: 4, core: 2. Of those that a mesh axis runs over, the one named last changes fastest.
Arguments:
- block_input: bfloat16 [4, 2, 2048, 1024], P(None, 'dp', 'row', 'col'), may hold values from -6 to 6
- segments: int32 [4, 2, 2048], P(None, 'dp', 'row'), may hold values from 0 to 11, never falling along the last dimension, each value on 1 to 1024 neighbouring positions
- decay_rate: float32 [8], P('col'), may hold values from 0 to 1, as said below
- w_query: bfloat16 [1024, 1024], P('row', 'col'), may hold values from -0.1875 to 0.1875
- w_key: bfloat16 [1024, 1024], P('row', 'col'), may hold values from -0.1875 to 0.1875
- w_value: bfloat16 [1024, 1024], P('row', 'col'), may hold values from -0.1875 to 0.1875
- w_output_gate: bfloat16 [1024, 1024], P('row', 'col'), may hold values from -0.1875 to 0.1875
- w_out: bfloat16 [1024, 1024], P('col', 'row'), may hold values from -0.375 to 0.375
- w_gate: bfloat16 [1024, 2816], P('row', 'col'), may hold values from -0.1875 to 0.1875
- w_up: bfloat16 [1024, 2816], P('row', 'col'), may hold values from -0.1875 to 0.1875
- w_down: bfloat16 [2816, 1024], P('col', 'row'), may hold values from -0.109375 to 0.109375
- out_grad: bfloat16 [4, 2, 2048, 1024], P(None, 'dp', 'row', 'col'), may hold values from -6 to 6
Outputs:
- block_output: bfloat16 [4, 2, 2048, 1024], P(None, 'dp', 'row', 'col')
- input_grad: bfloat16 [4, 2, 2048, 1024], P(None, 'dp', 'row', 'col')
- grad_query: float32 [1024, 1024], P(('row', 'dp'), 'col')
- grad_key: float32 [1024, 1024], P(('row', 'dp'), 'col')
- grad_value: float32 [1024, 1024], P(('row', 'dp'), 'col')
- grad_output_gate: float32 [1024, 1024], P(('row', 'dp'), 'col')
- grad_out: float32 [1024, 1024], P('col', ('row', 'dp'))
- grad_gate: float32 [1024, 2816], P(('row', 'dp'), 'col')
- grad_up: float32 [1024, 2816], P(('row', 'dp'), 'col')
- grad_down: float32 [2816, 1024], P('col', ('row', 'dp'))
Inputs may be any that keep to these rules, and one draw needn't show every extreme that they name: `segments`: along each sequence the document numbers never fall; a document spans 1 to 1024 tokens, and in every sequence one spans exactly 1024. A head's state is multiplied by exp(-decay_rate[h]) at every token.
All inputs are finite; a program needn't handle non-finite values.
Results may differ from a plain program's by a relative error of at most 0.012.
Values may be sent and summed in bfloat16 or wider, within the bound.
No kernel may reach another device: no remote copies, remote signals or barrier semaphores. Data moves between devices by JAX's collectives and lax.ppermute only.
A program may use at most 192 MiB of HBM per device.

v0:
```python
import jax
import jax.numpy as jnp
from jax import lax
from jax.sharding import PartitionSpec as P

D = 1024
HEAD = 128


norm_eps = 1e-06
highest = lax.Precision.HIGHEST


def prefix_2(part, axis, combine, identity, reverse):
    count = lax.axis_size(axis)
    place = lax.axis_index(axis)
    ahead = count - 1 - place if reverse else place
    gathered = jax.tree.map(lambda a: lax.all_gather(a, axis), part)
    state = jax.tree.map(lambda a, e: jnp.zeros_like(a) + jnp.asarray(e, a.dtype), part, identity)

    def one(hop, state):
        source = count - 1 - hop if reverse else hop
        return combine(
            state, jax.tree.map(lambda a: lax.dynamic_index_in_dim(a, source, 0, False), gathered)
        )

    return lax.fori_loop(0, ahead, one, state)


def silu_slope(pre_value):
    logistic = jax.nn.sigmoid(pre_value)
    return logistic * (1.0 + pre_value * (1.0 - logistic))


def spread(features):
    return lax.all_gather(features, "col", axis=1, tiled=True)


def summed(inputs, local_mats, form):
    total = jnp.einsum(form, inputs[0], local_mats[0], preferred_element_type=jnp.float32)
    for index in range(1, len(inputs)):
        total = total + jnp.einsum(
            form, inputs[index], local_mats[index], preferred_element_type=jnp.float32
        )
    return lax.psum_scatter(total, "col", scatter_dimension=1, tiled=True)


def row_total(row_values):
    return lax.psum(row_values, "col")


def chain_combine(early_item, late_item):
    early_factor, early_state, early_segment = early_item
    late_factor, late_state, late_segment = late_item
    linked = (
        (early_segment == late_segment) | (early_segment < 0.0) | (late_segment < 0.0)
    ).astype(jnp.float32)
    new_factor = early_factor * late_factor * linked
    new_state = late_state + (late_factor * linked)[:, None, None] * early_state
    new_segment = jnp.where(late_segment < 0.0, early_segment, late_segment)
    return (new_factor, new_state, new_segment)


def grad_combine(early_item, late_item):
    early_factor, early_grad = early_item
    late_factor, late_grad = late_item
    return (early_factor * late_factor, late_grad + late_factor[:, None, None] * early_grad)


def mixer_forward(query_heads, key_heads, value_heads, segment, head_rate):
    block_len = query_heads.shape[0]
    places = jnp.arange(block_len).astype(jnp.float32)
    seg_float = segment.astype(jnp.float32)
    last_segment = seg_float[block_len - 1]
    own_weight = (seg_float == last_segment).astype(jnp.float32)[:, None] * jnp.exp(
        -head_rate[None, :] * (block_len - 1.0 - places)[:, None]
    )
    local_state = jnp.einsum(
        "she,shf->hef",
        key_heads.astype(jnp.float32) * own_weight[:, :, None],
        value_heads.astype(jnp.float32),
        precision=highest,
    )
    whole_block = (seg_float[0] == last_segment).astype(jnp.float32)
    carry_factor = whole_block * jnp.exp(-head_rate * block_len)
    identity = (
        jnp.ones_like(head_rate),
        jnp.zeros_like(local_state),
        jnp.full((1,), -1.0, jnp.float32),
    )
    prefix = prefix_2(
        (carry_factor, local_state, last_segment[None]), "row", chain_combine, identity, False
    )
    entry_state = prefix[1]
    entry_segment = prefix[2]
    offsets = places[:, None] - places[None, :]
    visible = (offsets >= 0.0) & (seg_float[:, None] == seg_float[None, :])
    decay_mask = jnp.where(
        visible[None], jnp.exp(-head_rate[:, None, None] * jnp.maximum(offsets, 0.0)[None]), 0.0
    )
    scores = jnp.einsum("the,she->hts", query_heads, key_heads, preferred_element_type=jnp.float32)
    mix_weights = (scores * decay_mask).astype(jnp.bfloat16)
    inner_part = jnp.einsum(
        "hts,she->the", mix_weights, value_heads, preferred_element_type=jnp.float32
    )
    entry_scale = (seg_float == entry_segment[0]).astype(jnp.float32)[:, None] * jnp.exp(
        -head_rate[None, :] * (places[:, None] + 1.0)
    )
    carried = entry_scale[:, :, None] * jnp.einsum(
        "the,hef->thf", query_heads.astype(jnp.float32), entry_state, precision=highest
    )
    kept_values = (
        decay_mask,
        mix_weights,
        entry_state,
        entry_segment,
        entry_scale,
        own_weight,
        carry_factor,
        last_segment,
    )
    return (inner_part + carried, kept_values)


def mixer_backward(query_heads, key_heads, value_heads, mixed_grad, head_rate, kept_values):
    (
        decay_mask,
        mix_weights,
        entry_state,
        entry_segment,
        entry_scale,
        own_weight,
        carry_factor,
        last_segment,
    ) = kept_values
    weight_grad = jnp.einsum(
        "thf,shf->hts", mixed_grad, value_heads, preferred_element_type=jnp.float32
    )
    score_grad = (weight_grad * decay_mask).astype(jnp.bfloat16)
    grad_wide = mixed_grad.astype(jnp.float32)
    query_grad = jnp.einsum(
        "hts,she->the", score_grad, key_heads, preferred_element_type=jnp.float32
    )
    query_grad = query_grad + entry_scale[:, :, None] * jnp.einsum(
        "thf,hef->the", grad_wide, entry_state, precision=highest
    )
    key_grad = jnp.einsum(
        "hts,the->she", score_grad, query_heads, preferred_element_type=jnp.float32
    )
    value_grad = jnp.einsum(
        "hts,thf->shf", mix_weights, mixed_grad, preferred_element_type=jnp.float32
    )
    entry_grad = jnp.einsum(
        "the,thf->hef",
        query_heads.astype(jnp.float32) * entry_scale[:, :, None],
        grad_wide,
        precision=highest,
    )
    linked = ((entry_segment == last_segment) | (entry_segment < 0.0)).astype(jnp.float32)
    back_factor = carry_factor * linked
    suffix = prefix_2(
        (back_factor, entry_grad),
        "row",
        grad_combine,
        (jnp.ones_like(head_rate), jnp.zeros_like(entry_grad)),
        True,
    )
    state_grad = suffix[1]
    key_grad = key_grad + own_weight[:, :, None] * jnp.einsum(
        "hef,shf->she", state_grad, value_heads.astype(jnp.float32), precision=highest
    )
    value_grad = value_grad + own_weight[:, :, None] * jnp.einsum(
        "hef,she->shf", state_grad, key_heads.astype(jnp.float32), precision=highest
    )
    return (query_grad, key_grad, value_grad)


def micro_step(weight_full, input_rows, segment, head_rate, cotangent):
    full_query, full_key, full_value, full_open, full_out, full_gate, full_up, full_down = (
        weight_full
    )
    heads_local = head_rate.shape[0]
    block_len = input_rows.shape[0]
    rows_wide = input_rows.astype(jnp.float32)
    scale_in = lax.rsqrt(row_total(jnp.sum(rows_wide * rows_wide, axis=1)) / D + norm_eps)
    normed_in = spread((rows_wide * scale_in[:, None]).astype(jnp.bfloat16))
    pre_query = jnp.dot(normed_in, full_query, preferred_element_type=jnp.float32)
    pre_key = jnp.dot(normed_in, full_key, preferred_element_type=jnp.float32)
    pre_value = jnp.dot(normed_in, full_value, preferred_element_type=jnp.float32)
    pre_open = jnp.dot(normed_in, full_open, preferred_element_type=jnp.float32)
    query_heads = jax.nn.silu(pre_query).astype(jnp.bfloat16).reshape(block_len, heads_local, HEAD)
    key_heads = jax.nn.silu(pre_key).astype(jnp.bfloat16).reshape(block_len, heads_local, HEAD)
    value_heads = pre_value.astype(jnp.bfloat16).reshape(block_len, heads_local, HEAD)
    gate_open = jax.nn.sigmoid(pre_open)
    mixed_out, kept_values = mixer_forward(query_heads, key_heads, value_heads, segment, head_rate)
    mixed_rows = mixed_out.reshape(block_len, heads_local * HEAD)
    scale_mix = lax.rsqrt(row_total(jnp.sum(mixed_rows * mixed_rows, axis=1)) / D + norm_eps)
    normed_mix = mixed_rows * scale_mix[:, None]
    attended = (normed_mix * gate_open).astype(jnp.bfloat16)
    residual = rows_wide + summed((attended,), (full_out,), "tc,cd->td")
    scale_mid = lax.rsqrt(row_total(jnp.sum(residual * residual, axis=1)) / D + norm_eps)
    normed_mid = spread((residual * scale_mid[:, None]).astype(jnp.bfloat16))
    gate_pre = jnp.dot(normed_mid, full_gate, preferred_element_type=jnp.float32)
    up_pre = jnp.dot(normed_mid, full_up, preferred_element_type=jnp.float32)
    product = (gate_pre * up_pre).astype(jnp.bfloat16)
    block_out = (residual + summed((product,), (full_down,), "tc,cd->td")).astype(jnp.bfloat16)
    cot_full = spread(cotangent)
    grad_down = jnp.einsum("tf,td->fd", product, cot_full, preferred_element_type=jnp.float32)
    product_grad = jnp.einsum("td,fd->tf", cot_full, full_down, preferred_element_type=jnp.float32)
    gate_grad = (product_grad * up_pre).astype(jnp.bfloat16)
    up_grad = (product_grad * gate_pre).astype(jnp.bfloat16)
    grad_gate = jnp.einsum("td,tf->df", normed_mid, gate_grad, preferred_element_type=jnp.float32)
    grad_up = jnp.einsum("td,tf->df", normed_mid, up_grad, preferred_element_type=jnp.float32)
    mid_grad = summed((gate_grad, up_grad), (full_gate, full_up), "tf,df->td")
    mid_dot = row_total(jnp.sum(mid_grad * residual, axis=1))
    residual_grad = (
        cotangent.astype(jnp.float32)
        + scale_mid[:, None] * mid_grad
        - residual * (scale_mid**3 * mid_dot / D)[:, None]
    )
    branch_grad = spread(residual_grad.astype(jnp.bfloat16))
    grad_out = jnp.einsum("tc,td->cd", attended, branch_grad, preferred_element_type=jnp.float32)
    attended_grad = jnp.einsum(
        "td,cd->tc", branch_grad, full_out, preferred_element_type=jnp.float32
    )
    normed_grad = attended_grad * gate_open
    open_grad = (attended_grad * normed_mix * gate_open * (1.0 - gate_open)).astype(jnp.bfloat16)
    mix_dot = row_total(jnp.sum(normed_grad * mixed_rows, axis=1))
    mixed_grad = (
        scale_mix[:, None] * normed_grad - mixed_rows * (scale_mix**3 * mix_dot / D)[:, None]
    )
    mixed_grad = mixed_grad.astype(jnp.bfloat16).reshape(block_len, heads_local, HEAD)
    query_grad, key_grad, value_grad = mixer_backward(
        query_heads, key_heads, value_heads, mixed_grad, head_rate, kept_values
    )
    pre_query_grad = (
        query_grad.reshape(block_len, heads_local * HEAD) * silu_slope(pre_query)
    ).astype(jnp.bfloat16)
    pre_key_grad = (key_grad.reshape(block_len, heads_local * HEAD) * silu_slope(pre_key)).astype(
        jnp.bfloat16
    )
    pre_value_grad = value_grad.reshape(block_len, heads_local * HEAD).astype(jnp.bfloat16)
    grad_query = jnp.einsum(
        "td,tc->dc", normed_in, pre_query_grad, preferred_element_type=jnp.float32
    )
    grad_key = jnp.einsum("td,tc->dc", normed_in, pre_key_grad, preferred_element_type=jnp.float32)
    grad_value = jnp.einsum(
        "td,tc->dc", normed_in, pre_value_grad, preferred_element_type=jnp.float32
    )
    grad_open = jnp.einsum("td,tc->dc", normed_in, open_grad, preferred_element_type=jnp.float32)
    input_side = summed(
        (pre_query_grad, pre_key_grad, pre_value_grad, open_grad),
        (full_query, full_key, full_value, full_open),
        "tc,dc->td",
    )
    input_dot = row_total(jnp.sum(input_side * rows_wide, axis=1))
    input_grad = (
        residual_grad
        + scale_in[:, None] * input_side
        - rows_wide * (scale_in**3 * input_dot / D)[:, None]
    )
    step_grads = (
        grad_query,
        grad_key,
        grad_value,
        grad_open,
        grad_out,
        grad_gate,
        grad_up,
        grad_down,
    )
    return (block_out, input_grad.astype(jnp.bfloat16), step_grads)


def on_device(
    block_input,
    segments,
    decay_rate,
    w_query,
    w_key,
    w_value,
    w_output_gate,
    w_out,
    w_gate,
    w_up,
    w_down,
    out_grad,
):
    row_count = lax.axis_size("row")

    def widened(weight_shard, grow_dim):
        new_shape = list(weight_shard.shape)
        new_shape[grow_dim] = new_shape[grow_dim] * row_count
        return jnp.zeros(tuple(new_shape), jnp.float32)

    totals = [
        widened(w_query, 0),
        widened(w_key, 0),
        widened(w_value, 0),
        widened(w_output_gate, 0),
        widened(w_out, 1),
        widened(w_gate, 0),
        widened(w_up, 0),
        widened(w_down, 1),
    ]
    outputs = []
    input_grads = []
    for batch_index in range(block_input.shape[0]):
        fetched = (
            lax.all_gather(w_query, "row", axis=0, tiled=True),
            lax.all_gather(w_key, "row", axis=0, tiled=True),
            lax.all_gather(w_value, "row", axis=0, tiled=True),
            lax.all_gather(w_output_gate, "row", axis=0, tiled=True),
            lax.all_gather(w_out, "row", axis=1, tiled=True),
            lax.all_gather(w_gate, "row", axis=0, tiled=True),
            lax.all_gather(w_up, "row", axis=0, tiled=True),
            lax.all_gather(w_down, "row", axis=1, tiled=True),
        )
        block_out, input_grad, step_grads = micro_step(
            fetched,
            block_input[batch_index, 0],
            segments[batch_index, 0],
            decay_rate,
            out_grad[batch_index, 0],
        )
        totals = [acc_sum + addend for acc_sum, addend in zip(totals, step_grads)]
        outputs.append(block_out)
        input_grads.append(input_grad)
    reduced = (
        lax.psum_scatter(totals[0], ("row", "dp"), scatter_dimension=0, tiled=True),
        lax.psum_scatter(totals[1], ("row", "dp"), scatter_dimension=0, tiled=True),
        lax.psum_scatter(totals[2], ("row", "dp"), scatter_dimension=0, tiled=True),
        lax.psum_scatter(totals[3], ("row", "dp"), scatter_dimension=0, tiled=True),
        lax.psum_scatter(totals[4], ("row", "dp"), scatter_dimension=1, tiled=True),
        lax.psum_scatter(totals[5], ("row", "dp"), scatter_dimension=0, tiled=True),
        lax.psum_scatter(totals[6], ("row", "dp"), scatter_dimension=0, tiled=True),
        lax.psum_scatter(totals[7], ("row", "dp"), scatter_dimension=1, tiled=True),
    )
    return (
        jnp.stack(outputs)[:, None],
        jnp.stack(input_grads)[:, None],
        reduced[0],
        reduced[1],
        reduced[2],
        reduced[3],
        reduced[4],
        reduced[5],
        reduced[6],
        reduced[7],
    )


def solution(mesh):
    placed = (
        P(None, "dp", "row", "col"),
        P(None, "dp", "row"),
        P("col"),
        P("row", "col"),
        P("row", "col"),
        P("row", "col"),
        P("row", "col"),
        P("col", "row"),
        P("row", "col"),
        P("row", "col"),
        P("col", "row"),
        P(None, "dp", "row", "col"),
    )
    return jax.shard_map(
        on_device,
        mesh=mesh,
        in_specs=placed,
        out_specs=(
            P(None, "dp", "row", "col"),
            P(None, "dp", "row", "col"),
            P(("row", "dp"), "col"),
            P(("row", "dp"), "col"),
            P(("row", "dp"), "col"),
            P(("row", "dp"), "col"),
            P("col", ("row", "dp")),
            P(("row", "dp"), "col"),
            P(("row", "dp"), "col"),
            P("col", ("row", "dp")),
        ),
        check_vma=False,
    )
```

profile of v0, /device:TPU:0, one launch (start us, length us, event | category | flops | bytes accessed | tf_op | source)
XLA Modules:
  0.0 1782.0 jit_solution(5106329666992905665)
XLA Ops:
  8.6 8.4 psum.168
  19.4 15.8 all_gather.207
  35.2 16.1 all_gather.205
  65.4 12.3 all-reduce.19
  78.3 15.6 all_gather.206
  93.9 16.0 all_gather.213
  110.0 15.6 all_gather.214
  134.1 15.4 all-gather
  157.1 6.0 psum.169
  168.2 45.2 %reduce-scatter.25.cloned.1.call-done = f32[512,256]{1,0:T(8,128)} async-done(((f32[512,1024]{1,0:T(8,128)}), f32[512,256]{1,0:T(8,128)}) %reduce-scatter.25.cloned.1.call-update) | async-done | bytes 524304 | tf_op jit(solution)/shard_map/reduce_scatter | solution.py:45
  228.3 11.8 all-gather.54.cloned.1.call-done
  244.8 16.0 all-gather.3
  265.9 23.8 %all-gather.9 = f32[8,128,128]{2,1,0:T(8,128)S(1)} all-gather(f32[2,128,128]{2,1,0:T(8,128)S(1)} %fusion.135), channel_id=11, replica_groups=mesh['row'=4,'col'=4,'dp'=2] {'row'}, dimensions={0}, use_global_device_ids=true | all-gather | bytes 655360 | tf_op jit(solution)/shard_map/all_gather | solution.py:18
  295.2 29.7 %all-gather.6 = f32[8,128,128]{2,1,0:T(8,128)} all-gather(f32[2,128,128]{2,1,0:T(8,128)S(1)} %fusion.138), channel_id=8, replica_groups=mesh['row'=4,'col'=4,'dp'=2] {'row'}, dimensions={0}, use_global_device_ids=true | all-gather | bytes 655360 | tf_op jit(solution)/shard_map/all_gather | solution.py:18
  367.9 6.6 all-gather.50.cloned.1.call-done
  374.5 16.6 all-gather.46.cloned.1.call-done
  395.0 33.1 %all-gather.48.cloned.1.call-done = bf16[1024,704]{0,1:T(8,128)(2,1)} async-done(((bf16[256,704]{0,1:T(8,128)(2,1)}), bf16[1024,704]{0,1:T(8,128)(2,1)}) %all-gather.48.cloned.1.call-update) | async-done | bytes 1441808 | tf_op jit(solution)/shard_map/all_gather | solution.py:315
  441.7 18.4 %reduce-scatter.29.cloned.1.call-done = f32[512,256]{1,0:T(8,128)} async-done(((f32[512,1024]{1,0:T(8,128)}), f32[512,256]{1,0:T(8,128)}) %reduce-scatter.29.cloned.1.call-update) | async-done | bytes 524304 | tf_op jit(solution)/shard_map/reduce_scatter | solution.py:45
  460.0 33.6 %reduce-scatter.33.cloned.1.call-done = f32[512,256]{1,0:T(8,128)} async-done(((f32[512,1024]{1,0:T(8,128)}), f32[512,256]{1,0:T(8,128)}) %reduce-scatter.33.cloned.1.call-update) | async-done | bytes 524304 | tf_op jit(solution)/shard_map/reduce_scatter | solution.py:45
  493.6 33.7 %reduce-scatter.37.cloned.1.call-done = f32[512,256]{1,0:T(8,128)} async-done(((f32[512,1024]{1,0:T(8,128)}), f32[512,256]{1,0:T(8,128)}) %reduce-scatter.37.cloned.1.call-update) | async-done | bytes 524304 | tf_op jit(solution)/shard_map/reduce_scatter | solution.py:45
  527.3 33.6 %reduce-scatter.41.cloned.1.call-done = f32[512,256]{1,0:T(8,128)} async-done(((f32[512,1024]{1,0:T(8,128)}), f32[512,256]{1,0:T(8,128)}) %reduce-scatter.41.cloned.1.call-update) | async-done | bytes 524304 | tf_op jit(solution)/shard_map/reduce_scatter | solution.py:45
  560.9 33.6 %reduce-scatter.27.cloned.1.call-done = f32[512,256]{1,0:T(8,128)} async-done(((f32[512,1024]{1,0:T(8,128)}), f32[512,256]{1,0:T(8,128)}) %reduce-scatter.27.cloned.1.call-update) | async-done | bytes 524304 | tf_op jit(solution)/shard_map/reduce_scatter | solution.py:45
  605.1 17.6 all-gather.66.cloned.1.call-done
  640.8 12.4 all-reduce.18
  659.5 15.5 all-gather.13
  731.6 12.4 all-gather.76.cloned.1.call-done
  765.2 12.5 reduce-scatter.43.cloned.1.call-done
  777.8 33.6 %reduce-scatter.53.cloned.1.call-done = f32[512,256]{1,0:T(8,128)} async-done(((f32[512,1024]{1,0:T(8,128)}), f32[512,256]{1,0:T(8,128)}) %reduce-scatter.53.cloned.1.call-update) | async-done | bytes 524304 | tf_op jit(solution)/shard_map/reduce_scatter | solution.py:45
  811.3 33.7 %reduce-scatter.49.cloned.1.call-done = f32[512,256]{1,0:T(8,128)} async-done(((f32[512,1024]{1,0:T(8,128)}), f32[512,256]{1,0:T(8,128)}) %reduce-scatter.49.cloned.1.call-update) | async-done | bytes 524304 | tf_op jit(solution)/shard_map/reduce_scatter | solution.py:45
  845.0 33.6 %reduce-scatter.45.cloned.1.call-done = f32[512,256]{1,0:T(8,128)} async-done(((f32[512,1024]{1,0:T(8,128)}), f32[512,256]{1,0:T(8,128)}) %reduce-scatter.45.cloned.1.call-update) | async-done | bytes 524304 | tf_op jit(solution)/shard_map/reduce_scatter | solution.py:45
  878.6 33.6 %reduce-scatter.39.cloned.1.call-done = f32[512,256]{1,0:T(8,128)} async-done(((f32[512,1024]{1,0:T(8,128)}), f32[512,256]{1,0:T(8,128)}) %reduce-scatter.39.cloned.1.call-update) | async-done | bytes 524304 | tf_op jit(solution)/shard_map/reduce_scatter | solution.py:45
  912.2 33.7 %reduce-scatter.35.cloned.1.call-done = f32[512,256]{1,0:T(8,128)} async-done(((f32[512,1024]{1,0:T(8,128)}), f32[512,256]{1,0:T(8,128)}) %reduce-scatter.35.cloned.1.call-update) | async-done | bytes 524304 | tf_op jit(solution)/shard_map/reduce_scatter | solution.py:45
  945.9 33.7 %reduce-scatter.31.cloned.1.call-done = f32[512,256]{1,0:T(8,128)} async-done(((f32[512,1024]{1,0:T(8,128)}), f32[512,256]{1,0:T(8,128)}) %reduce-scatter.31.cloned.1.call-update) | async-done | bytes 524304 | tf_op jit(solution)/shard_map/reduce_scatter | solution.py:45
  996.1 14.7 all-gather.72.cloned.1.call-done
  1013.6 15.6 all-gather.68.cloned.1.call-done
  1032.0 16.2 all-gather.70.cloned.1.call-done
  1051.0 6.7 all-reduce.13
  1065.4 16.1 all-gather.22
  1098.0 15.6 all-gather.16
  1122.3 15.6 all-gather.19
  1228.5 58.2 %reduce-scatter.67.cloned.1.call-done = f32[128,704]{0,1:T(8,128)} async-done(((f32[1024,704]{0,1:T(8,128)}), f32[128,704]{0,1:T(8,128)}) %reduce-scatter.67.cloned.1.call-update) | async-done | bytes 360464 | tf_op jit(solution)/shard_map/reduce_scatter | solution.py:335
  1286.7 76.0 %reduce-scatter.69.cloned.1.call-done = f32[128,704]{0,1:T(8,128)} async-done(((f32[1024,704]{0,1:T(8,128)}), f32[128,704]{0,1:T(8,128)}) %reduce-scatter.69.cloned.1.call-update) | async-done | bytes 360464 | tf_op jit(solution)/shard_map/reduce_scatter | solution.py:336
  1362.7 76.2 %reduce-scatter.71.cloned.1.call-done = f32[704,128]{1,0:T(8,128)} async-done(((f32[704,1024]{1,0:T(8,128)}), f32[704,128]{1,0:T(8,128)}) %reduce-scatter.71.cloned.1.call-update) | async-done | bytes 360464 | tf_op jit(solution)/shard_map/reduce_scatter | solution.py:337
  1439.0 67.2 %reduce-scatter.57.cloned.1.call-done = f32[128,256]{1,0:T(8,128)} async-done(((f32[1024,256]{1,0:T(8,128)}), f32[128,256]{1,0:T(8,128)}) %reduce-scatter.57.cloned.1.call-update) | async-done | bytes 131088 | tf_op jit(solution)/shard_map/reduce_scatter | solution.py:330
  1506.2 67.1 %reduce-scatter.59.cloned.1.call-done = f32[128,256]{1,0:T(8,128)} async-done(((f32[1024,256]{1,0:T(8,128)}), f32[128,256]{1,0:T(8,128)}) %reduce-scatter.59.cloned.1.call-update) | async-done | bytes 131088 | tf_op jit(solution)/shard_map/reduce_scatter | solution.py:331
  1573.3 67.1 %reduce-scatter.61.cloned.1.call-done = f32[128,256]{1,0:T(8,128)} async-done(((f32[1024,256]{1,0:T(8,128)}), f32[128,256]{1,0:T(8,128)}) %reduce-scatter.61.cloned.1.call-update) | async-done | bytes 131088 | tf_op jit(solution)/shard_map/reduce_scatter | solution.py:332
  1640.4 67.1 %reduce-scatter.63.cloned.1.call-done = f32[128,256]{1,0:T(8,128)} async-done(((f32[1024,256]{1,0:T(8,128)}), f32[128,256]{1,0:T(8,128)}) %reduce-scatter.63.cloned.1.call-update) | async-done | bytes 131088 | tf_op jit(solution)/shard_map/reduce_scatter | solution.py:333
  1707.6 67.4 %reduce-scatter.65.cloned.1.call-done = f32[256,128]{1,0:T(8,128)} async-done(((f32[256,1024]{1,0:T(8,128)}), f32[256,128]{1,0:T(8,128)}) %reduce-scatter.65.cloned.1.call-update) | async-done | bytes 131088 | tf_op jit(solution)/shard_map/reduce_scatter | solution.py:334
  (959 shorter events, 397.4 us)
Async XLA Ops:
  7.2 123.3 %all-gather.44.cloned.1.call-start = ((), (), s32[]{:S(2)}) async-start(), calls=%async_computation.24 | async-start | bytes 1310720 | tf_op jit(solution)/shard_map/all_gather | solution.py:36
  18.8 194.6 %reduce-scatter.25.cloned.1.call-start = ((), (), s32[]{:S(2)}) async-start(), calls=%async_computation.25 | async-start | bytes 2621440 | tf_op jit(solution)/shard_map/reduce_scatter | solution.py:45
  35.2 256.9 %copy-start.19 = (bf16[1024,256]{1,0:T(8,128)(2,1)}, bf16[1024,256]{1,0:T(8,128)(2,1)S(1)}, u32[]{:S(2)}) copy-start(bf16[1024,256]{1,0:T(8,128)(2,1)S(1)} %all_gather.207) | copy-start | bytes 1572868
  168.1 71.9 %all-gather.54.cloned.1.call-start = ((), (), s32[]{:S(2)}) async-start(), calls=%async_computation.31 | async-start | bytes 1310720 | tf_op jit(solution)/shard_map/all_gather | solution.py:36
  222.4 38.7 %all-gather.62.cloned.1.call-start = ((), (), s32[]{:S(2)}) async-start(), calls=%async_computation.39 | async-start | bytes 1310720 | tf_op jit(solution)/shard_map/all_gather | solution.py:36
  223.0 67.3 %all-gather.58.cloned.1.call-start = ((), (), s32[]{:S(2)}) async-start(), calls=%async_computation.35 | async-start | bytes 1310720 | tf_op jit(solution)/shard_map/all_gather | solution.py:36
  223.6 140.5 %all-gather.74.cloned.1.call-start = ((), (), s32[]{:S(2)}) async-start(), calls=%async_computation.63 | async-start | bytes 1310720 | tf_op jit(solution)/shard_map/all_gather | solution.py:36
  225.9 138.2 %all-gather.52.cloned.1.call-start = ((), (), s32[]{:S(2)}) async-start(), calls=%async_computation.29 | async-start | bytes 1802240 | tf_op jit(solution)/shard_map/all_gather | solution.py:317
  226.7 147.8 %all-gather.50.cloned.1.call-start = ((), (), s32[]{:S(2)}) async-start(), calls=%async_computation.28 | async-start | bytes 1802240 | tf_op jit(solution)/shard_map/all_gather | solution.py:316
  227.4 163.7 %all-gather.46.cloned.1.call-start = ((), (), s32[]{:S(2)}) async-start(), calls=%async_computation.26 | async-start | bytes 1310720 | tf_op jit(solution)/shard_map/all_gather | solution.py:36
  347.5 80.6 %all-gather.48.cloned.1.call-start = ((), (), s32[]{:S(2)}) async-start(), calls=%async_computation.27 | async-start | bytes 1802240 | tf_op jit(solution)/shard_map/all_gather | solution.py:315
  348.1 111.9 %reduce-scatter.29.cloned.1.call-start = ((), (), s32[]{:S(2)}) async-start(), calls=%async_computation.32 | async-start | bytes 2621440 | tf_op jit(solution)/shard_map/reduce_scatter | solution.py:45
  353.3 140.3 %reduce-scatter.33.cloned.1.call-start = ((), (), s32[]{:S(2)}) async-start(), calls=%async_computation.36 | async-start | bytes 2621440 | tf_op jit(solution)/shard_map/reduce_scatter | solution.py:45
  358.6 168.7 %reduce-scatter.37.cloned.1.call-start = ((), (), s32[]{:S(2)}) async-start(), calls=%async_computation.40 | async-start | bytes 2621440 | tf_op jit(solution)/shard_map/reduce_scatter | solution.py:45
  363.8 197.1 %reduce-scatter.41.cloned.1.call-start = ((), (), s32[]{:S(2)}) async-start(), calls=%async_computation.43 | async-start | bytes 2621440 | tf_op jit(solution)/shard_map/reduce_scatter | solution.py:45
  436.7 157.8 %reduce-scatter.27.cloned.1.call-start = ((), (), s32[]{:S(2)}) async-start(), calls=%async_computation.30 | async-start | bytes 2621440 | tf_op jit(solution)/shard_map/reduce_scatter | solution.py:45
  441.6 181.0 %all-gather.66.cloned.1.call-start = ((), (), s32[]{:S(2)}) async-start(), calls=%async_computation.44 | async-start | bytes 1310720 | tf_op jit(solution)/shard_map/all_gather | solution.py:36
  605.0 85.6 %all-gather.64.cloned.1.call-start = ((), (), s32[]{:S(2)}) async-start(), calls=%async_computation.41 | async-start | bytes 1310720 | tf_op jit(solution)/shard_map/all_gather | solution.py:36
  634.3 62.4 %all-gather.80.cloned.1.call-start = ((), (), s32[]{:S(2)}) async-start(), calls=%async_computation.66 | async-start | bytes 1310720 | tf_op jit(solution)/shard_map/all_gather | solution.py:36
  634.8 70.9 %all-gather.60.cloned.1.call-start = ((), (), s32[]{:S(2)}) async-start(), calls=%async_computation.37 | async-start | bytes 1310720 | tf_op jit(solution)/shard_map/all_gather | solution.py:36
  635.6 76.2 %all-gather.78.cloned.1.call-start = ((), (), s32[]{:S(2)}) async-start(), calls=%async_computation.65 | async-start | bytes 1310720 | tf_op jit(solution)/shard_map/all_gather | solution.py:36
  636.2 89.4 %all-gather.56.cloned.1.call-start = ((), (), s32[]{:S(2)}) async-start(), calls=%async_computation.33 | async-start | bytes 1310720 | tf_op jit(solution)/shard_map/all_gather | solution.py:36
  637.0 107.1 %all-gather.76.cloned.1.call-start = ((), (), s32[]{:S(2)}) async-start(), calls=%async_computation.64 | async-start | bytes 1310720 | tf_op jit(solution)/shard_map/all_gather | solution.py:36
  637.7 140.1 %reduce-scatter.43.cloned.1.call-start = ((), (), s32[]{:S(2)}) async-start(), calls=%async_computation.45 | async-start | bytes 2621440 | tf_op jit(solution)/shard_map/reduce_scatter | solution.py:45
  690.5 120.8 %reduce-scatter.53.cloned.1.call-start = ((), (), s32[]{:S(2)}) async-start(), calls=%async_computation.52 | async-start | bytes 2621440 | tf_op jit(solution)/shard_map/reduce_scatter | solution.py:45
  705.7 139.3 %reduce-scatter.49.cloned.1.call-start = ((), (), s32[]{:S(2)}) async-start(), calls=%async_computation.49 | async-start | bytes 2621440 | tf_op jit(solution)/shard_map/reduce_scatter | solution.py:45
  720.7 157.9 %reduce-scatter.45.cloned.1.call-start = ((), (), s32[]{:S(2)}) async-start(), calls=%async_computation.46 | async-start | bytes 2621440 | tf_op jit(solution)/shard_map/reduce_scatter | solution.py:45
  752.8 159.3 %reduce-scatter.39.cloned.1.call-start = ((), (), s32[]{:S(2)}) async-start(), calls=%async_computation.42 | async-start | bytes 2621440 | tf_op jit(solution)/shard_map/reduce_scatter | solution.py:45
  757.1 188.8 %reduce-scatter.35.cloned.1.call-start = ((), (), s32[]{:S(2)}) async-start(), calls=%async_computation.38 | async-start | bytes 2621440 | tf_op jit(solution)/shard_map/reduce_scatter | solution.py:45
  761.1 218.5 %reduce-scatter.31.cloned.1.call-start = ((), (), s32[]{:S(2)}) async-start(), calls=%async_computation.34 | async-start | bytes 2621440 | tf_op jit(solution)/shard_map/reduce_scatter | solution.py:45
  765.1 224.5 %copy-start.244 = (f32[512]{0:T(512)S(1)}, f32[512]{0:T(512)}, u32[]{:S(2)}) copy-start(f32[512]{0:T(512)} %copy-done.243) | copy-start | bytes 6148
  765.2 224.5 %copy-start.226 = (f32[512]{0:T(512)S(1)}, f32[512]{0:T(512)}, u32[]{:S(2)}) copy-start(f32[512]{0:T(512)} %copy-done.225) | copy-start | bytes 6148
  765.2 224.5 %copy-start.228 = (f32[512]{0:T(512)S(1)}, f32[512]{0:T(512)}, u32[]{:S(2)}) copy-start(f32[512]{0:T(512)} %copy-done.227) | copy-start | bytes 6148
  765.2 224.5 %copy-start.230 = (f32[512]{0:T(512)S(1)}, f32[512]{0:T(512)}, u32[]{:S(2)}) copy-start(f32[512]{0:T(512)} %copy-done.229) | copy-start | bytes 6148
  765.2 245.6 %all-gather.72.cloned.1.call-start = ((), (), s32[]{:S(2)}) async-start(), calls=%async_computation.53 | async-start | bytes 1310720 | tf_op jit(solution)/shard_map/all_gather | solution.py:36
  993.2 36.0 %all-gather.68.cloned.1.call-start = ((), (), s32[]{:S(2)}) async-start(), calls=%async_computation.47 | async-start | bytes 1310720 | tf_op jit(solution)/shard_map/all_gather | solution.py:36
  993.9 54.3 %all-gather.70.cloned.1.call-start = ((), (), s32[]{:S(2)}) async-start(), calls=%async_computation.50 | async-start | bytes 1310720 | tf_op jit(solution)/shard_map/all_gather | solution.py:36
  994.7 222.7 %reduce-scatter.55.cloned.1.call-start = ((), (), s32[]{:S(2)}) async-start(), calls=%async_computation.54 | async-start | bytes 2621440 | tf_op jit(solution)/shard_map/reduce_scatter | solution.py:45
  1093.7 123.7 %reduce-scatter.47.cloned.1.call-start = ((), (), s32[]{:S(2)}) async-start(), calls=%async_computation.48 | async-start | bytes 2621440 | tf_op jit(solution)/shard_map/reduce_scatter | solution.py:45
  1146.4 71.0 %reduce-scatter.51.cloned.1.call-start = ((), (), s32[]{:S(2)}) async-start(), calls=%async_computation.51 | async-start | bytes 2621440 | tf_op jit(solution)/shard_map/reduce_scatter | solution.py:45
  1163.7 123.0 %reduce-scatter.67.cloned.1.call-start = ((), (), s32[]{:S(2)}) async-start(), calls=%async_computation.60 | async-start | bytes 3244032 | tf_op jit(solution)/shard_map/reduce_scatter | solution.py:335
  1171.9 190.9 %reduce-scatter.69.cloned.1.call-start = ((), (), s32[]{:S(2)}) async-start(), calls=%async_computation.61 | async-start | bytes 3244032 | tf_op jit(solution)/shard_map/reduce_scatter | solution.py:336
  1179.8 259.2 %reduce-scatter.71.cloned.1.call-start = ((), (), s32[]{:S(2)}) async-start(), calls=%async_computation.62 | async-start | bytes 3244032 | tf_op jit(solution)/shard_map/reduce_scatter | solution.py:337
  1189.2 317.0 %reduce-scatter.57.cloned.1.call-start = ((), (), s32[]{:S(2)}) async-start(), calls=%async_computation.55 | async-start | bytes 1179648 | tf_op jit(solution)/shard_map/reduce_scatter | solution.py:330
  1195.5 377.8 %reduce-scatter.59.cloned.1.call-start = ((), (), s32[]{:S(2)}) async-start(), calls=%async_computation.56 | async-start | bytes 1179648 | tf_op jit(solution)/shard_map/reduce_scatter | solution.py:331
  1200.6 439.9 %reduce-scatter.61.cloned.1.call-start = ((), (), s32[]{:S(2)}) async-start(), calls=%async_computation.57 | async-start | bytes 1179648 | tf_op jit(solution)/shard_map/reduce_scatter | solution.py:332
  1205.7 501.8 %reduce-scatter.63.cloned.1.call-start = ((), (), s32[]{:S(2)}) async-start(), calls=%async_computation.58 | async-start | bytes 1179648 | tf_op jit(solution)/shard_map/reduce_scatter | solution.py:333
  1210.8 564.1 %reduce-scatter.65.cloned.1.call-start = ((), (), s32[]{:S(2)}) async-start(), calls=%async_computation.59 | async-start | bytes 1179648 | tf_op jit(solution)/shard_map/reduce_scatter | solution.py:334
  (278 other events, 3402.1 us)
Sparse Core Ops, SparseCore 0:
  18.9 17.1 all-gather.43
  168.2 45.0 reduce-scatter.24
  222.6 17.4 all-gather.53
  241.4 16.8 all-gather.61
  259.7 16.8 all-gather.57
  278.0 16.7 all-gather.73
  296.4 42.1 all-gather.51
  340.1 34.3 all-gather.49
  376.0 14.9 all-gather.45
  392.5 35.5 all-gather.47
  430.7 29.3 reduce-scatter.28
  462.4 31.1 reduce-scatter.32
  496.1 31.1 reduce-scatter.36
  529.7 31.1 reduce-scatter.40
  563.3 31.1 reduce-scatter.26
  605.1 17.4 all-gather.65
  634.4 17.8 all-gather.63
  653.7 16.8 all-gather.79
  672.1 16.8 all-gather.59
  690.3 16.8 all-gather.77
  708.8 16.8 all-gather.55
  727.2 16.8 all-gather.75
  746.5 31.1 reduce-scatter.42
  780.1 31.1 reduce-scatter.52
  813.8 31.1 reduce-scatter.48
  847.4 31.1 reduce-scatter.44
  881.0 31.1 reduce-scatter.38
  914.7 31.1 reduce-scatter.34
  948.4 31.1 reduce-scatter.30
  993.3 17.4 all-gather.71
  1012.4 16.8 all-gather.67
  1031.4 16.8 all-gather.69
  1093.8 29.3 reduce-scatter.54
  1146.5 29.7 reduce-scatter.46
  1178.8 31.1 reduce-scatter.50
  1214.0 72.7 reduce-scatter.66
  1290.7 72.0 reduce-scatter.68
  1366.9 72.0 reduce-scatter.70
  1442.8 63.3 reduce-scatter.56
  1510.2 63.0 reduce-scatter.58
  1577.3 63.0 reduce-scatter.60
  1644.4 63.0 reduce-scatter.62
  1711.4 63.4 reduce-scatter.64
where the time goes:
time: 1790 us; the launch traced here: 1780 us
  waiting for transfers between devices  1120 us (63%)
  blocking collectives  307 us (17%)
  matrix products  209 us (12%)
  other arithmetic  63 us (4%)
  local copies, waits for them, and re-layouts  55 us (3%)
  between operations  26.8 us (1%)
    reduce_scatter x16, waiting for transfers between devices, summed(): return lax.psum_scatter(total, 'col', scatter_dimension=1, tiled=True)  412 us
    all_gather x8, blocking collectives, prefix_2(): gathered = jax.tree.map(lambda a: lax.all_gather(a, axis), part)  148 us
    all_gather x16, waiting for transfers between devices, spread(): return lax.all_gather(features, 'col', axis=1, tiled=True)  110 us
    reduce_scatter x1, waiting for transfers between devices, on_device(): lax.psum_scatter(totals[7], ('row', 'dp'), scatter_dimension=1, tiled=True)  76.2 us
    reduce_scatter x1, waiting for transfers between devices, on_device(): lax.psum_scatter(totals[6], ('row', 'dp'), scatter_dimension=0, tiled=True)  76 us
    reduce_scatter x1, waiting for transfers between devices, on_device(): lax.psum_scatter(totals[4], ('row', 'dp'), scatter_dimension=1, tiled=True)  67.4 us
    reduce_scatter x1, waiting for transfers between devices, on_device(): lax.psum_scatter(totals[0], ('row', 'dp'), scatter_dimension=0, tiled=True)  67.2 us
    reduce_scatter x1, waiting for transfers between devices, on_device(): lax.psum_scatter(totals[1], ('row', 'dp'), scatter_dimension=0, tiled=True)  67.1 us
  transfers between devices with their start and end apart: 43, of which 31 were waited for; matrix products, arithmetic and copies ran while one was open for 13% of the time, Pallas kernels for 0%

commit v1 on v0

v1 whole, which is shorter than its diff:
```python
import jax
import jax.numpy as jnp
from jax import lax
from jax.sharding import PartitionSpec as P

HEAD = 128
EPS = 1e-06
F32 = jnp.float32
BF16 = jnp.bfloat16


def swap(value, bits):
    count = lax.axis_size("col")
    return lax.ppermute(value, "col", [(i, i ^ bits) for i in range(count)])


def pair(value):
    return swap(value, 1)


def side(value):
    return swap(value, 2)


def shift(value, axis, by):
    count = lax.axis_size(axis)
    return lax.ppermute(value, axis, [(i, (i + by) % count) for i in range(count)])


def turned(value, dim, axis):
    count = lax.axis_size(axis)
    place = lax.axis_index(axis)
    back = jnp.flip(value, dim)
    both = jnp.concatenate([back, back], dim)
    return lax.dynamic_slice_in_dim(both, count - 1 - place, count, dim)


def reorder(rows):
    nz, ny = lax.axis_size("row"), lax.axis_size("dp")
    tokens, width = rows.shape
    split = rows.reshape(tokens, nz, ny, width // (nz * ny))
    return turned(turned(split, 1, "row"), 2, "dp").reshape(tokens, width)


def tokens_in(parts):
    col = lax.axis_index("col")
    got = [
        (lambda mine: mine if bits == 0 else swap(mine, bits))(
            lax.dynamic_index_in_dim(parts, col ^ bits, 0, False)
        )
        for bits in range(4)
    ]
    stack = jnp.stack(got)
    rows = [lax.dynamic_index_in_dim(stack, col ^ block, 0, False) for block in range(4)]
    return reorder(jnp.concatenate(rows, 1))


def tokens_out(rows):
    col = lax.axis_index("col")
    tokens, width = rows.shape
    blocks = reorder(rows).reshape(tokens, 4, width // 4)
    got = []
    for bits in range(4):
        mine = lax.dynamic_index_in_dim(blocks, col ^ bits, 1, False)
        got.append(mine if bits == 0 else swap(mine, bits))
    stack = jnp.stack(got)
    return jnp.stack(
        [lax.dynamic_index_in_dim(stack, col ^ micro, 0, False) for micro in range(4)]
    )


AXES = {"z": "row", "y": "dp"}


def gather_weight(shard, route):
    nz, ny = lax.axis_size("row"), lax.axis_size("dp")
    rows, width = shard.shape
    split = shard.reshape(ny, rows // ny, width)
    if "y" in route:
        value = lax.dynamic_index_in_dim(split, lax.axis_index("dp"), 0, False)
        dims = []
    else:
        value = turned(split, 0, "dp")
        dims = ["y"]
    values = [value]
    for step in route:
        if step == "x":
            values = [values[0], side(values[0])]
        else:
            axis = AXES[step]
            count = lax.axis_size(axis)
            values = [
                jnp.stack([v] + [shift(v, axis, k) for k in range(1, count)]) for v in values
            ]
            dims = [step] + dims
    if dims[0] == "y":
        values = [jnp.swapaxes(v, 0, 1) for v in values]
    return [v.reshape(nz * rows, width) for v in values]


def reduce_grad(own, other, route):
    nz, ny = lax.axis_size("row"), lax.axis_size("dp")
    depth, width = own.shape
    values = [v.reshape(nz, ny, depth // (nz * ny), width) for v in (own, other)]
    dims = ["z", "y"]
    for place, step in enumerate(route):
        last = place == len(route) - 1
        if step == "x":
            totals = [values[0].astype(F32) + side(values[1]).astype(F32)]
        else:
            axis = AXES[step]
            dim = dims.index(step)
            dims = dims[:dim] + dims[dim + 1 :]
            totals = []
            for v in values:
                pieces = [lax.index_in_dim(v, k, dim, False) for k in range(v.shape[dim])]
                total = pieces[0].astype(F32)
                for k in range(1, len(pieces)):
                    total = total + shift(pieces[k], axis, -k).astype(F32)
                totals.append(total)
        values = totals if last else [v.astype(BF16) for v in totals]
    return values[0]


def other_first(value):
    return jnp.flip(pair(value), 0)


def dot(left, right, form):
    return jnp.einsum(form, left, right, preferred_element_type=F32)


def silu_slope(pre):
    logistic = jax.nn.sigmoid(pre)
    return logistic * (1.0 + pre * (1.0 - logistic))


def chain(local, factor, reverse):
    count = lax.axis_size("row")
    entry = jnp.zeros_like(local)
    for hop in range(count - 1):
        out = (local + factor[:, :, None, None] * entry).astype(BF16)
        edge = (count - 1 - hop, count - 2 - hop) if reverse else (hop, hop + 1)
        entry = entry + lax.ppermute(out, "row", [edge]).astype(F32)
    return entry


def on_device(
    block_input,
    segments,
    decay_rate,
    w_query,
    w_key,
    w_value,
    w_output_gate,
    w_out,
    w_gate,
    w_up,
    w_down,
    out_grad,
):
    nz = lax.axis_size("row")
    col = lax.axis_index("col")
    place = lax.axis_index("row")
    tokens = block_input.shape[2]
    model = block_input.shape[3] * lax.axis_size("col")
    head_cols = w_query.shape[1]
    hidden = w_gate.shape[1]

    attn_a = gather_weight(jnp.concatenate([w_query, w_key], 1), "zxy")
    attn_b = gather_weight(jnp.concatenate([w_value, w_output_gate], 1), "zyx")
    out_w = gather_weight(w_out.T, "xz")
    gate_w = gather_weight(w_gate, "zxy")
    up_w = gather_weight(w_up, "zyx")
    down_w = gather_weight(w_down.T, "zxy")

    x_own = tokens_in(block_input[:, 0])
    g_own = tokens_in(out_grad[:, 0])
    rates = jnp.concatenate([decay_rate, side(decay_rate)])
    seg_all = segments[:, 0].astype(F32)
    seg = jnp.stack(
        [
            lax.dynamic_index_in_dim(seg_all, col, 0, False),
            lax.dynamic_index_in_dim(seg_all, col ^ 1, 0, False),
        ]
    )
    last = seg[:, tokens - 1]
    entry_seg = jnp.where(
        place == 0,
        -1.0,
        lax.ppermute(last, "row", [(i, i + 1) for i in range(nz - 1)]),
    )
    g_pair = jnp.stack([g_own, pair(g_own)]).reshape(2 * tokens, model)

    heads = rates.shape[0]
    places = jnp.arange(tokens).astype(F32)
    gaps = places[:, None] - places[None, :]
    visible = (gaps >= 0.0) & (seg[:, :, None] == seg[:, None, :])
    decay = jnp.where(
        visible[:, None],
        jnp.exp(-rates[:, None, None] * jnp.maximum(gaps, 0.0))[None],
        0.0,
    )
    own_weight = (seg == last[:, None]).astype(F32)[:, None, :] * jnp.exp(
        -rates[:, None] * (tokens - 1.0 - places)
    )
    entry_scale = (seg == entry_seg[:, None]).astype(F32)[:, None, :] * jnp.exp(
        -rates[:, None] * (places + 1.0)
    )
    linked = ((seg[:, 0] == last) & (entry_seg == last)).astype(F32)
    factor = linked[:, None] * jnp.exp(-rates * tokens)[None]

    x_wide = x_own.astype(F32)
    r1 = lax.rsqrt(jnp.mean(x_wide * x_wide, 1, keepdims=True) + EPS)
    a_own = (x_wide * r1).astype(BF16)
    a_pair = jnp.concatenate([a_own, pair(a_own)], 0)
    za = [dot(a_pair, w, "td,dc->tc") for w in attn_a]
    zb = [dot(a_pair, w, "td,dc->tc") for w in attn_b]
    zq = jnp.concatenate([z[:, :head_cols] for z in za], 1)
    zk = jnp.concatenate([z[:, head_cols:] for z in za], 1)
    zv = jnp.concatenate([z[:, :head_cols] for z in zb], 1)
    zu = jnp.concatenate([z[:, head_cols:] for z in zb], 1)

    def by_head(rows):
        return rows.reshape(2, tokens, heads, HEAD).transpose(0, 2, 1, 3)

    def by_row(value):
        return value.transpose(0, 2, 1, 3).reshape(2 * tokens, heads * HEAD)

    q = by_head(jax.nn.silu(zq).astype(BF16))
    k = by_head(jax.nn.silu(zk).astype(BF16))
    v = by_head(zv.astype(BF16))
    gate = jax.nn.sigmoid(zu)
    k_state = (k.astype(F32) * own_weight[..., None]).astype(BF16)
    local = dot(k_state, v, "bhse,bhsf->bhef")
    entry = chain(local, factor, False).astype(BF16)
    scores = dot(q, k, "bhte,bhse->bhts")
    mix = (scores * decay).astype(BF16)
    o = dot(mix, v, "bhts,bhsf->bhtf") + entry_scale[..., None] * dot(
        q, entry, "bhte,bhef->bhtf"
    )
    o = by_row(o)
    squares = jnp.sum(o * o, 1).reshape(2, tokens)
    squares = (squares + other_first(squares)).reshape(2 * tokens, 1)
    r2 = lax.rsqrt(squares / model + EPS)
    normed = o * r2
    y = (normed * gate).astype(BF16)
    y_x = [y[:, : y.shape[1] // 2], y[:, y.shape[1] // 2 :]]

    def back_sum(parts):
        total = parts.reshape(2, tokens, model)
        return total[0] + pair(total[1].astype(BF16)).astype(F32)

    h_part = dot(y_x[0], out_w[0], "tc,dc->td") + dot(y_x[1], out_w[1], "tc,dc->td")
    hres = x_wide + back_sum(h_part)
    r3 = lax.rsqrt(jnp.mean(hres * hres, 1, keepdims=True) + EPS)
    b_own = (hres * r3).astype(BF16)
    b_pair = jnp.concatenate([b_own, pair(b_own)], 0)
    z1 = [dot(b_pair, w, "td,df->tf") for w in gate_w]
    z2 = [dot(b_pair, w, "td,df->tf") for w in up_w]
    m = [(p * s).astype(BF16) for p, s in zip(z1, z2)]
    out_part = dot(m[0], down_w[0], "tf,df->td") + dot(m[1], down_w[1], "tf,df->td")
    block_out = tokens_out((hres + back_sum(out_part)).astype(BF16))

    grad_down = [dot(g_pair, p, "td,tf->df").astype(BF16) for p in m]
    dm = [dot(g_pair, w, "td,df->tf") for w in down_w]
    dz1 = [(d * s).astype(BF16) for d, s in zip(dm, z2)]
    dz2 = [(d * p).astype(BF16) for d, p in zip(dm, z1)]
    grad_gate = [dot(b_pair, d, "td,tf->df").astype(BF16) for d in dz1]
    grad_up = [dot(b_pair, d, "td,tf->df").astype(BF16) for d in dz2]
    db_part = (
        dot(dz1[0], gate_w[0], "tf,df->td")
        + dot(dz1[1], gate_w[1], "tf,df->td")
        + dot(dz2[0], up_w[0], "tf,df->td")
        + dot(dz2[1], up_w[1], "tf,df->td")
    )
    db = back_sum(db_part)
    dh = (
        g_own.astype(F32)
        + r3 * db
        - hres * (r3**3 * jnp.mean(db * hres, 1, keepdims=True))
    )
    dhr_own = dh.astype(BF16)
    dhr = jnp.concatenate([dhr_own, pair(dhr_own)], 0)

    grad_out = [dot(dhr, p, "td,tc->dc").astype(BF16) for p in y_x]
    dy = jnp.concatenate([dot(dhr, w, "td,dc->tc") for w in out_w], 1)
    dn = dy * gate
    dzu = (dy * normed * gate * (1.0 - gate)).astype(BF16)
    dots = jnp.sum(dn * o, 1).reshape(2, tokens)
    dots = (dots + other_first(dots)).reshape(2 * tokens, 1)
    do = by_head((r2 * dn - o * (r2**3 * dots / model)).astype(BF16))
    do_scaled = (do.astype(F32) * entry_scale[..., None]).astype(BF16)
    d_entry = dot(q, do_scaled, "bhte,bhtf->bhef")
    d_local = chain(d_entry, factor, True).astype(BF16)
    ds = (dot(do, v, "bhtf,bhsf->bhts") * decay).astype(BF16)
    dq = dot(ds, k, "bhts,bhse->bhte") + dot(do_scaled, entry, "bhtf,bhef->bhte")
    dk = dot(ds, q, "bhts,bhte->bhse") + own_weight[..., None] * dot(
        v, d_local, "bhsf,bhef->bhse"
    )
    dv = dot(mix, do, "bhts,bhtf->bhsf") + dot(k_state, d_local, "bhse,bhef->bhsf")
    dzq = (by_row(dq) * silu_slope(zq)).astype(BF16)
    dzk = (by_row(dk) * silu_slope(zk)).astype(BF16)
    dzv = by_row(dv).astype(BF16)

    def halves(value):
        return value[:, :head_cols], value[:, head_cols:]

    dza = [jnp.concatenate(p, 1) for p in zip(halves(dzq), halves(dzk))]
    dzb = [jnp.concatenate(p, 1) for p in zip(halves(dzv), halves(dzu))]
    grad_a = [dot(a_pair, d, "td,tc->dc").astype(BF16) for d in dza]
    grad_b = [dot(a_pair, d, "td,tc->dc").astype(BF16) for d in dzb]
    da_part = (
        dot(dza[0], attn_a[0], "tc,dc->td")
        + dot(dza[1], attn_a[1], "tc,dc->td")
        + dot(dzb[0], attn_b[0], "tc,dc->td")
        + dot(dzb[1], attn_b[1], "tc,dc->td")
    )
    da = back_sum(da_part)
    input_grad = tokens_out(
        (
            dh + r1 * da - x_wide * (r1**3 * jnp.mean(da * x_wide, 1, keepdims=True))
        ).astype(BF16)
    )

    total_down = reduce_grad(*grad_down, "xyz")
    total_gate = reduce_grad(*grad_gate, "yxz")
    total_up = reduce_grad(*grad_up, "xzy")
    total_out = reduce_grad(*grad_out, "yzx")
    total_a = reduce_grad(*grad_a, "xyz")
    total_b = reduce_grad(*grad_b, "yxz")
    return (
        block_out[:, None],
        input_grad[:, None],
        total_a[:, :head_cols],
        total_a[:, head_cols:],
        total_b[:, :head_cols],
        total_b[:, head_cols:],
        total_out.T,
        total_gate,
        total_up,
        total_down.T,
    )


def solution(mesh):
    placed = (
        P(None, "dp", "row", "col"),
        P(None, "dp", "row"),
        P("col"),
        P("row", "col"),
        P("row", "col"),
        P("row", "col"),
        P("row", "col"),
        P("col", "row"),
        P("row", "col"),
        P("row", "col"),
        P("col", "row"),
        P(None, "dp", "row", "col"),
    )
    return jax.shard_map(
        on_device,
        mesh=mesh,
        in_specs=placed,
        out_specs=(
            P(None, "dp", "row", "col"),
            P(None, "dp", "row", "col"),
            P(("row", "dp"), "col"),
            P(("row", "dp"), "col"),
            P(("row", "dp"), "col"),
            P(("row", "dp"), "col"),
            P("col", ("row", "dp")),
            P(("row", "dp"), "col"),
            P(("row", "dp"), "col"),
            P("col", ("row", "dp")),
        ),
        check_vma=False,
    )
```

time: 1790 us -> 710 us (0.40)
  waiting for transfers between devices: 1120 us -> 157 us
  blocking collectives: 307 us -> 0 us
  starting transfers between devices: 2.51 us -> 131 us
  local copies, waits for them, and re-layouts: 55 us -> 182 us
  matrix products: 209 us -> 115 us
  other arithmetic: 63 us -> 112 us
  between operations: 26.8 us -> 3.7 us
    reduce_scatter x24 -> x0, waiting for transfers between devices: 959 us -> none  [the longest x16 412 us: summed(): return lax.psum_scatter(total, 'col', scatter_dimension=1, tiled=True)]
    all_gather x13 -> x0, blocking collectives: 227 us -> none  [the longest x8 148 us: prefix_2(): gathered = jax.tree.map(lambda a: lax.all_gather(a, axis), part)]
    ppermute x0 -> x101, waiting for transfers between devices: none -> 157 us  [the longest x59 105 us: shift(): lax.ppermute(value, axis, [(i, (i + by) % count) for i in range(count)])]
    all_gather x19 -> x0, waiting for transfers between devices: 149 us -> none  [the longest x16 110 us: spread(): return lax.all_gather(features, 'col', axis=1, tiled=True)]
    ppermute x0 -> x101, starting transfers between devices: none -> 131 us  [the longest x59 99.3 us: shift(): lax.ppermute(value, axis, [(i, (i + by) % count) for i in range(count)])]
    dot_general x144 -> x48, matrix products: 209 us -> 115 us  [dot(): return jnp.einsum(form, left, right, preferred_element_type=F32)]
    psum x9 -> x0, blocking collectives: 56 us -> none  [row_total(): return lax.psum(row_values, 'col')]
    reshape x0 -> x16, local copies, waits for them, and re-layouts: none -> 37.4 us  [the longest x7 18.5 us: reduce_grad(): v.reshape(nz, ny, depth // (nz * ny), width)]
  transfers between devices with their start and end apart: 43 -> 101, of which waited for: 31 -> 27; matrix products, arithmetic and copies ran while one was open for 13% -> 49% of each run, Pallas kernels for 0% -> 0%
where the time goes in v1:
time: 710 us; the launch traced here: 701 us
  local copies, waits for them, and re-layouts  182 us (26%)
  waiting for transfers between devices  157 us (22%)
  starting transfers between devices  131 us (18%)
  matrix products  115 us (16%)
  other arithmetic  112 us (16%)
    dot_general x48, matrix products, dot(): return jnp.einsum(form, left, right, preferred_element_type=F32)  115 us
    ppermute x59, waiting for transfers between devices, shift(): lax.ppermute(value, axis, [(i, (i + by) % count) for i in range(count)])  105 us
    ppermute x59, starting transfers between devices, shift(): lax.ppermute(value, axis, [(i, (i + by) % count) for i in range(count)])  99.3 us
    ppermute x35, waiting for transfers between devices, swap(): return lax.ppermute(value, 'col', [(i, i ^ bits) for i in range(count)])  41.8 us
    unnamed x358, local copies, waits for them, and re-layouts  29.6 us
    another operation x14, other arithmetic, gather_weight(): jnp.stack([v] + [shift(v, axis, k) for k in range(1, count)])  25.9 us
    ppermute x35, starting transfers between devices, swap(): return lax.ppermute(value, 'col', [(i, i ^ bits) for i in range(count)])  20 us
    reshape x7, local copies, waits for them, and re-layouts, reduce_grad(): v.reshape(nz, ny, depth // (nz * ny), width)  18.5 us
  transfers between devices with their start and end apart: 101, of which 27 were waited for; matrix products, arithmetic and copies ran while one was open for 49% of the time, Pallas kernels for 0%

profile of v1, /device:TPU:0, one launch (start us, length us, event | category | flops | bytes accessed | tf_op | source)
XLA Modules:
  0.0 700.9 jit_solution(8967072849147468742)
XLA Ops:
  58.9 5.2 collective-permute-done.23
  64.1 4.8 collective-permute-start.30
  68.9 11.0 %collective-permute-done.35 = bf16[128,704]{0,1:T(8,128)(2,1)S(1)} collective-permute-done((bf16[128,704]{0,1:T(8,128)(2,1)S(1)}, bf16[128,704]{0,1:T(8,128)(2,1)S(1)}, u32[]{:S(2)}, u32[]{:S(2)}) %collective-permute-start.35) | collective-permute-done | bytes 180256 | tf_op jit(solution)/shard_map/ppermute | solution.py:27
  83.2 4.2 collective-permute-done.31
  107.4 8.3 %collective-permute-done.9 = bf16[4,128,512]{2,1,0:T(8,128)(2,1)S(1)} collective-permute-done((bf16[4,128,512]{2,1,0:T(8,128)(2,1)S(1)}, bf16[4,128,512]{2,1,0:T(8,128)(2,1)S(1)}, u32[]{:S(2)}, u32[]{:S(2)}) %collective-permute-start.9) | collective-permute-done | bytes 524320 | tf_op jit(solution)/shard_map/ppermute | solution.py:27
  121.5 4.0 concatenate.133
  125.6 4.1 copy.223
  151.0 4.7 collective-permute-start.17
  156.3 3.9 collective-permute-done.17
  165.3 12.2 %collective-permute-start.27 = (bf16[2,128,256]{2,1,0:T(8,128)(2,1)}, bf16[2,128,256]{2,1,0:T(8,128)(2,1)S(1)}, u32[]{:S(2)}, u32[]{:S(2)}) collective-permute-start(bf16[2,128,256]{2,1,0:T(8,128)(2,1)} %collective-permute-done.24), channel_id=1, source_target_pairs={{0,24},{8,0},{16,8},{24,16},{1,25},{9,1},{17,9},{25,17},{2,26},{10... | collective-permute-start | bytes 393224 | tf_op jit(solution)/shard_map/ppermute | solution.py:27
  213.6 6.2 collective-permute-done.37
  228.7 11.9 %collective-permute-done.45 = bf16[4,128,704]{1,0,2:T(4,128)(2,1)} collective-permute-done((bf16[4,128,704]{1,0,2:T(4,128)(2,1)}, bf16[4,128,704]{1,0,2:T(4,128)(2,1)}, u32[]{:S(2)}, u32[]{:S(2)}) %collective-permute-start.45) | collective-permute-done | bytes 720928 | tf_op jit(solution)/shard_map/ppermute | solution.py:14
  243.6 7.0 collective-permute-done.41
  259.4 4.6 reshape.607
  267.3 4.8 reshape.609
  302.2 3.7 fusion.114
  315.9 3.8 fusion.137
  333.2 4.0 reshape.629
  339.1 5.2 reshape.648
  344.3 4.3 convolution_convert_fusion.2
  348.7 3.8 reshape.628
  355.3 3.8 fusion.138
  359.2 4.3 convolution_convert_fusion.5
  363.5 4.2 reshape.626
  367.7 5.3 fusion.139
  373.0 4.3 convolution_convert_fusion.4
  377.3 3.8 reshape.627
  399.8 4.9 fusion.20
  404.7 5.4 reshape.645
  418.7 5.2 fusion.122
  436.2 4.2 collective-permute-start.92
  442.6 6.6 collective-permute-done.92
  449.3 4.3 collective-permute-start.88
  453.6 21.3 %collective-permute-done.93 = bf16[2,128,704]{1,2,0:T(8,128)(2,1)S(1)} collective-permute-done((bf16[2,128,704]{1,2,0:T(8,128)(2,1)S(1)}, bf16[2,128,704]{1,2,0:T(8,128)(2,1)S(1)}, u32[]{:S(2)}, u32[]{:S(2)}) %collective-permute-start.93) | collective-permute-done | bytes 360480 | tf_op jit(solution)/shard_map/ppermute | solution.py:27
  474.9 4.7 collective-permute-start.90
  481.4 4.2 collective-permute-done.89
  503.9 4.6 reshape.631
  526.0 4.1 copy.262
  542.6 4.7 collective-permute-start.81
  557.6 8.5 %collective-permute-start.78 = (bf16[128,256]{0,1:T(8,128)(2,1)S(1)}, bf16[128,256]{0,1:T(8,128)(2,1)S(1)}, u32[]{:S(2)}, u32[]{:S(2)}) collective-permute-start(bf16[128,256]{0,1:T(8,128)(2,1)S(1)} %get-tuple-element.126), channel_id=1, source_target_pairs={{0,16},{8,24},{16,0},{24,8},{1,17},{9,25},{17,1},{25,9},{2,18},{10... | collective-permute-start | bytes 196616 | tf_op jit(solution)/shard_map/ppermute | solution.py:27
  568.3 8.8 %collective-permute-done.99 = bf16[128,704]{0,1:T(8,128)(2,1)S(1)} collective-permute-done((bf16[128,704]{0,1:T(8,128)(2,1)S(1)}, bf16[128,704]{0,1:T(8,128)(2,1)S(1)}, u32[]{:S(2)}, u32[]{:S(2)}) %collective-permute-start.99) | collective-permute-done | bytes 180256 | tf_op jit(solution)/shard_map/ppermute | solution.py:27
  580.3 6.5 collective-permute-done.60
  623.2 11.0 %collective-permute-done.65 = bf16[4,2,128,512]{3,2,0,1:T(8,128)(2,1)S(1)} collective-permute-done((bf16[4,2,128,512]{3,2,0,1:T(8,128)(2,1)S(1)}, bf16[4,2,128,512]{3,2,0,1:T(8,128)(2,1)S(1)}, u32[]{:S(2)}, u32[]{:S(2)}) %collective-permute-start.65) | collective-permute-done | bytes 1048608 | tf_op jit(solution)/shard_map/ppermute | solution.py:14
  657.2 6.1 collective-permute-done.74
  667.5 4.4 collective-permute-done.64
  673.1 4.1 collective-permute-done.49
  677.1 5.8 collective-permute-done.50
  690.9 8.9 %collective-permute-done.68 = bf16[128,512]{1,0:T(8,128)(2,1)S(1)} collective-permute-done((bf16[128,512]{1,0:T(8,128)(2,1)S(1)}, bf16[128,512]{1,0:T(8,128)(2,1)S(1)}, u32[]{:S(2)}, u32[]{:S(2)}) %collective-permute-start.68) | collective-permute-done | bytes 131104 | tf_op jit(solution)/shard_map/ppermute | solution.py:27
  (786 shorter events, 411.2 us)
Async XLA Ops:
  2.3 30.0 %collective-permute-start.4 = (bf16[128,512]{1,0:T(8,128)(2,1)}, bf16[128,512]{1,0:T(8,128)(2,1)}, u32[]{:S(2)}, u32[]{:S(2)}) collective-permute-start(bf16[128,512]{1,0:T(8,128)(2,1)} %fusion.191), channel_id=1, source_target_pairs={{0,8},{8,16},{16,24},{24,0},{1,9},{9,17},{17,25},{25,1},{2,10},{10... | collective-permute-start | bytes 393224 | tf_op jit(solution)/shard_map/ppermute | solution.py:27
  5.4 27.6 %collective-permute-start.5 = (bf16[128,512]{1,0:T(8,128)(2,1)}, bf16[128,512]{1,0:T(8,128)(2,1)}, u32[]{:S(2)}, u32[]{:S(2)}) collective-permute-start(bf16[128,512]{1,0:T(8,128)(2,1)} %fusion.191), channel_id=1, source_target_pairs={{0,16},{8,24},{16,0},{24,8},{1,17},{9,25},{17,1},{25,9},{2,18},{10... | collective-permute-start | bytes 393224 | tf_op jit(solution)/shard_map/ppermute | solution.py:27
  8.0 25.4 %collective-permute-start.6 = (bf16[128,512]{1,0:T(8,128)(2,1)}, bf16[128,512]{1,0:T(8,128)(2,1)}, u32[]{:S(2)}, u32[]{:S(2)}) collective-permute-start(bf16[128,512]{1,0:T(8,128)(2,1)} %fusion.191), channel_id=1, source_target_pairs={{0,24},{8,0},{16,8},{24,16},{1,25},{9,1},{17,9},{25,17},{2,26},{10... | collective-permute-start | bytes 393224 | tf_op jit(solution)/shard_map/ppermute | solution.py:27
  11.5 23.9 %collective-permute-start = (bf16[512,256]{1,0:T(8,128)(2,1)}, bf16[512,256]{1,0:T(8,128)(2,1)}, u32[]{:S(2)}, u32[]{:S(2)}) collective-permute-start(bf16[512,256]{1,0:T(8,128)(2,1)} %get-tuple-element.101), channel_id=1, source_target_pairs={{0,2},{2,0},{4,6},{6,4},{1,3},{3,1},{5,7},{7,5},{8,10},{10,8},{12,... | collective-permute-start | bytes 786440 | tf_op jit(solution)/shard_map/ppermute | solution.py:14
  53.5 26.4 %collective-permute-start.35 = (bf16[128,704]{0,1:T(8,128)(2,1)S(1)}, bf16[128,704]{0,1:T(8,128)(2,1)S(1)}, u32[]{:S(2)}, u32[]{:S(2)}) collective-permute-start(bf16[128,704]{0,1:T(8,128)(2,1)S(1)} %bitcast.562), channel_id=1, source_target_pairs={{0,16},{8,24},{16,0},{24,8},{1,17},{9,25},{17,1},{25,9},{2,18},{10... | collective-permute-start | bytes 540680 | tf_op jit(solution)/shard_map/ppermute | solution.py:27
  55.7 25.7 %collective-permute-start.36 = (bf16[128,704]{0,1:T(8,128)(2,1)S(1)}, bf16[128,704]{0,1:T(8,128)(2,1)S(1)}, u32[]{:S(2)}, u32[]{:S(2)}) collective-permute-start(bf16[128,704]{0,1:T(8,128)(2,1)S(1)} %bitcast.563), channel_id=1, source_target_pairs={{0,24},{8,0},{16,8},{24,16},{1,25},{9,1},{17,9},{25,17},{2,26},{10... | collective-permute-start | bytes 540680 | tf_op jit(solution)/shard_map/ppermute | solution.py:27
  57.9 37.3 %collective-permute-start.8 = (bf16[4,128,512]{2,1,0:T(8,128)(2,1)S(1)}, bf16[4,128,512]{2,1,0:T(8,128)(2,1)S(1)}, u32[]{:S(2)}, u32[]{:S(2)}) collective-permute-start(bf16[4,128,512]{2,1,0:T(8,128)(2,1)S(1)} %copy-done.135), channel_id=1, source_target_pairs={{0,4},{2,6},{4,0},{6,2},{1,5},{3,7},{5,1},{7,3},{8,12},{10,14},{12... | collective-permute-start | bytes 1572872 | tf_op jit(solution)/shard_map/ppermute | solution.py:14
  79.9 20.9 %collective-permute-start.7 = (bf16[4,128,512]{2,1,0:T(8,128)(2,1)S(1)}, bf16[4,128,512]{2,1,0:T(8,128)(2,1)S(1)}, u32[]{:S(2)}, u32[]{:S(2)}) collective-permute-start(bf16[4,128,512]{2,1,0:T(8,128)(2,1)S(1)} %copy-done.135), channel_id=1, source_target_pairs={{0,1},{1,0},{2,3},{3,2},{4,5},{5,4},{6,7},{7,6},{8,9},{9,8},{10,11... | collective-permute-start | bytes 1572872 | tf_op jit(solution)/shard_map/ppermute | solution.py:27
  81.4 34.6 %collective-permute-start.3 = (bf16[512,1024]{0,1:T(8,128)(2,1)S(1)}, bf16[512,1024]{0,1:T(8,128)(2,1)S(1)}, u32[]{:S(2)}, u32[]{:S(2)}) collective-permute-start(bf16[512,1024]{0,1:T(8,128)(2,1)S(1)} %fusion.13), channel_id=1, source_target_pairs={{0,2},{2,0},{4,6},{6,4},{1,3},{3,1},{5,7},{7,5},{8,10},{10,8},{12,... | collective-permute-start | bytes 3145736 | tf_op jit(solution)/shard_map/ppermute | solution.py:14
  100.8 90.6 %collective-permute-start.38 = (bf16[128,704]{0,1:T(8,128)(2,1)}, bf16[128,704]{0,1:T(8,128)(2,1)}, u32[]{:S(2)}, u32[]{:S(2)}) collective-permute-start(bf16[128,704]{0,1:T(8,128)(2,1)} %bitcast.488), channel_id=1, source_target_pairs={{0,8},{8,16},{16,24},{24,0},{1,9},{9,17},{17,25},{25,1},{2,10},{10... | collective-permute-start | bytes 540680 | tf_op jit(solution)/shard_map/ppermute | solution.py:27
  102.8 91.3 %collective-permute-start.39 = (bf16[128,704]{0,1:T(8,128)(2,1)}, bf16[128,704]{0,1:T(8,128)(2,1)}, u32[]{:S(2)}, u32[]{:S(2)}) collective-permute-start(bf16[128,704]{0,1:T(8,128)(2,1)} %bitcast.488), channel_id=1, source_target_pairs={{0,16},{8,24},{16,0},{24,8},{1,17},{9,25},{17,1},{25,9},{2,18},{10... | collective-permute-start | bytes 540680 | tf_op jit(solution)/shard_map/ppermute | solution.py:27
  106.2 72.0 %collective-permute-start.25 = (bf16[2,128,256]{2,1,0:T(8,128)(2,1)}, bf16[2,128,256]{2,1,0:T(8,128)(2,1)}, u32[]{:S(2)}, u32[]{:S(2)}) collective-permute-start(bf16[2,128,256]{2,1,0:T(8,128)(2,1)} %collective-permute-done.24), channel_id=1, source_target_pairs={{0,8},{8,16},{16,24},{24,0},{1,9},{9,17},{17,25},{25,1},{2,10},{10... | collective-permute-start | bytes 393224 | tf_op jit(solution)/shard_map/ppermute | solution.py:27
  115.8 62.6 %collective-permute-start.26 = (bf16[2,128,256]{2,1,0:T(8,128)(2,1)}, bf16[2,128,256]{2,1,0:T(8,128)(2,1)}, u32[]{:S(2)}, u32[]{:S(2)}) collective-permute-start(bf16[2,128,256]{2,1,0:T(8,128)(2,1)} %collective-permute-done.24), channel_id=1, source_target_pairs={{0,16},{8,24},{16,0},{24,8},{1,17},{9,25},{17,1},{25,9},{2,18},{10... | collective-permute-start | bytes 393224 | tf_op jit(solution)/shard_map/ppermute | solution.py:27
  116.0 25.2 %collective-permute-start.15 = (bf16[2,4,128,512]{3,2,0,1:T(8,128)(2,1)}, bf16[2,4,128,512]{3,2,0,1:T(8,128)(2,1)}, u32[]{:S(2)}, u32[]{:S(2)}) collective-permute-start(bf16[2,4,128,512]{3,2,0,1:T(8,128)(2,1)} %pad_maximum_fusion.11), channel_id=1, source_target_pairs={{0,4},{2,6},{4,0},{6,2},{1,5},{3,7},{5,1},{7,3},{8,12},{10,14},{12... | collective-permute-start | bytes 3145736 | tf_op jit(solution)/shard_map/ppermute | solution.py:14
  178.2 22.3 %collective-permute-start.40 = (bf16[128,704]{0,1:T(8,128)(2,1)}, bf16[128,704]{0,1:T(8,128)(2,1)}, u32[]{:S(2)}, u32[]{:S(2)}) collective-permute-start(bf16[128,704]{0,1:T(8,128)(2,1)} %bitcast.488), channel_id=1, source_target_pairs={{0,24},{8,0},{16,8},{24,16},{1,25},{9,1},{17,9},{25,17},{2,26},{10... | collective-permute-start | bytes 540680 | tf_op jit(solution)/shard_map/ppermute | solution.py:27
  178.3 27.6 %collective-permute-start.52 = (bf16[512,256]{1,0:T(8,128)(2,1)}, bf16[512,256]{1,0:T(8,128)(2,1)}, u32[]{:S(2)}, u32[]{:S(2)}) collective-permute-start(bf16[512,256]{1,0:T(8,128)(2,1)} %get-tuple-element.87), channel_id=1, source_target_pairs={{0,4},{2,6},{4,0},{6,2},{1,5},{3,7},{5,1},{7,3},{8,12},{10,14},{12... | collective-permute-start | bytes 786440 | tf_op jit(solution)/shard_map/ppermute | solution.py:14
  194.1 30.8 %collective-permute-start.28 = (bf16[512,1024]{0,1:T(8,128)(2,1)}, bf16[512,1024]{0,1:T(8,128)(2,1)}, u32[]{:S(2)}, u32[]{:S(2)}) collective-permute-start(bf16[512,1024]{0,1:T(8,128)(2,1)} %slice.523), channel_id=1, source_target_pairs={{0,2},{2,0},{4,6},{6,4},{1,3},{3,1},{5,7},{7,5},{8,10},{10,8},{12,... | collective-permute-start | bytes 3145736 | tf_op jit(solution)/shard_map/ppermute | solution.py:14
  206.4 34.8 %collective-permute-start.33 = (bf16[4,128,704]{1,0,2:T(4,128)(2,1)}, bf16[4,128,704]{1,0,2:T(4,128)(2,1)}, u32[]{:S(2)}, u32[]{:S(2)}) collective-permute-start(bf16[4,128,704]{1,0,2:T(4,128)(2,1)} %pad_maximum_fusion.21), channel_id=1, source_target_pairs={{0,1},{1,0},{2,3},{3,2},{4,5},{5,4},{6,7},{7,6},{8,9},{9,8},{10,11... | collective-permute-start | bytes 2162696 | tf_op jit(solution)/shard_map/ppermute | solution.py:27
  206.9 33.7 %collective-permute-start.45 = (bf16[4,128,704]{1,0,2:T(4,128)(2,1)}, bf16[4,128,704]{1,0,2:T(4,128)(2,1)}, u32[]{:S(2)}, u32[]{:S(2)}) collective-permute-start(bf16[4,128,704]{1,0,2:T(4,128)(2,1)} %pad_maximum_fusion.23), channel_id=1, source_target_pairs={{0,4},{2,6},{4,0},{6,2},{1,5},{3,7},{5,1},{7,3},{8,12},{10,14},{12... | collective-permute-start | bytes 2162696 | tf_op jit(solution)/shard_map/ppermute | solution.py:14
  219.8 30.8 %collective-permute-start.41 = (bf16[4,128,704]{1,0,2:T(4,128)(2,1)}, bf16[4,128,704]{1,0,2:T(4,128)(2,1)S(1)}, u32[]{:S(2)}, u32[]{:S(2)}) collective-permute-start(bf16[4,128,704]{1,0,2:T(4,128)(2,1)} %pad_maximum_fusion.23), channel_id=1, source_target_pairs={{0,1},{1,0},{2,3},{3,2},{4,5},{5,4},{6,7},{7,6},{8,9},{9,8},{10,11... | collective-permute-start | bytes 2162696 | tf_op jit(solution)/shard_map/ppermute | solution.py:27
  224.9 52.4 %collective-permute-start.54 = (bf16[512,1024]{0,1:T(8,128)(2,1)S(1)}, bf16[512,1024]{0,1:T(8,128)(2,1)}, u32[]{:S(2)}, u32[]{:S(2)}) collective-permute-start(bf16[512,1024]{0,1:T(8,128)(2,1)S(1)} %bitcast.497), channel_id=1, source_target_pairs={{0,2},{2,0},{4,6},{6,4},{1,3},{3,1},{5,7},{7,5},{8,10},{10,8},{12,... | collective-permute-start | bytes 3145736 | tf_op jit(solution)/shard_map/ppermute | solution.py:14
  226.8 69.8 %collective-permute-start.44 = (bf16[2,4,128,704]{2,1,3,0:T(4,128)(2,1)}, bf16[2,4,128,704]{2,1,3,0:T(4,128)(2,1)}, u32[]{:S(2)}, u32[]{:S(2)}) collective-permute-start(bf16[2,4,128,704]{2,1,3,0:T(4,128)(2,1)} %get-tuple-element.62), channel_id=1, source_target_pairs={{0,4},{2,6},{4,0},{6,2},{1,5},{3,7},{5,1},{7,3},{8,12},{10,14},{12... | collective-permute-start | bytes 4325384 | tf_op jit(solution)/shard_map/ppermute | solution.py:14
  240.6 61.6 %collective-permute-start.29 = (bf16[512,1024]{0,1:T(8,128)(2,1)}, bf16[512,1024]{0,1:T(8,128)(2,1)}, u32[]{:S(2)}, u32[]{:S(2)}) collective-permute-start(bf16[512,1024]{0,1:T(8,128)(2,1)} %multiply_convert_fusion.10), channel_id=1, source_target_pairs={{0,2},{2,0},{4,6},{6,4},{1,3},{3,1},{5,7},{7,5},{8,10},{10,8},{12,... | collective-permute-start | bytes 3145736 | tf_op jit(solution)/shard_map/ppermute | solution.py:14
  241.3 41.8 %collective-permute-start.43 = (bf16[4,128,704]{1,0,2:T(4,128)(2,1)}, bf16[4,128,704]{1,0,2:T(4,128)(2,1)}, u32[]{:S(2)}, u32[]{:S(2)}) collective-permute-start(bf16[4,128,704]{1,0,2:T(4,128)(2,1)} %collective-permute-done.42), channel_id=1, source_target_pairs={{0,1},{1,0},{2,3},{3,2},{4,5},{5,4},{6,7},{7,6},{8,9},{9,8},{10,11... | collective-permute-start | bytes 2162696 | tf_op jit(solution)/shard_map/ppermute | solution.py:27
  250.6 39.4 %collective-permute-start.46 = (bf16[4,128,704]{1,0,2:T(4,128)(2,1)}, bf16[4,128,704]{1,0,2:T(4,128)(2,1)}, u32[]{:S(2)}, u32[]{:S(2)}) collective-permute-start(bf16[4,128,704]{1,0,2:T(4,128)(2,1)} %collective-permute-done.45), channel_id=1, source_target_pairs={{0,1},{1,0},{2,3},{3,2},{4,5},{5,4},{6,7},{7,6},{8,9},{9,8},{10,11... | collective-permute-start | bytes 2162696 | tf_op jit(solution)/shard_map/ppermute | solution.py:27
  338.6 91.6 %collective-permute-start.96 = (bf16[4,2,128,704]{2,3,0,1:T(8,128)(2,1)}, bf16[4,2,128,704]{2,3,0,1:T(8,128)(2,1)}, u32[]{:S(2)}, u32[]{:S(2)}) collective-permute-start(bf16[4,2,128,704]{2,3,0,1:T(8,128)(2,1)} %copy.291), channel_id=1, source_target_pairs={{0,4},{2,6},{4,0},{6,2},{1,5},{3,7},{5,1},{7,3},{8,12},{10,14},{12... | collective-permute-start | bytes 4325384 | tf_op jit(solution)/shard_map/ppermute | solution.py:14
  353.8 80.2 %collective-permute-start.91 = (bf16[4,2,128,704]{2,3,1,0:T(8,128)(2,1)}, bf16[4,2,128,704]{2,3,1,0:T(8,128)(2,1)}, u32[]{:S(2)}, u32[]{:S(2)}) collective-permute-start(bf16[4,2,128,704]{2,3,1,0:T(8,128)(2,1)} %copy.289), channel_id=1, source_target_pairs={{0,4},{2,6},{4,0},{6,2},{1,5},{3,7},{5,1},{7,3},{8,12},{10,14},{12... | collective-permute-start | bytes 4325384 | tf_op jit(solution)/shard_map/ppermute | solution.py:14
  385.2 25.9 %collective-permute-start.86 = (bf16[4,128,704]{1,2,0:T(8,128)(2,1)}, bf16[4,128,704]{1,2,0:T(8,128)(2,1)}, u32[]{:S(2)}, u32[]{:S(2)}) collective-permute-start(bf16[4,128,704]{1,2,0:T(8,128)(2,1)} %bitcast.486), channel_id=1, source_target_pairs={{0,1},{1,0},{2,3},{3,2},{4,5},{5,4},{6,7},{7,6},{8,9},{9,8},{10,11... | collective-permute-start | bytes 2162696 | tf_op jit(solution)/shard_map/ppermute | solution.py:27
  389.0 29.7 %collective-permute-start.47 = (bf16[512,1024]{0,1:T(8,128)(2,1)}, bf16[512,1024]{0,1:T(8,128)(2,1)}, u32[]{:S(2)}, u32[]{:S(2)}) collective-permute-start(bf16[512,1024]{0,1:T(8,128)(2,1)} %slice.522), channel_id=1, source_target_pairs={{0,2},{2,0},{4,6},{6,4},{1,3},{3,1},{5,7},{7,5},{8,10},{10,8},{12,... | collective-permute-start | bytes 3145736 | tf_op jit(solution)/shard_map/ppermute | solution.py:14
  411.1 29.2 %collective-permute-start.85 = (bf16[4,128,704]{1,2,0:T(8,128)(2,1)}, bf16[4,128,704]{1,2,0:T(8,128)(2,1)}, u32[]{:S(2)}, u32[]{:S(2)}) collective-permute-start(bf16[4,128,704]{1,2,0:T(8,128)(2,1)} %bitcast.487), channel_id=1, source_target_pairs={{0,1},{1,0},{2,3},{3,2},{4,5},{5,4},{6,7},{7,6},{8,9},{9,8},{10,11... | collective-permute-start | bytes 2162696 | tf_op jit(solution)/shard_map/ppermute | solution.py:27
  414.7 25.7 %collective-permute-start.87 = (bf16[4,128,704]{1,2,0:T(8,128)(2,1)}, bf16[4,128,704]{1,2,0:T(8,128)(2,1)}, u32[]{:S(2)}, u32[]{:S(2)}) collective-permute-start(bf16[4,128,704]{1,2,0:T(8,128)(2,1)} %fusion.22), channel_id=1, source_target_pairs={{0,4},{2,6},{4,0},{6,2},{1,5},{3,7},{5,1},{7,3},{8,12},{10,14},{12... | collective-permute-start | bytes 2162696 | tf_op jit(solution)/shard_map/ppermute | solution.py:14
  424.0 63.3 %collective-permute-start.56 = (bf16[512,1024]{0,1:T(8,128)(2,1)}, bf16[512,1024]{0,1:T(8,128)(2,1)}, u32[]{:S(2)}, u32[]{:S(2)}) collective-permute-start(bf16[512,1024]{0,1:T(8,128)(2,1)} %get-tuple-element.32), channel_id=1, source_target_pairs={{0,2},{2,0},{4,6},{6,4},{1,3},{3,1},{5,7},{7,5},{8,10},{10,8},{12,... | collective-permute-start | bytes 3145736 | tf_op jit(solution)/shard_map/ppermute | solution.py:14
  433.4 104.4 %collective-permute-start.97 = (bf16[4,128,704]{1,2,0:T(8,128)(2,1)}, bf16[4,128,704]{1,2,0:T(8,128)(2,1)}, u32[]{:S(2)}, u32[]{:S(2)}) collective-permute-start(bf16[4,128,704]{1,2,0:T(8,128)(2,1)} %slice_bitcast_fusion), channel_id=1, source_target_pairs={{0,1},{1,0},{2,3},{3,2},{4,5},{5,4},{6,7},{7,6},{8,9},{9,8},{10,11... | collective-permute-start | bytes 2162696 | tf_op jit(solution)/shard_map/ppermute | solution.py:27
  440.4 34.6 %collective-permute-start.93 = (bf16[2,128,704]{1,2,0:T(8,128)(2,1)S(1)}, bf16[2,128,704]{1,2,0:T(8,128)(2,1)S(1)}, u32[]{:S(2)}, u32[]{:S(2)}) collective-permute-start(bf16[2,128,704]{1,2,0:T(8,128)(2,1)S(1)} %get-tuple-element.57), channel_id=1, source_target_pairs={{0,16},{8,24},{16,0},{24,8},{1,17},{9,25},{17,1},{25,9},{2,18},{10... | collective-permute-start | bytes 1081352 | tf_op jit(solution)/shard_map/ppermute | solution.py:27
  440.4 34.6 %collective-permute-start.94 = (bf16[2,128,704]{1,2,0:T(8,128)(2,1)S(1)}, bf16[2,128,704]{1,2,0:T(8,128)(2,1)S(1)}, u32[]{:S(2)}, u32[]{:S(2)}) collective-permute-start(bf16[2,128,704]{1,2,0:T(8,128)(2,1)S(1)} %get-tuple-element.56), channel_id=1, source_target_pairs={{0,8},{8,16},{16,24},{24,0},{1,9},{9,17},{17,25},{25,1},{2,10},{10... | collective-permute-start | bytes 1081352 | tf_op jit(solution)/shard_map/ppermute | solution.py:27
  449.3 30.6 %collective-permute-start.88 = (bf16[128,704]{0,1:T(8,128)(2,1)S(1)}, bf16[128,704]{0,1:T(8,128)(2,1)S(1)}, u32[]{:S(2)}, u32[]{:S(2)}) collective-permute-start(bf16[128,704]{0,1:T(8,128)(2,1)S(1)} %get-tuple-element.107), channel_id=1, source_target_pairs={{0,24},{8,0},{16,8},{24,16},{1,25},{9,1},{17,9},{25,17},{2,26},{10... | collective-permute-start | bytes 540680 | tf_op jit(solution)/shard_map/ppermute | solution.py:27
  490.4 57.5 %collective-permute-start.76 = (bf16[4,128,256]{1,2,0:T(8,128)(2,1)}, bf16[4,128,256]{1,2,0:T(8,128)(2,1)}, u32[]{:S(2)}, u32[]{:S(2)}) collective-permute-start(bf16[4,128,256]{1,2,0:T(8,128)(2,1)} %bitcast.154), channel_id=1, source_target_pairs={{0,1},{1,0},{2,3},{3,2},{4,5},{5,4},{6,7},{7,6},{8,9},{9,8},{10,11... | collective-permute-start | bytes 786440 | tf_op jit(solution)/shard_map/ppermute | solution.py:27
  495.9 45.7 %collective-permute-start.80 = (bf16[4,128,256]{1,2,0:T(8,128)(2,1)}, bf16[4,128,256]{1,2,0:T(8,128)(2,1)}, u32[]{:S(2)}, u32[]{:S(2)}) collective-permute-start(bf16[4,128,256]{1,2,0:T(8,128)(2,1)} %bitcast.161), channel_id=1, source_target_pairs={{0,1},{1,0},{2,3},{3,2},{4,5},{5,4},{6,7},{7,6},{8,9},{9,8},{10,11... | collective-permute-start | bytes 786440 | tf_op jit(solution)/shard_map/ppermute | solution.py:27
  521.8 29.1 %collective-permute-start.58 = (bf16[2,4,128,128]{3,2,1,0:T(8,128)(2,1)}, bf16[2,4,128,128]{3,2,1,0:T(8,128)(2,1)S(1)}, u32[]{:S(2)}, u32[]{:S(2)}) collective-permute-start(bf16[2,4,128,128]{3,2,1,0:T(8,128)(2,1)} %get-tuple-element.148), channel_id=1, source_target_pairs={{24,16},{25,17},{26,18},{27,19},{28,20},{29,21},{30,22},{31,23}} | collective-permute-start | bytes 786440 | tf_op jit(solution)/shard_map/ppermute | solution.py:144
  539.3 27.0 %collective-permute-start.100 = (bf16[128,704]{0,1:T(8,128)(2,1)S(1)}, bf16[128,704]{0,1:T(8,128)(2,1)S(1)}, u32[]{:S(2)}, u32[]{:S(2)}) collective-permute-start(bf16[128,704]{0,1:T(8,128)(2,1)S(1)} %get-tuple-element.105), channel_id=1, source_target_pairs={{0,8},{8,16},{16,24},{24,0},{1,9},{9,17},{17,25},{25,1},{2,10},{10... | collective-permute-start | bytes 540680 | tf_op jit(solution)/shard_map/ppermute | solution.py:27
  556.9 22.3 %collective-permute-start.77 = (bf16[128,256]{0,1:T(8,128)(2,1)S(1)}, bf16[128,256]{0,1:T(8,128)(2,1)S(1)}, u32[]{:S(2)}, u32[]{:S(2)}) collective-permute-start(bf16[128,256]{0,1:T(8,128)(2,1)S(1)} %get-tuple-element.124), channel_id=1, source_target_pairs={{0,24},{8,0},{16,8},{24,16},{1,25},{9,1},{17,9},{25,17},{2,26},{10... | collective-permute-start | bytes 196616 | tf_op jit(solution)/shard_map/ppermute | solution.py:27
  557.6 22.1 %collective-permute-start.78 = (bf16[128,256]{0,1:T(8,128)(2,1)S(1)}, bf16[128,256]{0,1:T(8,128)(2,1)S(1)}, u32[]{:S(2)}, u32[]{:S(2)}) collective-permute-start(bf16[128,256]{0,1:T(8,128)(2,1)S(1)} %get-tuple-element.126), channel_id=1, source_target_pairs={{0,16},{8,24},{16,0},{24,8},{1,17},{9,25},{17,1},{25,9},{2,18},{10... | collective-permute-start | bytes 196616 | tf_op jit(solution)/shard_map/ppermute | solution.py:27
  595.5 24.8 %collective-permute-start.71 = (bf16[4,128,512]{2,1,0:T(8,128)(2,1)}, bf16[4,128,512]{2,1,0:T(8,128)(2,1)}, u32[]{:S(2)}, u32[]{:S(2)}) collective-permute-start(bf16[4,128,512]{2,1,0:T(8,128)(2,1)} %slice_bitcast_fusion.2), channel_id=1, source_target_pairs={{0,1},{1,0},{2,3},{3,2},{4,5},{5,4},{6,7},{7,6},{8,9},{9,8},{10,11... | collective-permute-start | bytes 1572872 | tf_op jit(solution)/shard_map/ppermute | solution.py:27
  608.1 26.1 %collective-permute-start.65 = (bf16[4,2,128,512]{3,2,0,1:T(8,128)(2,1)S(1)}, bf16[4,2,128,512]{3,2,0,1:T(8,128)(2,1)S(1)}, u32[]{:S(2)}, u32[]{:S(2)}) collective-permute-start(bf16[4,2,128,512]{3,2,0,1:T(8,128)(2,1)S(1)} %copy.275), channel_id=1, source_target_pairs={{0,4},{2,6},{4,0},{6,2},{1,5},{3,7},{5,1},{7,3},{8,12},{10,14},{12... | collective-permute-start | bytes 3145736 | tf_op jit(solution)/shard_map/ppermute | solution.py:14
  618.3 29.0 %collective-permute-start.70 = (bf16[4,128,512]{2,1,0:T(8,128)(2,1)}, bf16[4,128,512]{2,1,0:T(8,128)(2,1)}, u32[]{:S(2)}, u32[]{:S(2)}) collective-permute-start(bf16[4,128,512]{2,1,0:T(8,128)(2,1)} %slice_bitcast_fusion.4), channel_id=1, source_target_pairs={{0,1},{1,0},{2,3},{3,2},{4,5},{5,4},{6,7},{7,6},{8,9},{9,8},{10,11... | collective-permute-start | bytes 1572872 | tf_op jit(solution)/shard_map/ppermute | solution.py:27
  622.3 25.1 %collective-permute-start.72 = (bf16[4,128,512]{2,1,0:T(8,128)(2,1)}, bf16[4,128,512]{2,1,0:T(8,128)(2,1)}, u32[]{:S(2)}, u32[]{:S(2)}) collective-permute-start(bf16[4,128,512]{2,1,0:T(8,128)(2,1)} %fusion.34), channel_id=1, source_target_pairs={{0,4},{2,6},{4,0},{6,2},{1,5},{3,7},{5,1},{7,3},{8,12},{10,14},{12... | collective-permute-start | bytes 1572872 | tf_op jit(solution)/shard_map/ppermute | solution.py:14
  635.4 48.8 %collective-permute-start.66 = (bf16[4,128,512]{2,1,0:T(8,128)(2,1)}, bf16[4,128,512]{2,1,0:T(8,128)(2,1)}, u32[]{:S(2)}, u32[]{:S(2)}) collective-permute-start(bf16[4,128,512]{2,1,0:T(8,128)(2,1)} %slice_bitcast_fusion.6), channel_id=1, source_target_pairs={{0,1},{1,0},{2,3},{3,2},{4,5},{5,4},{6,7},{7,6},{8,9},{9,8},{10,11... | collective-permute-start | bytes 1572872 | tf_op jit(solution)/shard_map/ppermute | solution.py:27
  644.6 21.6 %collective-permute-start.62 = (bf16[512,256]{1,0:T(8,128)(2,1)}, bf16[512,256]{1,0:T(8,128)(2,1)}, u32[]{:S(2)}, u32[]{:S(2)}) collective-permute-start(bf16[512,256]{1,0:T(8,128)(2,1)} %bitcast.126), channel_id=1, source_target_pairs={{0,2},{2,0},{4,6},{6,4},{1,3},{3,1},{5,7},{7,5},{8,10},{10,8},{12,... | collective-permute-start | bytes 786440 | tf_op jit(solution)/shard_map/ppermute | solution.py:14
  (225 other events, 2624.5 us)

commit v2 on v1

v2 whole, which is shorter than its diff:
```python
import functools

import jax
import jax.numpy as jnp
from jax import lax
from jax.experimental import pallas as pl
from jax.experimental.pallas import tpu as pltpu
from jax.sharding import PartitionSpec as P

HEAD = 128
TILE = 256
EPS = 1e-06
F32 = jnp.float32
BF16 = jnp.bfloat16


def swap(value, axis, bits):
    count = lax.axis_size(axis)
    return lax.ppermute(value, axis, [(i, i ^ bits) for i in range(count)])


def pair(value):
    return swap(value, "col", 1)


def side(value):
    return swap(value, "col", 2)


def bits_of(axis):
    return [1 << b for b in range(lax.axis_size(axis).bit_length() - 1)]


def xor_turn(value, dim, place, count):
    bit = 1
    while bit < count:
        shape = value.shape
        split = value.reshape(shape[:dim] + (count // (2 * bit), 2, bit) + shape[dim + 1 :])
        flipped = jnp.flip(split, dim + 1)
        value = jnp.where((place & bit) != 0, flipped, split).reshape(shape)
        bit *= 2
    return value


def to_order(rows):
    nz, ny = lax.axis_size("row"), lax.axis_size("dp")
    tokens, width = rows.shape
    split = rows.reshape(tokens, nz, ny, width // (nz * ny))
    split = xor_turn(split, 1, lax.axis_index("row"), nz)
    split = xor_turn(split, 2, lax.axis_index("dp"), ny)
    return split.transpose(0, 2, 1, 3).reshape(tokens, width)


def from_order(rows):
    nz, ny = lax.axis_size("row"), lax.axis_size("dp")
    tokens, width = rows.shape
    split = rows.reshape(tokens, ny, nz, width // (nz * ny)).transpose(0, 2, 1, 3)
    split = xor_turn(split, 1, lax.axis_index("row"), nz)
    split = xor_turn(split, 2, lax.axis_index("dp"), ny)
    return split.reshape(tokens, width)


def small_slice():
    return lax.axis_size("row") == 4 and lax.axis_size("dp") == 2


def place_bits():
    turn = lax.axis_index("col") ^ lax.axis_index("row")
    return jnp.stack([turn & 1, turn >> 1, lax.axis_index("dp"), 0]).astype(jnp.int32)


def pick4(parts, low, high):
    first = [jnp.where(low, parts[k ^ 1], parts[k]) for k in range(4)]
    return [jnp.where(high, first[k ^ 2], first[k]) for k in range(4)]


def assemble_kernel(norm, bits, *refs):
    parts = [r[...].astype(F32) for r in refs[:4]]
    blocks = pick4(parts, bits[0] != 0, bits[1] != 0)
    odd = bits[2] != 0
    halves = [[], []]
    for b in blocks:
        low, high = b[:, :HEAD], b[:, HEAD:]
        halves[0].append(jnp.where(odd, high, low))
        halves[1].append(jnp.where(odd, low, high))
    rows = jnp.concatenate(halves[0] + halves[1], 1)
    refs[4][...] = rows.astype(BF16)
    if norm:
        scale = lax.rsqrt(jnp.mean(rows * rows, 1, keepdims=True) + EPS)
        refs[5][...] = (rows * scale).astype(BF16)
        refs[6][...] = scale


def assemble(parts, norm):
    tokens, width = parts[0].shape
    model = 4 * width
    if not small_slice():
        col = lax.axis_index("col")
        blocks = pick4(parts, (col & 1) != 0, (col & 2) != 0)
        rows = to_order(jnp.concatenate(blocks, 1))
        if not norm:
            return rows
        wide = rows.astype(F32)
        scale = lax.rsqrt(jnp.mean(wide * wide, 1, keepdims=True) + EPS)
        return rows, (wide * scale).astype(BF16), scale
    step = 128
    row = lambda n: pl.BlockSpec((step, n), lambda i: (i, 0))
    shape = [jax.ShapeDtypeStruct((tokens, model), BF16)]
    specs = [row(model)]
    if norm:
        shape += [shape[0], jax.ShapeDtypeStruct((tokens, 1), F32)]
        specs += [row(model), row(1)]
    out = pl.pallas_call(
        functools.partial(assemble_kernel, norm),
        grid=(tokens // step,),
        in_specs=[pl.BlockSpec(memory_space=pltpu.SMEM)] + [row(width)] * 4,
        out_specs=specs,
        out_shape=shape,
        name="assemble",
    )(place_bits(), *parts)
    return out if norm else out[0]


def divide_kernel(bits, rows_ref, *refs):
    rows = rows_ref[...].astype(F32)
    odd = bits[2] != 0
    blocks = []
    for k in range(4):
        low = rows[:, k * HEAD : (k + 1) * HEAD]
        high = rows[:, (4 + k) * HEAD : (5 + k) * HEAD]
        blocks.append(
            jnp.concatenate([jnp.where(odd, high, low), jnp.where(odd, low, high)], 1)
        )
    for ref, block in zip(refs, pick4(blocks, bits[0] != 0, bits[1] != 0)):
        ref[...] = block.astype(BF16)


def divide(rows):
    tokens, model = rows.shape
    width = model // 4
    if not small_slice():
        col = lax.axis_index("col")
        whole = from_order(rows)
        blocks = [whole[:, k * width : (k + 1) * width] for k in range(4)]
        return pick4(blocks, (col & 1) != 0, (col & 2) != 0)
    step = 128
    row = lambda n: pl.BlockSpec((step, n), lambda i: (i, 0))
    return pl.pallas_call(
        divide_kernel,
        grid=(tokens // step,),
        in_specs=[pl.BlockSpec(memory_space=pltpu.SMEM), row(model)],
        out_specs=[row(width)] * 4,
        out_shape=[jax.ShapeDtypeStruct((tokens, width), BF16)] * 4,
        name="divide",
    )(place_bits(), rows)


def tokens_in(parts, norm):
    col = lax.axis_index("col")
    got = []
    for bits in range(4):
        mine = lax.dynamic_index_in_dim(parts, col ^ bits, 0, False)
        got.append(mine if bits == 0 else swap(mine, "col", bits))
    return assemble(got, norm)


def tokens_out(rows):
    col = lax.axis_index("col")
    parts = divide(rows)
    got = [parts[0]] + [swap(parts[bits], "col", bits) for bits in range(1, 4)]
    return jnp.stack(pick4(got, (col & 1) != 0, (col & 2) != 0))


def gather_weight(shard, order):
    ny = lax.axis_size("dp")
    rows, width = shard.shape
    part = rows // ny
    start = lax.axis_index("dp") * part
    value = lax.dynamic_slice_in_dim(shard, start, part, 0)
    for bit in bits_of("row"):
        value = jnp.concatenate([value, swap(value, "row", bit)], 0)
    if order == "yx":
        for bit in bits_of("dp"):
            value = jnp.concatenate([value, swap(value, "dp", bit)], 0)
        return [value, side(value)]
    values = [value, side(value)]
    for bit in bits_of("dp"):
        values = [jnp.concatenate([v, swap(v, "dp", bit)], 0) for v in values]
    return values


def fold(value, axis):
    for bit in reversed(bits_of(axis)):
        half = value.shape[0] // 2
        got = swap(value[half:].astype(BF16), axis, bit)
        value = value[:half].astype(F32) + got.astype(F32)
    return value


def reduce_grad(own, other, order):
    if order == "xy":
        value = own.astype(F32) + side(other).astype(F32)
        value = fold(value, "dp")
    else:
        own, other = fold(own, "dp"), fold(other, "dp")
        value = own + side(other.astype(BF16)).astype(F32)
    return fold(value, "row")


def dot(left, right, form):
    return jnp.einsum(form, left, right, preferred_element_type=F32)


def nn(a, b):
    return jnp.dot(a, b, preferred_element_type=F32)


def nt(a, b):
    return lax.dot_general(a, b, (((1,), (1,)), ((), ())), preferred_element_type=F32)


def tn(a, b):
    return lax.dot_general(a, b, (((0,), (0,)), ((), ())), preferred_element_type=F32)


def silu_slope(pre):
    logistic = jax.nn.sigmoid(pre)
    return logistic * (1.0 + pre * (1.0 - logistic))


def tile_decay(rate, seg_col, seg_row, at, width):
    rows = seg_col.shape[0]
    shape = (rows, width)
    gap = lax.broadcasted_iota(jnp.int32, shape, 0) + at - lax.broadcasted_iota(jnp.int32, shape, 1)
    visible = (gap >= 0) & (seg_col == seg_row)
    return jnp.where(visible, jnp.exp(-rate * jnp.maximum(gap, 0).astype(F32)), 0.0)


def column(tokens):
    return lax.broadcasted_iota(jnp.int32, (tokens, 1), 0).astype(F32)


def own_weight(rate, seg_col, last):
    tokens = seg_col.shape[0]
    return jnp.where(seg_col == last, jnp.exp(-rate * (tokens - 1.0 - column(tokens))), 0.0)


def entry_weight(rate, seg_col, entry_seg):
    tokens = seg_col.shape[0]
    return jnp.where(seg_col == entry_seg, jnp.exp(-rate * (column(tokens) + 1.0)), 0.0)


def first_kernel(rates, marks, seg_c, seg_r, zq, zk, zv, q_out, k_out, v_out, o_out, state):
    block, head = pl.program_id(0), pl.program_id(1)
    rate = rates[head]
    pre_q, pre_k = zq[...], zk[...]
    q = (pre_q * jax.nn.sigmoid(pre_q)).astype(BF16)
    k_wide = pre_k * jax.nn.sigmoid(pre_k)
    k = k_wide.astype(BF16)
    v = zv[...].astype(BF16)
    q_out[...], k_out[...], v_out[...] = q, k, v
    seg = seg_c[0]
    weight = own_weight(rate, seg, marks[block, 0])
    state[0, 0] = tn((k.astype(F32) * weight).astype(BF16), v)
    tokens = q.shape[0]
    for at in range(0, tokens, TILE):
        width = at + TILE
        decay = tile_decay(rate, seg[at:width], seg_r[0, :, :width], at, width)
        mix = (nt(q[at:width], k[:width]) * decay).astype(BF16)
        o_out[at:width, :] = nn(mix, v[:width])


def carry_kernel(rates, marks, seg_c, o_in, q, entry, o_out, squares):
    block, head = pl.program_id(0), pl.program_id(1)
    weight = entry_weight(rates[head], seg_c[0], marks[block, 1])
    o = o_in[...] + weight * nn(q[...], entry[0, 0])
    o_out[...] = o

    @pl.when(head == 0)
    def _():
        squares[...] = jnp.zeros_like(squares)

    squares[...] += jnp.sum(o * o, 1, keepdims=True)


def entry_grad_kernel(rates, marks, seg_c, q, do, grad):
    block, head = pl.program_id(0), pl.program_id(1)
    weight = entry_weight(rates[head], seg_c[0], marks[block, 1])
    grad[0, 0] = tn(q[...], (do[...].astype(F32) * weight).astype(BF16))


def inner_grad_kernel(
    rates, marks, seg_c, seg_r, q_ref, k_ref, v_ref, do_ref, entry, zq, dzq, dk, dv
):
    block, head = pl.program_id(0), pl.program_id(1)
    rate = rates[head]
    seg = seg_c[0]
    weight = entry_weight(rate, seg, marks[block, 1])
    tokens = seg.shape[0]
    for at in range(0, tokens, TILE):
        width = at + TILE
        q, do = q_ref[at:width, :], do_ref[at:width, :]
        k, v = k_ref[:width, :], v_ref[:width, :]
        decay = tile_decay(rate, seg[at:width], seg_r[0, :, :width], at, width)
        mix = (nt(q, k) * decay).astype(BF16)
        ds = (nt(do, v) * decay).astype(BF16)
        scaled = (do.astype(F32) * weight[at:width]).astype(BF16)
        dq = nn(ds, k) + nt(scaled, entry[0, 0])
        dzq[at:width, :] = (dq * silu_slope(zq[at:width, :])).astype(BF16)
        dk_new, dv_new = tn(ds, q), tn(mix, do)
        if at:
            dk[:at, :] += dk_new[:at]
            dv[:at, :] += dv_new[:at]
        dk[at:width, :] = dk_new[at:]
        dv[at:width, :] = dv_new[at:]


def last_grad_kernel(rates, marks, seg_c, k, v, d_state, zk, dk, dv, dzk, dzv):
    block, head = pl.program_id(0), pl.program_id(1)
    weight = own_weight(rates[head], seg_c[0], marks[block, 0])
    state = d_state[0, 0]
    dk_all = dk[...] + weight * nt(v[...], state)
    dzk[...] = (dk_all * silu_slope(zk[...])).astype(BF16)
    scaled = (k[...].astype(F32) * weight).astype(BF16)
    dzv[...] = (dv[...] + nn(scaled, state)).astype(BF16)


def head_call(kernel, tokens, heads, kinds_in, kinds_out, args, flops, name):
    specs = {
        "s": pl.BlockSpec(memory_space=pltpu.SMEM),
        "c": pl.BlockSpec((1, tokens, 1), lambda b, h: (b, 0, 0)),
        "r": pl.BlockSpec((1, 1, tokens), lambda b, h: (b, 0, 0)),
        "t": pl.BlockSpec((tokens, HEAD), lambda b, h: (b, h)),
        "p": pl.BlockSpec((1, 1, HEAD, HEAD), lambda b, h: (b, h, 0, 0)),
        "n": pl.BlockSpec((tokens, 1), lambda b, h: (b, 0)),
    }
    shapes = {
        "T": jax.ShapeDtypeStruct((2 * tokens, heads * HEAD), F32),
        "t": jax.ShapeDtypeStruct((2 * tokens, heads * HEAD), BF16),
        "p": jax.ShapeDtypeStruct((2, heads, HEAD, HEAD), F32),
        "n": jax.ShapeDtypeStruct((2 * tokens, 1), F32),
    }
    return pl.pallas_call(
        kernel,
        grid=(2, heads),
        in_specs=[specs[k.lower()] for k in kinds_in],
        out_specs=[specs[k.lower()] for k in kinds_out],
        out_shape=[shapes[k] for k in kinds_out],
        cost_estimate=pl.CostEstimate(flops=flops, bytes_accessed=8 << 20, transcendentals=0),
        name=name,
    )(*args)


def chain(local, factor, reverse):
    count = lax.axis_size("row")
    entry = jnp.zeros(local.shape, BF16)
    for hop in range(count - 1):
        out = (local + factor[:, :, None, None] * entry.astype(F32)).astype(BF16)
        edge = (count - 1 - hop, count - 2 - hop) if reverse else (hop, hop + 1)
        entry = entry + lax.ppermute(out, "row", [edge])
    return entry


def other_first(value):
    return jnp.flip(pair(value), 0)


def on_device(
    block_input,
    segments,
    decay_rate,
    w_query,
    w_key,
    w_value,
    w_output_gate,
    w_out,
    w_gate,
    w_up,
    w_down,
    out_grad,
):
    nz = lax.axis_size("row")
    col = lax.axis_index("col")
    place = lax.axis_index("row")
    tokens = block_input.shape[2]
    model = block_input.shape[3] * lax.axis_size("col")
    wide = w_query.shape[1]

    parts = gather_weight(jnp.concatenate([w_query, w_key], 1), "xy")
    wq = jnp.concatenate([w[:, :wide] for w in parts], 1)
    wk = jnp.concatenate([w[:, wide:] for w in parts], 1)
    parts = gather_weight(jnp.concatenate([w_value, w_output_gate], 1), "yx")
    wv = jnp.concatenate([w[:, :wide] for w in parts], 1)
    wu = jnp.concatenate([w[:, wide:] for w in parts], 1)
    wo = jnp.concatenate(gather_weight(w_out.T, "xy"), 1)
    down_w = gather_weight(w_down.T, "xy")
    gate_w = gather_weight(w_gate, "yx")
    up_w = gather_weight(w_up, "xy")

    x_own, a_own, r1 = tokens_in(block_input[:, 0], True)
    g_own = tokens_in(out_grad[:, 0], False)
    rates = jnp.concatenate([decay_rate, side(decay_rate)])
    heads = rates.shape[0]
    seg_all = segments[:, 0].astype(F32)
    seg = jnp.stack(
        [
            lax.dynamic_index_in_dim(seg_all, col, 0, False),
            lax.dynamic_index_in_dim(seg_all, col ^ 1, 0, False),
        ]
    )
    last = seg[:, tokens - 1]
    before = lax.ppermute(last, "row", [(i, i + 1) for i in range(nz - 1)])
    entry_seg = jnp.where(place == 0, -1.0, before)
    linked = ((seg[:, 0] == last) & (entry_seg == last)).astype(F32)
    factor = linked[:, None] * jnp.exp(-rates * tokens)[None]
    marks = jnp.stack([last, entry_seg], 1)
    seg_c, seg_r = seg[:, :, None], seg[:, None, :]
    heads_of = functools.partial(head_call, tokens=tokens, heads=heads)
    unit = 2 * heads * 2 * tokens * tokens * HEAD

    def both(own):
        return jnp.concatenate([own, pair(own)], 0)

    def back_sum(lefts, rights, form):
        def total(rows):
            out = dot(lefts[0][rows], rights[0], form)
            for left, right in zip(lefts[1:], rights[1:]):
                out = out + dot(left[rows], right, form)
            return out

        sent = pair(total(slice(tokens, None)).astype(BF16))
        return total(slice(0, tokens)) + sent.astype(F32)

    a = both(a_own)
    g = both(g_own)
    zq, zk, zv, zu = [dot(a, w, "td,dc->tc") for w in (wq, wk, wv, wu)]
    q, k, v, o_inner, local = heads_of(
        first_kernel,
        kinds_in="sscrTTT",
        kinds_out="tttTp",
        args=(rates, marks, seg_c, seg_r, zq, zk, zv),
        flops=unit,
        name="mixer_first",
    )
    entry = chain(local, factor, False)
    o, squares = heads_of(
        carry_kernel,
        kinds_in="sscTtp",
        kinds_out="Tn",
        args=(rates, marks, seg_c, o_inner, q, entry),
        flops=unit // 8,
        name="mixer_carry",
    )
    gate = jax.nn.sigmoid(zu)
    squares = squares.reshape(2, tokens)
    squares = (squares + other_first(squares)).reshape(2 * tokens, 1)
    r2 = lax.rsqrt(squares / model + EPS)
    y = (o * r2 * gate).astype(BF16)
    hres = x_own.astype(F32) + back_sum((y,), (wo,), "tc,dc->td")
    r3 = lax.rsqrt(jnp.mean(hres * hres, 1, keepdims=True) + EPS)
    b = both((hres * r3).astype(BF16))
    z1 = [dot(b, w, "td,df->tf") for w in gate_w]
    z2 = [dot(b, w, "td,df->tf") for w in up_w]
    m = [(p * s).astype(BF16) for p, s in zip(z1, z2)]
    block_out = tokens_out((hres + back_sum(m, down_w, "tf,df->td")).astype(BF16))

    grad_down = [dot(g, p, "td,tf->df").astype(BF16) for p in m]
    dm = [dot(g, w, "td,df->tf") for w in down_w]
    dz1 = [(d * s).astype(BF16) for d, s in zip(dm, z2)]
    dz2 = [(d * p).astype(BF16) for d, p in zip(dm, z1)]
    grad_gate = [dot(b, d, "td,tf->df").astype(BF16) for d in dz1]
    grad_up = [dot(b, d, "td,tf->df").astype(BF16) for d in dz2]
    db = back_sum(dz1 + dz2, gate_w + up_w, "tf,df->td")
    dh = (
        g_own.astype(F32)
        + r3 * db
        - hres * (r3**3 * jnp.mean(db * hres, 1, keepdims=True))
    )
    dhr = both(dh.astype(BF16))

    grad_out = dot(dhr, y, "td,tc->dc").astype(BF16)
    dy = dot(dhr, wo, "td,dc->tc")
    dn = dy * gate
    dzu = (dy * o * r2 * gate * (1.0 - gate)).astype(BF16)
    dots = jnp.sum(dn * o, 1).reshape(2, tokens)
    dots = (dots + other_first(dots)).reshape(2 * tokens, 1)
    do = (r2 * dn - o * (r2**3 * dots / model)).astype(BF16)
    (d_entry,) = heads_of(
        entry_grad_kernel,
        kinds_in="ssctt",
        kinds_out="p",
        args=(rates, marks, seg_c, q, do),
        flops=unit // 8,
        name="mixer_entry_grad",
    )
    d_local = chain(d_entry, factor, True)
    dzq, dk, dv = heads_of(
        inner_grad_kernel,
        kinds_in="sscrttttpT",
        kinds_out="tTT",
        args=(rates, marks, seg_c, seg_r, q, k, v, do, entry, zq),
        flops=5 * unit // 2,
        name="mixer_inner_grad",
    )
    dzk, dzv = heads_of(
        last_grad_kernel,
        kinds_in="sscttpTTT",
        kinds_out="tt",
        args=(rates, marks, seg_c, k, v, d_local, zk, dk, dv),
        flops=unit // 4,
        name="mixer_last_grad",
    )
    grads = [dot(a, d, "td,tc->dc").astype(BF16) for d in (dzq, dzk, dzv, dzu)]
    da = back_sum((dzq, dzk, dzv, dzu), (wq, wk, wv, wu), "tc,dc->td")
    x_wide = x_own.astype(F32)
    input_grad = tokens_out(
        (
            dh + r1 * da - x_wide * (r1**3 * jnp.mean(da * x_wide, 1, keepdims=True))
        ).astype(BF16)
    )

    def halves(*mats):
        return [
            jnp.concatenate([g[:, at : at + wide] for g in mats], 1) for at in (0, wide)
        ]

    total_down = reduce_grad(*grad_down, "xy")
    total_gate = reduce_grad(*grad_gate, "yx")
    total_up = reduce_grad(*grad_up, "xy")
    total_ou = reduce_grad(*halves(grad_out, grads[3]), "yx")
    total_qk = reduce_grad(*halves(grads[0], grads[1]), "xy")
    total_v = reduce_grad(*halves(grads[2]), "yx")
    return (
        block_out[:, None],
        input_grad[:, None],
        total_qk[:, :wide],
        total_qk[:, wide:],
        total_v,
        total_ou[:, wide:],
        total_ou[:, :wide].T,
        total_gate,
        total_up,
        total_down.T,
    )


def solution(mesh):
    placed = (
        P(None, "dp", "row", "col"),
        P(None, "dp", "row"),
        P("col"),
        P("row", "col"),
        P("row", "col"),
        P("row", "col"),
        P("row", "col"),
        P("col", "row"),
        P("row", "col"),
        P("row", "col"),
        P("col", "row"),
        P(None, "dp", "row", "col"),
    )
    return jax.shard_map(
        on_device,
        mesh=mesh,
        in_specs=placed,
        out_specs=(
            P(None, "dp", "row", "col"),
            P(None, "dp", "row", "col"),
            P(("row", "dp"), "col"),
            P(("row", "dp"), "col"),
            P(("row", "dp"), "col"),
            P(("row", "dp"), "col"),
            P("col", ("row", "dp")),
            P(("row", "dp"), "col"),
            P(("row", "dp"), "col"),
            P("col", ("row", "dp")),
        ),
        check_vma=False,
    )
```

time: 710 us -> 612 us (0.86)
  local copies, waits for them, and re-layouts: 182 us -> 30.6 us
  waiting for transfers between devices: 157 us -> 261 us
  other arithmetic: 112 us -> 48.1 us
  Pallas kernels: 0 us -> 57.1 us
  starting transfers between devices: 131 us -> 95.5 us
    ppermute x101 -> x85, waiting for transfers between devices: 157 us -> 261 us  [the longest x78 252 us: swap(): return lax.ppermute(value, axis, [(i, i ^ bits) for i in range(count)])]
    pallas_call x0 -> x9, Pallas kernels: none -> 57.1 us  [the longest x5 42.6 us: head_call(): pl.pallas_call(kernel, grid=(2, heads), in_specs=[specs[k.lower()] for k...]
    reshape x16 -> x2, local copies, waits for them, and re-layouts: 37.4 us -> 0.02 us  [the longest x1 0.01 us: on_device(): squares = squares.reshape(2, tokens)]
    ppermute x101 -> x85, starting transfers between devices: 131 us -> 95.5 us  [the longest x78 87.5 us: swap(): return lax.ppermute(value, axis, [(i, i ^ bits) for i in range(count)])]
    another operation x20 -> x5, other arithmetic: 32.1 us -> 2.55 us  [the longest x2 1.29 us: tokens_out(): return jnp.stack(pick4(got, col & 1 != 0, col & 2 != 0))]
    convert_element_type x27 -> x12, other arithmetic: 28.8 us -> 11.3 us  [the longest x1 4.23 us: on_device(): do = (r2 * dn - o * (r2 ** 3 * dots / model)).astype(BF16)]
    transpose x8 -> x1, local copies, waits for them, and re-layouts: 17.1 us -> 0.67 us  [on_device(): total_ou[:, :wide]]
    dynamic_slice x29 -> x4, local copies, waits for them, and re-layouts: 15 us -> 0.07 us  [gather_weight(): value = lax.dynamic_slice_in_dim(shard, start, part, 0)]
  transfers between devices with their start and end apart: 101 -> 85, of which waited for: 27 -> 33; matrix products, arithmetic and copies ran while one was open for 49% -> 28% of each run, Pallas kernels for 0% -> 8%
where the time goes in v2:
time: 612 us; the launch traced here: 603 us
  waiting for transfers between devices  261 us (43%)
  matrix products  109 us (18%)
  starting transfers between devices  95.5 us (16%)
  Pallas kernels  57.1 us (9%)
  other arithmetic  48.1 us (8%)
  local copies, waits for them, and re-layouts  30.6 us (5%)
    ppermute x78, waiting for transfers between devices, swap(): return lax.ppermute(value, axis, [(i, i ^ bits) for i in range(count)])  252 us
    dot_general x44, matrix products, dot(): return jnp.einsum(form, left, right, preferred_element_type=F32)  109 us
    ppermute x78, starting transfers between devices, swap(): return lax.ppermute(value, axis, [(i, i ^ bits) for i in range(count)])  87.5 us
    pallas_call x5, Pallas kernels, head_call(): pl.pallas_call(kernel, grid=(2, heads), in_specs=[specs[k.lower()] for k...  42.6 us
    unnamed x229, local copies, waits for them, and re-layouts  15.3 us
  transfers between devices with their start and end apart: 85, of which 33 were waited for; matrix products, arithmetic and copies ran while one was open for 28% of the time, Pallas kernels for 8%

profile of v2, /device:TPU:0, one launch (start us, length us, event | category | flops | bytes accessed | tf_op | source)
XLA Modules:
  0.0 603.5 jit_solution(11760382954080545573)
XLA Ops:
  19.5 3.2 collective-permute-start.7
  23.4 12.8 %collective-permute-done.12 = bf16[256,512]{1,0:T(8,128)(2,1)S(1)} collective-permute-done((bf16[256,512]{1,0:T(8,128)(2,1)S(1)}, bf16[256,512]{1,0:T(8,128)(2,1)S(1)}, u32[]{:S(2)}, u32[]{:S(2)}) %collective-permute-start.12) | collective-permute-done | bytes 262176 | tf_op jit(solution)/shard_map/ppermute | solution.py:19
  37.8 3.3 collective-permute-done.7
  45.4 3.8 assemble.2
  50.5 5.5 collective-permute-done.13
  60.2 7.0 %collective-permute-done.8 = bf16[512,512]{1,0:T(8,128)(2,1)} collective-permute-done((bf16[512,512]{1,0:T(8,128)(2,1)S(1)}, bf16[512,512]{1,0:T(8,128)(2,1)}, u32[]{:S(2)}, u32[]{:S(2)}) %collective-permute-start.8) | collective-permute-done | bytes 524320 | tf_op jit(solution)/shard_map/ppermute | solution.py:19
  69.4 7.3 %collective-permute-done.10 = bf16[512,512]{1,0:T(8,128)(2,1)S(1)} collective-permute-done((bf16[512,512]{1,0:T(8,128)(2,1)S(1)}, bf16[512,512]{1,0:T(8,128)(2,1)S(1)}, u32[]{:S(2)}, u32[]{:S(2)}) %collective-permute-start.10) | collective-permute-done | bytes 524320 | tf_op jit(solution)/shard_map/ppermute | solution.py:19
  84.8 9.6 %mixer_first.1 = (bf16[1024,512]{1,0:T(8,128)(2,1)}, bf16[1024,512]{1,0:T(8,128)(2,1)}, bf16[1024,512]{1,0:T(8,128)(2,1)}, f32[1024,512]{1,0:T(8,128)}, f32[2,4,128,128]{3,2,1,0:T(8,128)}) custom-call(f32[4]{0:T(128)} %get-tuple-element.85.rates, f32[2,2]{1,0:T(2,128)} %pad_maximum_fusion.42.marks, f32[2,512,1]{2,1,0:T(8,128)} %copy.36.seg_c, ...), custom_call_target="tpu_custom_call" | custom-call | flops 536870912 | bytes 8388608 | tf_op jit(solution)/shard_map/mixer_first/pallas_call | solution.py:343
  97.1 4.5 collective-permute-done.15
  110.0 5.7 collective-permute-start.26
  120.8 7.0 %mixer_carry.1 = (f32[1024,512]{1,0:T(8,128)}, f32[1024,1]{1,0:T(8,128)}) custom-call(f32[4]{0:T(128)} %get-tuple-element.85.rates, f32[2,2]{1,0:T(2,128)} %pad_maximum_fusion.42.marks, f32[2,512,1]{2,1,0:T(8,128)} %copy.36.seg_c, f32[1024,512]{1,0:T(8,128)} %get-tuple-element.35.o_in, bf16[1024,512]{1,0:T(8,128)(2,1)} %get-tuple-element.36.q.q_ref, ...), custom_call_target="tpu_custom_call" | custom-call | flops 67108864 | bytes 8388608 | tf_op jit(solution)/shard_map/mixer_carry/pallas_call | solution.py:343
  130.0 3.7 collective-permute-start.27
  135.8 5.2 multiply_convert_fusion.8
  142.8 5.0 collective-permute-done.23
  158.7 21.7 %collective-permute-done.30 = bf16[256,704]{0,1:T(8,128)(2,1)S(1)} collective-permute-done((bf16[256,704]{0,1:T(8,128)(2,1)S(1)}, bf16[256,704]{0,1:T(8,128)(2,1)S(1)}, u32[]{:S(2)}, u32[]{:S(2)}) %collective-permute-start.30) | collective-permute-done | bytes 360480 | tf_op jit(solution)/shard_map/ppermute | solution.py:19
  182.1 5.9 collective-permute-done.33
  196.0 3.8 collective-permute-done.36
  201.3 14.0 %collective-permute-done.38 = bf16[512,704]{0,1:T(8,128)(2,1)} collective-permute-done((bf16[512,704]{0,1:T(8,128)(2,1)S(1)}, bf16[512,704]{0,1:T(8,128)(2,1)}, u32[]{:S(2)}, u32[]{:S(2)}) %collective-permute-start.38) | collective-permute-done | bytes 720928 | tf_op jit(solution)/shard_map/ppermute | solution.py:19
  216.7 33.9 %collective-permute-done.45.refs_2_ = bf16[512,256]{1,0:T(8,128)(2,1)S(1)} collective-permute-done((bf16[512,256]{1,0:T(8,128)(2,1)S(1)}, bf16[512,256]{1,0:T(8,128)(2,1)S(1)}, u32[]{:S(2)}, u32[]{:S(2)}) %collective-permute-start.45) | collective-permute-done | bytes 262176 | tf_op jit(solution)/shard_map/ppermute | solution.py:19
  251.4 8.8 %collective-permute-done.46.refs_3_ = bf16[512,256]{1,0:T(8,128)(2,1)} collective-permute-done((bf16[512,256]{1,0:T(8,128)(2,1)}, bf16[512,256]{1,0:T(8,128)(2,1)}, u32[]{:S(2)}, u32[]{:S(2)}) %collective-permute-start.46) | collective-permute-done | bytes 262176 | tf_op jit(solution)/shard_map/ppermute | solution.py:19
  260.2 3.7 assemble.3
  274.2 3.8 fusion.82
  283.6 4.0 convolution_convert_fusion.2
  295.2 4.5 fusion.79
  302.6 4.4 multiply_convert_fusion.3
  337.8 24.9 %collective-permute-done.74 = bf16[512,704]{0,1:T(8,128)(2,1)S(1)} collective-permute-done((bf16[512,704]{0,1:T(8,128)(2,1)S(1)}, bf16[512,704]{0,1:T(8,128)(2,1)S(1)}, u32[]{:S(2)}, u32[]{:S(2)}) %collective-permute-start.74) | collective-permute-done | bytes 720928 | tf_op jit(solution)/shard_map/ppermute | solution.py:19
  365.1 14.2 %collective-permute-done.75 = bf16[256,704]{0,1:T(8,128)(2,1)S(1)} collective-permute-done((bf16[256,704]{0,1:T(8,128)(2,1)S(1)}, bf16[256,704]{0,1:T(8,128)(2,1)S(1)}, u32[]{:S(2)}, u32[]{:S(2)}) %collective-permute-start.75) | collective-permute-done | bytes 360480 | tf_op jit(solution)/shard_map/ppermute | solution.py:19
  382.6 3.4 collective-permute-done.76
  386.9 3.8 multiply_reduce_fusion
  395.0 4.2 subtract_convert_fusion
  408.7 6.8 %mixer_entry_grad.1 = f32[2,4,128,128]{3,2,1,0:T(8,128)} custom-call(f32[4]{0:T(128)} %get-tuple-element.85.rates, f32[2,2]{1,0:T(2,128)} %pad_maximum_fusion.42.marks, f32[2,512,1]{2,1,0:T(8,128)} %copy.36.seg_c, bf16[1024,512]{1,0:T(8,128)(2,1)} %get-tuple-element.36.q.q_ref, bf16[1024,512]{1,0:T(8,128)(2,1)} %get-tuple-element.88.do_ref.do), custom_call_target="tpu_custom_call" | custom-call | flops 67108864 | bytes 8388608 | tf_op jit(solution)/shard_map/mixer_entry_grad/pallas_call | solution.py:343
  416.7 11.3 %mixer_inner_grad.1 = (bf16[1024,512]{1,0:T(8,128)(2,1)}, f32[1024,512]{1,0:T(8,128)}, f32[1024,512]{1,0:T(8,128)}) custom-call(f32[4]{0:T(128)} %get-tuple-element.85.rates, f32[2,2]{1,0:T(2,128)} %pad_maximum_fusion.42.marks, f32[2,512,1]{2,1,0:T(8,128)} %copy.36.seg_c, f32[2,1,512]{2,1,0:T(1,128)} %copy.35.seg_r, ...), custom_call_target="tpu_custom_call" | custom-call | flops 1342177280 | bytes 8388608 | tf_op jit(solution)/shard_map/mixer_inner_grad/pallas_call | solution.py:343
  427.9 4.3 convolution_convert_fusion.10
  438.0 6.8 %collective-permute-start.79 = (bf16[256,704]{0,1:T(8,128)(2,1)S(1)}, bf16[256,704]{0,1:T(8,128)(2,1)S(1)}, u32[]{:S(2)}, u32[]{:S(2)}) collective-permute-start(bf16[256,704]{0,1:T(8,128)(2,1)S(1)} %slice.564), channel_id=1, source_target_pairs={{0,16},{8,24},{16,0},{24,8},{1,17},{9,25},{17,1},{25,9},{2,18},{10... | collective-permute-start | bytes 1081352 | tf_op jit(solution)/shard_map/ppermute | solution.py:19
  445.0 17.3 %collective-permute-done.83 = bf16[256,704]{0,1:T(8,128)(2,1)S(1)} collective-permute-done((bf16[256,704]{0,1:T(8,128)(2,1)S(1)}, bf16[256,704]{0,1:T(8,128)(2,1)S(1)}, u32[]{:S(2)}, u32[]{:S(2)}) %collective-permute-start.83) | collective-permute-done | bytes 360480 | tf_op jit(solution)/shard_map/ppermute | solution.py:19
  463.0 6.9 %collective-permute-done.79 = bf16[256,704]{0,1:T(8,128)(2,1)S(1)} collective-permute-done((bf16[256,704]{0,1:T(8,128)(2,1)S(1)}, bf16[256,704]{0,1:T(8,128)(2,1)S(1)}, u32[]{:S(2)}, u32[]{:S(2)}) %collective-permute-start.79) | collective-permute-done | bytes 360480 | tf_op jit(solution)/shard_map/ppermute | solution.py:19
  480.5 4.2 collective-permute-done.53
  485.4 7.9 %mixer_last_grad.1 = (bf16[1024,512]{1,0:T(8,128)(2,1)}, bf16[1024,512]{1,0:T(8,128)(2,1)}) custom-call(f32[4]{0:T(128)} %get-tuple-element.85.rates, f32[2,2]{1,0:T(2,128)} %pad_maximum_fusion.42.marks, f32[2,512,1]{2,1,0:T(8,128)} %copy.36.seg_c, bf16[1024,512]{1,0:T(8,128)(2,1)} %get-tuple-element.45.k_ref.k, ...), custom_call_target="tpu_custom_call" | custom-call | flops 134217728 | bytes 8388608 | tf_op jit(solution)/shard_map/mixer_last_grad/pallas_call | solution.py:343
  493.4 3.3 convolution_convert_fusion.9
  515.8 6.0 collective-permute-done.70
  522.0 15.1 %collective-permute-done.64 = bf16[512,256]{1,0:T(8,128)(2,1)S(1)} collective-permute-done((bf16[512,256]{1,0:T(8,128)(2,1)S(1)}, bf16[512,256]{1,0:T(8,128)(2,1)S(1)}, u32[]{:S(2)}, u32[]{:S(2)}) %collective-permute-start.64) | collective-permute-done | bytes 262176 | tf_op jit(solution)/shard_map/ppermute | solution.py:19
  539.4 4.1 collective-permute-done.65
  545.2 6.3 %fusion = (f32[512]{0:T(512)S(1)}, f32[512,1024]{1,0:T(8,128)}) fusion(bf16[512,1024]{1,0:T(8,128)(2,1)} %get-tuple-element.33, bf16[512,1024]{1,0:T(8,128)(2,1)} %collective-permute-done.54, f32[512,1024]{1,0:T(8,128)} %fusion.30, f32[512,1024]{1,0:T(8,128)} %fusion.39, f32[512,1024]{1,0:T(8,128)} %fusion.41, bf16[1024,256]{1,0:T(8,128)(2,1)} %copy-done.12, ...), kind=kOutput, calls=%fused_computation.11 | convolution fusion | flops 543161856 | bytes 12060672 | tf_op jit(solution)/shard_map/tc,dc->td/dot_general | solution.py:211
  552.8 5.6 fusion.2
  558.5 3.6 divide.3
  568.0 3.5 divide.2
  586.3 10.2 %collective-permute-done.60 = bf16[256,512]{0,1:T(8,128)(2,1)S(1)} collective-permute-done((bf16[256,512]{0,1:T(8,128)(2,1)S(1)}, bf16[256,512]{0,1:T(8,128)(2,1)S(1)}, u32[]{:S(2)}, u32[]{:S(2)}) %collective-permute-start.60) | collective-permute-done | bytes 262176 | tf_op jit(solution)/shard_map/ppermute | solution.py:19
  597.8 3.9 collective-permute-done.61
  (528 shorter events, 231.3 us)
Async XLA Ops:
  2.9 41.2 %collective-permute-start = (bf16[512,256]{1,0:T(8,128)(2,1)}, bf16[512,256]{1,0:T(8,128)(2,1)}, u32[]{:S(2)}, u32[]{:S(2)}) collective-permute-start(bf16[512,256]{1,0:T(8,128)(2,1)} %get-tuple-element.129), channel_id=1, source_target_pairs={{0,2},{2,0},{4,6},{6,4},{1,3},{3,1},{5,7},{7,5},{8,10},{10,8},{12,... | collective-permute-start | bytes 786440 | tf_op jit(solution)/shard_map/ppermute | solution.py:19
  3.4 42.0 %collective-permute-start.1 = (bf16[512,256]{1,0:T(8,128)(2,1)}, bf16[512,256]{1,0:T(8,128)(2,1)}, u32[]{:S(2)}, u32[]{:S(2)}) collective-permute-start(bf16[512,256]{1,0:T(8,128)(2,1)} %get-tuple-element.131), channel_id=1, source_target_pairs={{0,4},{2,6},{4,0},{6,2},{1,5},{3,7},{5,1},{7,3},{8,12},{10,14},{12... | collective-permute-start | bytes 786440 | tf_op jit(solution)/shard_map/ppermute | solution.py:19
  5.9 39.5 %collective-permute-start.2 = (bf16[512,256]{1,0:T(8,128)(2,1)S(1)}, bf16[512,256]{1,0:T(8,128)(2,1)}, u32[]{:S(2)}, u32[]{:S(2)}) collective-permute-start(bf16[512,256]{1,0:T(8,128)(2,1)S(1)} %get-tuple-element.128), channel_id=1, source_target_pairs={{0,6},{2,4},{4,2},{6,0},{1,7},{3,5},{5,3},{7,1},{8,14},{10,12},{12... | collective-permute-start | bytes 786440 | tf_op jit(solution)/shard_map/ppermute | solution.py:19
  15.6 20.6 %collective-permute-start.12 = (bf16[256,512]{1,0:T(8,128)(2,1)S(1)}, bf16[256,512]{1,0:T(8,128)(2,1)S(1)}, u32[]{:S(2)}, u32[]{:S(2)}) collective-permute-start(bf16[256,512]{1,0:T(8,128)(2,1)S(1)} %pad_maximum_fusion.38), channel_id=1, source_target_pairs={{0,16},{8,24},{16,0},{24,8},{1,17},{9,25},{17,1},{25,9},{2,18},{10... | collective-permute-start | bytes 786440 | tf_op jit(solution)/shard_map/ppermute | solution.py:19
  19.5 21.6 %collective-permute-start.7 = (bf16[256,512]{1,0:T(8,128)(2,1)S(1)}, bf16[256,512]{1,0:T(8,128)(2,1)S(1)}, u32[]{:S(2)}, u32[]{:S(2)}) collective-permute-start(bf16[256,512]{1,0:T(8,128)(2,1)S(1)} %pad_maximum_fusion.37), channel_id=1, source_target_pairs={{0,16},{8,24},{16,0},{24,8},{1,17},{9,25},{17,1},{25,9},{2,18},{10... | collective-permute-start | bytes 786440 | tf_op jit(solution)/shard_map/ppermute | solution.py:19
  44.2 23.0 %collective-permute-start.8 = (bf16[512,512]{1,0:T(8,128)(2,1)S(1)}, bf16[512,512]{1,0:T(8,128)(2,1)}, u32[]{:S(2)}, u32[]{:S(2)}) collective-permute-start(bf16[512,512]{1,0:T(8,128)(2,1)S(1)} %pad_maximum_fusion.20), channel_id=1, source_target_pairs={{0,1},{1,0},{2,3},{3,2},{4,5},{5,4},{6,7},{7,6},{8,9},{9,8},{10,11... | collective-permute-start | bytes 1572872 | tf_op jit(solution)/shard_map/ppermute | solution.py:19
  49.2 20.1 %collective-permute-start.5 = (bf16[512,1024]{1,0:T(8,128)(2,1)}, bf16[512,1024]{1,0:T(8,128)(2,1)S(1)}, u32[]{:S(2)}, u32[]{:S(2)}) collective-permute-start(bf16[512,1024]{1,0:T(8,128)(2,1)} %get-tuple-element.34), channel_id=1, source_target_pairs={{0,2},{2,0},{4,6},{6,4},{1,3},{3,1},{5,7},{7,5},{8,10},{10,8},{12,... | collective-permute-start | bytes 3145736 | tf_op jit(solution)/shard_map/ppermute | solution.py:19
  57.1 25.0 %collective-permute-start.14 = (bf16[1024,512]{1,0:T(8,128)(2,1)S(1)}, bf16[1024,512]{1,0:T(8,128)(2,1)S(1)}, u32[]{:S(2)}, u32[]{:S(2)}) collective-permute-start(bf16[1024,512]{1,0:T(8,128)(2,1)S(1)} %pad_maximum_fusion.11), channel_id=1, source_target_pairs={{0,4},{2,6},{4,0},{6,2},{1,5},{3,7},{5,1},{7,3},{8,12},{10,14},{12... | collective-permute-start | bytes 3145736 | tf_op jit(solution)/shard_map/ppermute | solution.py:19
  58.6 18.1 %collective-permute-start.10 = (bf16[512,512]{1,0:T(8,128)(2,1)S(1)}, bf16[512,512]{1,0:T(8,128)(2,1)S(1)}, u32[]{:S(2)}, u32[]{:S(2)}) collective-permute-start(bf16[512,512]{1,0:T(8,128)(2,1)S(1)} %collective-permute-done.9), channel_id=1, source_target_pairs={{0,1},{1,0},{2,3},{3,2},{4,5},{5,4},{6,7},{7,6},{8,9},{9,8},{10,11... | collective-permute-start | bytes 1572872 | tf_op jit(solution)/shard_map/ppermute | solution.py:19
  110.0 19.2 %collective-permute-start.26 = (bf16[128,704]{0,1:T(8,128)(2,1)S(1)}, bf16[128,704]{0,1:T(8,128)(2,1)S(1)}, u32[]{:S(2)}, u32[]{:S(2)}) collective-permute-start(bf16[128,704]{0,1:T(8,128)(2,1)S(1)} %constant_dynamic-slice_fusion.1), channel_id=1, source_target_pairs={{0,8},{8,0},{16,24},{24,16},{1,9},{9,1},{17,25},{25,17},{2,10},{10... | collective-permute-start | bytes 540680 | tf_op jit(solution)/shard_map/ppermute | solution.py:19
  115.8 19.4 %collective-permute-start.22 = (bf16[512,256]{0,1:T(8,128)(2,1)S(1)}, bf16[512,256]{0,1:T(8,128)(2,1)S(1)}, u32[]{:S(2)}, u32[]{:S(2)}) collective-permute-start(bf16[512,256]{0,1:T(8,128)(2,1)S(1)} %pad_maximum_fusion.39), channel_id=1, source_target_pairs={{0,4},{2,6},{4,0},{6,2},{1,5},{3,7},{5,1},{7,3},{8,12},{10,14},{12... | collective-permute-start | bytes 786440 | tf_op jit(solution)/shard_map/ppermute | solution.py:19
  117.3 36.6 %collective-permute-start.29 = (bf16[128,704]{0,1:T(8,128)(2,1)S(1)}, bf16[128,704]{0,1:T(8,128)(2,1)S(1)}, u32[]{:S(2)}, u32[]{:S(2)}) collective-permute-start(bf16[128,704]{0,1:T(8,128)(2,1)S(1)} %constant_dynamic-slice_fusion), channel_id=1, source_target_pairs={{0,8},{8,0},{16,24},{24,16},{1,9},{9,1},{17,25},{25,17},{2,10},{10... | collective-permute-start | bytes 540680 | tf_op jit(solution)/shard_map/ppermute | solution.py:19
  130.0 22.3 %collective-permute-start.27 = (bf16[256,704]{0,1:T(8,128)(2,1)}, bf16[256,704]{0,1:T(8,128)(2,1)S(1)}, u32[]{:S(2)}, u32[]{:S(2)}) collective-permute-start(bf16[256,704]{0,1:T(8,128)(2,1)} %pad_maximum_fusion.22), channel_id=1, source_target_pairs={{0,16},{8,24},{16,0},{24,8},{1,17},{9,25},{17,1},{25,9},{2,18},{10... | collective-permute-start | bytes 1081352 | tf_op jit(solution)/shard_map/ppermute | solution.py:19
  149.6 42.6 %collective-permute-start.24 = (bf16[512,1024]{1,0:T(8,128)(2,1)S(1)}, bf16[512,1024]{1,0:T(8,128)(2,1)S(1)}, u32[]{:S(2)}, u32[]{:S(2)}) collective-permute-start(bf16[512,1024]{1,0:T(8,128)(2,1)S(1)} %convolution_convert_fusion.11), channel_id=1, source_target_pairs={{0,2},{2,0},{4,6},{6,4},{1,3},{3,1},{5,7},{7,5},{8,10},{10,8},{12,... | collective-permute-start | bytes 3145736 | tf_op jit(solution)/shard_map/ppermute | solution.py:19
  152.3 38.0 %collective-permute-start.28 = (bf16[512,704]{0,1:T(8,128)(2,1)S(1)}, bf16[512,704]{0,1:T(8,128)(2,1)S(1)}, u32[]{:S(2)}, u32[]{:S(2)}) collective-permute-start(bf16[512,704]{0,1:T(8,128)(2,1)S(1)} %pad_maximum_fusion.15), channel_id=1, source_target_pairs={{0,1},{1,0},{2,3},{3,2},{4,5},{5,4},{6,7},{7,6},{8,9},{9,8},{10,11... | collective-permute-start | bytes 2162696 | tf_op jit(solution)/shard_map/ppermute | solution.py:19
  153.9 26.5 %collective-permute-start.30 = (bf16[256,704]{0,1:T(8,128)(2,1)S(1)}, bf16[256,704]{0,1:T(8,128)(2,1)S(1)}, u32[]{:S(2)}, u32[]{:S(2)}) collective-permute-start(bf16[256,704]{0,1:T(8,128)(2,1)S(1)} %pad_maximum_fusion.23), channel_id=1, source_target_pairs={{0,16},{8,24},{16,0},{24,8},{1,17},{9,25},{17,1},{25,9},{2,18},{10... | collective-permute-start | bytes 1081352 | tf_op jit(solution)/shard_map/ppermute | solution.py:19
  157.5 30.6 %collective-permute-start.33 = (bf16[256,704]{0,1:T(8,128)(2,1)S(1)}, bf16[256,704]{0,1:T(8,128)(2,1)S(1)}, u32[]{:S(2)}, u32[]{:S(2)}) collective-permute-start(bf16[256,704]{0,1:T(8,128)(2,1)S(1)} %pad_maximum_fusion.24), channel_id=1, source_target_pairs={{0,16},{8,24},{16,0},{24,8},{1,17},{9,25},{17,1},{25,9},{2,18},{10... | collective-permute-start | bytes 1081352 | tf_op jit(solution)/shard_map/ppermute | solution.py:19
  158.7 35.7 %collective-permute-start.44 = (bf16[512,256]{1,0:T(8,128)(2,1)S(1)}, bf16[512,256]{1,0:T(8,128)(2,1)S(1)}, u32[]{:S(2)}, u32[]{:S(2)}) collective-permute-start(bf16[512,256]{1,0:T(8,128)(2,1)S(1)} %get-tuple-element.113), channel_id=1, source_target_pairs={{0,2},{2,0},{4,6},{6,4},{1,3},{3,1},{5,7},{7,5},{8,10},{10,8},{12,... | collective-permute-start | bytes 786440 | tf_op jit(solution)/shard_map/ppermute | solution.py:19
  180.6 19.2 %collective-permute-start.36 = (bf16[512,704]{0,1:T(8,128)(2,1)S(1)}, bf16[512,704]{0,1:T(8,128)(2,1)}, u32[]{:S(2)}, u32[]{:S(2)}) collective-permute-start(bf16[512,704]{0,1:T(8,128)(2,1)S(1)} %pad_maximum_fusion.16), channel_id=1, source_target_pairs={{0,4},{2,6},{4,0},{6,2},{1,5},{3,7},{5,1},{7,3},{8,12},{10,14},{12... | collective-permute-start | bytes 2162696 | tf_op jit(solution)/shard_map/ppermute | solution.py:19
  188.8 26.4 %collective-permute-start.38 = (bf16[512,704]{0,1:T(8,128)(2,1)S(1)}, bf16[512,704]{0,1:T(8,128)(2,1)}, u32[]{:S(2)}, u32[]{:S(2)}) collective-permute-start(bf16[512,704]{0,1:T(8,128)(2,1)S(1)} %pad_maximum_fusion.17), channel_id=1, source_target_pairs={{0,4},{2,6},{4,0},{6,2},{1,5},{3,7},{5,1},{7,3},{8,12},{10,14},{12... | collective-permute-start | bytes 2162696 | tf_op jit(solution)/shard_map/ppermute | solution.py:19
  191.6 82.6 %collective-permute-start.35 = (bf16[1024,704]{0,1:T(8,128)(2,1)}, bf16[1024,704]{0,1:T(8,128)(2,1)}, u32[]{:S(2)}, u32[]{:S(2)}) collective-permute-start(bf16[1024,704]{0,1:T(8,128)(2,1)} %pad_maximum_fusion.3), channel_id=1, source_target_pairs={{0,4},{2,6},{4,0},{6,2},{1,5},{3,7},{5,1},{7,3},{8,12},{10,14},{12... | collective-permute-start | bytes 4325384 | tf_op jit(solution)/shard_map/ppermute | solution.py:19
  194.4 76.9 %collective-permute-start.25 = (bf16[512,1024]{1,0:T(8,128)(2,1)S(1)}, bf16[512,1024]{1,0:T(8,128)(2,1)}, u32[]{:S(2)}, u32[]{:S(2)}) collective-permute-start(bf16[512,1024]{1,0:T(8,128)(2,1)S(1)} %multiply_convert_fusion.7), channel_id=1, source_target_pairs={{0,2},{2,0},{4,6},{6,4},{1,3},{3,1},{5,7},{7,5},{8,10},{10,8},{12,... | collective-permute-start | bytes 3145736 | tf_op jit(solution)/shard_map/ppermute | solution.py:19
  194.5 56.1 %collective-permute-start.45 = (bf16[512,256]{1,0:T(8,128)(2,1)S(1)}, bf16[512,256]{1,0:T(8,128)(2,1)S(1)}, u32[]{:S(2)}, u32[]{:S(2)}) collective-permute-start(bf16[512,256]{1,0:T(8,128)(2,1)S(1)} %get-tuple-element.115), channel_id=1, source_target_pairs={{0,4},{2,6},{4,0},{6,2},{1,5},{3,7},{5,1},{7,3},{8,12},{10,14},{12... | collective-permute-start | bytes 786440 | tf_op jit(solution)/shard_map/ppermute | solution.py:19
  199.8 66.9 %collective-permute-start.37 = (bf16[512,704]{0,1:T(8,128)(2,1)}, bf16[512,704]{0,1:T(8,128)(2,1)}, u32[]{:S(2)}, u32[]{:S(2)}) collective-permute-start(bf16[512,704]{0,1:T(8,128)(2,1)} %collective-permute-done.36), channel_id=1, source_target_pairs={{0,1},{1,0},{2,3},{3,2},{4,5},{5,4},{6,7},{7,6},{8,9},{9,8},{10,11... | collective-permute-start | bytes 2162696 | tf_op jit(solution)/shard_map/ppermute | solution.py:19
  215.2 52.7 %collective-permute-start.39 = (bf16[512,704]{0,1:T(8,128)(2,1)}, bf16[512,704]{0,1:T(8,128)(2,1)}, u32[]{:S(2)}, u32[]{:S(2)}) collective-permute-start(bf16[512,704]{0,1:T(8,128)(2,1)} %collective-permute-done.38), channel_id=1, source_target_pairs={{0,1},{1,0},{2,3},{3,2},{4,5},{5,4},{6,7},{7,6},{8,9},{9,8},{10,11... | collective-permute-start | bytes 2162696 | tf_op jit(solution)/shard_map/ppermute | solution.py:19
  266.7 28.6 %collective-permute-start.31 = (bf16[512,704]{0,1:T(8,128)(2,1)S(1)}, bf16[512,704]{0,1:T(8,128)(2,1)S(1)}, u32[]{:S(2)}, u32[]{:S(2)}) collective-permute-start(bf16[512,704]{0,1:T(8,128)(2,1)S(1)} %copy-done.56), channel_id=1, source_target_pairs={{0,1},{1,0},{2,3},{3,2},{4,5},{5,4},{6,7},{7,6},{8,9},{9,8},{10,11... | collective-permute-start | bytes 2162696 | tf_op jit(solution)/shard_map/ppermute | solution.py:19
  268.0 34.6 %collective-permute-start.34 = (bf16[512,704]{0,1:T(8,128)(2,1)S(1)}, bf16[512,704]{0,1:T(8,128)(2,1)S(1)}, u32[]{:S(2)}, u32[]{:S(2)}) collective-permute-start(bf16[512,704]{0,1:T(8,128)(2,1)S(1)} %copy-done.58), channel_id=1, source_target_pairs={{0,1},{1,0},{2,3},{3,2},{4,5},{5,4},{6,7},{7,6},{8,9},{9,8},{10,11... | collective-permute-start | bytes 2162696 | tf_op jit(solution)/shard_map/ppermute | solution.py:19
  282.9 80.3 %collective-permute-start.81 = (bf16[1024,704]{0,1:T(8,128)(2,1)}, bf16[1024,704]{0,1:T(8,128)(2,1)S(1)}, u32[]{:S(2)}, u32[]{:S(2)}) collective-permute-start(bf16[1024,704]{0,1:T(8,128)(2,1)} %convolution_convert_fusion), channel_id=1, source_target_pairs={{0,4},{2,6},{4,0},{6,2},{1,5},{3,7},{5,1},{7,3},{8,12},{10,14},{12... | collective-permute-start | bytes 4325384 | tf_op jit(solution)/shard_map/ppermute | solution.py:19
  287.6 92.0 %collective-permute-start.77 = (bf16[1024,704]{0,1:T(8,128)(2,1)}, bf16[1024,704]{0,1:T(8,128)(2,1)S(1)}, u32[]{:S(2)}, u32[]{:S(2)}) collective-permute-start(bf16[1024,704]{0,1:T(8,128)(2,1)} %convolution_convert_fusion.2), channel_id=1, source_target_pairs={{0,4},{2,6},{4,0},{6,2},{1,5},{3,7},{5,1},{7,3},{8,12},{10,14},{12... | collective-permute-start | bytes 4325384 | tf_op jit(solution)/shard_map/ppermute | solution.py:19
  292.0 42.3 %collective-permute-start.73 = (bf16[512,704]{0,1:T(8,128)(2,1)S(1)}, bf16[512,704]{0,1:T(8,128)(2,1)S(1)}, u32[]{:S(2)}, u32[]{:S(2)}) collective-permute-start(bf16[512,704]{0,1:T(8,128)(2,1)S(1)} %slice.430), channel_id=1, source_target_pairs={{0,1},{1,0},{2,3},{3,2},{4,5},{5,4},{6,7},{7,6},{8,9},{9,8},{10,11... | collective-permute-start | bytes 2162696 | tf_op jit(solution)/shard_map/ppermute | solution.py:19
  311.1 26.7 %collective-permute-start.72 = (bf16[512,704]{0,1:T(8,128)(2,1)S(1)}, bf16[512,704]{0,1:T(8,128)(2,1)S(1)}, u32[]{:S(2)}, u32[]{:S(2)}) collective-permute-start(bf16[512,704]{0,1:T(8,128)(2,1)S(1)} %slice.428), channel_id=1, source_target_pairs={{0,1},{1,0},{2,3},{3,2},{4,5},{5,4},{6,7},{7,6},{8,9},{9,8},{10,11... | collective-permute-start | bytes 2162696 | tf_op jit(solution)/shard_map/ppermute | solution.py:19
  318.5 16.4 %collective-permute-start.48 = (bf16[512,1024]{1,0:T(8,128)(2,1)S(1)}, bf16[512,1024]{1,0:T(8,128)(2,1)S(1)}, u32[]{:S(2)}, u32[]{:S(2)}) collective-permute-start(bf16[512,1024]{1,0:T(8,128)(2,1)S(1)} %add_convert_fusion.1), channel_id=1, source_target_pairs={{0,2},{2,0},{4,6},{6,4},{1,3},{3,1},{5,7},{7,5},{8,10},{10,8},{12,... | collective-permute-start | bytes 3145736 | tf_op jit(solution)/shard_map/ppermute | solution.py:19
  334.4 218.5 %collective-permute-start.40 = (bf16[512,1024]{1,0:T(8,128)(2,1)}, bf16[512,1024]{1,0:T(8,128)(2,1)}, u32[]{:S(2)}, u32[]{:S(2)}) collective-permute-start(bf16[512,1024]{1,0:T(8,128)(2,1)} %add_convert_fusion.3), channel_id=1, source_target_pairs={{0,2},{2,0},{4,6},{6,4},{1,3},{3,1},{5,7},{7,5},{8,10},{10,8},{12,... | collective-permute-start | bytes 3145736 | tf_op jit(solution)/shard_map/ppermute | solution.py:19
  335.0 27.7 %collective-permute-start.74 = (bf16[512,704]{0,1:T(8,128)(2,1)S(1)}, bf16[512,704]{0,1:T(8,128)(2,1)S(1)}, u32[]{:S(2)}, u32[]{:S(2)}) collective-permute-start(bf16[512,704]{0,1:T(8,128)(2,1)S(1)} %add_convert_fusion.4), channel_id=1, source_target_pairs={{0,4},{2,6},{4,0},{6,2},{1,5},{3,7},{5,1},{7,3},{8,12},{10,14},{12... | collective-permute-start | bytes 2162696 | tf_op jit(solution)/shard_map/ppermute | solution.py:19
  337.8 49.0 %collective-permute-start.49 = (bf16[512,1024]{1,0:T(8,128)(2,1)S(1)}, bf16[512,1024]{1,0:T(8,128)(2,1)S(1)}, u32[]{:S(2)}, u32[]{:S(2)}) collective-permute-start(bf16[512,1024]{1,0:T(8,128)(2,1)S(1)} %fusion.80), channel_id=1, source_target_pairs={{0,2},{2,0},{4,6},{6,4},{1,3},{3,1},{5,7},{7,5},{8,10},{10,8},{12,... | collective-permute-start | bytes 3145736 | tf_op jit(solution)/shard_map/ppermute | solution.py:19
  363.1 16.2 %collective-permute-start.75 = (bf16[256,704]{0,1:T(8,128)(2,1)S(1)}, bf16[256,704]{0,1:T(8,128)(2,1)S(1)}, u32[]{:S(2)}, u32[]{:S(2)}) collective-permute-start(bf16[256,704]{0,1:T(8,128)(2,1)S(1)} %slice.565), channel_id=1, source_target_pairs={{0,16},{8,24},{16,0},{24,8},{1,17},{9,25},{17,1},{25,9},{2,18},{10... | collective-permute-start | bytes 1081352 | tf_op jit(solution)/shard_map/ppermute | solution.py:19
  364.8 67.4 %collective-permute-start.82 = (bf16[512,704]{0,1:T(8,128)(2,1)}, bf16[512,704]{0,1:T(8,128)(2,1)}, u32[]{:S(2)}, u32[]{:S(2)}) collective-permute-start(bf16[512,704]{0,1:T(8,128)(2,1)} %slice.560), channel_id=1, source_target_pairs={{0,1},{1,0},{2,3},{3,2},{4,5},{5,4},{6,7},{7,6},{8,9},{9,8},{10,11... | collective-permute-start | bytes 2162696 | tf_op jit(solution)/shard_map/ppermute | solution.py:19
  382.1 52.5 %collective-permute-start.78 = (bf16[512,704]{0,1:T(8,128)(2,1)}, bf16[512,704]{0,1:T(8,128)(2,1)}, u32[]{:S(2)}, u32[]{:S(2)}) collective-permute-start(bf16[512,704]{0,1:T(8,128)(2,1)} %slice.561), channel_id=1, source_target_pairs={{0,1},{1,0},{2,3},{3,2},{4,5},{5,4},{6,7},{7,6},{8,9},{9,8},{10,11... | collective-permute-start | bytes 2162696 | tf_op jit(solution)/shard_map/ppermute | solution.py:19
  405.9 104.1 %collective-permute-start.67 = (bf16[512,512]{0,1:T(8,128)(2,1)}, bf16[512,512]{0,1:T(8,128)(2,1)}, u32[]{:S(2)}, u32[]{:S(2)}) collective-permute-start(bf16[512,512]{0,1:T(8,128)(2,1)} %pad_maximum_fusion.19), channel_id=1, source_target_pairs={{0,1},{1,0},{2,3},{3,2},{4,5},{5,4},{6,7},{7,6},{8,9},{9,8},{10,11... | collective-permute-start | bytes 1572872 | tf_op jit(solution)/shard_map/ppermute | solution.py:19
  407.3 62.8 %collective-permute-start.68 = (bf16[512,512]{0,1:T(8,128)(2,1)}, bf16[512,512]{0,1:T(8,128)(2,1)}, u32[]{:S(2)}, u32[]{:S(2)}) collective-permute-start(bf16[512,512]{0,1:T(8,128)(2,1)} %pad_maximum_fusion.18), channel_id=1, source_target_pairs={{0,1},{1,0},{2,3},{3,2},{4,5},{5,4},{6,7},{7,6},{8,9},{9,8},{10,11... | collective-permute-start | bytes 1572872 | tf_op jit(solution)/shard_map/ppermute | solution.py:19
  434.5 27.7 %collective-permute-start.83 = (bf16[256,704]{0,1:T(8,128)(2,1)S(1)}, bf16[256,704]{0,1:T(8,128)(2,1)S(1)}, u32[]{:S(2)}, u32[]{:S(2)}) collective-permute-start(bf16[256,704]{0,1:T(8,128)(2,1)S(1)} %slice.563), channel_id=1, source_target_pairs={{0,16},{8,24},{16,0},{24,8},{1,17},{9,25},{17,1},{25,9},{2,18},{10... | collective-permute-start | bytes 1081352 | tf_op jit(solution)/shard_map/ppermute | solution.py:19
  438.0 31.9 %collective-permute-start.79 = (bf16[256,704]{0,1:T(8,128)(2,1)S(1)}, bf16[256,704]{0,1:T(8,128)(2,1)S(1)}, u32[]{:S(2)}, u32[]{:S(2)}) collective-permute-start(bf16[256,704]{0,1:T(8,128)(2,1)S(1)} %slice.564), channel_id=1, source_target_pairs={{0,16},{8,24},{16,0},{24,8},{1,17},{9,25},{17,1},{25,9},{2,18},{10... | collective-permute-start | bytes 1081352 | tf_op jit(solution)/shard_map/ppermute | solution.py:19
  474.3 36.5 %collective-permute-start.69 = (bf16[512,512]{0,1:T(8,128)(2,1)}, bf16[512,512]{0,1:T(8,128)(2,1)}, u32[]{:S(2)}, u32[]{:S(2)}) collective-permute-start(bf16[512,512]{0,1:T(8,128)(2,1)} %add_convert_fusion.5), channel_id=1, source_target_pairs={{0,4},{2,6},{4,0},{6,2},{1,5},{3,7},{5,1},{7,3},{8,12},{10,14},{12... | collective-permute-start | bytes 1572872 | tf_op jit(solution)/shard_map/ppermute | solution.py:19
  503.5 18.4 %collective-permute-start.62 = (bf16[512,256]{1,0:T(8,128)(2,1)S(1)}, bf16[512,256]{1,0:T(8,128)(2,1)S(1)}, u32[]{:S(2)}, u32[]{:S(2)}) collective-permute-start(bf16[512,256]{1,0:T(8,128)(2,1)S(1)} %get-tuple-element.102), channel_id=1, source_target_pairs={{0,1},{1,0},{2,3},{3,2},{4,5},{5,4},{6,7},{7,6},{8,9},{9,8},{10,11... | collective-permute-start | bytes 786440 | tf_op jit(solution)/shard_map/ppermute | solution.py:19
  510.0 53.9 %collective-permute-start.58 = (bf16[1024,512]{0,1:T(8,128)(2,1)}, bf16[1024,512]{0,1:T(8,128)(2,1)}, u32[]{:S(2)}, u32[]{:S(2)}) collective-permute-start(bf16[1024,512]{0,1:T(8,128)(2,1)} %pad_maximum_fusion.14), channel_id=1, source_target_pairs={{0,4},{2,6},{4,0},{6,2},{1,5},{3,7},{5,1},{7,3},{8,12},{10,14},{12... | collective-permute-start | bytes 3145736 | tf_op jit(solution)/shard_map/ppermute | solution.py:19
  512.4 24.7 %collective-permute-start.64 = (bf16[512,256]{1,0:T(8,128)(2,1)S(1)}, bf16[512,256]{1,0:T(8,128)(2,1)S(1)}, u32[]{:S(2)}, u32[]{:S(2)}) collective-permute-start(bf16[512,256]{1,0:T(8,128)(2,1)S(1)} %add_convert_fusion.6), channel_id=1, source_target_pairs={{0,4},{2,6},{4,0},{6,2},{1,5},{3,7},{5,1},{7,3},{8,12},{10,14},{12... | collective-permute-start | bytes 786440 | tf_op jit(solution)/shard_map/ppermute | solution.py:19
  521.8 23.4 %collective-permute-start.54 = (bf16[512,1024]{1,0:T(8,128)(2,1)}, bf16[512,1024]{1,0:T(8,128)(2,1)}, u32[]{:S(2)}, u32[]{:S(2)}) collective-permute-start(bf16[512,1024]{1,0:T(8,128)(2,1)} %add_convert_fusion), channel_id=1, source_target_pairs={{0,2},{2,0},{4,6},{6,4},{1,3},{3,1},{5,7},{7,5},{8,10},{10,8},{12,... | collective-permute-start | bytes 3145736 | tf_op jit(solution)/shard_map/ppermute | solution.py:19
  545.1 22.2 %collective-permute-start.66 = (bf16[128,256]{1,0:T(8,128)(2,1)S(1)}, bf16[128,256]{1,0:T(8,128)(2,1)S(1)}, u32[]{:S(2)}, u32[]{:S(2)}) collective-permute-start(bf16[128,256]{1,0:T(8,128)(2,1)S(1)} %slice.574), channel_id=1, source_target_pairs={{0,8},{8,0},{16,24},{24,16},{1,9},{9,1},{17,25},{25,17},{2,10},{10... | collective-permute-start | bytes 196616 | tf_op jit(solution)/shard_map/ppermute | solution.py:19
  (147 other events, 1633.2 us)

commit v3 on v2

--- a/solution.py
+++ b/solution.py
@@ -14,17 +14,21 @@
 BF16 = jnp.bfloat16
 
 
+COL = ("cx", "cc")
+CHIPS = ("cx", "row", "dp")
+
+
 def swap(value, axis, bits):
     count = lax.axis_size(axis)
     return lax.ppermute(value, axis, [(i, i ^ bits) for i in range(count)])
 
 
 def pair(value):
-    return swap(value, "col", 1)
+    return swap(value, COL, 1)
 
 
 def side(value):
-    return swap(value, "col", 2)
+    return swap(value, COL, 2)
 
 
 def bits_of(axis):
@@ -65,7 +69,7 @@
 
 
 def place_bits():
-    turn = lax.axis_index("col") ^ lax.axis_index("row")
+    turn = lax.axis_index(COL) ^ lax.axis_index("row")
     return jnp.stack([turn & 1, turn >> 1, lax.axis_index("dp"), 0]).astype(jnp.int32)
 
 
@@ -95,7 +99,7 @@
     tokens, width = parts[0].shape
     model = 4 * width
     if not small_slice():
-        col = lax.axis_index("col")
+        col = lax.axis_index(COL)
         blocks = pick4(parts, (col & 1) != 0, (col & 2) != 0)
         rows = to_order(jnp.concatenate(blocks, 1))
         if not norm:
@@ -139,7 +143,7 @@
     tokens, model = rows.shape
     width = model // 4
     if not small_slice():
-        col = lax.axis_index("col")
+        col = lax.axis_index(COL)
         whole = from_order(rows)
         blocks = [whole[:, k * width : (k + 1) * width] for k in range(4)]
         return pick4(blocks, (col & 1) != 0, (col & 2) != 0)
@@ -156,18 +160,18 @@
 
 
 def tokens_in(parts, norm):
-    col = lax.axis_index("col")
+    col = lax.axis_index(COL)
     got = []
     for bits in range(4):
         mine = lax.dynamic_index_in_dim(parts, col ^ bits, 0, False)
-        got.append(mine if bits == 0 else swap(mine, "col", bits))
+        got.append(mine if bits == 0 else swap(mine, COL, bits))
     return assemble(got, norm)
 
 
 def tokens_out(rows):
-    col = lax.axis_index("col")
+    col = lax.axis_index(COL)
     parts = divide(rows)
-    got = [parts[0]] + [swap(parts[bits], "col", bits) for bits in range(1, 4)]
+    got = [parts[0]] + [swap(parts[bits], COL, bits) for bits in range(1, 4)]
     return jnp.stack(pick4(got, (col & 1) != 0, (col & 2) != 0))
 
 
@@ -365,6 +369,104 @@
     return jnp.flip(pair(value), 0)
 
 
+def ff_gather(w_gate, w_up, w_down):
+    nx, nz, ny = [lax.axis_size(a) for a in CHIPS]
+    rows = jnp.concatenate([w_gate.T, w_up.T, w_down], 0)
+    part = rows.shape[1] // ny
+    shard = lax.dynamic_slice_in_dim(rows, lax.axis_index("dp") * part, part, 1)
+    blocks = lax.all_gather(shard, CHIPS, axis=0, tiled=True)
+    hidden = rows.shape[0]
+    z, y = lax.axis_index("row"), lax.axis_index("dp")
+    if small_slice():
+        blocks = blocks.reshape(nx, nz * ny, hidden, part)
+        kz, ky = jnp.arange(nz * ny) % nz, jnp.arange(nz * ny) // nz
+        tables = jnp.stack([(z ^ kz) * ny + (y ^ ky), (y ^ ky) * nz + (z ^ kz)])
+        return blocks, tables.astype(jnp.int32)
+    blocks = blocks.reshape(nx, nz, ny, hidden, part)
+    blocks = xor_turn(xor_turn(blocks, 1, z, nz), 2, y, ny).transpose(0, 2, 1, 3, 4)
+    blocks = blocks.reshape(nx, -1, HEAD // part, hidden, part).transpose(0, 1, 3, 2, 4)
+    blocks = blocks.reshape(nx, -1, hidden, HEAD)
+    same = jnp.arange(blocks.shape[1], dtype=jnp.int32)
+    return blocks, jnp.stack([same, same])
+
+
+def ff_scatter_xy(grads):
+    nx, nz, ny = [lax.axis_size(a) for a in CHIPS]
+    hidden = grads.shape[2]
+    part = grads.shape[1] * HEAD // (nz * ny)
+    if not small_slice():
+        z, y = lax.axis_index("row"), lax.axis_index("dp")
+        grads = grads.reshape(nx, -1, hidden, HEAD // part, part).transpose(0, 1, 3, 2, 4)
+        grads = grads.reshape(nx, ny, nz, hidden, part)
+        grads = xor_turn(xor_turn(grads, 1, y, ny), 2, z, nz)
+    grads = grads.reshape(-1, part)
+    return lax.psum_scatter(grads, ("cx", "dp"), scatter_dimension=0, tiled=True)
+
+
+def ff_kernel(tables, b_ref, g_ref, w_ref, out, out_send, db, db_send, grads, *scratch):
+    m_all, d1_all, d2_all, out_acc, db_acc = scratch
+    step = pl.program_id(0)
+    blocks, hidden = w_ref.shape[1], w_ref.shape[2] // 3
+    tokens = out.shape[0]
+
+    def weight(i):
+        at = slice(i * hidden, (i + 1) * hidden)
+        return jnp.concatenate([w_ref[0, tables[0, p], at, :] for p in range(blocks)], 1)
+
+    gate_w, up_w, down_w = weight(0), weight(1), weight(2)
+    for half in range(2):
+        rows = slice(half * tokens, (half + 1) * tokens)
+        b, g = b_ref[rows, :], g_ref[rows, :]
+        z1, z2, dm = nt(b, gate_w), nt(b, up_w), nt(g, down_w)
+        m, d1, d2 = (z1 * z2).astype(BF16), (dm * z2).astype(BF16), (dm * z1).astype(BF16)
+        m_all[rows, :], d1_all[rows, :], d2_all[rows, :] = m, d1, d2
+        sums = nn(m, down_w), nn(d1, gate_w) + nn(d2, up_w)
+        kept = (out_acc, db_acc) if half else (out, db)
+
+        @pl.when(step == 0)
+        def _():
+            for ref, value in zip(kept, sums):
+                ref[...] = value
+
+        @pl.when(step != 0)
+        def _():
+            sent = (out_send, db_send) if half else kept
+            for to, ref, value in zip(sent, kept, sums):
+                to[...] = (ref[...] + value).astype(to.dtype)
+
+    for i, (left, right) in enumerate(((d1_all, b_ref), (d2_all, b_ref), (m_all, g_ref))):
+        grad = tn(left[...], right[...]).astype(BF16)
+        at = slice(i * hidden, (i + 1) * hidden)
+        for p in range(blocks):
+            grads[0, tables[1, p], at, :] = grad[:, p * HEAD : (p + 1) * HEAD]
+
+
+def feed_forward(b, g, weights, tables):
+    rows, model = b.shape
+    tokens = rows // 2
+    nx, blocks, hidden, width = weights.shape
+    once = pl.Buffered(1)
+    fixed = lambda n: pl.BlockSpec((n, model), lambda x: (0, 0), pipeline_mode=once)
+    turn = pl.BlockSpec((1, blocks, hidden, width), lambda x: (x, 0, 0, 0))
+    wide = jax.ShapeDtypeStruct((tokens, model), F32)
+    narrow = jax.ShapeDtypeStruct((tokens, model), BF16)
+    product = pltpu.VMEM((rows, hidden // 3), BF16)
+    total = pltpu.VMEM((tokens, model), F32)
+    return pl.pallas_call(
+        ff_kernel,
+        grid=(nx,),
+        in_specs=[pl.BlockSpec(memory_space=pltpu.SMEM), fixed(rows), fixed(rows), turn],
+        out_specs=[fixed(tokens)] * 4 + [turn],
+        out_shape=[wide, narrow, wide, narrow, jax.ShapeDtypeStruct(weights.shape, BF16)],
+        scratch_shapes=[product] * 3 + [total] * 2,
+        compiler_params=pltpu.CompilerParams(vmem_limit_bytes=60 << 20),
+        cost_estimate=pl.CostEstimate(
+            flops=6 * nx * rows * model * hidden, bytes_accessed=36 << 20, transcendentals=0
+        ),
+        name="feed_forward",
+    )(tables, b, g, weights)
+
+
 def on_device(
     block_input,
     segments,
@@ -380,10 +482,10 @@
     out_grad,
 ):
     nz = lax.axis_size("row")
-    col = lax.axis_index("col")
+    col = lax.axis_index(COL)
     place = lax.axis_index("row")
     tokens = block_input.shape[2]
-    model = block_input.shape[3] * lax.axis_size("col")
+    model = block_input.shape[3] * lax.axis_size(COL)
     wide = w_query.shape[1]
 
     parts = gather_weight(jnp.concatenate([w_query, w_key], 1), "xy")
@@ -393,9 +495,7 @@
     wv = jnp.concatenate([w[:, :wide] for w in parts], 1)
     wu = jnp.concatenate([w[:, wide:] for w in parts], 1)
     wo = jnp.concatenate(gather_weight(w_out.T, "xy"), 1)
-    down_w = gather_weight(w_down.T, "xy")
-    gate_w = gather_weight(w_gate, "yx")
-    up_w = gather_weight(w_up, "xy")
+    ff_weights, tables = ff_gather(w_gate, w_up, w_down)
 
     x_own, a_own, r1 = tokens_in(block_input[:, 0], True)
     g_own = tokens_in(out_grad[:, 0], False)
@@ -459,18 +559,11 @@
     hres = x_own.astype(F32) + back_sum((y,), (wo,), "tc,dc->td")
     r3 = lax.rsqrt(jnp.mean(hres * hres, 1, keepdims=True) + EPS)
     b = both((hres * r3).astype(BF16))
-    z1 = [dot(b, w, "td,df->tf") for w in gate_w]
-    z2 = [dot(b, w, "td,df->tf") for w in up_w]
-    m = [(p * s).astype(BF16) for p, s in zip(z1, z2)]
-    block_out = tokens_out((hres + back_sum(m, down_w, "tf,df->td")).astype(BF16))
-
-    grad_down = [dot(g, p, "td,tf->df").astype(BF16) for p in m]
-    dm = [dot(g, w, "td,df->tf") for w in down_w]
-    dz1 = [(d * s).astype(BF16) for d, s in zip(dm, z2)]
-    dz2 = [(d * p).astype(BF16) for d, p in zip(dm, z1)]
-    grad_gate = [dot(b, d, "td,tf->df").astype(BF16) for d in dz1]
-    grad_up = [dot(b, d, "td,tf->df").astype(BF16) for d in dz2]
-    db = back_sum(dz1 + dz2, gate_w + up_w, "tf,df->td")
+    out, out_send, db, db_send, ff_grads = feed_forward(b, g, ff_weights, tables)
+    db = db + pair(db_send).astype(F32)
+    block_out = tokens_out((hres + out + pair(out_send).astype(F32)).astype(BF16))
+
+    ff_part = ff_scatter_xy(ff_grads)
     dh = (
         g_own.astype(F32)
         + r3 * db
@@ -524,9 +617,10 @@
             jnp.concatenate([g[:, at : at + wide] for g in mats], 1) for at in (0, wide)
         ]
 
-    total_down = reduce_grad(*grad_down, "xy")
-    total_gate = reduce_grad(*grad_gate, "yx")
-    total_up = reduce_grad(*grad_up, "xy")
+    ff_part, _ = lax.optimization_barrier((ff_part, dzk))
+    ff_total = lax.psum_scatter(ff_part, "row", scatter_dimension=0, tiled=True).astype(F32)
+    hidden = w_down.shape[0]
+    total_gate, total_up = ff_total[:hidden].T, ff_total[hidden : 2 * hidden].T
     total_ou = reduce_grad(*halves(grad_out, grads[3]), "yx")
     total_qk = reduce_grad(*halves(grads[0], grads[1]), "xy")
     total_v = reduce_grad(*halves(grads[2]), "yx")
@@ -540,40 +634,44 @@
         total_ou[:, :wide].T,
         total_gate,
         total_up,
-        total_down.T,
+        ff_total[2 * hidden :],
     )
 
 
 def solution(mesh):
+    rows, cols, copies = [mesh.shape[a] for a in ("row", "col", "dp")]
+    split = jax.sharding.Mesh(
+        mesh.devices.reshape(rows, cols // 2, 2, copies), ("row", "cx", "cc", "dp")
+    )
     placed = (
-        P(None, "dp", "row", "col"),
+        P(None, "dp", "row", COL),
         P(None, "dp", "row"),
-        P("col"),
-        P("row", "col"),
-        P("row", "col"),
-        P("row", "col"),
-        P("row", "col"),
-        P("col", "row"),
-        P("row", "col"),
-        P("row", "col"),
-        P("col", "row"),
-        P(None, "dp", "row", "col"),
+        P(COL),
+        P("row", COL),
+        P("row", COL),
+        P("row", COL),
+        P("row", COL),
+        P(COL, "row"),
+        P("row", COL),
+        P("row", COL),
+        P(COL, "row"),
+        P(None, "dp", "row", COL),
     )
     return jax.shard_map(
         on_device,
-        mesh=mesh,
+        mesh=split,
         in_specs=placed,
         out_specs=(
-            P(None, "dp", "row", "col"),
-            P(None, "dp", "row", "col"),
-            P(("row", "dp"), "col"),
-            P(("row", "dp"), "col"),
-            P(("row", "dp"), "col"),
-            P(("row", "dp"), "col"),
-            P("col", ("row", "dp")),
-            P(("row", "dp"), "col"),
-            P(("row", "dp"), "col"),
-            P("col", ("row", "dp")),
+            P(None, "dp", "row", COL),
+            P(None, "dp", "row", COL),
+            P(("row", "dp"), COL),
+            P(("row", "dp"), COL),
+            P(("row", "dp"), COL),
+            P(("row", "dp"), COL),
+            P(COL, ("row", "dp")),
+            P(("row", "dp"), COL),
+            P(("row", "dp"), COL),
+            P(COL, ("row", "dp")),
         ),
         check_vma=False,
     )

time: 612 us -> 512 us (0.84)
  waiting for transfers between devices: 261 us -> 188 us
  matrix products: 109 us -> 50.9 us
  Pallas kernels: 57.1 us -> 96.6 us
  starting transfers between devices: 95.5 us -> 77.5 us
  between operations: 2.98 us -> 15.1 us
  local copies, waits for them, and re-layouts: 30.6 us -> 23.6 us
    ppermute x78 -> x51, waiting for transfers between devices: 252 us -> 166 us  [swap(): return lax.ppermute(value, axis, [(i, i ^ bits) for i in range(count)])]
    dot_general x44 -> x20, matrix products: 109 us -> 50.9 us  [dot(): return jnp.einsum(form, left, right, preferred_element_type=F32)]
    pallas_call x0 -> x1, Pallas kernels: none -> 39.2 us  [feed_forward(): pl.pallas_call(ff_kernel, grid=(nx,), in_specs=[pl.BlockSpec(memory_space...]
    ppermute x78 -> x51, starting transfers between devices: 87.5 us -> 67.5 us  [swap(): return lax.ppermute(value, axis, [(i, i ^ bits) for i in range(count)])]
    ppermute x6, waiting for transfers between devices: 8.62 us -> 22.3 us  [chain(): entry = entry + lax.ppermute(out, 'row', [edge])]
    unnamed x229 -> x135, local copies, waits for them, and re-layouts: 15.3 us -> 11.9 us
  transfers between devices with their start and end apart: 85 -> 61, of which waited for: 33 -> 30; matrix products, arithmetic and copies ran while one was open for 28% -> 23% of each run, Pallas kernels for 8% -> 11%
where the time goes in v3:
time: 512 us; the launch traced here: 504 us
  waiting for transfers between devices  188 us (37%)
  Pallas kernels  96.6 us (19%)
  starting transfers between devices  77.5 us (15%)
  other arithmetic  52.4 us (10%)
  matrix products  50.9 us (10%)
  local copies, waits for them, and re-layouts  23.6 us (5%)
  between operations  15.1 us (3%)
    ppermute x51, waiting for transfers between devices, swap(): return lax.ppermute(value, axis, [(i, i ^ bits) for i in range(count)])  166 us
    ppermute x51, starting transfers between devices, swap(): return lax.ppermute(value, axis, [(i, i ^ bits) for i in range(count)])  67.5 us
    dot_general x20, matrix products, dot(): return jnp.einsum(form, left, right, preferred_element_type=F32)  50.9 us
    pallas_call x5, Pallas kernels, head_call(): pl.pallas_call(kernel, grid=(2, heads), in_specs=[specs[k.lower()] for k...  43.3 us
    pallas_call x1, Pallas kernels, feed_forward(): pl.pallas_call(ff_kernel, grid=(nx,), in_specs=[pl.BlockSpec(memory_space...  39.2 us
    ppermute x6, waiting for transfers between devices, chain(): entry = entry + lax.ppermute(out, 'row', [edge])  22.3 us
    unnamed x135, local copies, waits for them, and re-layouts  11.9 us
  transfers between devices with their start and end apart: 61, of which 30 were waited for; matrix products, arithmetic and copies ran while one was open for 23% of the time, Pallas kernels for 11%

profile of v3, /device:TPU:0, one launch (start us, length us, event | category | flops | bytes accessed | tf_op | source)
XLA Modules:
  0.0 504.4 jit_solution(14349458979834636153)
XLA Ops:
  19.9 3.0 collective-permute-start.6
  24.1 5.9 %collective-permute-done.6 = bf16[128,512]{1,0:T(8,128)(2,1)S(1)} collective-permute-done((bf16[128,512]{1,0:T(8,128)(2,1)S(1)}, bf16[128,512]{1,0:T(8,128)(2,1)S(1)}, u32[]{:S(2)}, u32[]{:S(2)}) %collective-permute-start.6) | collective-permute-done | bytes 131104 | tf_op jit(solution)/shard_map/ppermute | solution.py:23
  33.1 21.6 %collective-permute-done.12 = bf16[256,512]{1,0:T(8,128)(2,1)S(1)} collective-permute-done((bf16[256,512]{1,0:T(8,128)(2,1)S(1)}, bf16[256,512]{1,0:T(8,128)(2,1)S(1)}, u32[]{:S(2)}, u32[]{:S(2)}) %collective-permute-start.12) | collective-permute-done | bytes 262176 | tf_op jit(solution)/shard_map/ppermute | solution.py:23
  57.0 3.0 collective-permute-done.7
  65.8 3.7 assemble.2
  70.9 9.8 %collective-permute-done.13 = bf16[512,512]{1,0:T(8,128)(2,1)} collective-permute-done((bf16[512,512]{1,0:T(8,128)(2,1)}, bf16[512,512]{1,0:T(8,128)(2,1)}, u32[]{:S(2)}, u32[]{:S(2)}) %collective-permute-start.13) | collective-permute-done | bytes 524320 | tf_op jit(solution)/shard_map/ppermute | solution.py:23
  83.2 5.1 %collective-permute-done.9 = bf16[512,512]{1,0:T(8,128)(2,1)} collective-permute-done((bf16[512,512]{1,0:T(8,128)(2,1)}, bf16[512,512]{1,0:T(8,128)(2,1)}, u32[]{:S(2)}, u32[]{:S(2)}) %collective-permute-start.9) | collective-permute-done | bytes 524320 | tf_op jit(solution)/shard_map/ppermute | solution.py:23
  94.7 7.9 %collective-permute-done.10 = bf16[512,512]{1,0:T(8,128)(2,1)S(1)} collective-permute-done((bf16[512,512]{1,0:T(8,128)(2,1)}, bf16[512,512]{1,0:T(8,128)(2,1)S(1)}, u32[]{:S(2)}, u32[]{:S(2)}) %collective-permute-start.10) | collective-permute-done | bytes 524320 | tf_op jit(solution)/shard_map/ppermute | solution.py:23
  108.0 4.1 collective-permute-done.14
  114.9 9.5 %mixer_first.1 = (bf16[1024,512]{1,0:T(8,128)(2,1)}, bf16[1024,512]{1,0:T(8,128)(2,1)}, bf16[1024,512]{1,0:T(8,128)(2,1)}, f32[1024,512]{1,0:T(8,128)}, f32[2,4,128,128]{3,2,1,0:T(8,128)}) custom-call(f32[4]{0:T(128)} %get-tuple-element.97.rates, f32[2,2]{1,0:T(2,128)} %pad_maximum_fusion.33.marks, f32[2,512,1]{2,1,0:T(8,128)} %copy.36.seg_c, ...), custom_call_target="tpu_custom_call" | custom-call | flops 536870912 | bytes 8388608 | tf_op jit(solution)/shard_map/mixer_first/pallas_call | solution.py:347
  125.6 3.6 collective-permute-start.15
  129.2 11.5 %collective-permute-done.15 = bf16[2,4,128,128]{3,2,1,0:T(8,128)(2,1)S(1)} collective-permute-done((bf16[2,4,128,128]{3,2,1,0:T(8,128)(2,1)S(1)}, bf16[2,4,128,128]{3,2,1,0:T(8,128)(2,1)S(1)}, u32[]{:S(2)}, u32[]{:S(2)}) %collective-permute-start.15) | collective-permute-done | bytes 262176 | tf_op jit(solution)/shard_map/ppermute | solution.py:364
  142.6 3.2 collective-permute-start.19
  145.8 5.9 %collective-permute-done.19 = bf16[128,256]{0,1:T(8,128)(2,1)S(1)} collective-permute-done((bf16[128,256]{0,1:T(8,128)(2,1)S(1)}, bf16[128,256]{0,1:T(8,128)(2,1)S(1)}, u32[]{:S(2)}, u32[]{:S(2)}) %collective-permute-start.19) | collective-permute-done | bytes 65568 | tf_op jit(solution)/shard_map/ppermute | solution.py:23
  152.8 12.5 %collective-permute-done.20 = bf16[256,256]{0,1:T(8,128)(2,1)S(1)} collective-permute-done((bf16[256,256]{0,1:T(8,128)(2,1)S(1)}, bf16[256,256]{0,1:T(8,128)(2,1)S(1)}, u32[]{:S(2)}, u32[]{:S(2)}) %collective-permute-start.20) | collective-permute-done | bytes 131104 | tf_op jit(solution)/shard_map/ppermute | solution.py:23
  167.5 6.9 %mixer_carry.1 = (f32[1024,512]{1,0:T(8,128)}, f32[1024,1]{1,0:T(8,128)}) custom-call(f32[4]{0:T(128)} %get-tuple-element.97.rates, f32[2,2]{1,0:T(2,128)} %pad_maximum_fusion.33.marks, f32[2,512,1]{2,1,0:T(8,128)} %copy.36.seg_c, f32[1024,512]{1,0:T(8,128)} %get-tuple-element.41.o_in, bf16[1024,512]{1,0:T(8,128)(2,1)} %get-tuple-element.42.q.q_ref, ...), custom_call_target="tpu_custom_call" | custom-call | flops 67108864 | bytes 8388608 | tf_op jit(solution)/shard_map/mixer_carry/pallas_call | solution.py:347
  178.0 4.5 multiply_convert_fusion.2
  185.3 5.1 %collective-permute-done.23 = bf16[512,256]{0,1:T(8,128)(2,1)} collective-permute-done((bf16[512,256]{0,1:T(8,128)(2,1)}, bf16[512,256]{0,1:T(8,128)(2,1)}, u32[]{:S(2)}, u32[]{:S(2)}) %collective-permute-start.23) | collective-permute-done | bytes 262176 | tf_op jit(solution)/shard_map/ppermute | solution.py:23
  196.5 7.2 %collective-permute-done.27.refs_2_ = bf16[512,256]{1,0:T(8,128)(2,1)S(1)} collective-permute-done((bf16[512,256]{1,0:T(8,128)(2,1)S(1)}, bf16[512,256]{1,0:T(8,128)(2,1)S(1)}, u32[]{:S(2)}, u32[]{:S(2)}) %collective-permute-start.27) | collective-permute-done | bytes 262176 | tf_op jit(solution)/shard_map/ppermute | solution.py:23
  203.7 3.7 collective-permute-done.28.refs_3_
  208.1 3.5 assemble.3
  220.4 39.2 %feed_forward.1 = (f32[512,1024]{1,0:T(8,128)}, bf16[512,1024]{1,0:T(8,128)(2,1)}, f32[512,1024]{1,0:T(8,128)}, bf16[512,1024]{1,0:T(8,128)(2,1)}, bf16[2,8,2112,128]{3,2,1,0:T(8,128)(2,1)}) custom-call(s32[2,8]{1,0:T(2,128)} %pad_add_fusion.tables, bf16[1024,1024]{1,0:T(8,128)(2,1)} %pad_maximum_fusion.b_ref, bf16[1024,1024]{1,0:T(8,128)(2,1)} %pad_maximum_fusion.1.g_ref, ...), custom_call_target="tpu_custom_call" | custom-call | flops 26575110144 | bytes 37748736 | tf_op jit(solution)/shard_map/feed_forward/pallas_call | solution.py:455
  268.5 3.4 divide.2
  273.9 11.3 %collective-permute-done.31 = bf16[512,256]{1,0:T(8,128)(2,1)S(1)} collective-permute-done((bf16[512,256]{1,0:T(8,128)(2,1)}, bf16[512,256]{1,0:T(8,128)(2,1)S(1)}, u32[]{:S(2)}, u32[]{:S(2)}) %collective-permute-start.31) | collective-permute-done | bytes 262176 | tf_op jit(solution)/shard_map/ppermute | solution.py:23
  285.2 10.7 %collective-permute-done.32 = bf16[512,256]{1,0:T(8,128)(2,1)S(1)} collective-permute-done((bf16[512,256]{1,0:T(8,128)(2,1)}, bf16[512,256]{1,0:T(8,128)(2,1)S(1)}, u32[]{:S(2)}, u32[]{:S(2)}) %collective-permute-start.32) | collective-permute-done | bytes 262176 | tf_op jit(solution)/shard_map/ppermute | solution.py:23
  298.5 4.2 multiply_reduce_fusion
  305.9 4.3 subtract_convert_fusion
  310.1 7.3 %mixer_entry_grad.1 = f32[2,4,128,128]{3,2,1,0:T(8,128)} custom-call(f32[4]{0:T(128)} %get-tuple-element.97.rates, f32[2,2]{1,0:T(2,128)} %pad_maximum_fusion.33.marks, f32[2,512,1]{2,1,0:T(8,128)} %copy.36.seg_c, bf16[1024,512]{1,0:T(8,128)(2,1)} %get-tuple-element.42.q.q_ref, bf16[1024,512]{1,0:T(8,128)(2,1)} %get-tuple-element.100.do_ref.do), custom_call_target="tpu_custom_call" | custom-call | flops 67108864 | bytes 8388608 | tf_op jit(solution)/shard_map/mixer_entry_grad/pallas_call | solution.py:347
  319.3 3.0 convolution_convert_fusion
  326.3 11.3 %mixer_inner_grad.1 = (bf16[1024,512]{1,0:T(8,128)(2,1)}, f32[1024,512]{1,0:T(8,128)}, f32[1024,512]{1,0:T(8,128)}) custom-call(f32[4]{0:T(128)} %get-tuple-element.97.rates, f32[2,2]{1,0:T(2,128)} %pad_maximum_fusion.33.marks, f32[2,512,1]{2,1,0:T(8,128)} %copy.36.seg_c, f32[2,1,512]{2,1,0:T(1,128)} %copy.35.seg_r, ...), custom_call_target="tpu_custom_call" | custom-call | flops 1342177280 | bytes 8388608 | tf_op jit(solution)/shard_map/mixer_inner_grad/pallas_call | solution.py:347
  337.6 3.2 convolution_convert_fusion.4
  348.1 7.6 %collective-permute-done.54 = bf16[512,512]{0,1:T(8,128)(2,1)} collective-permute-done((bf16[512,512]{0,1:T(8,128)(2,1)}, bf16[512,512]{0,1:T(8,128)(2,1)}, u32[]{:S(2)}, u32[]{:S(2)}) %collective-permute-start.54) | collective-permute-done | bytes 524320 | tf_op jit(solution)/shard_map/ppermute | solution.py:23
  359.3 10.8 %collective-permute-done.39 = bf16[2,4,128,128]{3,2,1,0:T(8,128)(2,1)S(1)} collective-permute-done((bf16[2,4,128,128]{3,2,1,0:T(8,128)(2,1)S(1)}, bf16[2,4,128,128]{3,2,1,0:T(8,128)(2,1)S(1)}, u32[]{:S(2)}, u32[]{:S(2)}) %collective-permute-start.39) | collective-permute-done | bytes 262176 | tf_op jit(solution)/shard_map/ppermute | solution.py:364
  370.8 8.2 %mixer_last_grad.1 = (bf16[1024,512]{1,0:T(8,128)(2,1)}, bf16[1024,512]{1,0:T(8,128)(2,1)}) custom-call(f32[4]{0:T(128)} %get-tuple-element.97.rates, f32[2,2]{1,0:T(2,128)} %pad_maximum_fusion.33.marks, f32[2,512,1]{2,1,0:T(8,128)} %copy.36.seg_c, bf16[1024,512]{1,0:T(8,128)(2,1)} %get-tuple-element.55.k_ref.k, ...), custom_call_target="tpu_custom_call" | custom-call | flops 134217728 | bytes 8388608 | tf_op jit(solution)/shard_map/mixer_last_grad/pallas_call | solution.py:347
  379.1 3.3 convolution_convert_fusion.2
  400.7 8.8 %collective-permute-start.56 = (bf16[256,512]{0,1:T(8,128)(2,1)}, bf16[256,512]{0,1:T(8,128)(2,1)}, u32[]{:S(2)}, u32[]{:S(2)}) collective-permute-start(bf16[256,512]{0,1:T(8,128)(2,1)} %slice.366), channel_id=1, source_target_pairs={{0,16},{8,24},{16,0},{24,8},{1,17},{9,25},{17,1},{25,9},{2,18},{10... | collective-permute-start | bytes 786440 | tf_op jit(solution)/shard_map/ppermute | solution.py:23
  414.0 5.0 collective-permute-done.50
  420.1 10.1 %collective-permute-start.51 = (bf16[256,256]{1,0:T(8,128)(2,1)S(1)}, bf16[256,256]{1,0:T(8,128)(2,1)S(1)}, u32[]{:S(2)}, u32[]{:S(2)}) collective-permute-start(bf16[256,256]{1,0:T(8,128)(2,1)S(1)} %slice.369), channel_id=1, source_target_pairs={{0,16},{8,24},{16,0},{24,8},{1,17},{9,25},{17,1},{25,9},{2,18},{10... | collective-permute-start | bytes 393224 | tf_op jit(solution)/shard_map/ppermute | solution.py:23
  431.4 3.2 collective-permute-start.57
  434.6 8.1 %collective-permute-done.51 = bf16[256,256]{1,0:T(8,128)(2,1)S(1)} collective-permute-done((bf16[256,256]{1,0:T(8,128)(2,1)S(1)}, bf16[256,256]{1,0:T(8,128)(2,1)S(1)}, u32[]{:S(2)}, u32[]{:S(2)}) %collective-permute-start.51) | collective-permute-done | bytes 131104 | tf_op jit(solution)/shard_map/ppermute | solution.py:23
  443.8 3.0 collective-permute-done.57
  458.2 3.9 fusion
  462.5 4.2 fusion.2.rows_ref
  466.7 3.4 divide.3
  474.6 4.4 collective-permute-done.41
  479.0 5.0 collective-permute-done.42
  484.1 4.1 collective-permute-done.46
  489.4 3.9 collective-permute-done.47
  (341 shorter events, 153.1 us)
Async XLA Ops:
  7.2 213.2 %all-gather.2.cloned.1.call-start = ((), (), s32[]{:S(2)}) async-start(), calls=%async_computation.2 | async-start | bytes 9191424 | tf_op jit(solution)/shard_map/all_gather | solution.py:377
  9.4 404.5 %reduce-scatter.3.cloned.1.call-start = ((), (), s32[]{:S(2)}) async-start(), calls=%async_computation.3 | async-start | bytes 10813440 | tf_op jit(solution)/shard_map/reduce_scatter | solution.py:403
  10.3 53.6 %collective-permute-start = (bf16[512,256]{1,0:T(8,128)(2,1)S(1)}, bf16[512,256]{1,0:T(8,128)(2,1)S(1)}, u32[]{:S(2)}, u32[]{:S(2)}) collective-permute-start(bf16[512,256]{1,0:T(8,128)(2,1)S(1)} %get-tuple-element.136), channel_id=1, source_target_pairs={{0,2},{2,0},{4,6},{6,4},{1,3},{3,1},{5,7},{7,5},{8,10},{10,8},{12,... | collective-permute-start | bytes 786440 | tf_op jit(solution)/shard_map/ppermute | solution.py:23
  10.8 54.3 %collective-permute-start.1 = (bf16[512,256]{1,0:T(8,128)(2,1)S(1)}, bf16[512,256]{1,0:T(8,128)(2,1)S(1)}, u32[]{:S(2)}, u32[]{:S(2)}) collective-permute-start(bf16[512,256]{1,0:T(8,128)(2,1)S(1)} %get-tuple-element.138), channel_id=1, source_target_pairs={{0,4},{2,6},{4,0},{6,2},{1,5},{3,7},{5,1},{7,3},{8,12},{10,14},{12... | collective-permute-start | bytes 786440 | tf_op jit(solution)/shard_map/ppermute | solution.py:23
  13.2 51.8 %collective-permute-start.2 = (bf16[512,256]{1,0:T(8,128)(2,1)S(1)}, bf16[512,256]{1,0:T(8,128)(2,1)S(1)}, u32[]{:S(2)}, u32[]{:S(2)}) collective-permute-start(bf16[512,256]{1,0:T(8,128)(2,1)S(1)} %get-tuple-element.135), channel_id=1, source_target_pairs={{0,6},{2,4},{4,2},{6,0},{1,7},{3,5},{5,3},{7,1},{8,14},{10,12},{12... | collective-permute-start | bytes 786440 | tf_op jit(solution)/shard_map/ppermute | solution.py:23
  13.4 9.6 %collective-permute-start.11 = (bf16[128,512]{1,0:T(8,128)(2,1)S(1)}, bf16[128,512]{1,0:T(8,128)(2,1)S(1)}, u32[]{:S(2)}, u32[]{:S(2)}) collective-permute-start(bf16[128,512]{1,0:T(8,128)(2,1)S(1)} %fusion.29), channel_id=1, source_target_pairs={{0,8},{8,0},{16,24},{24,16},{1,9},{9,1},{17,25},{25,17},{2,10},{10... | collective-permute-start | bytes 393224 | tf_op jit(solution)/shard_map/ppermute | solution.py:23
  19.9 10.1 %collective-permute-start.6 = (bf16[128,512]{1,0:T(8,128)(2,1)S(1)}, bf16[128,512]{1,0:T(8,128)(2,1)S(1)}, u32[]{:S(2)}, u32[]{:S(2)}) collective-permute-start(bf16[128,512]{1,0:T(8,128)(2,1)S(1)} %fusion.30), channel_id=1, source_target_pairs={{0,8},{8,0},{16,24},{24,16},{1,9},{9,1},{17,25},{25,17},{2,10},{10... | collective-permute-start | bytes 393224 | tf_op jit(solution)/shard_map/ppermute | solution.py:23
  23.0 31.7 %collective-permute-start.12 = (bf16[256,512]{1,0:T(8,128)(2,1)S(1)}, bf16[256,512]{1,0:T(8,128)(2,1)S(1)}, u32[]{:S(2)}, u32[]{:S(2)}) collective-permute-start(bf16[256,512]{1,0:T(8,128)(2,1)S(1)} %pad_maximum_fusion.29), channel_id=1, source_target_pairs={{0,16},{8,24},{16,0},{24,8},{1,17},{9,25},{17,1},{25,9},{2,18},{10... | collective-permute-start | bytes 786440 | tf_op jit(solution)/shard_map/ppermute | solution.py:23
  30.0 30.0 %collective-permute-start.7 = (bf16[256,512]{1,0:T(8,128)(2,1)S(1)}, bf16[256,512]{1,0:T(8,128)(2,1)S(1)}, u32[]{:S(2)}, u32[]{:S(2)}) collective-permute-start(bf16[256,512]{1,0:T(8,128)(2,1)S(1)} %pad_maximum_fusion.28), channel_id=1, source_target_pairs={{0,16},{8,24},{16,0},{24,8},{1,17},{9,25},{17,1},{25,9},{2,18},{10... | collective-permute-start | bytes 786440 | tf_op jit(solution)/shard_map/ppermute | solution.py:23
  60.0 20.6 %collective-permute-start.13 = (bf16[512,512]{1,0:T(8,128)(2,1)}, bf16[512,512]{1,0:T(8,128)(2,1)}, u32[]{:S(2)}, u32[]{:S(2)}) collective-permute-start(bf16[512,512]{1,0:T(8,128)(2,1)} %pad_maximum_fusion.15), channel_id=1, source_target_pairs={{0,1},{1,0},{2,3},{3,2},{4,5},{5,4},{6,7},{7,6},{8,9},{9,8},{10,11... | collective-permute-start | bytes 1572872 | tf_op jit(solution)/shard_map/ppermute | solution.py:23
  62.4 26.0 %collective-permute-start.9 = (bf16[512,512]{1,0:T(8,128)(2,1)}, bf16[512,512]{1,0:T(8,128)(2,1)}, u32[]{:S(2)}, u32[]{:S(2)}) collective-permute-start(bf16[512,512]{1,0:T(8,128)(2,1)} %pad_maximum_fusion.14), channel_id=1, source_target_pairs={{0,4},{2,6},{4,0},{6,2},{1,5},{3,7},{5,1},{7,3},{8,12},{10,14},{12... | collective-permute-start | bytes 1572872 | tf_op jit(solution)/shard_map/ppermute | solution.py:23
  63.9 28.0 %collective-permute-start.8 = (bf16[512,512]{1,0:T(8,128)(2,1)}, bf16[512,512]{1,0:T(8,128)(2,1)}, u32[]{:S(2)}, u32[]{:S(2)}) collective-permute-start(bf16[512,512]{1,0:T(8,128)(2,1)} %pad_maximum_fusion.14), channel_id=1, source_target_pairs={{0,1},{1,0},{2,3},{3,2},{4,5},{5,4},{6,7},{7,6},{8,9},{9,8},{10,11... | collective-permute-start | bytes 1572872 | tf_op jit(solution)/shard_map/ppermute | solution.py:23
  69.5 25.1 %collective-permute-start.5 = (bf16[512,1024]{1,0:T(8,128)(2,1)}, bf16[512,1024]{1,0:T(8,128)(2,1)S(1)}, u32[]{:S(2)}, u32[]{:S(2)}) collective-permute-start(bf16[512,1024]{1,0:T(8,128)(2,1)} %get-tuple-element.40), channel_id=1, source_target_pairs={{0,2},{2,0},{4,6},{6,4},{1,3},{3,1},{5,7},{7,5},{8,10},{10,8},{12,... | collective-permute-start | bytes 3145736 | tf_op jit(solution)/shard_map/ppermute | solution.py:23
  81.7 30.5 %collective-permute-start.14 = (bf16[1024,512]{1,0:T(8,128)(2,1)S(1)}, bf16[1024,512]{1,0:T(8,128)(2,1)S(1)}, u32[]{:S(2)}, u32[]{:S(2)}) collective-permute-start(bf16[1024,512]{1,0:T(8,128)(2,1)S(1)} %pad_maximum_fusion.8), channel_id=1, source_target_pairs={{0,4},{2,6},{4,0},{6,2},{1,5},{3,7},{5,1},{7,3},{8,12},{10,14},{12... | collective-permute-start | bytes 3145736 | tf_op jit(solution)/shard_map/ppermute | solution.py:23
  88.4 14.2 %collective-permute-start.10 = (bf16[512,512]{1,0:T(8,128)(2,1)}, bf16[512,512]{1,0:T(8,128)(2,1)S(1)}, u32[]{:S(2)}, u32[]{:S(2)}) collective-permute-start(bf16[512,512]{1,0:T(8,128)(2,1)} %collective-permute-done.9), channel_id=1, source_target_pairs={{0,1},{1,0},{2,3},{3,2},{4,5},{5,4},{6,7},{7,6},{8,9},{9,8},{10,11... | collective-permute-start | bytes 1572872 | tf_op jit(solution)/shard_map/ppermute | solution.py:23
  125.6 15.1 %collective-permute-start.15 = (bf16[2,4,128,128]{3,2,1,0:T(8,128)(2,1)S(1)}, bf16[2,4,128,128]{3,2,1,0:T(8,128)(2,1)S(1)}, u32[]{:S(2)}, u32[]{:S(2)}) collective-permute-start(bf16[2,4,128,128]{3,2,1,0:T(8,128)(2,1)S(1)} %add_convert_fusion.9), channel_id=1, source_target_pairs={{0,8},{1,9},{2,10},{3,11},{4,12},{5,13},{6,14},{7,15}} | collective-permute-start | bytes 786440 | tf_op jit(solution)/shard_map/ppermute | solution.py:364
  141.9 10.0 %collective-permute-start.16 = (bf16[2,4,128,128]{3,2,1,0:T(8,128)(2,1)S(1)}, bf16[2,4,128,128]{3,2,1,0:T(8,128)(2,1)S(1)}, u32[]{:S(2)}, u32[]{:S(2)}) collective-permute-start(bf16[2,4,128,128]{3,2,1,0:T(8,128)(2,1)S(1)} %add_convert_fusion.8), channel_id=1, source_target_pairs={{8,16},{9,17},{10,18},{11,19},{12,20},{13,21},{14,22},{15,23}} | collective-permute-start | bytes 786440 | tf_op jit(solution)/shard_map/ppermute | solution.py:364
  142.6 9.1 %collective-permute-start.19 = (bf16[128,256]{0,1:T(8,128)(2,1)S(1)}, bf16[128,256]{0,1:T(8,128)(2,1)S(1)}, u32[]{:S(2)}, u32[]{:S(2)}) collective-permute-start(bf16[128,256]{0,1:T(8,128)(2,1)S(1)} %dynamic-slice_bitcast_fusion.8), channel_id=1, source_target_pairs={{0,8},{8,0},{16,24},{24,16},{1,9},{9,1},{17,25},{25,17},{2,10},{10... | collective-permute-start | bytes 196616 | tf_op jit(solution)/shard_map/ppermute | solution.py:23
  151.7 13.6 %collective-permute-start.20 = (bf16[256,256]{0,1:T(8,128)(2,1)S(1)}, bf16[256,256]{0,1:T(8,128)(2,1)S(1)}, u32[]{:S(2)}, u32[]{:S(2)}) collective-permute-start(bf16[256,256]{0,1:T(8,128)(2,1)S(1)} %pad_maximum_fusion.31), channel_id=1, source_target_pairs={{0,16},{8,24},{16,0},{24,8},{1,17},{9,25},{17,1},{25,9},{2,18},{10... | collective-permute-start | bytes 393224 | tf_op jit(solution)/shard_map/ppermute | solution.py:23
  152.0 14.7 %collective-permute-start.17 = (bf16[2,4,128,128]{3,2,1,0:T(8,128)(2,1)S(1)}, bf16[2,4,128,128]{3,2,1,0:T(8,128)(2,1)S(1)}, u32[]{:S(2)}, u32[]{:S(2)}) collective-permute-start(bf16[2,4,128,128]{3,2,1,0:T(8,128)(2,1)S(1)} %get-tuple-element.94), channel_id=1, source_target_pairs={{16,24},{17,25},{18,26},{19,27},{20,28},{21,29},{22,30},{23,31}} | collective-permute-start | bytes 786440 | tf_op jit(solution)/shard_map/ppermute | solution.py:364
  166.1 11.1 %collective-permute-start.22 = (bf16[512,256]{0,1:T(8,128)(2,1)}, bf16[512,256]{0,1:T(8,128)(2,1)}, u32[]{:S(2)}, u32[]{:S(2)}) collective-permute-start(bf16[512,256]{0,1:T(8,128)(2,1)} %pad_maximum_fusion.30), channel_id=1, source_target_pairs={{0,4},{2,6},{4,0},{6,2},{1,5},{3,7},{5,1},{7,3},{8,12},{10,14},{12... | collective-permute-start | bytes 786440 | tf_op jit(solution)/shard_map/ppermute | solution.py:23
  175.7 9.6 %collective-permute-start.21 = (bf16[512,256]{0,1:T(8,128)(2,1)}, bf16[512,256]{0,1:T(8,128)(2,1)}, u32[]{:S(2)}, u32[]{:S(2)}) collective-permute-start(bf16[512,256]{0,1:T(8,128)(2,1)} %pad_maximum_fusion.30), channel_id=1, source_target_pairs={{0,1},{1,0},{2,3},{3,2},{4,5},{5,4},{6,7},{7,6},{8,9},{9,8},{10,11... | collective-permute-start | bytes 786440 | tf_op jit(solution)/shard_map/ppermute | solution.py:23
  177.2 13.2 %collective-permute-start.23 = (bf16[512,256]{0,1:T(8,128)(2,1)}, bf16[512,256]{0,1:T(8,128)(2,1)}, u32[]{:S(2)}, u32[]{:S(2)}) collective-permute-start(bf16[512,256]{0,1:T(8,128)(2,1)} %collective-permute-done.22), channel_id=1, source_target_pairs={{0,1},{1,0},{2,3},{3,2},{4,5},{5,4},{6,7},{7,6},{8,9},{9,8},{10,11... | collective-permute-start | bytes 786440 | tf_op jit(solution)/shard_map/ppermute | solution.py:23
  193.3 19.2 %collective-permute-start.24 = (bf16[512,1024]{1,0:T(8,128)(2,1)}, bf16[512,1024]{1,0:T(8,128)(2,1)S(1)}, u32[]{:S(2)}, u32[]{:S(2)}) collective-permute-start(bf16[512,1024]{1,0:T(8,128)(2,1)} %convolution_convert_fusion.5), channel_id=1, source_target_pairs={{0,2},{2,0},{4,6},{6,4},{1,3},{3,1},{5,7},{7,5},{8,10},{10,8},{12,... | collective-permute-start | bytes 3145736 | tf_op jit(solution)/shard_map/ppermute | solution.py:23
  194.5 9.2 %collective-permute-start.27 = (bf16[512,256]{1,0:T(8,128)(2,1)S(1)}, bf16[512,256]{1,0:T(8,128)(2,1)S(1)}, u32[]{:S(2)}, u32[]{:S(2)}) collective-permute-start(bf16[512,256]{1,0:T(8,128)(2,1)S(1)} %get-tuple-element.126), channel_id=1, source_target_pairs={{0,4},{2,6},{4,0},{6,2},{1,5},{3,7},{5,1},{7,3},{8,12},{10,14},{12... | collective-permute-start | bytes 786440 | tf_op jit(solution)/shard_map/ppermute | solution.py:23
  195.9 11.5 %collective-permute-start.28 = (bf16[512,256]{1,0:T(8,128)(2,1)S(1)}, bf16[512,256]{1,0:T(8,128)(2,1)S(1)}, u32[]{:S(2)}, u32[]{:S(2)}) collective-permute-start(bf16[512,256]{1,0:T(8,128)(2,1)S(1)} %get-tuple-element.123), channel_id=1, source_target_pairs={{0,6},{2,4},{4,2},{6,0},{1,7},{3,5},{5,3},{7,1},{8,14},{10,12},{12... | collective-permute-start | bytes 786440 | tf_op jit(solution)/shard_map/ppermute | solution.py:23
  259.6 235.2 %reduce-scatter.5.cloned.1.call-start = ((), (), s32[]{:S(2)}) async-start(), calls=%async_computation.4 | async-start | bytes 2703360 | tf_op jit(solution)/shard_map/reduce_scatter | solution.py:621
  268.4 29.9 %collective-permute-start.35 = (bf16[512,1024]{1,0:T(8,128)(2,1)}, bf16[512,1024]{1,0:T(8,128)(2,1)S(1)}, u32[]{:S(2)}, u32[]{:S(2)}) collective-permute-start(bf16[512,1024]{1,0:T(8,128)(2,1)} %get-tuple-element.92), channel_id=1, source_target_pairs={{0,2},{2,0},{4,6},{6,4},{1,3},{3,1},{5,7},{7,5},{8,10},{10,8},{12,... | collective-permute-start | bytes 3145736 | tf_op jit(solution)/shard_map/ppermute | solution.py:23
  271.9 13.3 %collective-permute-start.31 = (bf16[512,256]{1,0:T(8,128)(2,1)}, bf16[512,256]{1,0:T(8,128)(2,1)S(1)}, u32[]{:S(2)}, u32[]{:S(2)}) collective-permute-start(bf16[512,256]{1,0:T(8,128)(2,1)} %get-tuple-element.48), channel_id=1, source_target_pairs={{0,6},{2,4},{4,2},{6,0},{1,7},{3,5},{5,3},{7,1},{8,14},{10,12},{12... | collective-permute-start | bytes 786440 | tf_op jit(solution)/shard_map/ppermute | solution.py:23
  273.3 22.6 %collective-permute-start.32 = (bf16[512,256]{1,0:T(8,128)(2,1)}, bf16[512,256]{1,0:T(8,128)(2,1)S(1)}, u32[]{:S(2)}, u32[]{:S(2)}) collective-permute-start(bf16[512,256]{1,0:T(8,128)(2,1)} %get-tuple-element.49), channel_id=1, source_target_pairs={{0,4},{2,6},{4,0},{6,2},{1,5},{3,7},{5,1},{7,3},{8,12},{10,14},{12... | collective-permute-start | bytes 786440 | tf_op jit(solution)/shard_map/ppermute | solution.py:23
  273.9 22.0 %collective-permute-start.33 = (bf16[512,256]{1,0:T(8,128)(2,1)}, bf16[512,256]{1,0:T(8,128)(2,1)S(1)}, u32[]{:S(2)}, u32[]{:S(2)}) collective-permute-start(bf16[512,256]{1,0:T(8,128)(2,1)} %get-tuple-element.50), channel_id=1, source_target_pairs={{0,2},{2,0},{4,6},{6,4},{1,3},{3,1},{5,7},{7,5},{8,10},{10,8},{12,... | collective-permute-start | bytes 786440 | tf_op jit(solution)/shard_map/ppermute | solution.py:23
  318.6 24.3 %collective-permute-start.37 = (bf16[2,4,128,128]{3,2,1,0:T(8,128)(2,1)S(1)}, bf16[2,4,128,128]{3,2,1,0:T(8,128)(2,1)S(1)}, u32[]{:S(2)}, u32[]{:S(2)}) collective-permute-start(bf16[2,4,128,128]{3,2,1,0:T(8,128)(2,1)S(1)} %add_convert_fusion.6), channel_id=1, source_target_pairs={{24,16},{25,17},{26,18},{27,19},{28,20},{29,21},{30,22},{31,23}} | collective-permute-start | bytes 786440 | tf_op jit(solution)/shard_map/ppermute | solution.py:364
  323.5 73.5 %collective-permute-start.53 = (bf16[512,512]{0,1:T(8,128)(2,1)}, bf16[512,512]{0,1:T(8,128)(2,1)}, u32[]{:S(2)}, u32[]{:S(2)}) collective-permute-start(bf16[512,512]{0,1:T(8,128)(2,1)} %pad_maximum_fusion.13), channel_id=1, source_target_pairs={{0,1},{1,0},{2,3},{3,2},{4,5},{5,4},{6,7},{7,6},{8,9},{9,8},{10,11... | collective-permute-start | bytes 1572872 | tf_op jit(solution)/shard_map/ppermute | solution.py:23
  325.8 29.9 %collective-permute-start.54 = (bf16[512,512]{0,1:T(8,128)(2,1)}, bf16[512,512]{0,1:T(8,128)(2,1)}, u32[]{:S(2)}, u32[]{:S(2)}) collective-permute-start(bf16[512,512]{0,1:T(8,128)(2,1)} %pad_maximum_fusion.12), channel_id=1, source_target_pairs={{0,1},{1,0},{2,3},{3,2},{4,5},{5,4},{6,7},{7,6},{8,9},{9,8},{10,11... | collective-permute-start | bytes 1572872 | tf_op jit(solution)/shard_map/ppermute | solution.py:23
  345.8 24.3 %collective-permute-start.39 = (bf16[2,4,128,128]{3,2,1,0:T(8,128)(2,1)S(1)}, bf16[2,4,128,128]{3,2,1,0:T(8,128)(2,1)S(1)}, u32[]{:S(2)}, u32[]{:S(2)}) collective-permute-start(bf16[2,4,128,128]{3,2,1,0:T(8,128)(2,1)S(1)} %get-tuple-element.90), channel_id=1, source_target_pairs={{8,0},{9,1},{10,2},{11,3},{12,4},{13,5},{14,6},{15,7}} | collective-permute-start | bytes 786440 | tf_op jit(solution)/shard_map/ppermute | solution.py:364
  357.7 39.2 %collective-permute-start.55 = (bf16[512,512]{0,1:T(8,128)(2,1)}, bf16[512,512]{0,1:T(8,128)(2,1)}, u32[]{:S(2)}, u32[]{:S(2)}) collective-permute-start(bf16[512,512]{0,1:T(8,128)(2,1)} %add_convert_fusion.2), channel_id=1, source_target_pairs={{0,4},{2,6},{4,0},{6,2},{1,5},{3,7},{5,1},{7,3},{8,12},{10,14},{12... | collective-permute-start | bytes 1572872 | tf_op jit(solution)/shard_map/ppermute | solution.py:23
  383.2 26.4 %collective-permute-start.49 = (bf16[512,256]{1,0:T(8,128)(2,1)S(1)}, bf16[512,256]{1,0:T(8,128)(2,1)S(1)}, u32[]{:S(2)}, u32[]{:S(2)}) collective-permute-start(bf16[512,256]{1,0:T(8,128)(2,1)S(1)} %get-tuple-element.110), channel_id=1, source_target_pairs={{0,1},{1,0},{2,3},{3,2},{4,5},{5,4},{6,7},{7,6},{8,9},{9,8},{10,11... | collective-permute-start | bytes 786440 | tf_op jit(solution)/shard_map/ppermute | solution.py:23
  385.5 28.4 %collective-permute-start.48 = (bf16[512,256]{1,0:T(8,128)(2,1)}, bf16[512,256]{1,0:T(8,128)(2,1)S(1)}, u32[]{:S(2)}, u32[]{:S(2)}) collective-permute-start(bf16[512,256]{1,0:T(8,128)(2,1)} %get-tuple-element.109), channel_id=1, source_target_pairs={{0,1},{1,0},{2,3},{3,2},{4,5},{5,4},{6,7},{7,6},{8,9},{9,8},{10,11... | collective-permute-start | bytes 786440 | tf_op jit(solution)/shard_map/ppermute | solution.py:23
  389.1 63.4 %collective-permute-start.44 = (bf16[1024,512]{0,1:T(8,128)(2,1)}, bf16[1024,512]{0,1:T(8,128)(2,1)}, u32[]{:S(2)}, u32[]{:S(2)}) collective-permute-start(bf16[1024,512]{0,1:T(8,128)(2,1)} %pad_maximum_fusion.11), channel_id=1, source_target_pairs={{0,4},{2,6},{4,0},{6,2},{1,5},{3,7},{5,1},{7,3},{8,12},{10,14},{12... | collective-permute-start | bytes 3145736 | tf_op jit(solution)/shard_map/ppermute | solution.py:23
  400.7 29.5 %collective-permute-start.56 = (bf16[256,512]{0,1:T(8,128)(2,1)}, bf16[256,512]{0,1:T(8,128)(2,1)}, u32[]{:S(2)}, u32[]{:S(2)}) collective-permute-start(bf16[256,512]{0,1:T(8,128)(2,1)} %slice.366), channel_id=1, source_target_pairs={{0,16},{8,24},{16,0},{24,8},{1,17},{9,25},{17,1},{25,9},{2,18},{10... | collective-permute-start | bytes 786440 | tf_op jit(solution)/shard_map/ppermute | solution.py:23
  413.9 44.3 %collective-permute-start.40 = (bf16[512,1024]{1,0:T(8,128)(2,1)}, bf16[512,1024]{1,0:T(8,128)(2,1)}, u32[]{:S(2)}, u32[]{:S(2)}) collective-permute-start(bf16[512,1024]{1,0:T(8,128)(2,1)} %add_convert_fusion), channel_id=1, source_target_pairs={{0,2},{2,0},{4,6},{6,4},{1,3},{3,1},{5,7},{7,5},{8,10},{10,8},{12,... | collective-permute-start | bytes 3145736 | tf_op jit(solution)/shard_map/ppermute | solution.py:23
  420.1 22.7 %collective-permute-start.51 = (bf16[256,256]{1,0:T(8,128)(2,1)S(1)}, bf16[256,256]{1,0:T(8,128)(2,1)S(1)}, u32[]{:S(2)}, u32[]{:S(2)}) collective-permute-start(bf16[256,256]{1,0:T(8,128)(2,1)S(1)} %slice.369), channel_id=1, source_target_pairs={{0,16},{8,24},{16,0},{24,8},{1,17},{9,25},{17,1},{25,9},{2,18},{10... | collective-permute-start | bytes 393224 | tf_op jit(solution)/shard_map/ppermute | solution.py:23
  431.4 15.4 %collective-permute-start.57 = (bf16[128,512]{0,1:T(8,128)(2,1)S(1)}, bf16[128,512]{0,1:T(8,128)(2,1)S(1)}, u32[]{:S(2)}, u32[]{:S(2)}) collective-permute-start(bf16[128,512]{0,1:T(8,128)(2,1)S(1)} %slice.368), channel_id=1, source_target_pairs={{0,8},{8,0},{16,24},{24,16},{1,9},{9,1},{17,25},{25,17},{2,10},{10... | collective-permute-start | bytes 393224 | tf_op jit(solution)/shard_map/ppermute | solution.py:23
  456.8 15.2 %collective-permute-start.45 = (bf16[512,512]{0,1:T(8,128)(2,1)}, bf16[512,512]{0,1:T(8,128)(2,1)}, u32[]{:S(2)}, u32[]{:S(2)}) collective-permute-start(bf16[512,512]{0,1:T(8,128)(2,1)} %slice.365), channel_id=1, source_target_pairs={{0,1},{1,0},{2,3},{3,2},{4,5},{5,4},{6,7},{7,6},{8,9},{9,8},{10,11... | collective-permute-start | bytes 1572872 | tf_op jit(solution)/shard_map/ppermute | solution.py:23
  470.1 8.9 %collective-permute-start.41 = (bf16[512,256]{1,0:T(8,128)(2,1)}, bf16[512,256]{1,0:T(8,128)(2,1)S(1)}, u32[]{:S(2)}, u32[]{:S(2)}) collective-permute-start(bf16[512,256]{1,0:T(8,128)(2,1)} %get-tuple-element.62), channel_id=1, source_target_pairs={{0,6},{2,4},{4,2},{6,0},{1,7},{3,5},{5,3},{7,1},{8,14},{10,12},{12... | collective-permute-start | bytes 786440 | tf_op jit(solution)/shard_map/ppermute | solution.py:23
  470.2 13.8 %collective-permute-start.42 = (bf16[512,256]{1,0:T(8,128)(2,1)}, bf16[512,256]{1,0:T(8,128)(2,1)S(1)}, u32[]{:S(2)}, u32[]{:S(2)}) collective-permute-start(bf16[512,256]{1,0:T(8,128)(2,1)} %get-tuple-element.63), channel_id=1, source_target_pairs={{0,4},{2,6},{4,0},{6,2},{1,5},{3,7},{5,1},{7,3},{8,12},{10,14},{12... | collective-permute-start | bytes 786440 | tf_op jit(solution)/shard_map/ppermute | solution.py:23
  471.4 12.6 %collective-permute-start.43 = (bf16[512,256]{1,0:T(8,128)(2,1)}, bf16[512,256]{1,0:T(8,128)(2,1)S(1)}, u32[]{:S(2)}, u32[]{:S(2)}) collective-permute-start(bf16[512,256]{1,0:T(8,128)(2,1)} %get-tuple-element.64), channel_id=1, source_target_pairs={{0,2},{2,0},{4,6},{6,4},{1,3},{3,1},{5,7},{7,5},{8,10},{10,8},{12,... | collective-permute-start | bytes 786440 | tf_op jit(solution)/shard_map/ppermute | solution.py:23
  473.3 14.8 %collective-permute-start.46 = (bf16[256,512]{0,1:T(8,128)(2,1)S(1)}, bf16[256,512]{0,1:T(8,128)(2,1)S(1)}, u32[]{:S(2)}, u32[]{:S(2)}) collective-permute-start(bf16[256,512]{0,1:T(8,128)(2,1)S(1)} %slice.367), channel_id=1, source_target_pairs={{0,16},{8,24},{16,0},{24,8},{1,17},{9,25},{17,1},{25,9},{2,18},{10... | collective-permute-start | bytes 786440 | tf_op jit(solution)/shard_map/ppermute | solution.py:23
  (77 other events, 892.3 us)
Sparse Core Ops, SparseCore 0:
  10.7 155.9 all-gather.1
  259.8 116.2 reduce-scatter.2
  414.1 52.5 reduce-scatter.4

commit v4 on v3

--- a/solution.py
+++ b/solution.py
@@ -175,22 +175,19 @@
     return jnp.stack(pick4(got, (col & 1) != 0, (col & 2) != 0))
 
 
-def gather_weight(shard, order):
+def gather_weights(first, second):
     ny = lax.axis_size("dp")
-    rows, width = shard.shape
-    part = rows // ny
-    start = lax.axis_index("dp") * part
-    value = lax.dynamic_slice_in_dim(shard, start, part, 0)
+    part, width = first.shape[0] // ny, first.shape[1]
+    value = jnp.concatenate([first, second], 1)
+    value = lax.dynamic_slice_in_dim(value, lax.axis_index("dp") * part, part, 0)
     for bit in bits_of("row"):
         value = jnp.concatenate([value, swap(value, "row", bit)], 0)
-    if order == "yx":
-        for bit in bits_of("dp"):
-            value = jnp.concatenate([value, swap(value, "dp", bit)], 0)
-        return [value, side(value)]
-    values = [value, side(value)]
+    one, two = value[:, :width], value[:, width:]
+    one = jnp.concatenate([one, side(one)], 1)
     for bit in bits_of("dp"):
-        values = [jnp.concatenate([v, swap(v, "dp", bit)], 0) for v in values]
-    return values
+        two = jnp.concatenate([two, swap(two, "dp", bit)], 0)
+        one = jnp.concatenate([one, swap(one, "dp", bit)], 0)
+    return one, jnp.concatenate([two, side(two)], 1), value
 
 
 def fold(value, axis):
@@ -201,14 +198,18 @@
     return value
 
 
-def reduce_grad(own, other, order):
-    if order == "xy":
-        value = own.astype(F32) + side(other).astype(F32)
-        value = fold(value, "dp")
-    else:
-        own, other = fold(own, "dp"), fold(other, "dp")
-        value = own + side(other.astype(BF16)).astype(F32)
-    return fold(value, "row")
+def fold_side(value):
+    half = value.shape[1] // 2
+    got = side(value[:, half:].astype(BF16))
+    return value[:, :half].astype(F32) + got.astype(F32)
+
+
+def reduce_first(one, two):
+    return fold_side(one), fold(two, "dp")
+
+
+def reduce_rest(one, two):
+    return fold(jnp.concatenate([fold(one, "dp"), fold_side(two)], 1), "row")
 
 
 def dot(left, right, form):
@@ -254,89 +255,100 @@
     return jnp.where(seg_col == entry_seg, jnp.exp(-rate * (column(tokens) + 1.0)), 0.0)
 
 
-def first_kernel(rates, marks, seg_c, seg_r, zq, zk, zv, q_out, k_out, v_out, o_out, state):
-    block, head = pl.program_id(0), pl.program_id(1)
-    rate = rates[head]
-    pre_q, pre_k = zq[...], zk[...]
-    q = (pre_q * jax.nn.sigmoid(pre_q)).astype(BF16)
-    k_wide = pre_k * jax.nn.sigmoid(pre_k)
-    k = k_wide.astype(BF16)
-    v = zv[...].astype(BF16)
-    q_out[...], k_out[...], v_out[...] = q, k, v
-    seg = seg_c[0]
-    weight = own_weight(rate, seg, marks[block, 0])
-    state[0, 0] = tn((k.astype(F32) * weight).astype(BF16), v)
-    tokens = q.shape[0]
-    for at in range(0, tokens, TILE):
-        width = at + TILE
-        decay = tile_decay(rate, seg[at:width], seg_r[0, :, :width], at, width)
-        mix = (nt(q[at:width], k[:width]) * decay).astype(BF16)
-        o_out[at:width, :] = nn(mix, v[:width])
+def lanes(head):
+    return slice(head * HEAD, (head + 1) * HEAD)
+
+
+def local_kernel(rates, marks, seg_c, zk, zv, k_out, v_out, state):
+    last = marks[pl.program_id(0), 0]
+    for head in range(state.shape[1]):
+        at = lanes(head)
+        pre = zk[:, at]
+        k, v = (pre * jax.nn.sigmoid(pre)).astype(BF16), zv[:, at].astype(BF16)
+        k_out[:, at], v_out[:, at] = k, v
+        weight = own_weight(rates[head], seg_c[0], last)
+        state[0, head] = tn((k.astype(F32) * weight).astype(BF16), v)
+
+
+def inner_kernel(rates, marks, seg_c, seg_r, zq, k_ref, v_ref, q_out, o_out):
+    seg, tokens = seg_c[0], seg_c.shape[1]
+    for head in range(zq.shape[1] // HEAD):
+        at = lanes(head)
+        pre = zq[:, at]
+        q_out[:, at] = (pre * jax.nn.sigmoid(pre)).astype(BF16)
+        for top in range(0, tokens, TILE):
+            width = top + TILE
+            decay = tile_decay(rates[head], seg[top:width], seg_r[0, :, :width], top, width)
+            mix = (nt(q_out[top:width, at], k_ref[:width, at]) * decay).astype(BF16)
+            o_out[top:width, at] = nn(mix, v_ref[:width, at])
 
 
 def carry_kernel(rates, marks, seg_c, o_in, q, entry, o_out, squares):
-    block, head = pl.program_id(0), pl.program_id(1)
-    weight = entry_weight(rates[head], seg_c[0], marks[block, 1])
-    o = o_in[...] + weight * nn(q[...], entry[0, 0])
-    o_out[...] = o
-
-    @pl.when(head == 0)
-    def _():
-        squares[...] = jnp.zeros_like(squares)
-
-    squares[...] += jnp.sum(o * o, 1, keepdims=True)
+    before = marks[pl.program_id(0), 1]
+    total = 0.0
+    for head in range(entry.shape[1]):
+        at = lanes(head)
+        weight = entry_weight(rates[head], seg_c[0], before)
+        o = o_in[:, at] + weight * nn(q[:, at], entry[0, head])
+        o_out[:, at] = o
+        total = total + o * o
+    squares[...] = jnp.sum(total, 1, keepdims=True)
 
 
 def entry_grad_kernel(rates, marks, seg_c, q, do, grad):
-    block, head = pl.program_id(0), pl.program_id(1)
-    weight = entry_weight(rates[head], seg_c[0], marks[block, 1])
-    grad[0, 0] = tn(q[...], (do[...].astype(F32) * weight).astype(BF16))
+    before = marks[pl.program_id(0), 1]
+    for head in range(grad.shape[1]):
+        at = lanes(head)
+        weight = entry_weight(rates[head], seg_c[0], before)
+        grad[0, head] = tn(q[:, at], (do[:, at].astype(F32) * weight).astype(BF16))
 
 
 def inner_grad_kernel(
     rates, marks, seg_c, seg_r, q_ref, k_ref, v_ref, do_ref, entry, zq, dzq, dk, dv
 ):
-    block, head = pl.program_id(0), pl.program_id(1)
-    rate = rates[head]
-    seg = seg_c[0]
-    weight = entry_weight(rate, seg, marks[block, 1])
-    tokens = seg.shape[0]
-    for at in range(0, tokens, TILE):
-        width = at + TILE
-        q, do = q_ref[at:width, :], do_ref[at:width, :]
-        k, v = k_ref[:width, :], v_ref[:width, :]
-        decay = tile_decay(rate, seg[at:width], seg_r[0, :, :width], at, width)
-        mix = (nt(q, k) * decay).astype(BF16)
-        ds = (nt(do, v) * decay).astype(BF16)
-        scaled = (do.astype(F32) * weight[at:width]).astype(BF16)
-        dq = nn(ds, k) + nt(scaled, entry[0, 0])
-        dzq[at:width, :] = (dq * silu_slope(zq[at:width, :])).astype(BF16)
-        dk_new, dv_new = tn(ds, q), tn(mix, do)
-        if at:
-            dk[:at, :] += dk_new[:at]
-            dv[:at, :] += dv_new[:at]
-        dk[at:width, :] = dk_new[at:]
-        dv[at:width, :] = dv_new[at:]
+    before = marks[pl.program_id(0), 1]
+    seg, tokens = seg_c[0], seg_c.shape[1]
+    for head in range(entry.shape[1]):
+        at = lanes(head)
+        weight = entry_weight(rates[head], seg, before)
+        for top in range(0, tokens, TILE):
+            width = top + TILE
+            q, do = q_ref[top:width, at], do_ref[top:width, at]
+            k, v = k_ref[:width, at], v_ref[:width, at]
+            decay = tile_decay(rates[head], seg[top:width], seg_r[0, :, :width], top, width)
+            mix = (nt(q, k) * decay).astype(BF16)
+            ds = (nt(do, v) * decay).astype(BF16)
+            scaled = (do.astype(F32) * weight[top:width]).astype(BF16)
+            dq = nn(ds, k) + nt(scaled, entry[0, head])
+            dzq[top:width, at] = (dq * silu_slope(zq[top:width, at])).astype(BF16)
+            dk_new, dv_new = tn(ds, q), tn(mix, do)
+            if top:
+                dk[:top, at] += dk_new[:top]
+                dv[:top, at] += dv_new[:top]
+            dk[top:width, at] = dk_new[top:]
+            dv[top:width, at] = dv_new[top:]
 
 
 def last_grad_kernel(rates, marks, seg_c, k, v, d_state, zk, dk, dv, dzk, dzv):
-    block, head = pl.program_id(0), pl.program_id(1)
-    weight = own_weight(rates[head], seg_c[0], marks[block, 0])
-    state = d_state[0, 0]
-    dk_all = dk[...] + weight * nt(v[...], state)
-    dzk[...] = (dk_all * silu_slope(zk[...])).astype(BF16)
-    scaled = (k[...].astype(F32) * weight).astype(BF16)
-    dzv[...] = (dv[...] + nn(scaled, state)).astype(BF16)
+    last = marks[pl.program_id(0), 0]
+    for head in range(d_state.shape[1]):
+        at = lanes(head)
+        weight = own_weight(rates[head], seg_c[0], last)
+        state = d_state[0, head]
+        dk_all = dk[:, at] + weight * nt(v[:, at], state)
+        dzk[:, at] = (dk_all * silu_slope(zk[:, at])).astype(BF16)
+        scaled = (k[:, at].astype(F32) * weight).astype(BF16)
+        dzv[:, at] = (dv[:, at] + nn(scaled, state)).astype(BF16)
 
 
 def head_call(kernel, tokens, heads, kinds_in, kinds_out, args, flops, name):
     specs = {
         "s": pl.BlockSpec(memory_space=pltpu.SMEM),
-        "c": pl.BlockSpec((1, tokens, 1), lambda b, h: (b, 0, 0)),
-        "r": pl.BlockSpec((1, 1, tokens), lambda b, h: (b, 0, 0)),
-        "t": pl.BlockSpec((tokens, HEAD), lambda b, h: (b, h)),
-        "p": pl.BlockSpec((1, 1, HEAD, HEAD), lambda b, h: (b, h, 0, 0)),
-        "n": pl.BlockSpec((tokens, 1), lambda b, h: (b, 0)),
+        "c": pl.BlockSpec((1, tokens, 1), lambda b: (b, 0, 0)),
+        "r": pl.BlockSpec((1, 1, tokens), lambda b: (b, 0, 0)),
+        "t": pl.BlockSpec((tokens, heads * HEAD), lambda b: (b, 0)),
+        "p": pl.BlockSpec((1, heads, HEAD, HEAD), lambda b: (b, 0, 0, 0)),
+        "n": pl.BlockSpec((tokens, 1), lambda b: (b, 0)),
     }
     shapes = {
         "T": jax.ShapeDtypeStruct((2 * tokens, heads * HEAD), F32),
@@ -346,7 +358,7 @@
     }
     return pl.pallas_call(
         kernel,
-        grid=(2, heads),
+        grid=(2,),
         in_specs=[specs[k.lower()] for k in kinds_in],
         out_specs=[specs[k.lower()] for k in kinds_out],
         out_shape=[shapes[k] for k in kinds_out],
@@ -369,9 +381,9 @@
     return jnp.flip(pair(value), 0)
 
 
-def ff_gather(w_gate, w_up, w_down):
+def ff_gather(w_out, w_gate, w_up, w_down):
     nx, nz, ny = [lax.axis_size(a) for a in CHIPS]
-    rows = jnp.concatenate([w_gate.T, w_up.T, w_down], 0)
+    rows = jnp.concatenate([w_out, w_gate.T, w_up.T, w_down], 0)
     part = rows.shape[1] // ny
     shard = lax.dynamic_slice_in_dim(rows, lax.axis_index("dp") * part, part, 1)
     blocks = lax.all_gather(shard, CHIPS, axis=0, tiled=True)
@@ -403,20 +415,58 @@
     return lax.psum_scatter(grads, ("cx", "dp"), scatter_dimension=0, tiled=True)
 
 
-def ff_kernel(tables, b_ref, g_ref, w_ref, out, out_send, db, db_send, grads, *scratch):
+def out_kernel(tables, side_of, y_ref, w_ref, own, send, w_all):
+    tokens, width = own.shape[0], w_ref.shape[2]
+    total = 0.0
+    for i in range(w_ref.shape[0]):
+        x = jnp.bitwise_xor(side_of[0], i)
+        blocks = [w_ref[x, tables[0, p], :, :] for p in range(w_ref.shape[1])]
+        w = jnp.concatenate(blocks, 1)
+        at = slice(i * width, (i + 1) * width)
+        w_all[at, :] = w
+        total = total + nn(y_ref[:, at], w)
+    own[...] = total[:tokens]
+    send[...] = total[tokens:].astype(BF16)
+
+
+def project_out(y, weights, tables):
+    rows, width = y.shape
+    nx, blocks, _, lane = weights.shape
+    model = blocks * lane
+    smem = pl.BlockSpec(memory_space=pltpu.SMEM)
+    whole = lambda *shape: pl.BlockSpec(shape, lambda i: (0,) * len(shape))
+    return pl.pallas_call(
+        out_kernel,
+        grid=(1,),
+        in_specs=[smem, smem, whole(rows, width), whole(nx, blocks, width // nx, lane)],
+        out_specs=[whole(rows // 2, model), whole(rows // 2, model), whole(width, model)],
+        out_shape=[
+            jax.ShapeDtypeStruct((rows // 2, model), F32),
+            jax.ShapeDtypeStruct((rows // 2, model), BF16),
+            jax.ShapeDtypeStruct((width, model), BF16),
+        ],
+        cost_estimate=pl.CostEstimate(
+            flops=2 * rows * width * model, bytes_accessed=6 << 20, transcendentals=0
+        ),
+        name="project_out",
+    )(tables, lax.axis_index("cx").reshape(1).astype(jnp.int32), y, weights)
+
+
+def ff_kernel(tables, b0, b1, g0, g1, w_ref, out, out_send, db, db_send, grads, *scratch):
     m_all, d1_all, d2_all, out_acc, db_acc = scratch
     step = pl.program_id(0)
-    blocks, hidden = w_ref.shape[1], w_ref.shape[2] // 3
+    blocks, hidden = w_ref.shape[1], grads.shape[2] // 3
+    base = w_ref.shape[2] - grads.shape[2]
     tokens = out.shape[0]
 
     def weight(i):
-        at = slice(i * hidden, (i + 1) * hidden)
+        at = slice(base + i * hidden, base + (i + 1) * hidden)
         return jnp.concatenate([w_ref[0, tables[0, p], at, :] for p in range(blocks)], 1)
 
     gate_w, up_w, down_w = weight(0), weight(1), weight(2)
     for half in range(2):
         rows = slice(half * tokens, (half + 1) * tokens)
-        b, g = b_ref[rows, :], g_ref[rows, :]
+        b, g = (b1[...], g1[...]) if half else (b0[...], g0[...])
         z1, z2, dm = nt(b, gate_w), nt(b, up_w), nt(g, down_w)
         m, d1, d2 = (z1 * z2).astype(BF16), (dm * z2).astype(BF16), (dm * z1).astype(BF16)
         m_all[rows, :], d1_all[rows, :], d2_all[rows, :] = m, d1, d2
@@ -434,37 +484,39 @@
             for to, ref, value in zip(sent, kept, sums):
                 to[...] = (ref[...] + value).astype(to.dtype)
 
-    for i, (left, right) in enumerate(((d1_all, b_ref), (d2_all, b_ref), (m_all, g_ref))):
-        grad = tn(left[...], right[...]).astype(BF16)
+    for i, (left, own, other) in enumerate(((d1_all, b0, b1), (d2_all, b0, b1), (m_all, g0, g1))):
+        grad = tn(left[:tokens, :], own[...]) + tn(left[tokens:, :], other[...])
+        grad = grad.astype(BF16)
         at = slice(i * hidden, (i + 1) * hidden)
         for p in range(blocks):
             grads[0, tables[1, p], at, :] = grad[:, p * HEAD : (p + 1) * HEAD]
 
 
-def feed_forward(b, g, weights, tables):
-    rows, model = b.shape
-    tokens = rows // 2
-    nx, blocks, hidden, width = weights.shape
+def feed_forward(b_own, b_pair, g_own, g_pair, weights, tables, hidden):
+    tokens, model = b_own.shape
+    rows = 2 * tokens
+    nx, blocks, height, width = weights.shape
     once = pl.Buffered(1)
     fixed = lambda n: pl.BlockSpec((n, model), lambda x: (0, 0), pipeline_mode=once)
-    turn = pl.BlockSpec((1, blocks, hidden, width), lambda x: (x, 0, 0, 0))
+    turn = lambda n: pl.BlockSpec((1, blocks, n, width), lambda x: (x, 0, 0, 0))
     wide = jax.ShapeDtypeStruct((tokens, model), F32)
     narrow = jax.ShapeDtypeStruct((tokens, model), BF16)
-    product = pltpu.VMEM((rows, hidden // 3), BF16)
+    product = pltpu.VMEM((rows, hidden), BF16)
     total = pltpu.VMEM((tokens, model), F32)
     return pl.pallas_call(
         ff_kernel,
         grid=(nx,),
-        in_specs=[pl.BlockSpec(memory_space=pltpu.SMEM), fixed(rows), fixed(rows), turn],
-        out_specs=[fixed(tokens)] * 4 + [turn],
-        out_shape=[wide, narrow, wide, narrow, jax.ShapeDtypeStruct(weights.shape, BF16)],
+        in_specs=[pl.BlockSpec(memory_space=pltpu.SMEM)] + [fixed(tokens)] * 4 + [turn(height)],
+        out_specs=[fixed(tokens)] * 4 + [turn(3 * hidden)],
+        out_shape=[wide, narrow, wide, narrow]
+        + [jax.ShapeDtypeStruct((nx, blocks, 3 * hidden, width), BF16)],
         scratch_shapes=[product] * 3 + [total] * 2,
         compiler_params=pltpu.CompilerParams(vmem_limit_bytes=60 << 20),
         cost_estimate=pl.CostEstimate(
-            flops=6 * nx * rows * model * hidden, bytes_accessed=36 << 20, transcendentals=0
+            flops=18 * nx * rows * model * hidden, bytes_accessed=36 << 20, transcendentals=0
         ),
         name="feed_forward",
-    )(tables, b, g, weights)
+    )(tables, b_own, b_pair, g_own, g_pair, weights)
 
 
 def on_device(
@@ -488,17 +540,12 @@
     model = block_input.shape[3] * lax.axis_size(COL)
     wide = w_query.shape[1]
 
-    parts = gather_weight(jnp.concatenate([w_query, w_key], 1), "xy")
-    wq = jnp.concatenate([w[:, :wide] for w in parts], 1)
-    wk = jnp.concatenate([w[:, wide:] for w in parts], 1)
-    parts = gather_weight(jnp.concatenate([w_value, w_output_gate], 1), "yx")
-    wv = jnp.concatenate([w[:, :wide] for w in parts], 1)
-    wu = jnp.concatenate([w[:, wide:] for w in parts], 1)
-    wo = jnp.concatenate(gather_weight(w_out.T, "xy"), 1)
-    ff_weights, tables = ff_gather(w_gate, w_up, w_down)
+    wk, wv, sent = gather_weights(w_key, w_value)
+    w_query, w_output_gate, _ = lax.optimization_barrier((w_query, w_output_gate, sent))
+    wq, wu, _ = gather_weights(w_query, w_output_gate)
+    gathered, tables = ff_gather(w_out, w_gate, w_up, w_down)
 
     x_own, a_own, r1 = tokens_in(block_input[:, 0], True)
-    g_own = tokens_in(out_grad[:, 0], False)
     rates = jnp.concatenate([decay_rate, side(decay_rate)])
     heads = rates.shape[0]
     seg_all = segments[:, 0].astype(F32)
@@ -532,17 +579,28 @@
         return total(slice(0, tokens)) + sent.astype(F32)
 
     a = both(a_own)
-    g = both(g_own)
     zq, zk, zv, zu = [dot(a, w, "td,dc->tc") for w in (wq, wk, wv, wu)]
-    q, k, v, o_inner, local = heads_of(
-        first_kernel,
-        kinds_in="sscrTTT",
-        kinds_out="tttTp",
-        args=(rates, marks, seg_c, seg_r, zq, zk, zv),
+    zk, g_parts = lax.optimization_barrier((zk, out_grad[:, 0]))
+    g_own = tokens_in(g_parts, False)
+    g_pair = pair(g_own)
+    k, v, local = heads_of(
+        local_kernel,
+        kinds_in="sscTT",
+        kinds_out="ttp",
+        args=(rates, marks, seg_c, zk, zv),
+        flops=unit // 8,
+        name="mixer_local",
+    )
+    q, o_inner = heads_of(
+        inner_kernel,
+        kinds_in="sscrTtt",
+        kinds_out="tT",
+        args=(rates, marks, seg_c, seg_r, zq, k, v),
         flops=unit,
-        name="mixer_first",
+        name="mixer_inner",
     )
     entry = chain(local, factor, False)
+    entry, _, _ = lax.optimization_barrier((entry, g_own, g_pair))
     o, squares = heads_of(
         carry_kernel,
         kinds_in="sscTtp",
@@ -556,12 +614,14 @@
     squares = (squares + other_first(squares)).reshape(2 * tokens, 1)
     r2 = lax.rsqrt(squares / model + EPS)
     y = (o * r2 * gate).astype(BF16)
-    hres = x_own.astype(F32) + back_sum((y,), (wo,), "tc,dc->td")
+    attended, attended_send, wo = project_out(y, gathered, tables)
+    hres = x_own.astype(F32) + attended + pair(attended_send).astype(F32)
     r3 = lax.rsqrt(jnp.mean(hres * hres, 1, keepdims=True) + EPS)
-    b = both((hres * r3).astype(BF16))
-    out, out_send, db, db_send, ff_grads = feed_forward(b, g, ff_weights, tables)
+    b = (hres * r3).astype(BF16)
+    out, out_send, db, db_send, ff_grads = feed_forward(
+        b, pair(b), g_own, g_pair, gathered, tables, w_down.shape[0]
+    )
     db = db + pair(db_send).astype(F32)
-    block_out = tokens_out((hres + out + pair(out_send).astype(F32)).astype(BF16))
 
     ff_part = ff_scatter_xy(ff_grads)
     dh = (
@@ -572,12 +632,15 @@
     dhr = both(dh.astype(BF16))
 
     grad_out = dot(dhr, y, "td,tc->dc").astype(BF16)
-    dy = dot(dhr, wo, "td,dc->tc")
+    dy = dot(dhr, wo, "td,cd->tc")
     dn = dy * gate
     dzu = (dy * o * r2 * gate * (1.0 - gate)).astype(BF16)
     dots = jnp.sum(dn * o, 1).reshape(2, tokens)
     dots = (dots + other_first(dots)).reshape(2 * tokens, 1)
     do = (r2 * dn - o * (r2**3 * dots / model)).astype(BF16)
+    out_rows = (hres + out + pair(out_send).astype(F32)).astype(BF16)
+    out_rows, do = lax.optimization_barrier((out_rows, do))
+    block_out = tokens_out(out_rows)
     (d_entry,) = heads_of(
         entry_grad_kernel,
         kinds_in="ssctt",
@@ -595,6 +658,21 @@
         flops=5 * unit // 2,
         name="mixer_inner_grad",
     )
+    grad_u, grad_q = [dot(a, d, "td,tc->dc").astype(BF16) for d in (dzu, dzq)]
+    cut = wide // 2
+    early = [
+        jnp.concatenate(
+            [
+                piece
+                for x in (0, wide)
+                for piece in (g[:, x : x + wide], grad_q[:, x + at : x + at + cut])
+            ],
+            1,
+        )
+        for g, at in ((grad_out, 0), (grad_u, cut))
+    ]
+    early = reduce_first(*early)
+    *early, _ = lax.optimization_barrier((*early, d_local))
     dzk, dzv = heads_of(
         last_grad_kernel,
         kinds_in="sscttpTTT",
@@ -603,7 +681,7 @@
         flops=unit // 4,
         name="mixer_last_grad",
     )
-    grads = [dot(a, d, "td,tc->dc").astype(BF16) for d in (dzq, dzk, dzv, dzu)]
+    grad_k, grad_v = [dot(a, d, "td,tc->dc").astype(BF16) for d in (dzk, dzv)]
     da = back_sum((dzq, dzk, dzv, dzu), (wq, wk, wv, wu), "tc,dc->td")
     x_wide = x_own.astype(F32)
     input_grad = tokens_out(
@@ -612,26 +690,21 @@
         ).astype(BF16)
     )
 
-    def halves(*mats):
-        return [
-            jnp.concatenate([g[:, at : at + wide] for g in mats], 1) for at in (0, wide)
-        ]
-
+    total = reduce_rest(*early)
+    total_kv = reduce_rest(*reduce_first(grad_k, grad_v))
+    total_q = jnp.concatenate([total[:, wide : wide + cut], total[:, 2 * wide + cut :]], 1)
     ff_part, _ = lax.optimization_barrier((ff_part, dzk))
     ff_total = lax.psum_scatter(ff_part, "row", scatter_dimension=0, tiled=True).astype(F32)
     hidden = w_down.shape[0]
     total_gate, total_up = ff_total[:hidden].T, ff_total[hidden : 2 * hidden].T
-    total_ou = reduce_grad(*halves(grad_out, grads[3]), "yx")
-    total_qk = reduce_grad(*halves(grads[0], grads[1]), "xy")
-    total_v = reduce_grad(*halves(grads[2]), "yx")
     return (
         block_out[:, None],
         input_grad[:, None],
-        total_qk[:, :wide],
-        total_qk[:, wide:],
-        total_v,
-        total_ou[:, wide:],
-        total_ou[:, :wide].T,
+        total_q,
+        total_kv[:, :wide],
+        total_kv[:, wide:],
+        total[:, wide + cut : 2 * wide + cut],
+        total[:, :wide].T,
         total_gate,
         total_up,
         ff_total[2 * hidden :],

time: 512 us -> 472 us (0.922)
  starting transfers between devices: 77.5 us -> 53.9 us
    ppermute x51 -> x47, starting transfers between devices: 67.5 us -> 41.7 us  [swap(): return lax.ppermute(value, axis, [(i, i ^ bits) for i in range(count)])]
    ppermute x6, waiting for transfers between devices: 22.3 us -> 3.38 us  [chain(): entry = entry + lax.ppermute(out, 'row', [edge])]
    all_gather x1, waiting for transfers between devices: 0.01 us -> 11.3 us  [ff_gather(): blocks = lax.all_gather(shard, CHIPS, axis=0, tiled=True)]
    concatenate x16 -> x14, other arithmetic: 12.6 us -> 4.36 us  [the longest x1 2.07 us: ff_gather(): rows = jnp.concatenate([w_out, w_gate.T, w_up.T, w_down], 0)]
    reduce_sum x0 -> x2, other arithmetic: none -> 7.97 us  [the longest x1 5.87 us: on_device(): jnp.mean(da * x_wide, 1, keepdims=True)]
    pallas_call x5 -> x7, Pallas kernels: 43.3 us -> 37.4 us  [the longest x6 32.5 us: head_call(): pl.pallas_call(kernel, grid=(2,), in_specs=[specs[k.lower()] for k in kin...]
    ppermute x51 -> x47, waiting for transfers between devices: 166 us -> 170 us  [swap(): return lax.ppermute(value, axis, [(i, i ^ bits) for i in range(count)])]
    dot_general x20 -> x18, matrix products: 50.9 us -> 48.2 us  [dot(): return jnp.einsum(form, left, right, preferred_element_type=F32)]
  transfers between devices with their start and end apart: 61 -> 57, of which waited for: 30 -> 23; matrix products, arithmetic and copies ran while one was open for 23% -> 23% of each run, Pallas kernels for 11% -> 10%
where the time goes in v4:
time: 472 us; the launch traced here: 465 us
  waiting for transfers between devices  185 us (39%)
  Pallas kernels  91.7 us (19%)
  starting transfers between devices  53.9 us (11%)
  other arithmetic  49.4 us (10%)
  matrix products  48.2 us (10%)
  local copies, waits for them, and re-layouts  22 us (5%)
  between operations  15.2 us (3%)
    ppermute x47, waiting for transfers between devices, swap(): return lax.ppermute(value, axis, [(i, i ^ bits) for i in range(count)])  170 us
    dot_general x18, matrix products, dot(): return jnp.einsum(form, left, right, preferred_element_type=F32)  48.2 us
    ppermute x47, starting transfers between devices, swap(): return lax.ppermute(value, axis, [(i, i ^ bits) for i in range(count)])  41.7 us
    pallas_call x1, Pallas kernels, feed_forward(): pl.pallas_call(ff_kernel, grid=(nx,), in_specs=[pl.BlockSpec(memory_space...  40.1 us
    pallas_call x6, Pallas kernels, head_call(): pl.pallas_call(kernel, grid=(2,), in_specs=[specs[k.lower()] for k in kin...  32.5 us
    all_gather x1, waiting for transfers between devices, ff_gather(): blocks = lax.all_gather(shard, CHIPS, axis=0, tiled=True)  11.3 us
    unnamed x143, local copies, waits for them, and re-layouts  10.3 us
    ppermute x6, starting transfers between devices, chain(): entry = entry + lax.ppermute(out, 'row', [edge])  9.98 us
  transfers between devices with their start and end apart: 57, of which 23 were waited for; matrix products, arithmetic and copies ran while one was open for 23% of the time, Pallas kernels for 10%

profile of v4, /device:TPU:0, one launch (start us, length us, event | category | flops | bytes accessed | tf_op | source)
XLA Modules:
  0.0 465.5 jit_solution(9967480999648750396)
XLA Ops:
  10.7 2.5 collective-permute-start.1
  21.2 4.0 collective-permute-start.7
  28.7 3.8 assemble.2
  32.6 15.7 %collective-permute-done.7 = bf16[256,512]{1,0:T(8,128)(2,1)S(1)} collective-permute-done((bf16[256,512]{1,0:T(8,128)(2,1)S(1)}, bf16[256,512]{1,0:T(8,128)(2,1)S(1)}, u32[]{:S(2)}, u32[]{:S(2)}) %collective-permute-start.7) | collective-permute-done | bytes 262176 | tf_op jit(solution)/shard_map/ppermute | solution.py:23
  50.7 4.1 collective-permute-done.12
  56.7 12.5 %collective-permute-done.8 = bf16[128,512]{1,0:T(8,128)(2,1)S(1)} collective-permute-done((bf16[128,512]{1,0:T(8,128)(2,1)S(1)}, bf16[128,512]{1,0:T(8,128)(2,1)S(1)}, u32[]{:S(2)}, u32[]{:S(2)}) %collective-permute-start.8) | collective-permute-done | bytes 131104 | tf_op jit(solution)/shard_map/ppermute | solution.py:23
  74.0 2.6 fusion.52.zk
  79.3 6.5 %collective-permute-done.15 = bf16[1024,256]{1,0:T(8,128)(2,1)S(1)} collective-permute-done((bf16[1024,256]{1,0:T(8,128)(2,1)S(1)}, bf16[1024,256]{1,0:T(8,128)(2,1)S(1)}, u32[]{:S(2)}, u32[]{:S(2)}) %collective-permute-start.15) | collective-permute-done | bytes 524320 | tf_op jit(solution)/shard_map/ppermute | solution.py:23
  85.8 2.7 fusion.51.zv
  88.5 4.1 mixer_local.1
  94.4 4.6 collective-permute-start.16
  101.9 3.5 assemble.3.g0
  105.4 3.4 collective-permute-done.16
  116.8 19.9 %collective-permute-done.11 = bf16[512,512]{1,0:T(8,128)(2,1)S(1)} collective-permute-done((bf16[512,512]{1,0:T(8,128)(2,1)S(1)}, bf16[512,512]{1,0:T(8,128)(2,1)S(1)}, u32[]{:S(2)}, u32[]{:S(2)}) %collective-permute-start.11) | collective-permute-done | bytes 524320 | tf_op jit(solution)/shard_map/ppermute | solution.py:23
  136.7 3.8 fusion.53.zq
  140.5 5.6 %mixer_inner.1 = (bf16[1024,512]{1,0:T(8,128)(2,1)}, f32[1024,512]{1,0:T(8,128)}) custom-call(f32[4]{0:T(128)} %get-tuple-element.125.rates, f32[2,2]{1,0:T(2,128)} %pad_maximum_fusion.21.marks, f32[2,512,1]{2,1,0:T(8,128)} %copy.38.seg_c, f32[2,1,512]{2,1,0:T(1,128)} %copy.37.seg_r, f32[1024,512]{1,0:T(8,128)} %fusion.53.zq, ...), custom_call_target="tpu_custom_call" | custom-call | flops 536870912 | bytes 8388608 | tf_op jit(solution)/shard_map/mixer_inner/pallas_call | solution.py:359
  146.9 3.6 mixer_carry.1
  153.2 5.6 %multiply_convert_fusion.2 = (bf16[1024,512]{1,0:T(8,128)(2,1)}, f32[1024,512]{1,0:T(8,128)}) fusion(f32[1024,512]{1,0:T(8,128)} %get-tuple-element.63, f32[1024]{0:T(1024)S(1)} %bitcast.92, bf16[1024,1024]{1,0:T(8,128)(2,1)} %copy-done.37, bf16[1024,256]{1,0:T(8,128)(2,1)S(1)} %collective-permute-done.25, ...), kind=kOutput, calls=%fused_computation.19 | convolution fusion | flops 1080033280 | bytes 8392704 | tf_op jit(solution)/shard_map/td,dc->tc/dot_general | solution.py:216
  158.8 11.3 %all-gather.2.cloned.1.call-done = bf16[37888,128]{1,0:T(8,128)(2,1)} async-done(((bf16[2368,128]{1,0:T(8,128)(2,1)}), bf16[37888,128]{1,0:T(8,128)(2,1)}) %all-gather.2.cloned.1.call-update) | async-done | bytes 9699344 | tf_op jit(solution)/shard_map/all_gather | solution.py:389
  170.1 4.9 %project_out.1 = (f32[512,1024]{1,0:T(8,128)}, bf16[512,1024]{1,0:T(8,128)(2,1)}, bf16[512,1024]{1,0:T(8,128)(2,1)}) custom-call(s32[2,8]{1,0:T(2,128)} %pad_add_fusion.tables, s32[1]{0:T(128)} %bitcast.7.side_of, bf16[1024,512]{1,0:T(8,128)(2,1)} %get-tuple-element.174.y_ref, bf16[2,8,2368,128]{3,2,1,0:T(8,128)(2,1)} %bitcast.86), custom_call_target="tpu_custom_call" | custom-call | flops 1073741824 | bytes 6291456 | tf_op jit(solution)/shard_map/project_out/pallas_call | solution.py:438
  175.0 2.9 collective-permute-done.26
  181.3 2.7 collective-permute-done.27.b1
  184.0 40.1 %feed_forward.1 = (f32[512,1024]{1,0:T(8,128)}, bf16[512,1024]{1,0:T(8,128)(2,1)}, f32[512,1024]{1,0:T(8,128)}, bf16[512,1024]{1,0:T(8,128)(2,1)}, bf16[2,8,2112,128]{3,2,1,0:T(8,128)(2,1)}) custom-call(s32[2,8]{1,0:T(2,128)} %pad_add_fusion.tables, bf16[512,1024]{1,0:T(8,128)(2,1)} %copy-done.25, bf16[512,1024]{1,0:T(8,128)(2,1)} %collective-permute-done.27.b1, ...), custom_call_target="tpu_custom_call" | custom-call | flops 26575110144 | bytes 37748736 | tf_op jit(solution)/shard_map/feed_forward/pallas_call | solution.py:506
  230.3 2.9 fusion.55
  233.3 2.7 collective-permute-done.30
  236.1 5.8 %multiply_reduce_fusion = (f32[1024]{0:T(1024)S(1)}, f32[1024,512]{1,0:T(8,128)}) fusion(f32[1024,512]{1,0:T(8,128)} %get-tuple-element.63, f32[1024,512]{1,0:T(8,128)} %get-tuple-element.175, bf16[512,1024]{1,0:T(8,128)(2,1)} %get-tuple-element.71, bf16[512,1024]{1,0:T(8,128)(2,1)S(1)} %collective-permute-done.30, bf16[512,1024]{1,0:T(8,128)(2,1)} %get-tuple-element.118), kind=kOutput, calls=%fused_computation.12 | convolution fusion | flops 1079507968 | bytes 9441280 | tf_op jit(solution)/shard_map/td,cd->tc/dot_general | solution.py:216
  242.0 2.5 convolution_convert_fusion.4
  246.5 3.6 multiply_convert_fusion
  250.2 3.3 mixer_entry_grad.1
  256.7 10.3 %mixer_inner_grad.1 = (bf16[1024,512]{1,0:T(8,128)(2,1)}, f32[1024,512]{1,0:T(8,128)}, f32[1024,512]{1,0:T(8,128)}) custom-call(f32[4]{0:T(128)} %get-tuple-element.125.rates, f32[2,2]{1,0:T(2,128)} %pad_maximum_fusion.21.marks, f32[2,512,1]{2,1,0:T(8,128)} %copy.38.seg_c, f32[2,1,512]{2,1,0:T(1,128)} %copy.37.seg_r, ...), custom_call_target="tpu_custom_call" | custom-call | flops 1342177280 | bytes 8388608 | tf_op jit(solution)/shard_map/mixer_inner_grad/pallas_call | solution.py:359
  266.9 3.3 convolution_convert_fusion.3
  277.7 3.4 divide.2
  282.8 3.4 fusion.30
  290.4 3.1 fusion.24
  294.8 20.5 %collective-permute-done.32 = bf16[512,256]{1,0:T(8,128)(2,1)S(1)} collective-permute-done((bf16[512,256]{1,0:T(8,128)(2,1)}, bf16[512,256]{1,0:T(8,128)(2,1)S(1)}, u32[]{:S(2)}, u32[]{:S(2)}) %collective-permute-start.32) | collective-permute-done | bytes 262176 | tf_op jit(solution)/shard_map/ppermute | solution.py:23
  316.6 9.7 %collective-permute-done.33 = bf16[512,256]{1,0:T(8,128)(2,1)S(1)} collective-permute-done((bf16[512,256]{1,0:T(8,128)(2,1)}, bf16[512,256]{1,0:T(8,128)(2,1)S(1)}, u32[]{:S(2)}, u32[]{:S(2)}) %collective-permute-start.33) | collective-permute-done | bytes 262176 | tf_op jit(solution)/shard_map/ppermute | solution.py:23
  328.2 5.7 %mixer_last_grad.1 = (bf16[1024,512]{1,0:T(8,128)(2,1)}, bf16[1024,512]{1,0:T(8,128)(2,1)}) custom-call(f32[4]{0:T(128)} %get-tuple-element.125.rates, f32[2,2]{1,0:T(2,128)} %pad_maximum_fusion.21.marks, f32[2,512,1]{2,1,0:T(8,128)} %copy.38.seg_c, bf16[1024,512]{1,0:T(8,128)(2,1)} %get-tuple-element.56.k_ref.k, ...), custom_call_target="tpu_custom_call" | custom-call | flops 134217728 | bytes 8388608 | tf_op jit(solution)/shard_map/mixer_last_grad/pallas_call | solution.py:359
  333.9 3.3 convolution_convert_fusion
  355.7 6.3 %collective-permute-done.45 = bf16[512,384]{0,1:T(8,128)(2,1)S(1)} collective-permute-done((bf16[512,384]{0,1:T(8,128)(2,1)S(1)}, bf16[512,384]{0,1:T(8,128)(2,1)S(1)}, u32[]{:S(2)}, u32[]{:S(2)}) %collective-permute-start.45) | collective-permute-done | bytes 393248 | tf_op jit(solution)/shard_map/ppermute | solution.py:23
  370.5 25.1 %collective-permute-done.46 = bf16[256,768]{0,1:T(8,128)(2,1)S(1)} collective-permute-done((bf16[256,768]{0,1:T(8,128)(2,1)S(1)}, bf16[256,768]{0,1:T(8,128)(2,1)S(1)}, u32[]{:S(2)}, u32[]{:S(2)}) %collective-permute-start.46) | collective-permute-done | bytes 393248 | tf_op jit(solution)/shard_map/ppermute | solution.py:23
  397.0 2.9 collective-permute-start.52
  400.0 13.8 %collective-permute-done.47 = bf16[128,768]{0,1:T(8,128)(2,1)S(1)} collective-permute-done((bf16[128,768]{0,1:T(8,128)(2,1)S(1)}, bf16[128,768]{0,1:T(8,128)(2,1)S(1)}, u32[]{:S(2)}, u32[]{:S(2)}) %collective-permute-start.47) | collective-permute-done | bytes 196640 | tf_op jit(solution)/shard_map/ppermute | solution.py:23
  416.1 8.7 %collective-permute-done.52 = bf16[256,512]{0,1:T(8,128)(2,1)S(1)} collective-permute-done((bf16[256,512]{0,1:T(8,128)(2,1)S(1)}, bf16[256,512]{0,1:T(8,128)(2,1)S(1)}, u32[]{:S(2)}, u32[]{:S(2)}) %collective-permute-start.52) | collective-permute-done | bytes 262176 | tf_op jit(solution)/shard_map/ppermute | solution.py:23
  425.7 5.9 %fusion.1 = (f32[512]{0:T(512)S(1)}, f32[512,1024]{1,0:T(8,128)}) fusion(bf16[512,1024]{1,0:T(8,128)(2,1)S(1)} %copy-done, bf16[512,1024]{1,0:T(8,128)(2,1)} %collective-permute-done.38, f32[512,1024]{1,0:T(8,128)} %fusion.18, f32[512,1024]{1,0:T(8,128)} %fusion.26, f32[512,1024]{1,0:T(8,128)} %fusion.30, f32[512,1024]{1,0:T(8,128)} %fusion.28), kind=kLoop, calls=%fused_computation.4 | loop fusion | flops 4193792 | bytes 12584960 | tf_op jit(solution)/shard_map/reduce_sum | solution.py:689
  432.9 3.0 fusion.3.rows_ref
  435.9 3.4 divide.3
  443.7 4.1 collective-permute-done.39
  447.8 5.9 %collective-permute-done.40 = bf16[512,256]{1,0:T(8,128)(2,1)S(1)} collective-permute-done((bf16[512,256]{1,0:T(8,128)(2,1)}, bf16[512,256]{1,0:T(8,128)(2,1)S(1)}, u32[]{:S(2)}, u32[]{:S(2)}) %collective-permute-start.40) | collective-permute-done | bytes 262176 | tf_op jit(solution)/shard_map/ppermute | solution.py:23
  (340 shorter events, 117.2 us)
Async XLA Ops:
  7.2 162.9 %all-gather.2.cloned.1.call-start = ((), (), s32[]{:S(2)}) async-start(), calls=%async_computation.2 | async-start | bytes 10305536 | tf_op jit(solution)/shard_map/all_gather | solution.py:389
  9.4 357.9 %reduce-scatter.3.cloned.1.call-start = ((), (), s32[]{:S(2)}) async-start(), calls=%async_computation.3 | async-start | bytes 10813440 | tf_op jit(solution)/shard_map/reduce_scatter | solution.py:415
  10.2 15.6 %collective-permute-start = (bf16[512,256]{1,0:T(8,128)(2,1)S(1)}, bf16[512,256]{1,0:T(8,128)(2,1)S(1)}, u32[]{:S(2)}, u32[]{:S(2)}) collective-permute-start(bf16[512,256]{1,0:T(8,128)(2,1)S(1)} %get-tuple-element.154), channel_id=1, source_target_pairs={{0,2},{2,0},{4,6},{6,4},{1,3},{3,1},{5,7},{7,5},{8,10},{10,8},{12,... | collective-permute-start | bytes 786440 | tf_op jit(solution)/shard_map/ppermute | solution.py:23
  10.7 15.2 %collective-permute-start.1 = (bf16[512,256]{1,0:T(8,128)(2,1)S(1)}, bf16[512,256]{1,0:T(8,128)(2,1)S(1)}, u32[]{:S(2)}, u32[]{:S(2)}) collective-permute-start(bf16[512,256]{1,0:T(8,128)(2,1)S(1)} %get-tuple-element.156), channel_id=1, source_target_pairs={{0,4},{2,6},{4,0},{6,2},{1,5},{3,7},{5,1},{7,3},{8,12},{10,14},{12... | collective-permute-start | bytes 786440 | tf_op jit(solution)/shard_map/ppermute | solution.py:23
  13.2 14.8 %collective-permute-start.2 = (bf16[512,256]{1,0:T(8,128)(2,1)S(1)}, bf16[512,256]{1,0:T(8,128)(2,1)S(1)}, u32[]{:S(2)}, u32[]{:S(2)}) collective-permute-start(bf16[512,256]{1,0:T(8,128)(2,1)S(1)} %get-tuple-element.153), channel_id=1, source_target_pairs={{0,6},{2,4},{4,2},{6,0},{1,7},{3,5},{5,3},{7,1},{8,14},{10,12},{12... | collective-permute-start | bytes 786440 | tf_op jit(solution)/shard_map/ppermute | solution.py:23
  13.3 7.8 %collective-permute-start.6 = (bf16[128,512]{1,0:T(8,128)(2,1)S(1)}, bf16[128,512]{1,0:T(8,128)(2,1)S(1)}, u32[]{:S(2)}, u32[]{:S(2)}) collective-permute-start(bf16[128,512]{1,0:T(8,128)(2,1)S(1)} %fusion.35), channel_id=1, source_target_pairs={{0,8},{8,0},{16,24},{24,16},{1,9},{9,1},{17,25},{25,17},{2,10},{10... | collective-permute-start | bytes 393224 | tf_op jit(solution)/shard_map/ppermute | solution.py:23
  19.3 29.2 %collective-permute-start.3 = (f32[2]{0:T(128)S(1)}, f32[2]{0:T(128)S(1)}, u32[]{:S(2)}, u32[]{:S(2)}) collective-permute-start(f32[2]{0:T(128)S(1)} %copy-done.57), channel_id=1, source_target_pairs={{0,4},{2,6},{4,0},{6,2},{1,5},{3,7},{5,1},{7,3},{8,12},{10,14},{12... | collective-permute-start | bytes 32 | tf_op jit(solution)/shard_map/ppermute | solution.py:23
  21.2 27.1 %collective-permute-start.7 = (bf16[256,512]{1,0:T(8,128)(2,1)S(1)}, bf16[256,512]{1,0:T(8,128)(2,1)S(1)}, u32[]{:S(2)}, u32[]{:S(2)}) collective-permute-start(bf16[256,512]{1,0:T(8,128)(2,1)S(1)} %pad_maximum_fusion.17), channel_id=1, source_target_pairs={{0,16},{8,24},{16,0},{24,8},{1,17},{9,25},{17,1},{25,9},{2,18},{10... | collective-permute-start | bytes 786440 | tf_op jit(solution)/shard_map/ppermute | solution.py:23
  32.5 38.9 %collective-permute-start.5 = (bf16[512,1024]{1,0:T(8,128)(2,1)}, bf16[512,1024]{1,0:T(8,128)(2,1)S(1)}, u32[]{:S(2)}, u32[]{:S(2)}) collective-permute-start(bf16[512,1024]{1,0:T(8,128)(2,1)} %get-tuple-element.52), channel_id=1, source_target_pairs={{0,2},{2,0},{4,6},{6,4},{1,3},{3,1},{5,7},{7,5},{8,10},{10,8},{12,... | collective-permute-start | bytes 3145736 | tf_op jit(solution)/shard_map/ppermute | solution.py:23
  48.4 6.4 %collective-permute-start.12 = (bf16[512,256]{1,0:T(8,128)(2,1)S(1)}, bf16[512,256]{1,0:T(8,128)(2,1)S(1)}, u32[]{:S(2)}, u32[]{:S(2)}) collective-permute-start(bf16[512,256]{1,0:T(8,128)(2,1)S(1)} %get-tuple-element.158), channel_id=1, source_target_pairs={{0,4},{2,6},{4,0},{6,2},{1,5},{3,7},{5,1},{7,3},{8,12},{10,14},{12... | collective-permute-start | bytes 786440 | tf_op jit(solution)/shard_map/ppermute | solution.py:23
  49.1 21.0 %collective-permute-start.14 = (bf16[512,256]{1,0:T(8,128)(2,1)S(1)}, bf16[512,256]{1,0:T(8,128)(2,1)S(1)}, u32[]{:S(2)}, u32[]{:S(2)}) collective-permute-start(bf16[512,256]{1,0:T(8,128)(2,1)S(1)} %get-tuple-element.157), channel_id=1, source_target_pairs={{0,1},{1,0},{2,3},{3,2},{4,5},{5,4},{6,7},{7,6},{8,9},{9,8},{10,11... | collective-permute-start | bytes 786440 | tf_op jit(solution)/shard_map/ppermute | solution.py:23
  54.9 19.1 %collective-permute-start.13 = (bf16[512,512]{1,0:T(8,128)(2,1)S(1)}, bf16[512,512]{1,0:T(8,128)(2,1)S(1)}, u32[]{:S(2)}, u32[]{:S(2)}) collective-permute-start(bf16[512,512]{1,0:T(8,128)(2,1)S(1)} %pad_maximum_fusion.14), channel_id=1, source_target_pairs={{0,1},{1,0},{2,3},{3,2},{4,5},{5,4},{6,7},{7,6},{8,9},{9,8},{10,11... | collective-permute-start | bytes 1572872 | tf_op jit(solution)/shard_map/ppermute | solution.py:23
  56.5 12.7 %collective-permute-start.8 = (bf16[128,512]{1,0:T(8,128)(2,1)S(1)}, bf16[128,512]{1,0:T(8,128)(2,1)S(1)}, u32[]{:S(2)}, u32[]{:S(2)}) collective-permute-start(bf16[128,512]{1,0:T(8,128)(2,1)S(1)} %fusion.34), channel_id=1, source_target_pairs={{0,8},{8,0},{16,24},{24,16},{1,9},{9,1},{17,25},{25,17},{2,10},{10... | collective-permute-start | bytes 393224 | tf_op jit(solution)/shard_map/ppermute | solution.py:23
  69.2 29.8 %collective-permute-start.9 = (bf16[256,512]{1,0:T(8,128)(2,1)S(1)}, bf16[256,512]{1,0:T(8,128)(2,1)S(1)}, u32[]{:S(2)}, u32[]{:S(2)}) collective-permute-start(bf16[256,512]{1,0:T(8,128)(2,1)S(1)} %pad_maximum_fusion.18), channel_id=1, source_target_pairs={{0,16},{8,24},{16,0},{24,8},{1,17},{9,25},{17,1},{25,9},{2,18},{10... | collective-permute-start | bytes 786440 | tf_op jit(solution)/shard_map/ppermute | solution.py:23
  70.2 15.6 %collective-permute-start.15 = (bf16[1024,256]{1,0:T(8,128)(2,1)S(1)}, bf16[1024,256]{1,0:T(8,128)(2,1)S(1)}, u32[]{:S(2)}, u32[]{:S(2)}) collective-permute-start(bf16[1024,256]{1,0:T(8,128)(2,1)S(1)} %pad_maximum_fusion.15), channel_id=1, source_target_pairs={{0,4},{2,6},{4,0},{6,2},{1,5},{3,7},{5,1},{7,3},{8,12},{10,14},{12... | collective-permute-start | bytes 1572872 | tf_op jit(solution)/shard_map/ppermute | solution.py:23
  77.4 22.8 %collective-permute-start.19 = (bf16[512,256]{1,0:T(8,128)(2,1)}, bf16[512,256]{1,0:T(8,128)(2,1)S(1)}, u32[]{:S(2)}, u32[]{:S(2)}) collective-permute-start(bf16[512,256]{1,0:T(8,128)(2,1)} %get-tuple-element.151), channel_id=1, source_target_pairs={{0,2},{2,0},{4,6},{6,4},{1,3},{3,1},{5,7},{7,5},{8,10},{10,8},{12,... | collective-permute-start | bytes 786440 | tf_op jit(solution)/shard_map/ppermute | solution.py:23
  77.4 23.7 %collective-permute-start.20 = (bf16[512,256]{1,0:T(8,128)(2,1)S(1)}, bf16[512,256]{1,0:T(8,128)(2,1)S(1)}, u32[]{:S(2)}, u32[]{:S(2)}) collective-permute-start(bf16[512,256]{1,0:T(8,128)(2,1)S(1)} %get-tuple-element.150), channel_id=1, source_target_pairs={{0,4},{2,6},{4,0},{6,2},{1,5},{3,7},{5,1},{7,3},{8,12},{10,14},{12... | collective-permute-start | bytes 786440 | tf_op jit(solution)/shard_map/ppermute | solution.py:23
  77.7 23.4 %collective-permute-start.21 = (bf16[512,256]{1,0:T(8,128)(2,1)S(1)}, bf16[512,256]{1,0:T(8,128)(2,1)S(1)}, u32[]{:S(2)}, u32[]{:S(2)}) collective-permute-start(bf16[512,256]{1,0:T(8,128)(2,1)S(1)} %get-tuple-element.149), channel_id=1, source_target_pairs={{0,6},{2,4},{4,2},{6,0},{1,7},{3,5},{5,3},{7,1},{8,14},{10,12},{12... | collective-permute-start | bytes 786440 | tf_op jit(solution)/shard_map/ppermute | solution.py:23
  94.4 14.3 %collective-permute-start.16 = (bf16[2,4,128,128]{3,2,1,0:T(8,128)(2,1)}, bf16[2,4,128,128]{3,2,1,0:T(8,128)(2,1)S(1)}, u32[]{:S(2)}, u32[]{:S(2)}) collective-permute-start(bf16[2,4,128,128]{3,2,1,0:T(8,128)(2,1)} %add_convert_fusion.7), channel_id=1, source_target_pairs={{0,8},{1,9},{2,10},{3,11},{4,12},{5,13},{6,14},{7,15}} | collective-permute-start | bytes 786440 | tf_op jit(solution)/shard_map/ppermute | solution.py:376
  99.1 12.1 %collective-permute-start.10 = (bf16[512,256]{1,0:T(8,128)(2,1)S(1)}, bf16[512,256]{1,0:T(8,128)(2,1)}, u32[]{:S(2)}, u32[]{:S(2)}) collective-permute-start(bf16[512,256]{1,0:T(8,128)(2,1)S(1)} %get-tuple-element.159), channel_id=1, source_target_pairs={{0,4},{2,6},{4,0},{6,2},{1,5},{3,7},{5,1},{7,3},{8,12},{10,14},{12... | collective-permute-start | bytes 786440 | tf_op jit(solution)/shard_map/ppermute | solution.py:23
  100.2 13.8 %collective-permute-start.24 = (bf16[512,256]{1,0:T(8,128)(2,1)S(1)}, bf16[512,256]{1,0:T(8,128)(2,1)S(1)}, u32[]{:S(2)}, u32[]{:S(2)}) collective-permute-start(bf16[512,256]{1,0:T(8,128)(2,1)S(1)} %get-tuple-element.160), channel_id=1, source_target_pairs={{0,1},{1,0},{2,3},{3,2},{4,5},{5,4},{6,7},{7,6},{8,9},{9,8},{10,11... | collective-permute-start | bytes 786440 | tf_op jit(solution)/shard_map/ppermute | solution.py:23
  105.4 41.5 %collective-permute-start.22 = (bf16[512,1024]{1,0:T(8,128)(2,1)}, bf16[512,1024]{1,0:T(8,128)(2,1)}, u32[]{:S(2)}, u32[]{:S(2)}) collective-permute-start(bf16[512,1024]{1,0:T(8,128)(2,1)} %assemble.3.g0), channel_id=1, source_target_pairs={{0,2},{2,0},{4,6},{6,4},{1,3},{3,1},{5,7},{7,5},{8,10},{10,8},{12,... | collective-permute-start | bytes 3145736 | tf_op jit(solution)/shard_map/ppermute | solution.py:23
  108.9 5.9 %collective-permute-start.17 = (bf16[2,4,128,128]{3,2,1,0:T(8,128)(2,1)S(1)}, bf16[2,4,128,128]{3,2,1,0:T(8,128)(2,1)S(1)}, u32[]{:S(2)}, u32[]{:S(2)}) collective-permute-start(bf16[2,4,128,128]{3,2,1,0:T(8,128)(2,1)S(1)} %add_convert_fusion.6), channel_id=1, source_target_pairs={{8,16},{9,17},{10,18},{11,19},{12,20},{13,21},{14,22},{15,23}} | collective-permute-start | bytes 786440 | tf_op jit(solution)/shard_map/ppermute | solution.py:376
  112.2 24.5 %collective-permute-start.11 = (bf16[512,512]{1,0:T(8,128)(2,1)S(1)}, bf16[512,512]{1,0:T(8,128)(2,1)S(1)}, u32[]{:S(2)}, u32[]{:S(2)}) collective-permute-start(bf16[512,512]{1,0:T(8,128)(2,1)S(1)} %pad_maximum_fusion.13), channel_id=1, source_target_pairs={{0,1},{1,0},{2,3},{3,2},{4,5},{5,4},{6,7},{7,6},{8,9},{9,8},{10,11... | collective-permute-start | bytes 1572872 | tf_op jit(solution)/shard_map/ppermute | solution.py:23
  114.0 39.1 %collective-permute-start.25 = (bf16[1024,256]{1,0:T(8,128)(2,1)S(1)}, bf16[1024,256]{1,0:T(8,128)(2,1)S(1)}, u32[]{:S(2)}, u32[]{:S(2)}) collective-permute-start(bf16[1024,256]{1,0:T(8,128)(2,1)S(1)} %pad_maximum_fusion.16), channel_id=1, source_target_pairs={{0,4},{2,6},{4,0},{6,2},{1,5},{3,7},{5,1},{7,3},{8,12},{10,14},{12... | collective-permute-start | bytes 1572872 | tf_op jit(solution)/shard_map/ppermute | solution.py:23
  115.7 30.4 %collective-permute-start.18 = (bf16[2,4,128,128]{3,2,1,0:T(8,128)(2,1)}, bf16[2,4,128,128]{3,2,1,0:T(8,128)(2,1)S(1)}, u32[]{:S(2)}, u32[]{:S(2)}) collective-permute-start(bf16[2,4,128,128]{3,2,1,0:T(8,128)(2,1)} %get-tuple-element.122), channel_id=1, source_target_pairs={{16,24},{17,25},{18,26},{19,27},{20,28},{21,29},{22,30},{23,31}} | collective-permute-start | bytes 786440 | tf_op jit(solution)/shard_map/ppermute | solution.py:376
  224.2 231.8 %reduce-scatter.5.cloned.1.call-start = ((), (), s32[]{:S(2)}) async-start(), calls=%async_computation.4 | async-start | bytes 2703360 | tf_op jit(solution)/shard_map/reduce_scatter | solution.py:697
  255.3 33.1 %collective-permute-start.35 = (bf16[2,4,128,128]{3,2,1,0:T(8,128)(2,1)}, bf16[2,4,128,128]{3,2,1,0:T(8,128)(2,1)}, u32[]{:S(2)}, u32[]{:S(2)}) collective-permute-start(bf16[2,4,128,128]{3,2,1,0:T(8,128)(2,1)} %add_convert_fusion.4), channel_id=1, source_target_pairs={{24,16},{25,17},{26,18},{27,19},{28,20},{29,21},{30,22},{31,23}} | collective-permute-start | bytes 786440 | tf_op jit(solution)/shard_map/ppermute | solution.py:376
  274.1 69.6 %collective-permute-start.43 = (bf16[512,768]{0,1:T(8,128)(2,1)}, bf16[512,768]{0,1:T(8,128)(2,1)}, u32[]{:S(2)}, u32[]{:S(2)}) collective-permute-start(bf16[512,768]{0,1:T(8,128)(2,1)} %slice.243), channel_id=1, source_target_pairs={{0,1},{1,0},{2,3},{3,2},{4,5},{5,4},{6,7},{7,6},{8,9},{9,8},{10,11... | collective-permute-start | bytes 2359304 | tf_op jit(solution)/shard_map/ppermute | solution.py:23
  276.3 65.9 %collective-permute-start.42 = (bf16[1024,384]{0,1:T(8,128)(2,1)}, bf16[1024,384]{0,1:T(8,128)(2,1)}, u32[]{:S(2)}, u32[]{:S(2)}) collective-permute-start(bf16[1024,384]{0,1:T(8,128)(2,1)} %pad_maximum_fusion.9), channel_id=1, source_target_pairs={{0,4},{2,6},{4,0},{6,2},{1,5},{3,7},{5,1},{7,3},{8,12},{10,14},{12... | collective-permute-start | bytes 2359304 | tf_op jit(solution)/shard_map/ppermute | solution.py:23
  281.2 34.1 %collective-permute-start.32 = (bf16[512,256]{1,0:T(8,128)(2,1)}, bf16[512,256]{1,0:T(8,128)(2,1)S(1)}, u32[]{:S(2)}, u32[]{:S(2)}) collective-permute-start(bf16[512,256]{1,0:T(8,128)(2,1)} %get-tuple-element.73), channel_id=1, source_target_pairs={{0,6},{2,4},{4,2},{6,0},{1,7},{3,5},{5,3},{7,1},{8,14},{10,12},{12... | collective-permute-start | bytes 786440 | tf_op jit(solution)/shard_map/ppermute | solution.py:23
  281.9 44.3 %collective-permute-start.33 = (bf16[512,256]{1,0:T(8,128)(2,1)}, bf16[512,256]{1,0:T(8,128)(2,1)S(1)}, u32[]{:S(2)}, u32[]{:S(2)}) collective-permute-start(bf16[512,256]{1,0:T(8,128)(2,1)} %get-tuple-element.74), channel_id=1, source_target_pairs={{0,4},{2,6},{4,0},{6,2},{1,5},{3,7},{5,1},{7,3},{8,12},{10,14},{12... | collective-permute-start | bytes 786440 | tf_op jit(solution)/shard_map/ppermute | solution.py:23
  293.5 32.8 %collective-permute-start.34 = (bf16[512,256]{1,0:T(8,128)(2,1)S(1)}, bf16[512,256]{1,0:T(8,128)(2,1)S(1)}, u32[]{:S(2)}, u32[]{:S(2)}) collective-permute-start(bf16[512,256]{1,0:T(8,128)(2,1)S(1)} %copy-done.67), channel_id=1, source_target_pairs={{0,2},{2,0},{4,6},{6,4},{1,3},{3,1},{5,7},{7,5},{8,10},{10,8},{12,... | collective-permute-start | bytes 786440 | tf_op jit(solution)/shard_map/ppermute | solution.py:23
  315.3 12.1 %collective-permute-start.37 = (bf16[2,4,128,128]{3,2,1,0:T(8,128)(2,1)S(1)}, bf16[2,4,128,128]{3,2,1,0:T(8,128)(2,1)S(1)}, u32[]{:S(2)}, u32[]{:S(2)}) collective-permute-start(bf16[2,4,128,128]{3,2,1,0:T(8,128)(2,1)S(1)} %get-tuple-element.116), channel_id=1, source_target_pairs={{8,0},{9,1},{10,2},{11,3},{12,4},{13,5},{14,6},{15,7}} | collective-permute-start | bytes 786440 | tf_op jit(solution)/shard_map/ppermute | solution.py:376
  337.2 27.0 %collective-permute-start.50 = (bf16[512,512]{0,1:T(8,128)(2,1)S(1)}, bf16[512,512]{0,1:T(8,128)(2,1)S(1)}, u32[]{:S(2)}, u32[]{:S(2)}) collective-permute-start(bf16[512,512]{0,1:T(8,128)(2,1)S(1)} %slice.257), channel_id=1, source_target_pairs={{0,1},{1,0},{2,3},{3,2},{4,5},{5,4},{6,7},{7,6},{8,9},{9,8},{10,11... | collective-permute-start | bytes 1572872 | tf_op jit(solution)/shard_map/ppermute | solution.py:23
  339.8 27.5 %collective-permute-start.48 = (bf16[1024,256]{0,1:T(8,128)(2,1)}, bf16[1024,256]{0,1:T(8,128)(2,1)}, u32[]{:S(2)}, u32[]{:S(2)}) collective-permute-start(bf16[1024,256]{0,1:T(8,128)(2,1)} %slice.253), channel_id=1, source_target_pairs={{0,4},{2,6},{4,0},{6,2},{1,5},{3,7},{5,1},{7,3},{8,12},{10,14},{12... | collective-permute-start | bytes 1572872 | tf_op jit(solution)/shard_map/ppermute | solution.py:23
  345.2 16.8 %collective-permute-start.45 = (bf16[512,384]{0,1:T(8,128)(2,1)S(1)}, bf16[512,384]{0,1:T(8,128)(2,1)S(1)}, u32[]{:S(2)}, u32[]{:S(2)}) collective-permute-start(bf16[512,384]{0,1:T(8,128)(2,1)S(1)} %slice.339), channel_id=1, source_target_pairs={{0,4},{2,6},{4,0},{6,2},{1,5},{3,7},{5,1},{7,3},{8,12},{10,14},{12... | collective-permute-start | bytes 1179656 | tf_op jit(solution)/shard_map/ppermute | solution.py:23
  345.3 16.8 %collective-permute-start.44 = (bf16[512,384]{0,1:T(8,128)(2,1)S(1)}, bf16[512,384]{0,1:T(8,128)(2,1)S(1)}, u32[]{:S(2)}, u32[]{:S(2)}) collective-permute-start(bf16[512,384]{0,1:T(8,128)(2,1)S(1)} %slice.340), channel_id=1, source_target_pairs={{0,1},{1,0},{2,3},{3,2},{4,5},{5,4},{6,7},{7,6},{8,9},{9,8},{10,11... | collective-permute-start | bytes 1179656 | tf_op jit(solution)/shard_map/ppermute | solution.py:23
  351.6 74.1 %collective-permute-start.38 = (bf16[512,1024]{1,0:T(8,128)(2,1)}, bf16[512,1024]{1,0:T(8,128)(2,1)}, u32[]{:S(2)}, u32[]{:S(2)}) collective-permute-start(bf16[512,1024]{1,0:T(8,128)(2,1)} %add_convert_fusion), channel_id=1, source_target_pairs={{0,2},{2,0},{4,6},{6,4},{1,3},{3,1},{5,7},{7,5},{8,10},{10,8},{12,... | collective-permute-start | bytes 3145736 | tf_op jit(solution)/shard_map/ppermute | solution.py:23
  362.3 33.3 %collective-permute-start.46 = (bf16[256,768]{0,1:T(8,128)(2,1)S(1)}, bf16[256,768]{0,1:T(8,128)(2,1)S(1)}, u32[]{:S(2)}, u32[]{:S(2)}) collective-permute-start(bf16[256,768]{0,1:T(8,128)(2,1)S(1)} %fusion.7), channel_id=1, source_target_pairs={{0,16},{8,24},{16,0},{24,8},{1,17},{9,25},{17,1},{25,9},{2,18},{10... | collective-permute-start | bytes 1179656 | tf_op jit(solution)/shard_map/ppermute | solution.py:23
  366.2 29.7 %collective-permute-start.51 = (bf16[512,256]{0,1:T(8,128)(2,1)}, bf16[512,256]{0,1:T(8,128)(2,1)}, u32[]{:S(2)}, u32[]{:S(2)}) collective-permute-start(bf16[512,256]{0,1:T(8,128)(2,1)} %slice.341), channel_id=1, source_target_pairs={{0,4},{2,6},{4,0},{6,2},{1,5},{3,7},{5,1},{7,3},{8,12},{10,14},{12... | collective-permute-start | bytes 786440 | tf_op jit(solution)/shard_map/ppermute | solution.py:23
  368.7 28.2 %collective-permute-start.49 = (bf16[512,256]{0,1:T(8,128)(2,1)S(1)}, bf16[512,256]{0,1:T(8,128)(2,1)S(1)}, u32[]{:S(2)}, u32[]{:S(2)}) collective-permute-start(bf16[512,256]{0,1:T(8,128)(2,1)S(1)} %slice.342), channel_id=1, source_target_pairs={{0,1},{1,0},{2,3},{3,2},{4,5},{5,4},{6,7},{7,6},{8,9},{9,8},{10,11... | collective-permute-start | bytes 786440 | tf_op jit(solution)/shard_map/ppermute | solution.py:23
  395.8 18.0 %collective-permute-start.47 = (bf16[128,768]{0,1:T(8,128)(2,1)S(1)}, bf16[128,768]{0,1:T(8,128)(2,1)S(1)}, u32[]{:S(2)}, u32[]{:S(2)}) collective-permute-start(bf16[128,768]{0,1:T(8,128)(2,1)S(1)} %slice.343), channel_id=1, source_target_pairs={{0,8},{8,0},{16,24},{24,16},{1,9},{9,1},{17,25},{25,17},{2,10},{10... | collective-permute-start | bytes 589832 | tf_op jit(solution)/shard_map/ppermute | solution.py:23
  397.0 27.7 %collective-permute-start.52 = (bf16[256,512]{0,1:T(8,128)(2,1)S(1)}, bf16[256,512]{0,1:T(8,128)(2,1)S(1)}, u32[]{:S(2)}, u32[]{:S(2)}) collective-permute-start(bf16[256,512]{0,1:T(8,128)(2,1)S(1)} %fusion.13), channel_id=1, source_target_pairs={{0,16},{8,24},{16,0},{24,8},{1,17},{9,25},{17,1},{25,9},{2,18},{10... | collective-permute-start | bytes 786440 | tf_op jit(solution)/shard_map/ppermute | solution.py:23
  425.5 15.6 %collective-permute-start.53 = (bf16[128,512]{0,1:T(8,128)(2,1)}, bf16[128,512]{0,1:T(8,128)(2,1)S(1)}, u32[]{:S(2)}, u32[]{:S(2)}) collective-permute-start(bf16[128,512]{0,1:T(8,128)(2,1)} %slice.344), channel_id=1, source_target_pairs={{0,8},{8,0},{16,24},{24,16},{1,9},{9,1},{17,25},{25,17},{2,10},{10... | collective-permute-start | bytes 393224 | tf_op jit(solution)/shard_map/ppermute | solution.py:23
  439.3 8.5 %collective-permute-start.39 = (bf16[512,256]{1,0:T(8,128)(2,1)}, bf16[512,256]{1,0:T(8,128)(2,1)S(1)}, u32[]{:S(2)}, u32[]{:S(2)}) collective-permute-start(bf16[512,256]{1,0:T(8,128)(2,1)} %get-tuple-element.84), channel_id=1, source_target_pairs={{0,6},{2,4},{4,2},{6,0},{1,7},{3,5},{5,3},{7,1},{8,14},{10,12},{12... | collective-permute-start | bytes 786440 | tf_op jit(solution)/shard_map/ppermute | solution.py:23
  440.2 13.6 %collective-permute-start.40 = (bf16[512,256]{1,0:T(8,128)(2,1)}, bf16[512,256]{1,0:T(8,128)(2,1)S(1)}, u32[]{:S(2)}, u32[]{:S(2)}) collective-permute-start(bf16[512,256]{1,0:T(8,128)(2,1)} %get-tuple-element.85), channel_id=1, source_target_pairs={{0,4},{2,6},{4,0},{6,2},{1,5},{3,7},{5,1},{7,3},{8,12},{10,14},{12... | collective-permute-start | bytes 786440 | tf_op jit(solution)/shard_map/ppermute | solution.py:23
  441.1 12.6 %collective-permute-start.41 = (bf16[512,256]{1,0:T(8,128)(2,1)}, bf16[512,256]{1,0:T(8,128)(2,1)S(1)}, u32[]{:S(2)}, u32[]{:S(2)}) collective-permute-start(bf16[512,256]{1,0:T(8,128)(2,1)} %get-tuple-element.86), channel_id=1, source_target_pairs={{0,2},{2,0},{4,6},{6,4},{1,3},{3,1},{5,7},{7,5},{8,10},{10,8},{12,... | collective-permute-start | bytes 786440 | tf_op jit(solution)/shard_map/ppermute | solution.py:23
  (77 other events, 585.1 us)
Sparse Core Ops, SparseCore 0:
  10.7 159.3 all-gather.1
  224.3 108.4 reduce-scatter.2
  367.4 59.5 reduce-scatter.4

commit v5 on v4

--- a/solution.py
+++ b/solution.py
@@ -208,8 +208,11 @@
     return fold_side(one), fold(two, "dp")
 
 
-def reduce_rest(one, two):
-    return fold(jnp.concatenate([fold(one, "dp"), fold_side(two)], 1), "row")
+def reduce_rest(one, two, after=None):
+    joined = jnp.concatenate([fold(one, "dp"), fold_side(two)], 1)
+    if after is not None:
+        joined, _ = lax.optimization_barrier((joined, after))
+    return fold(joined, "row")
 
 
 def dot(left, right, form):
@@ -639,8 +642,6 @@
     dots = (dots + other_first(dots)).reshape(2 * tokens, 1)
     do = (r2 * dn - o * (r2**3 * dots / model)).astype(BF16)
     out_rows = (hres + out + pair(out_send).astype(F32)).astype(BF16)
-    out_rows, do = lax.optimization_barrier((out_rows, do))
-    block_out = tokens_out(out_rows)
     (d_entry,) = heads_of(
         entry_grad_kernel,
         kinds_in="ssctt",
@@ -684,16 +685,17 @@
     grad_k, grad_v = [dot(a, d, "td,tc->dc").astype(BF16) for d in (dzk, dzv)]
     da = back_sum((dzq, dzk, dzv, dzu), (wq, wk, wv, wu), "tc,dc->td")
     x_wide = x_own.astype(F32)
-    input_grad = tokens_out(
-        (
-            dh + r1 * da - x_wide * (r1**3 * jnp.mean(da * x_wide, 1, keepdims=True))
-        ).astype(BF16)
-    )
+    in_rows = (
+        dh + r1 * da - x_wide * (r1**3 * jnp.mean(da * x_wide, 1, keepdims=True))
+    ).astype(BF16)
+    input_grad = tokens_out(in_rows)
+    out_rows, _ = lax.optimization_barrier((out_rows, dzk))
+    block_out = tokens_out(out_rows)
 
     total = reduce_rest(*early)
-    total_kv = reduce_rest(*reduce_first(grad_k, grad_v))
+    grad_k, grad_v, ff_part = lax.optimization_barrier((grad_k, grad_v, ff_part))
+    total_kv = reduce_rest(*reduce_first(grad_k, grad_v), in_rows)
     total_q = jnp.concatenate([total[:, wide : wide + cut], total[:, 2 * wide + cut :]], 1)
-    ff_part, _ = lax.optimization_barrier((ff_part, dzk))
     ff_total = lax.psum_scatter(ff_part, "row", scatter_dimension=0, tiled=True).astype(F32)
     hidden = w_down.shape[0]
     total_gate, total_up = ff_total[:hidden].T, ff_total[hidden : 2 * hidden].T

time: 472 us -> 433 us (0.917)
  waiting for transfers between devices: 185 us -> 149 us
  other arithmetic: 49.4 us -> 44 us
    ppermute x47, waiting for transfers between devices: 170 us -> 123 us  [swap(): return lax.ppermute(value, axis, [(i, i ^ bits) for i in range(count)])]
    ppermute x6, waiting for transfers between devices: 3.38 us -> 14.7 us  [chain(): entry = entry + lax.ppermute(out, 'row', [edge])]
    unnamed x143 -> x153, local copies, waits for them, and re-layouts: 10.3 us -> 11.3 us
  transfers between devices with their start and end apart: 57 -> 57, of which waited for: 23 -> 25; matrix products, arithmetic and copies ran while one was open for 23% -> 24% of each run, Pallas kernels for 10% -> 11%
where the time goes in v5:
time: 433 us; the launch traced here: 427 us
  waiting for transfers between devices  149 us (34%)
  Pallas kernels  91.4 us (21%)
  starting transfers between devices  53.4 us (12%)
  matrix products  49.5 us (11%)
  other arithmetic  44 us (10%)
  local copies, waits for them, and re-layouts  24.3 us (6%)
  between operations  15.2 us (4%)
    ppermute x47, waiting for transfers between devices, swap(): return lax.ppermute(value, axis, [(i, i ^ bits) for i in range(count)])  123 us
    dot_general x18, matrix products, dot(): return jnp.einsum(form, left, right, preferred_element_type=F32)  49.5 us
    ppermute x47, starting transfers between devices, swap(): return lax.ppermute(value, axis, [(i, i ^ bits) for i in range(count)])  41.8 us
    pallas_call x1, Pallas kernels, feed_forward(): pl.pallas_call(ff_kernel, grid=(nx,), in_specs=[pl.BlockSpec(memory_space...  40.2 us
    pallas_call x6, Pallas kernels, head_call(): pl.pallas_call(kernel, grid=(2,), in_specs=[specs[k.lower()] for k in kin...  32.1 us
    ppermute x6, waiting for transfers between devices, chain(): entry = entry + lax.ppermute(out, 'row', [edge])  14.7 us
    all_gather x1, waiting for transfers between devices, ff_gather(): blocks = lax.all_gather(shard, CHIPS, axis=0, tiled=True)  11.3 us
    unnamed x153, local copies, waits for them, and re-layouts  11.3 us
  transfers between devices with their start and end apart: 57, of which 25 were waited for; matrix products, arithmetic and copies ran while one was open for 24% of the time, Pallas kernels for 11%

profile of v5, /device:TPU:0, one launch (start us, length us, event | category | flops | bytes accessed | tf_op | source)
XLA Modules:
  0.0 426.7 jit_solution(9019677081317074704)
XLA Ops:
  10.7 2.5 collective-permute-start.1
  21.2 4.1 collective-permute-start.7
  28.7 3.8 assemble.2
  32.5 15.7 %collective-permute-done.7 = bf16[256,512]{1,0:T(8,128)(2,1)S(1)} collective-permute-done((bf16[256,512]{1,0:T(8,128)(2,1)S(1)}, bf16[256,512]{1,0:T(8,128)(2,1)S(1)}, u32[]{:S(2)}, u32[]{:S(2)}) %collective-permute-start.7) | collective-permute-done | bytes 262176 | tf_op jit(solution)/shard_map/ppermute | solution.py:23
  50.7 4.1 collective-permute-done.12
  56.7 12.5 %collective-permute-done.8 = bf16[128,512]{1,0:T(8,128)(2,1)S(1)} collective-permute-done((bf16[128,512]{1,0:T(8,128)(2,1)S(1)}, bf16[128,512]{1,0:T(8,128)(2,1)S(1)}, u32[]{:S(2)}, u32[]{:S(2)}) %collective-permute-start.8) | collective-permute-done | bytes 131104 | tf_op jit(solution)/shard_map/ppermute | solution.py:23
  71.5 2.5 collective-permute-done.13
  74.0 2.6 fusion.49.zk
  79.3 6.5 %collective-permute-done.15 = bf16[1024,256]{1,0:T(8,128)(2,1)S(1)} collective-permute-done((bf16[1024,256]{1,0:T(8,128)(2,1)S(1)}, bf16[1024,256]{1,0:T(8,128)(2,1)S(1)}, u32[]{:S(2)}, u32[]{:S(2)}) %collective-permute-start.15) | collective-permute-done | bytes 524320 | tf_op jit(solution)/shard_map/ppermute | solution.py:23
  85.8 2.7 fusion.48.zv
  88.5 4.1 mixer_local.1
  94.4 4.6 %collective-permute-start.16 = (bf16[2,4,128,128]{3,2,1,0:T(8,128)(2,1)}, bf16[2,4,128,128]{3,2,1,0:T(8,128)(2,1)S(1)}, u32[]{:S(2)}, u32[]{:S(2)}) collective-permute-start(bf16[2,4,128,128]{3,2,1,0:T(8,128)(2,1)} %add_convert_fusion.7), channel_id=1, source_target_pairs={{0,8},{1,9},{2,10},{3,11},{4,12},{5,13},{6,14},{7,15}} | collective-permute-start | bytes 786440 | tf_op jit(solution)/shard_map/ppermute | solution.py:379
  101.9 3.5 assemble.3.g0
  105.4 3.3 collective-permute-done.16
  116.7 19.9 %collective-permute-done.11 = bf16[512,512]{1,0:T(8,128)(2,1)S(1)} collective-permute-done((bf16[512,512]{1,0:T(8,128)(2,1)S(1)}, bf16[512,512]{1,0:T(8,128)(2,1)S(1)}, u32[]{:S(2)}, u32[]{:S(2)}) %collective-permute-start.11) | collective-permute-done | bytes 524320 | tf_op jit(solution)/shard_map/ppermute | solution.py:23
  136.7 3.8 fusion.50.zq
  140.5 5.6 %mixer_inner.1 = (bf16[1024,512]{1,0:T(8,128)(2,1)}, f32[1024,512]{1,0:T(8,128)}) custom-call(f32[4]{0:T(128)} %get-tuple-element.129.rates, f32[2,2]{1,0:T(2,128)} %pad_maximum_fusion.21.marks, f32[2,512,1]{2,1,0:T(8,128)} %copy.36.seg_c, f32[2,1,512]{2,1,0:T(1,128)} %copy.35.seg_r, f32[1024,512]{1,0:T(8,128)} %fusion.50.zq, ...), custom_call_target="tpu_custom_call" | custom-call | flops 536870912 | bytes 8388608 | tf_op jit(solution)/shard_map/mixer_inner/pallas_call | solution.py:362
  146.8 3.5 mixer_carry.1
  153.0 5.6 %multiply_convert_fusion.2 = (bf16[1024,512]{1,0:T(8,128)(2,1)}, f32[1024,512]{1,0:T(8,128)}) fusion(f32[1024,512]{1,0:T(8,128)} %get-tuple-element.65, f32[1024]{0:T(1024)S(1)} %bitcast.92, bf16[1024,1024]{1,0:T(8,128)(2,1)} %copy-done.39, bf16[1024,256]{1,0:T(8,128)(2,1)S(1)} %collective-permute-done.25, ...), kind=kOutput, calls=%fused_computation.19 | convolution fusion | flops 1080033280 | bytes 8392704 | tf_op jit(solution)/shard_map/td,dc->tc/dot_general | solution.py:219
  158.7 11.3 %all-gather.2.cloned.1.call-done = bf16[37888,128]{1,0:T(8,128)(2,1)} async-done(((bf16[2368,128]{1,0:T(8,128)(2,1)}), bf16[37888,128]{1,0:T(8,128)(2,1)}) %all-gather.2.cloned.1.call-update) | async-done | bytes 9699344 | tf_op jit(solution)/shard_map/all_gather | solution.py:392
  170.0 4.9 %project_out.1 = (f32[512,1024]{1,0:T(8,128)}, bf16[512,1024]{1,0:T(8,128)(2,1)}, bf16[512,1024]{1,0:T(8,128)(2,1)}) custom-call(s32[2,8]{1,0:T(2,128)} %pad_add_fusion.tables, s32[1]{0:T(128)} %bitcast.7.side_of, bf16[1024,512]{1,0:T(8,128)(2,1)} %get-tuple-element.178.y_ref, bf16[2,8,2368,128]{3,2,1,0:T(8,128)(2,1)} %bitcast.86), custom_call_target="tpu_custom_call" | custom-call | flops 1073741824 | bytes 6291456 | tf_op jit(solution)/shard_map/project_out/pallas_call | solution.py:441
  174.9 2.9 collective-permute-done.26
  181.1 2.7 collective-permute-done.27.b1
  183.8 40.2 %feed_forward.1 = (f32[512,1024]{1,0:T(8,128)}, bf16[512,1024]{1,0:T(8,128)(2,1)}, f32[512,1024]{1,0:T(8,128)}, bf16[512,1024]{1,0:T(8,128)(2,1)}, bf16[2,8,2112,128]{3,2,1,0:T(8,128)(2,1)}) custom-call(s32[2,8]{1,0:T(2,128)} %pad_add_fusion.tables, bf16[512,1024]{1,0:T(8,128)(2,1)} %copy-done.27, bf16[512,1024]{1,0:T(8,128)(2,1)} %collective-permute-done.27.b1, ...), custom_call_target="tpu_custom_call" | custom-call | flops 26575110144 | bytes 37748736 | tf_op jit(solution)/shard_map/feed_forward/pallas_call | solution.py:509
  230.1 2.8 fusion.52
  233.1 2.7 collective-permute-done.30
  235.9 5.9 %multiply_reduce_fusion = (f32[1024]{0:T(1024)S(1)}, f32[1024,512]{1,0:T(8,128)}) fusion(f32[1024,512]{1,0:T(8,128)} %get-tuple-element.65, f32[1024,512]{1,0:T(8,128)} %get-tuple-element.179, bf16[512,1024]{1,0:T(8,128)(2,1)} %get-tuple-element.73, bf16[512,1024]{1,0:T(8,128)(2,1)S(1)} %collective-permute-done.30, bf16[512,1024]{1,0:T(8,128)(2,1)} %get-tuple-element.122), kind=kOutput, calls=%fused_computation.12 | convolution fusion | flops 1079507968 | bytes 9441280 | tf_op jit(solution)/shard_map/td,cd->tc/dot_general | solution.py:219
  241.9 2.5 convolution_convert_fusion.4
  246.4 3.6 multiply_convert_fusion
  250.0 3.3 mixer_entry_grad.1
  255.8 10.0 %mixer_inner_grad.1 = (bf16[1024,512]{1,0:T(8,128)(2,1)}, f32[1024,512]{1,0:T(8,128)}, f32[1024,512]{1,0:T(8,128)}) custom-call(f32[4]{0:T(128)} %get-tuple-element.129.rates, f32[2,2]{1,0:T(2,128)} %pad_maximum_fusion.21.marks, f32[2,512,1]{2,1,0:T(8,128)} %copy.36.seg_c, f32[2,1,512]{2,1,0:T(1,128)} %copy.35.seg_r, ...), custom_call_target="tpu_custom_call" | custom-call | flops 1342177280 | bytes 8388608 | tf_op jit(solution)/shard_map/mixer_inner_grad/pallas_call | solution.py:362
  265.8 3.5 convolution_convert_fusion.3
  275.5 3.1 fusion.27
  283.3 3.1 fusion.21
  286.4 11.4 %collective-permute-done.34 = bf16[2,4,128,128]{3,2,1,0:T(8,128)(2,1)S(1)} collective-permute-done((bf16[2,4,128,128]{3,2,1,0:T(8,128)(2,1)S(1)}, bf16[2,4,128,128]{3,2,1,0:T(8,128)(2,1)S(1)}, u32[]{:S(2)}, u32[]{:S(2)}) %collective-permute-start.34) | collective-permute-done | bytes 262176 | tf_op jit(solution)/shard_map/ppermute | solution.py:379
  298.5 2.7 collective-permute-done.42
  306.7 5.6 %mixer_last_grad.1 = (bf16[1024,512]{1,0:T(8,128)(2,1)}, bf16[1024,512]{1,0:T(8,128)(2,1)}) custom-call(f32[4]{0:T(128)} %get-tuple-element.129.rates, f32[2,2]{1,0:T(2,128)} %pad_maximum_fusion.21.marks, f32[2,512,1]{2,1,0:T(8,128)} %copy.36.seg_c, bf16[1024,512]{1,0:T(8,128)(2,1)} %get-tuple-element.58.k_ref.k, ...), custom_call_target="tpu_custom_call" | custom-call | flops 134217728 | bytes 8388608 | tf_op jit(solution)/shard_map/mixer_last_grad/pallas_call | solution.py:362
  322.5 3.4 divide.2
  337.2 14.5 %collective-permute-done.46 = bf16[256,768]{0,1:T(8,128)(2,1)S(1)} collective-permute-done((bf16[256,768]{0,1:T(8,128)(2,1)S(1)}, bf16[256,768]{0,1:T(8,128)(2,1)S(1)}, u32[]{:S(2)}, u32[]{:S(2)}) %collective-permute-start.46) | collective-permute-done | bytes 393248 | tf_op jit(solution)/shard_map/ppermute | solution.py:23
  353.6 4.9 %collective-permute-done.47 = bf16[128,768]{0,1:T(8,128)(2,1)S(1)} collective-permute-done((bf16[128,768]{0,1:T(8,128)(2,1)S(1)}, bf16[128,768]{0,1:T(8,128)(2,1)S(1)}, u32[]{:S(2)}, u32[]{:S(2)}) %collective-permute-start.47) | collective-permute-done | bytes 196640 | tf_op jit(solution)/shard_map/ppermute | solution.py:23
  363.1 4.4 %fusion.1 = (f32[512]{0:T(512)S(1)}, f32[512,1024]{1,0:T(8,128)S(1)}) fusion(bf16[512,1024]{1,0:T(8,128)(2,1)S(1)} %copy-done, bf16[512,1024]{1,0:T(8,128)(2,1)} %collective-permute-done.38, f32[512,1024]{1,0:T(8,128)} %fusion.15, f32[512,1024]{1,0:T(8,128)} %fusion.23, f32[512,1024]{1,0:T(8,128)} %fusion.27, f32[512,1024]{1,0:T(8,128)} %fusion.25), kind=kLoop, calls=%fused_computation.4 | loop fusion | flops 4193792 | bytes 12584960 | tf_op jit(solution)/shard_map/reduce_sum | solution.py:689
  370.3 4.2 collective-permute-done.48
  378.5 4.8 %collective-permute-done.50 = bf16[512,512]{1,0:T(8,128)(2,1)} collective-permute-done((bf16[512,512]{1,0:T(8,128)(2,1)}, bf16[512,512]{1,0:T(8,128)(2,1)}, u32[]{:S(2)}, u32[]{:S(2)}) %collective-permute-start.50) | collective-permute-done | bytes 524320 | tf_op jit(solution)/shard_map/ppermute | solution.py:23
  387.9 3.5 divide.3
  395.9 2.7 collective-permute-start.52
  399.8 6.1 %collective-permute-done.40 = bf16[512,256]{1,0:T(8,128)(2,1)S(1)} collective-permute-done((bf16[512,256]{1,0:T(8,128)(2,1)}, bf16[512,256]{1,0:T(8,128)(2,1)S(1)}, u32[]{:S(2)}, u32[]{:S(2)}) %collective-permute-start.40) | collective-permute-done | bytes 262176 | tf_op jit(solution)/shard_map/ppermute | solution.py:23
  406.0 5.2 %collective-permute-done.52 = bf16[256,512]{1,0:T(8,128)(2,1)S(1)} collective-permute-done((bf16[256,512]{1,0:T(8,128)(2,1)S(1)}, bf16[256,512]{1,0:T(8,128)(2,1)S(1)}, u32[]{:S(2)}, u32[]{:S(2)}) %collective-permute-start.52) | collective-permute-done | bytes 262176 | tf_op jit(solution)/shard_map/ppermute | solution.py:23
  413.2 3.2 collective-permute-done.53
  (351 shorter events, 121.5 us)
Async XLA Ops:
  7.2 162.8 %all-gather.2.cloned.1.call-start = ((), (), s32[]{:S(2)}) async-start(), calls=%async_computation.2 | async-start | bytes 10305536 | tf_op jit(solution)/shard_map/all_gather | solution.py:392
  9.4 344.2 %reduce-scatter.3.cloned.1.call-start = ((), (), s32[]{:S(2)}) async-start(), calls=%async_computation.3 | async-start | bytes 10813440 | tf_op jit(solution)/shard_map/reduce_scatter | solution.py:418
  10.2 15.6 %collective-permute-start = (bf16[512,256]{1,0:T(8,128)(2,1)S(1)}, bf16[512,256]{1,0:T(8,128)(2,1)S(1)}, u32[]{:S(2)}, u32[]{:S(2)}) collective-permute-start(bf16[512,256]{1,0:T(8,128)(2,1)S(1)} %get-tuple-element.158), channel_id=1, source_target_pairs={{0,2},{2,0},{4,6},{6,4},{1,3},{3,1},{5,7},{7,5},{8,10},{10,8},{12,... | collective-permute-start | bytes 786440 | tf_op jit(solution)/shard_map/ppermute | solution.py:23
  10.7 15.2 %collective-permute-start.1 = (bf16[512,256]{1,0:T(8,128)(2,1)S(1)}, bf16[512,256]{1,0:T(8,128)(2,1)S(1)}, u32[]{:S(2)}, u32[]{:S(2)}) collective-permute-start(bf16[512,256]{1,0:T(8,128)(2,1)S(1)} %get-tuple-element.160), channel_id=1, source_target_pairs={{0,4},{2,6},{4,0},{6,2},{1,5},{3,7},{5,1},{7,3},{8,12},{10,14},{12... | collective-permute-start | bytes 786440 | tf_op jit(solution)/shard_map/ppermute | solution.py:23
  13.2 14.8 %collective-permute-start.2 = (bf16[512,256]{1,0:T(8,128)(2,1)S(1)}, bf16[512,256]{1,0:T(8,128)(2,1)S(1)}, u32[]{:S(2)}, u32[]{:S(2)}) collective-permute-start(bf16[512,256]{1,0:T(8,128)(2,1)S(1)} %get-tuple-element.157), channel_id=1, source_target_pairs={{0,6},{2,4},{4,2},{6,0},{1,7},{3,5},{5,3},{7,1},{8,14},{10,12},{12... | collective-permute-start | bytes 786440 | tf_op jit(solution)/shard_map/ppermute | solution.py:23
  13.3 7.8 %collective-permute-start.6 = (bf16[128,512]{1,0:T(8,128)(2,1)S(1)}, bf16[128,512]{1,0:T(8,128)(2,1)S(1)}, u32[]{:S(2)}, u32[]{:S(2)}) collective-permute-start(bf16[128,512]{1,0:T(8,128)(2,1)S(1)} %fusion.32), channel_id=1, source_target_pairs={{0,8},{8,0},{16,24},{24,16},{1,9},{9,1},{17,25},{25,17},{2,10},{10... | collective-permute-start | bytes 393224 | tf_op jit(solution)/shard_map/ppermute | solution.py:23
  19.3 29.2 %collective-permute-start.3 = (f32[2]{0:T(128)S(1)}, f32[2]{0:T(128)S(1)}, u32[]{:S(2)}, u32[]{:S(2)}) collective-permute-start(f32[2]{0:T(128)S(1)} %copy-done.61), channel_id=1, source_target_pairs={{0,4},{2,6},{4,0},{6,2},{1,5},{3,7},{5,1},{7,3},{8,12},{10,14},{12... | collective-permute-start | bytes 32 | tf_op jit(solution)/shard_map/ppermute | solution.py:23
  21.2 27.1 %collective-permute-start.7 = (bf16[256,512]{1,0:T(8,128)(2,1)S(1)}, bf16[256,512]{1,0:T(8,128)(2,1)S(1)}, u32[]{:S(2)}, u32[]{:S(2)}) collective-permute-start(bf16[256,512]{1,0:T(8,128)(2,1)S(1)} %pad_maximum_fusion.17), channel_id=1, source_target_pairs={{0,16},{8,24},{16,0},{24,8},{1,17},{9,25},{17,1},{25,9},{2,18},{10... | collective-permute-start | bytes 786440 | tf_op jit(solution)/shard_map/ppermute | solution.py:23
  32.5 39.0 %collective-permute-start.5 = (bf16[512,1024]{1,0:T(8,128)(2,1)}, bf16[512,1024]{1,0:T(8,128)(2,1)S(1)}, u32[]{:S(2)}, u32[]{:S(2)}) collective-permute-start(bf16[512,1024]{1,0:T(8,128)(2,1)} %get-tuple-element.54), channel_id=1, source_target_pairs={{0,2},{2,0},{4,6},{6,4},{1,3},{3,1},{5,7},{7,5},{8,10},{10,8},{12,... | collective-permute-start | bytes 3145736 | tf_op jit(solution)/shard_map/ppermute | solution.py:23
  48.4 6.4 %collective-permute-start.12 = (bf16[512,256]{1,0:T(8,128)(2,1)S(1)}, bf16[512,256]{1,0:T(8,128)(2,1)S(1)}, u32[]{:S(2)}, u32[]{:S(2)}) collective-permute-start(bf16[512,256]{1,0:T(8,128)(2,1)S(1)} %get-tuple-element.162), channel_id=1, source_target_pairs={{0,4},{2,6},{4,0},{6,2},{1,5},{3,7},{5,1},{7,3},{8,12},{10,14},{12... | collective-permute-start | bytes 786440 | tf_op jit(solution)/shard_map/ppermute | solution.py:23
  49.1 21.0 %collective-permute-start.14 = (bf16[512,256]{1,0:T(8,128)(2,1)S(1)}, bf16[512,256]{1,0:T(8,128)(2,1)S(1)}, u32[]{:S(2)}, u32[]{:S(2)}) collective-permute-start(bf16[512,256]{1,0:T(8,128)(2,1)S(1)} %get-tuple-element.161), channel_id=1, source_target_pairs={{0,1},{1,0},{2,3},{3,2},{4,5},{5,4},{6,7},{7,6},{8,9},{9,8},{10,11... | collective-permute-start | bytes 786440 | tf_op jit(solution)/shard_map/ppermute | solution.py:23
  54.9 19.1 %collective-permute-start.13 = (bf16[512,512]{1,0:T(8,128)(2,1)S(1)}, bf16[512,512]{1,0:T(8,128)(2,1)S(1)}, u32[]{:S(2)}, u32[]{:S(2)}) collective-permute-start(bf16[512,512]{1,0:T(8,128)(2,1)S(1)} %pad_maximum_fusion.14), channel_id=1, source_target_pairs={{0,1},{1,0},{2,3},{3,2},{4,5},{5,4},{6,7},{7,6},{8,9},{9,8},{10,11... | collective-permute-start | bytes 1572872 | tf_op jit(solution)/shard_map/ppermute | solution.py:23
  56.5 12.7 %collective-permute-start.8 = (bf16[128,512]{1,0:T(8,128)(2,1)S(1)}, bf16[128,512]{1,0:T(8,128)(2,1)S(1)}, u32[]{:S(2)}, u32[]{:S(2)}) collective-permute-start(bf16[128,512]{1,0:T(8,128)(2,1)S(1)} %fusion.31), channel_id=1, source_target_pairs={{0,8},{8,0},{16,24},{24,16},{1,9},{9,1},{17,25},{25,17},{2,10},{10... | collective-permute-start | bytes 393224 | tf_op jit(solution)/shard_map/ppermute | solution.py:23
  69.2 29.8 %collective-permute-start.9 = (bf16[256,512]{1,0:T(8,128)(2,1)S(1)}, bf16[256,512]{1,0:T(8,128)(2,1)S(1)}, u32[]{:S(2)}, u32[]{:S(2)}) collective-permute-start(bf16[256,512]{1,0:T(8,128)(2,1)S(1)} %pad_maximum_fusion.18), channel_id=1, source_target_pairs={{0,16},{8,24},{16,0},{24,8},{1,17},{9,25},{17,1},{25,9},{2,18},{10... | collective-permute-start | bytes 786440 | tf_op jit(solution)/shard_map/ppermute | solution.py:23
  70.2 15.6 %collective-permute-start.15 = (bf16[1024,256]{1,0:T(8,128)(2,1)S(1)}, bf16[1024,256]{1,0:T(8,128)(2,1)S(1)}, u32[]{:S(2)}, u32[]{:S(2)}) collective-permute-start(bf16[1024,256]{1,0:T(8,128)(2,1)S(1)} %pad_maximum_fusion.15), channel_id=1, source_target_pairs={{0,4},{2,6},{4,0},{6,2},{1,5},{3,7},{5,1},{7,3},{8,12},{10,14},{12... | collective-permute-start | bytes 1572872 | tf_op jit(solution)/shard_map/ppermute | solution.py:23
  77.4 22.8 %collective-permute-start.19 = (bf16[512,256]{1,0:T(8,128)(2,1)}, bf16[512,256]{1,0:T(8,128)(2,1)S(1)}, u32[]{:S(2)}, u32[]{:S(2)}) collective-permute-start(bf16[512,256]{1,0:T(8,128)(2,1)} %get-tuple-element.155), channel_id=1, source_target_pairs={{0,2},{2,0},{4,6},{6,4},{1,3},{3,1},{5,7},{7,5},{8,10},{10,8},{12,... | collective-permute-start | bytes 786440 | tf_op jit(solution)/shard_map/ppermute | solution.py:23
  77.4 23.7 %collective-permute-start.20 = (bf16[512,256]{1,0:T(8,128)(2,1)S(1)}, bf16[512,256]{1,0:T(8,128)(2,1)S(1)}, u32[]{:S(2)}, u32[]{:S(2)}) collective-permute-start(bf16[512,256]{1,0:T(8,128)(2,1)S(1)} %get-tuple-element.154), channel_id=1, source_target_pairs={{0,4},{2,6},{4,0},{6,2},{1,5},{3,7},{5,1},{7,3},{8,12},{10,14},{12... | collective-permute-start | bytes 786440 | tf_op jit(solution)/shard_map/ppermute | solution.py:23
  77.7 23.4 %collective-permute-start.21 = (bf16[512,256]{1,0:T(8,128)(2,1)S(1)}, bf16[512,256]{1,0:T(8,128)(2,1)S(1)}, u32[]{:S(2)}, u32[]{:S(2)}) collective-permute-start(bf16[512,256]{1,0:T(8,128)(2,1)S(1)} %get-tuple-element.153), channel_id=1, source_target_pairs={{0,6},{2,4},{4,2},{6,0},{1,7},{3,5},{5,3},{7,1},{8,14},{10,12},{12... | collective-permute-start | bytes 786440 | tf_op jit(solution)/shard_map/ppermute | solution.py:23
  94.4 14.3 %collective-permute-start.16 = (bf16[2,4,128,128]{3,2,1,0:T(8,128)(2,1)}, bf16[2,4,128,128]{3,2,1,0:T(8,128)(2,1)S(1)}, u32[]{:S(2)}, u32[]{:S(2)}) collective-permute-start(bf16[2,4,128,128]{3,2,1,0:T(8,128)(2,1)} %add_convert_fusion.7), channel_id=1, source_target_pairs={{0,8},{1,9},{2,10},{3,11},{4,12},{5,13},{6,14},{7,15}} | collective-permute-start | bytes 786440 | tf_op jit(solution)/shard_map/ppermute | solution.py:379
  99.1 12.0 %collective-permute-start.10 = (bf16[512,256]{1,0:T(8,128)(2,1)S(1)}, bf16[512,256]{1,0:T(8,128)(2,1)}, u32[]{:S(2)}, u32[]{:S(2)}) collective-permute-start(bf16[512,256]{1,0:T(8,128)(2,1)S(1)} %get-tuple-element.163), channel_id=1, source_target_pairs={{0,4},{2,6},{4,0},{6,2},{1,5},{3,7},{5,1},{7,3},{8,12},{10,14},{12... | collective-permute-start | bytes 786440 | tf_op jit(solution)/shard_map/ppermute | solution.py:23
  100.2 13.8 %collective-permute-start.24 = (bf16[512,256]{1,0:T(8,128)(2,1)S(1)}, bf16[512,256]{1,0:T(8,128)(2,1)S(1)}, u32[]{:S(2)}, u32[]{:S(2)}) collective-permute-start(bf16[512,256]{1,0:T(8,128)(2,1)S(1)} %get-tuple-element.164), channel_id=1, source_target_pairs={{0,1},{1,0},{2,3},{3,2},{4,5},{5,4},{6,7},{7,6},{8,9},{9,8},{10,11... | collective-permute-start | bytes 786440 | tf_op jit(solution)/shard_map/ppermute | solution.py:23
  105.4 41.4 %collective-permute-start.22 = (bf16[512,1024]{1,0:T(8,128)(2,1)}, bf16[512,1024]{1,0:T(8,128)(2,1)}, u32[]{:S(2)}, u32[]{:S(2)}) collective-permute-start(bf16[512,1024]{1,0:T(8,128)(2,1)} %assemble.3.g0), channel_id=1, source_target_pairs={{0,2},{2,0},{4,6},{6,4},{1,3},{3,1},{5,7},{7,5},{8,10},{10,8},{12,... | collective-permute-start | bytes 3145736 | tf_op jit(solution)/shard_map/ppermute | solution.py:23
  108.9 5.9 %collective-permute-start.17 = (bf16[2,4,128,128]{3,2,1,0:T(8,128)(2,1)S(1)}, bf16[2,4,128,128]{3,2,1,0:T(8,128)(2,1)S(1)}, u32[]{:S(2)}, u32[]{:S(2)}) collective-permute-start(bf16[2,4,128,128]{3,2,1,0:T(8,128)(2,1)S(1)} %add_convert_fusion.6), channel_id=1, source_target_pairs={{8,16},{9,17},{10,18},{11,19},{12,20},{13,21},{14,22},{15,23}} | collective-permute-start | bytes 786440 | tf_op jit(solution)/shard_map/ppermute | solution.py:379
  112.1 24.5 %collective-permute-start.11 = (bf16[512,512]{1,0:T(8,128)(2,1)S(1)}, bf16[512,512]{1,0:T(8,128)(2,1)S(1)}, u32[]{:S(2)}, u32[]{:S(2)}) collective-permute-start(bf16[512,512]{1,0:T(8,128)(2,1)S(1)} %pad_maximum_fusion.13), channel_id=1, source_target_pairs={{0,1},{1,0},{2,3},{3,2},{4,5},{5,4},{6,7},{7,6},{8,9},{9,8},{10,11... | collective-permute-start | bytes 1572872 | tf_op jit(solution)/shard_map/ppermute | solution.py:23
  114.1 39.0 %collective-permute-start.25 = (bf16[1024,256]{1,0:T(8,128)(2,1)S(1)}, bf16[1024,256]{1,0:T(8,128)(2,1)S(1)}, u32[]{:S(2)}, u32[]{:S(2)}) collective-permute-start(bf16[1024,256]{1,0:T(8,128)(2,1)S(1)} %pad_maximum_fusion.16), channel_id=1, source_target_pairs={{0,4},{2,6},{4,0},{6,2},{1,5},{3,7},{5,1},{7,3},{8,12},{10,14},{12... | collective-permute-start | bytes 1572872 | tf_op jit(solution)/shard_map/ppermute | solution.py:23
  115.6 30.5 %collective-permute-start.18 = (bf16[2,4,128,128]{3,2,1,0:T(8,128)(2,1)}, bf16[2,4,128,128]{3,2,1,0:T(8,128)(2,1)S(1)}, u32[]{:S(2)}, u32[]{:S(2)}) collective-permute-start(bf16[2,4,128,128]{3,2,1,0:T(8,128)(2,1)} %get-tuple-element.126), channel_id=1, source_target_pairs={{16,24},{17,25},{18,26},{19,27},{20,28},{21,29},{22,30},{23,31}} | collective-permute-start | bytes 786440 | tf_op jit(solution)/shard_map/ppermute | solution.py:379
  224.0 193.2 %reduce-scatter.5.cloned.1.call-start = ((), (), s32[]{:S(2)}) async-start(), calls=%async_computation.4 | async-start | bytes 2703360 | tf_op jit(solution)/shard_map/reduce_scatter | solution.py:699
  255.2 23.4 %collective-permute-start.32 = (bf16[2,4,128,128]{3,2,1,0:T(8,128)(2,1)}, bf16[2,4,128,128]{3,2,1,0:T(8,128)(2,1)S(1)}, u32[]{:S(2)}, u32[]{:S(2)}) collective-permute-start(bf16[2,4,128,128]{3,2,1,0:T(8,128)(2,1)} %add_convert_fusion.4), channel_id=1, source_target_pairs={{24,16},{25,17},{26,18},{27,19},{28,20},{29,21},{30,22},{31,23}} | collective-permute-start | bytes 786440 | tf_op jit(solution)/shard_map/ppermute | solution.py:379
  272.3 29.3 %collective-permute-start.43 = (bf16[512,768]{0,1:T(8,128)(2,1)S(1)}, bf16[512,768]{0,1:T(8,128)(2,1)S(1)}, u32[]{:S(2)}, u32[]{:S(2)}) collective-permute-start(bf16[512,768]{0,1:T(8,128)(2,1)S(1)} %slice.243), channel_id=1, source_target_pairs={{0,1},{1,0},{2,3},{3,2},{4,5},{5,4},{6,7},{7,6},{8,9},{9,8},{10,11... | collective-permute-start | bytes 2359304 | tf_op jit(solution)/shard_map/ppermute | solution.py:23
  273.9 27.4 %collective-permute-start.42 = (bf16[1024,384]{0,1:T(8,128)(2,1)S(1)}, bf16[1024,384]{0,1:T(8,128)(2,1)S(1)}, u32[]{:S(2)}, u32[]{:S(2)}) collective-permute-start(bf16[1024,384]{0,1:T(8,128)(2,1)S(1)} %pad_maximum_fusion.10), channel_id=1, source_target_pairs={{0,4},{2,6},{4,0},{6,2},{1,5},{3,7},{5,1},{7,3},{8,12},{10,14},{12... | collective-permute-start | bytes 2359304 | tf_op jit(solution)/shard_map/ppermute | solution.py:23
  281.9 15.9 %collective-permute-start.34 = (bf16[2,4,128,128]{3,2,1,0:T(8,128)(2,1)S(1)}, bf16[2,4,128,128]{3,2,1,0:T(8,128)(2,1)S(1)}, u32[]{:S(2)}, u32[]{:S(2)}) collective-permute-start(bf16[2,4,128,128]{3,2,1,0:T(8,128)(2,1)S(1)} %get-tuple-element.120), channel_id=1, source_target_pairs={{8,0},{9,1},{10,2},{11,3},{12,4},{13,5},{14,6},{15,7}} | collective-permute-start | bytes 786440 | tf_op jit(solution)/shard_map/ppermute | solution.py:379
  303.8 24.3 %collective-permute-start.45 = (bf16[512,384]{0,1:T(8,128)(2,1)}, bf16[512,384]{0,1:T(8,128)(2,1)}, u32[]{:S(2)}, u32[]{:S(2)}) collective-permute-start(bf16[512,384]{0,1:T(8,128)(2,1)} %slice.328), channel_id=1, source_target_pairs={{0,4},{2,6},{4,0},{6,2},{1,5},{3,7},{5,1},{7,3},{8,12},{10,14},{12... | collective-permute-start | bytes 1179656 | tf_op jit(solution)/shard_map/ppermute | solution.py:23
  305.8 23.7 %collective-permute-start.44 = (bf16[512,384]{0,1:T(8,128)(2,1)}, bf16[512,384]{0,1:T(8,128)(2,1)}, u32[]{:S(2)}, u32[]{:S(2)}) collective-permute-start(bf16[512,384]{0,1:T(8,128)(2,1)} %slice.329), channel_id=1, source_target_pairs={{0,1},{1,0},{2,3},{3,2},{4,5},{5,4},{6,7},{7,6},{8,9},{9,8},{10,11... | collective-permute-start | bytes 1179656 | tf_op jit(solution)/shard_map/ppermute | solution.py:23
  322.4 40.6 %collective-permute-start.38 = (bf16[512,1024]{1,0:T(8,128)(2,1)}, bf16[512,1024]{1,0:T(8,128)(2,1)}, u32[]{:S(2)}, u32[]{:S(2)}) collective-permute-start(bf16[512,1024]{1,0:T(8,128)(2,1)} %add_convert_fusion), channel_id=1, source_target_pairs={{0,2},{2,0},{4,6},{6,4},{1,3},{3,1},{5,7},{7,5},{8,10},{10,8},{12,... | collective-permute-start | bytes 3145736 | tf_op jit(solution)/shard_map/ppermute | solution.py:23
  325.9 26.4 %collective-permute-start.35 = (bf16[512,256]{1,0:T(8,128)(2,1)}, bf16[512,256]{1,0:T(8,128)(2,1)S(1)}, u32[]{:S(2)}, u32[]{:S(2)}) collective-permute-start(bf16[512,256]{1,0:T(8,128)(2,1)} %get-tuple-element.78), channel_id=1, source_target_pairs={{0,6},{2,4},{4,2},{6,0},{1,7},{3,5},{5,3},{7,1},{8,14},{10,12},{12... | collective-permute-start | bytes 786440 | tf_op jit(solution)/shard_map/ppermute | solution.py:23
  327.5 24.8 %collective-permute-start.36 = (bf16[512,256]{1,0:T(8,128)(2,1)}, bf16[512,256]{1,0:T(8,128)(2,1)S(1)}, u32[]{:S(2)}, u32[]{:S(2)}) collective-permute-start(bf16[512,256]{1,0:T(8,128)(2,1)} %get-tuple-element.79), channel_id=1, source_target_pairs={{0,4},{2,6},{4,0},{6,2},{1,5},{3,7},{5,1},{7,3},{8,12},{10,14},{12... | collective-permute-start | bytes 786440 | tf_op jit(solution)/shard_map/ppermute | solution.py:23
  328.0 24.3 %collective-permute-start.37 = (bf16[512,256]{1,0:T(8,128)(2,1)}, bf16[512,256]{1,0:T(8,128)(2,1)S(1)}, u32[]{:S(2)}, u32[]{:S(2)}) collective-permute-start(bf16[512,256]{1,0:T(8,128)(2,1)} %get-tuple-element.80), channel_id=1, source_target_pairs={{0,2},{2,0},{4,6},{6,4},{1,3},{3,1},{5,7},{7,5},{8,10},{10,8},{12,... | collective-permute-start | bytes 786440 | tf_op jit(solution)/shard_map/ppermute | solution.py:23
  330.8 20.9 %collective-permute-start.46 = (bf16[256,768]{0,1:T(8,128)(2,1)S(1)}, bf16[256,768]{0,1:T(8,128)(2,1)S(1)}, u32[]{:S(2)}, u32[]{:S(2)}) collective-permute-start(bf16[256,768]{0,1:T(8,128)(2,1)S(1)} %fusion.7), channel_id=1, source_target_pairs={{0,16},{8,24},{16,0},{24,8},{1,17},{9,25},{17,1},{25,9},{2,18},{10... | collective-permute-start | bytes 1179656 | tf_op jit(solution)/shard_map/ppermute | solution.py:23
  351.9 6.5 %collective-permute-start.47 = (bf16[128,768]{0,1:T(8,128)(2,1)S(1)}, bf16[128,768]{0,1:T(8,128)(2,1)S(1)}, u32[]{:S(2)}, u32[]{:S(2)}) collective-permute-start(bf16[128,768]{0,1:T(8,128)(2,1)S(1)} %slice.333), channel_id=1, source_target_pairs={{0,8},{8,0},{16,24},{24,16},{1,9},{9,1},{17,25},{25,17},{2,10},{10... | collective-permute-start | bytes 589832 | tf_op jit(solution)/shard_map/ppermute | solution.py:23
  361.6 13.0 %collective-permute-start.48 = (bf16[1024,256]{1,0:T(8,128)(2,1)}, bf16[1024,256]{1,0:T(8,128)(2,1)}, u32[]{:S(2)}, u32[]{:S(2)}) collective-permute-start(bf16[1024,256]{1,0:T(8,128)(2,1)} %slice.206), channel_id=1, source_target_pairs={{0,4},{2,6},{4,0},{6,2},{1,5},{3,7},{5,1},{7,3},{8,12},{10,14},{12... | collective-permute-start | bytes 1572872 | tf_op jit(solution)/shard_map/ppermute | solution.py:23
  368.3 15.1 %collective-permute-start.50 = (bf16[512,512]{1,0:T(8,128)(2,1)}, bf16[512,512]{1,0:T(8,128)(2,1)}, u32[]{:S(2)}, u32[]{:S(2)}) collective-permute-start(bf16[512,512]{1,0:T(8,128)(2,1)} %slice.210), channel_id=1, source_target_pairs={{0,1},{1,0},{2,3},{3,2},{4,5},{5,4},{6,7},{7,6},{8,9},{9,8},{10,11... | collective-permute-start | bytes 1572872 | tf_op jit(solution)/shard_map/ppermute | solution.py:23
  377.6 16.0 %collective-permute-start.49 = (bf16[512,256]{1,0:T(8,128)(2,1)}, bf16[512,256]{1,0:T(8,128)(2,1)S(1)}, u32[]{:S(2)}, u32[]{:S(2)}) collective-permute-start(bf16[512,256]{1,0:T(8,128)(2,1)} %slice.332), channel_id=1, source_target_pairs={{0,1},{1,0},{2,3},{3,2},{4,5},{5,4},{6,7},{7,6},{8,9},{9,8},{10,11... | collective-permute-start | bytes 786440 | tf_op jit(solution)/shard_map/ppermute | solution.py:23
  386.4 8.3 %collective-permute-start.51 = (bf16[512,256]{1,0:T(8,128)(2,1)}, bf16[512,256]{1,0:T(8,128)(2,1)}, u32[]{:S(2)}, u32[]{:S(2)}) collective-permute-start(bf16[512,256]{1,0:T(8,128)(2,1)} %slice.331), channel_id=1, source_target_pairs={{0,4},{2,6},{4,0},{6,2},{1,5},{3,7},{5,1},{7,3},{8,12},{10,14},{12... | collective-permute-start | bytes 786440 | tf_op jit(solution)/shard_map/ppermute | solution.py:23
  391.5 8.3 %collective-permute-start.39 = (bf16[512,256]{1,0:T(8,128)(2,1)}, bf16[512,256]{1,0:T(8,128)(2,1)S(1)}, u32[]{:S(2)}, u32[]{:S(2)}) collective-permute-start(bf16[512,256]{1,0:T(8,128)(2,1)} %get-tuple-element.85), channel_id=1, source_target_pairs={{0,6},{2,4},{4,2},{6,0},{1,7},{3,5},{5,3},{7,1},{8,14},{10,12},{12... | collective-permute-start | bytes 786440 | tf_op jit(solution)/shard_map/ppermute | solution.py:23
  391.5 14.4 %collective-permute-start.40 = (bf16[512,256]{1,0:T(8,128)(2,1)}, bf16[512,256]{1,0:T(8,128)(2,1)S(1)}, u32[]{:S(2)}, u32[]{:S(2)}) collective-permute-start(bf16[512,256]{1,0:T(8,128)(2,1)} %get-tuple-element.86), channel_id=1, source_target_pairs={{0,4},{2,6},{4,0},{6,2},{1,5},{3,7},{5,1},{7,3},{8,12},{10,14},{12... | collective-permute-start | bytes 786440 | tf_op jit(solution)/shard_map/ppermute | solution.py:23
  393.5 12.4 %collective-permute-start.41 = (bf16[512,256]{1,0:T(8,128)(2,1)}, bf16[512,256]{1,0:T(8,128)(2,1)S(1)}, u32[]{:S(2)}, u32[]{:S(2)}) collective-permute-start(bf16[512,256]{1,0:T(8,128)(2,1)} %get-tuple-element.87), channel_id=1, source_target_pairs={{0,2},{2,0},{4,6},{6,4},{1,3},{3,1},{5,7},{7,5},{8,10},{10,8},{12,... | collective-permute-start | bytes 786440 | tf_op jit(solution)/shard_map/ppermute | solution.py:23
  395.9 15.3 %collective-permute-start.52 = (bf16[256,512]{1,0:T(8,128)(2,1)S(1)}, bf16[256,512]{1,0:T(8,128)(2,1)S(1)}, u32[]{:S(2)}, u32[]{:S(2)}) collective-permute-start(bf16[256,512]{1,0:T(8,128)(2,1)S(1)} %slice.330), channel_id=1, source_target_pairs={{0,16},{8,24},{16,0},{24,8},{1,17},{9,25},{17,1},{25,9},{2,18},{10... | collective-permute-start | bytes 786440 | tf_op jit(solution)/shard_map/ppermute | solution.py:23
  411.3 5.1 %collective-permute-start.53 = (bf16[128,512]{1,0:T(8,128)(2,1)S(1)}, bf16[128,512]{1,0:T(8,128)(2,1)S(1)}, u32[]{:S(2)}, u32[]{:S(2)}) collective-permute-start(bf16[128,512]{1,0:T(8,128)(2,1)S(1)} %slice.334), channel_id=1, source_target_pairs={{0,8},{8,0},{16,24},{24,16},{1,9},{9,1},{17,25},{25,17},{2,10},{10... | collective-permute-start | bytes 393224 | tf_op jit(solution)/shard_map/ppermute | solution.py:23
  (83 other events, 604.4 us)
Sparse Core Ops, SparseCore 0:
  10.7 159.2 all-gather.1
  224.1 105.0 reduce-scatter.2
  353.7 45.1 reduce-scatter.4

commit v6 on v5

--- a/solution.py
+++ b/solution.py
@@ -33,6 +33,20 @@
 
 def bits_of(axis):
     return [1 << b for b in range(lax.axis_size(axis).bit_length() - 1)]
+
+
+def row_places():
+    count = lax.axis_size("row")
+    places = [0]
+    for bit in reversed(bits_of("row")):
+        places = places + [p | bit for p in places]
+    assert len(places) == count
+    return places
+
+
+def reorder(value, dim):
+    take = lambda p: lax.slice_in_dim(value, p, p + 1, axis=dim)
+    return jnp.concatenate([take(p) for p in row_places()], dim)
 
 
 def xor_turn(value, dim, place, count):
@@ -51,7 +65,7 @@
     tokens, width = rows.shape
     split = rows.reshape(tokens, nz, ny, width // (nz * ny))
     split = xor_turn(split, 1, lax.axis_index("row"), nz)
-    split = xor_turn(split, 2, lax.axis_index("dp"), ny)
+    split = reorder(xor_turn(split, 2, lax.axis_index("dp"), ny), 1)
     return split.transpose(0, 2, 1, 3).reshape(tokens, width)
 
 
@@ -59,6 +73,7 @@
     nz, ny = lax.axis_size("row"), lax.axis_size("dp")
     tokens, width = rows.shape
     split = rows.reshape(tokens, ny, nz, width // (nz * ny)).transpose(0, 2, 1, 3)
+    split = reorder(split, 1)
     split = xor_turn(split, 1, lax.axis_index("row"), nz)
     split = xor_turn(split, 2, lax.axis_index("dp"), ny)
     return split.reshape(tokens, width)
@@ -78,7 +93,7 @@
     return [jnp.where(high, first[k ^ 2], first[k]) for k in range(4)]
 
 
-def assemble_kernel(norm, bits, *refs):
+def assemble_kernel(norm, places, bits, *refs):
     parts = [r[...].astype(F32) for r in refs[:4]]
     blocks = pick4(parts, bits[0] != 0, bits[1] != 0)
     odd = bits[2] != 0
@@ -87,7 +102,7 @@
         low, high = b[:, :HEAD], b[:, HEAD:]
         halves[0].append(jnp.where(odd, high, low))
         halves[1].append(jnp.where(odd, low, high))
-    rows = jnp.concatenate(halves[0] + halves[1], 1)
+    rows = jnp.concatenate([half[k] for half in halves for k in places], 1)
     refs[4][...] = rows.astype(BF16)
     if norm:
         scale = lax.rsqrt(jnp.mean(rows * rows, 1, keepdims=True) + EPS)
@@ -115,7 +130,7 @@
         shape += [shape[0], jax.ShapeDtypeStruct((tokens, 1), F32)]
         specs += [row(model), row(1)]
     out = pl.pallas_call(
-        functools.partial(assemble_kernel, norm),
+        functools.partial(assemble_kernel, norm, row_places()),
         grid=(tokens // step,),
         in_specs=[pl.BlockSpec(memory_space=pltpu.SMEM)] + [row(width)] * 4,
         out_specs=specs,
@@ -125,18 +140,19 @@
     return out if norm else out[0]
 
 
-def divide_kernel(bits, rows_ref, *refs):
+def divide_kernel(places, bits, rows_ref, *refs):
     rows = rows_ref[...].astype(F32)
     odd = bits[2] != 0
     blocks = []
-    for k in range(4):
+    for k in places:
         low = rows[:, k * HEAD : (k + 1) * HEAD]
         high = rows[:, (4 + k) * HEAD : (5 + k) * HEAD]
         blocks.append(
             jnp.concatenate([jnp.where(odd, high, low), jnp.where(odd, low, high)], 1)
         )
-    for ref, block in zip(refs, pick4(blocks, bits[0] != 0, bits[1] != 0)):
-        ref[...] = block.astype(BF16)
+    parts = pick4(blocks, bits[0] != 0, bits[1] != 0)
+    for ref, pieces in zip(refs, (parts[:2], parts[2:])):
+        ref[...] = jnp.concatenate(pieces, 1).astype(BF16)
 
 
 def divide(rows):
@@ -146,15 +162,16 @@
         col = lax.axis_index(COL)
         whole = from_order(rows)
         blocks = [whole[:, k * width : (k + 1) * width] for k in range(4)]
-        return pick4(blocks, (col & 1) != 0, (col & 2) != 0)
-    step = 128
+        parts = pick4(blocks, (col & 1) != 0, (col & 2) != 0)
+        return jnp.concatenate(parts[:2], 1), jnp.concatenate(parts[2:], 1)
+    step = 256
     row = lambda n: pl.BlockSpec((step, n), lambda i: (i, 0))
     return pl.pallas_call(
-        divide_kernel,
+        functools.partial(divide_kernel, row_places()),
         grid=(tokens // step,),
         in_specs=[pl.BlockSpec(memory_space=pltpu.SMEM), row(model)],
-        out_specs=[row(width)] * 4,
-        out_shape=[jax.ShapeDtypeStruct((tokens, width), BF16)] * 4,
+        out_specs=[row(2 * width)] * 2,
+        out_shape=[jax.ShapeDtypeStruct((tokens, 2 * width), BF16)] * 2,
         name="divide",
     )(place_bits(), rows)
 
@@ -168,10 +185,14 @@
     return assemble(got, norm)
 
 
-def tokens_out(rows):
+def tokens_out(divided):
     col = lax.axis_index(COL)
-    parts = divide(rows)
-    got = [parts[0]] + [swap(parts[bits], COL, bits) for bits in range(1, 4)]
+    near, far = divided
+    width = near.shape[1] // 2
+    far = side(far)
+    mine = near[:, :width]
+    near = pair(jnp.concatenate([near[:, width:], far[:, width:]], 1))
+    got = [mine, near[:, :width], far[:, :width], near[:, width:]]
     return jnp.stack(pick4(got, (col & 1) != 0, (col & 2) != 0))
 
 
@@ -180,7 +201,7 @@
     part, width = first.shape[0] // ny, first.shape[1]
     value = jnp.concatenate([first, second], 1)
     value = lax.dynamic_slice_in_dim(value, lax.axis_index("dp") * part, part, 0)
-    for bit in bits_of("row"):
+    for bit in reversed(bits_of("row")):
         value = jnp.concatenate([value, swap(value, "row", bit)], 0)
     one, two = value[:, :width], value[:, width:]
     one = jnp.concatenate([one, side(one)], 1)
@@ -190,29 +211,32 @@
     return one, jnp.concatenate([two, side(two)], 1), value
 
 
-def fold(value, axis):
-    for bit in reversed(bits_of(axis)):
+def held(value, after):
+    return value if after is None else lax.optimization_barrier((value, after))[0]
+
+
+def fold(value, axis, after=None, bits=None):
+    if bits is None:
+        bits = bits_of(axis) if axis == "row" else reversed(bits_of(axis))
+    for bit in bits:
         half = value.shape[0] // 2
-        got = swap(value[half:].astype(BF16), axis, bit)
+        got = held(swap(value[half:].astype(BF16), axis, bit), after)
         value = value[:half].astype(F32) + got.astype(F32)
     return value
 
 
-def fold_side(value):
+def fold_side(value, after=None):
     half = value.shape[1] // 2
-    got = side(value[:, half:].astype(BF16))
+    got = held(side(value[:, half:].astype(BF16)), after)
     return value[:, :half].astype(F32) + got.astype(F32)
 
 
-def reduce_first(one, two):
-    return fold_side(one), fold(two, "dp")
-
-
-def reduce_rest(one, two, after=None):
-    joined = jnp.concatenate([fold(one, "dp"), fold_side(two)], 1)
-    if after is not None:
-        joined, _ = lax.optimization_barrier((joined, after))
-    return fold(joined, "row")
+def reduce_first(one, two, after):
+    return fold_side(one, after), fold(two, "dp", after)
+
+
+def reduce_second(one, two, after=None):
+    return jnp.concatenate([fold(one, "dp", after), fold_side(two, after)], 1)
 
 
 def dot(left, right, form):
@@ -394,11 +418,12 @@
     z, y = lax.axis_index("row"), lax.axis_index("dp")
     if small_slice():
         blocks = blocks.reshape(nx, nz * ny, hidden, part)
-        kz, ky = jnp.arange(nz * ny) % nz, jnp.arange(nz * ny) // nz
+        kz, ky = jnp.array(row_places() * ny), jnp.arange(nz * ny) // nz
         tables = jnp.stack([(z ^ kz) * ny + (y ^ ky), (y ^ ky) * nz + (z ^ kz)])
         return blocks, tables.astype(jnp.int32)
     blocks = blocks.reshape(nx, nz, ny, hidden, part)
-    blocks = xor_turn(xor_turn(blocks, 1, z, nz), 2, y, ny).transpose(0, 2, 1, 3, 4)
+    blocks = reorder(xor_turn(xor_turn(blocks, 1, z, nz), 2, y, ny), 1)
+    blocks = blocks.transpose(0, 2, 1, 3, 4)
     blocks = blocks.reshape(nx, -1, HEAD // part, hidden, part).transpose(0, 1, 3, 2, 4)
     blocks = blocks.reshape(nx, -1, hidden, HEAD)
     same = jnp.arange(blocks.shape[1], dtype=jnp.int32)
@@ -413,7 +438,7 @@
         z, y = lax.axis_index("row"), lax.axis_index("dp")
         grads = grads.reshape(nx, -1, hidden, HEAD // part, part).transpose(0, 1, 3, 2, 4)
         grads = grads.reshape(nx, ny, nz, hidden, part)
-        grads = xor_turn(xor_turn(grads, 1, y, ny), 2, z, nz)
+        grads = xor_turn(xor_turn(reorder(grads, 2), 1, y, ny), 2, z, nz)
     grads = grads.reshape(-1, part)
     return lax.psum_scatter(grads, ("cx", "dp"), scatter_dimension=0, tiled=True)
 
@@ -578,8 +603,8 @@
                 out = out + dot(left[rows], right, form)
             return out
 
-        sent = pair(total(slice(tokens, None)).astype(BF16))
-        return total(slice(0, tokens)) + sent.astype(F32)
+        send = total(slice(tokens, None)).astype(BF16)
+        return total(slice(0, tokens)) + pair(send).astype(F32), send
 
     a = both(a_own)
     zq, zk, zv, zu = [dot(a, w, "td,dc->tc") for w in (wq, wk, wv, wu)]
@@ -672,8 +697,6 @@
         )
         for g, at in ((grad_out, 0), (grad_u, cut))
     ]
-    early = reduce_first(*early)
-    *early, _ = lax.optimization_barrier((*early, d_local))
     dzk, dzv = heads_of(
         last_grad_kernel,
         kinds_in="sscttpTTT",
@@ -683,18 +706,22 @@
         name="mixer_last_grad",
     )
     grad_k, grad_v = [dot(a, d, "td,tc->dc").astype(BF16) for d in (dzk, dzv)]
-    da = back_sum((dzq, dzk, dzv, dzu), (wq, wk, wv, wu), "tc,dc->td")
+    da, da_send = back_sum((dzq, dzk, dzv, dzu), (wq, wk, wv, wu), "tc,dc->td")
     x_wide = x_own.astype(F32)
     in_rows = (
         dh + r1 * da - x_wide * (r1**3 * jnp.mean(da * x_wide, 1, keepdims=True))
     ).astype(BF16)
-    input_grad = tokens_out(in_rows)
-    out_rows, _ = lax.optimization_barrier((out_rows, dzk))
-    block_out = tokens_out(out_rows)
-
-    total = reduce_rest(*early)
-    grad_k, grad_v, ff_part = lax.optimization_barrier((grad_k, grad_v, ff_part))
-    total_kv = reduce_rest(*reduce_first(grad_k, grad_v), in_rows)
+    in_rows, ff_part = lax.optimization_barrier((in_rows, ff_part))
+    divided = divide(in_rows)
+    ready = divided[1]
+    input_grad = tokens_out(divided)
+    block_out = tokens_out(divide(held(out_rows, ready)))
+
+    early = reduce_second(*reduce_first(*early, d_local), in_rows)
+    early = fold(early, "row", ready, bits_of("row")[:1])
+    total = fold(early, "row", None, bits_of("row")[1:])
+    late = reduce_second(*reduce_first(grad_k, grad_v, ready))
+    total_kv = fold(held(late, early), "row")
     total_q = jnp.concatenate([total[:, wide : wide + cut], total[:, 2 * wide + cut :]], 1)
     ff_total = lax.psum_scatter(ff_part, "row", scatter_dimension=0, tiled=True).astype(F32)
     hidden = w_down.shape[0]

time: 433 us -> 428 us (0.988)
  waiting for transfers between devices: 149 us -> 141 us
  local copies, waits for them, and re-layouts: 24.3 us -> 32.1 us
  other arithmetic: 44 us -> 50.1 us
  matrix products: 49.5 us -> 43.9 us
    ppermute x47 -> x45, waiting for transfers between devices: 123 us -> 113 us  [swap(): return lax.ppermute(value, axis, [(i, i ^ bits) for i in range(count)])]
    ppermute x47 -> x45, starting transfers between devices: 41.8 us -> 35.4 us  [swap(): return lax.ppermute(value, axis, [(i, i ^ bits) for i in range(count)])]
    dot_general x18, matrix products: 49.5 us -> 43.9 us  [dot(): return jnp.einsum(form, left, right, preferred_element_type=F32)]
    unnamed x153 -> x161, local copies, waits for them, and re-layouts: 11.3 us -> 15.2 us
  transfers between devices with their start and end apart: 57 -> 55, of which waited for: 25 -> 20; matrix products, arithmetic and copies ran while one was open for 24% -> 25% of each run, Pallas kernels for 11% -> 10%
where the time goes in v6:
time: 428 us; the launch traced here: 421 us
  waiting for transfers between devices  141 us (33%)
  Pallas kernels  89 us (21%)
  other arithmetic  50.1 us (12%)
  starting transfers between devices  49.2 us (11%)
  matrix products  43.9 us (10%)
  local copies, waits for them, and re-layouts  32.1 us (8%)
  between operations  15.2 us (4%)
    ppermute x45, waiting for transfers between devices, swap(): return lax.ppermute(value, axis, [(i, i ^ bits) for i in range(count)])  113 us
    dot_general x18, matrix products, dot(): return jnp.einsum(form, left, right, preferred_element_type=F32)  43.9 us
    pallas_call x1, Pallas kernels, feed_forward(): pl.pallas_call(ff_kernel, grid=(nx,), in_specs=[pl.BlockSpec(memory_space...  40.2 us
    ppermute x45, starting transfers between devices, swap(): return lax.ppermute(value, axis, [(i, i ^ bits) for i in range(count)])  35.4 us
    pallas_call x6, Pallas kernels, head_call(): pl.pallas_call(kernel, grid=(2,), in_specs=[specs[k.lower()] for k in kin...  32.3 us
    all_gather x1, waiting for transfers between devices, ff_gather(): blocks = lax.all_gather(shard, CHIPS, axis=0, tiled=True)  15.4 us
    unnamed x161, local copies, waits for them, and re-layouts  15.2 us
    ppermute x6, waiting for transfers between devices, chain(): entry = entry + lax.ppermute(out, 'row', [edge])  12.5 us
  transfers between devices with their start and end apart: 55, of which 20 were waited for; matrix products, arithmetic and copies ran while one was open for 25% of the time, Pallas kernels for 10%

profile of v6, /device:TPU:0, one launch (start us, length us, event | category | flops | bytes accessed | tf_op | source)
XLA Modules:
  0.0 420.8 jit_solution(16853576402741122152)
XLA Ops:
  10.8 2.5 collective-permute-start.1
  13.4 2.9 collective-permute-start.6
  16.5 3.5 collective-permute-start.4
  23.2 2.2 collective-permute-start.7
  25.4 2.6 collective-permute-done.3
  29.7 3.8 assemble.2
  33.5 9.2 %collective-permute-done.7 = bf16[256,512]{1,0:T(8,128)(2,1)S(1)} collective-permute-done((bf16[256,512]{1,0:T(8,128)(2,1)S(1)}, bf16[256,512]{1,0:T(8,128)(2,1)S(1)}, u32[]{:S(2)}, u32[]{:S(2)}) %collective-permute-start.7) | collective-permute-done | bytes 262176 | tf_op jit(solution)/shard_map/ppermute | solution.py:23
  47.7 4.3 %collective-permute-done.8 = bf16[128,512]{1,0:T(8,128)(2,1)S(1)} collective-permute-done((bf16[128,512]{1,0:T(8,128)(2,1)S(1)}, bf16[128,512]{1,0:T(8,128)(2,1)S(1)}, u32[]{:S(2)}, u32[]{:S(2)}) %collective-permute-start.8) | collective-permute-done | bytes 131104 | tf_op jit(solution)/shard_map/ppermute | solution.py:23
  53.9 4.5 %collective-permute-done.14 = bf16[512,256]{1,0:T(8,128)(2,1)S(1)} collective-permute-done((bf16[512,256]{1,0:T(8,128)(2,1)S(1)}, bf16[512,256]{1,0:T(8,128)(2,1)S(1)}, u32[]{:S(2)}, u32[]{:S(2)}) %collective-permute-start.14) | collective-permute-done | bytes 262176 | tf_op jit(solution)/shard_map/ppermute | solution.py:23
  58.5 13.9 %collective-permute-done.9 = bf16[256,512]{1,0:T(8,128)(2,1)S(1)} collective-permute-done((bf16[256,512]{1,0:T(8,128)(2,1)S(1)}, bf16[256,512]{1,0:T(8,128)(2,1)S(1)}, u32[]{:S(2)}, u32[]{:S(2)}) %collective-permute-start.9) | collective-permute-done | bytes 262176 | tf_op jit(solution)/shard_map/ppermute | solution.py:23
  73.3 2.6 fusion.51.zk
  78.6 3.8 collective-permute-done.15
  82.3 2.7 fusion.50.zv
  85.0 4.1 mixer_local.1
  90.3 5.0 %collective-permute-start.16 = (bf16[2,4,128,128]{3,2,1,0:T(8,128)(2,1)S(1)}, bf16[2,4,128,128]{3,2,1,0:T(8,128)(2,1)S(1)}, u32[]{:S(2)}, u32[]{:S(2)}) collective-permute-start(bf16[2,4,128,128]{3,2,1,0:T(8,128)(2,1)S(1)} %add_convert_fusion.7), channel_id=1, source_target_pairs={{0,8},{1,9},{2,10},{3,11},{4,12},{5,13},{6,14},{7,15}} | collective-permute-start | bytes 786440 | tf_op jit(solution)/shard_map/ppermute | solution.py:403
  101.2 3.5 assemble.3.g0
  105.8 5.3 %collective-permute-done.24 = bf16[512,256]{1,0:T(8,128)(2,1)S(1)} collective-permute-done((bf16[512,256]{1,0:T(8,128)(2,1)S(1)}, bf16[512,256]{1,0:T(8,128)(2,1)S(1)}, u32[]{:S(2)}, u32[]{:S(2)}) %collective-permute-start.24) | collective-permute-done | bytes 262176 | tf_op jit(solution)/shard_map/ppermute | solution.py:23
  114.7 15.1 %collective-permute-done.11 = bf16[512,512]{1,0:T(8,128)(2,1)} collective-permute-done((bf16[512,512]{1,0:T(8,128)(2,1)}, bf16[512,512]{1,0:T(8,128)(2,1)}, u32[]{:S(2)}, u32[]{:S(2)}) %collective-permute-start.11) | collective-permute-done | bytes 524320 | tf_op jit(solution)/shard_map/ppermute | solution.py:23
  129.7 3.7 fusion.52.zq
  133.4 5.6 %mixer_inner.1 = (bf16[1024,512]{1,0:T(8,128)(2,1)}, f32[1024,512]{1,0:T(8,128)}) custom-call(f32[4]{0:T(128)} %get-tuple-element.129.rates, f32[2,2]{1,0:T(2,128)} %pad_maximum_fusion.23.marks, f32[2,512,1]{2,1,0:T(8,128)} %copy.39.seg_c, f32[2,1,512]{2,1,0:T(1,128)} %copy.38.seg_r, f32[1024,512]{1,0:T(8,128)} %fusion.52.zq, ...), custom_call_target="tpu_custom_call" | custom-call | flops 536870912 | bytes 8388608 | tf_op jit(solution)/shard_map/mixer_inner/pallas_call | solution.py:386
  139.8 3.6 mixer_carry.1
  146.0 5.7 %multiply_convert_fusion.2 = (bf16[1024,512]{1,0:T(8,128)(2,1)}, f32[1024,512]{1,0:T(8,128)}) fusion(f32[1024,512]{1,0:T(8,128)} %get-tuple-element.65, f32[1024]{0:T(1024)S(1)} %bitcast.96, bf16[1024,1024]{1,0:T(8,128)(2,1)} %copy-done.42, bf16[1024,256]{1,0:T(8,128)(2,1)S(1)} %collective-permute-done.25, ...), kind=kOutput, calls=%fused_computation.19 | convolution fusion | flops 1080033280 | bytes 8392704 | tf_op jit(solution)/shard_map/td,dc->tc/dot_general | solution.py:243
  151.7 15.4 %all-gather.2.cloned.1.call-done = bf16[37888,128]{1,0:T(8,128)(2,1)} async-done(((bf16[2368,128]{1,0:T(8,128)(2,1)}), bf16[37888,128]{1,0:T(8,128)(2,1)}) %all-gather.2.cloned.1.call-update) | async-done | bytes 9699344 | tf_op jit(solution)/shard_map/all_gather | solution.py:416
  167.2 4.8 %project_out.1 = (f32[512,1024]{1,0:T(8,128)}, bf16[512,1024]{1,0:T(8,128)(2,1)}, bf16[512,1024]{1,0:T(8,128)(2,1)}) custom-call(s32[2,8]{1,0:T(2,128)} %pad_add_fusion.tables, s32[1]{0:T(128)} %bitcast.9.side_of, bf16[1024,512]{1,0:T(8,128)(2,1)} %get-tuple-element.180.y_ref, bf16[2,8,2368,128]{3,2,1,0:T(8,128)(2,1)} %bitcast.90), custom_call_target="tpu_custom_call" | custom-call | flops 1073741824 | bytes 6291456 | tf_op jit(solution)/shard_map/project_out/pallas_call | solution.py:466
  172.0 2.9 collective-permute-done.26
  178.3 2.7 collective-permute-done.27.b1
  180.9 40.2 %feed_forward.1 = (f32[512,1024]{1,0:T(8,128)}, bf16[512,1024]{1,0:T(8,128)(2,1)}, f32[512,1024]{1,0:T(8,128)}, bf16[512,1024]{1,0:T(8,128)(2,1)}, bf16[2,8,2112,128]{3,2,1,0:T(8,128)(2,1)}) custom-call(s32[2,8]{1,0:T(2,128)} %pad_add_fusion.tables, bf16[512,1024]{1,0:T(8,128)(2,1)} %copy-done.30, bf16[512,1024]{1,0:T(8,128)(2,1)} %collective-permute-done.27.b1, ...), custom_call_target="tpu_custom_call" | custom-call | flops 26575110144 | bytes 37748736 | tf_op jit(solution)/shard_map/feed_forward/pallas_call | solution.py:534
  221.8 2.4 collective-permute-done.29
  228.0 2.9 fusion.54
  231.0 2.7 collective-permute-done.30
  233.7 5.9 %multiply_reduce_fusion = (f32[1024]{0:T(1024)S(1)}, f32[1024,512]{1,0:T(8,128)}) fusion(f32[1024,512]{1,0:T(8,128)} %get-tuple-element.65, f32[1024,512]{1,0:T(8,128)} %get-tuple-element.181, bf16[512,1024]{1,0:T(8,128)(2,1)} %get-tuple-element.74, bf16[512,1024]{1,0:T(8,128)(2,1)S(1)} %collective-permute-done.30, bf16[512,1024]{1,0:T(8,128)(2,1)} %get-tuple-element.122), kind=kOutput, calls=%fused_computation.12 | convolution fusion | flops 1079507968 | bytes 9441280 | tf_op jit(solution)/shard_map/td,cd->tc/dot_general | solution.py:243
  239.7 2.5 convolution_convert_fusion.4
  244.2 3.7 multiply_convert_fusion
  247.9 3.3 mixer_entry_grad.1
  254.5 10.2 %mixer_inner_grad.1 = (bf16[1024,512]{1,0:T(8,128)(2,1)}, f32[1024,512]{1,0:T(8,128)}, f32[1024,512]{1,0:T(8,128)}) custom-call(f32[4]{0:T(128)} %get-tuple-element.129.rates, f32[2,2]{1,0:T(2,128)} %pad_maximum_fusion.23.marks, f32[2,512,1]{2,1,0:T(8,128)} %copy.39.seg_c, f32[2,1,512]{2,1,0:T(1,128)} %copy.38.seg_r, ...), custom_call_target="tpu_custom_call" | custom-call | flops 1342177280 | bytes 8388608 | tf_op jit(solution)/shard_map/mixer_inner_grad/pallas_call | solution.py:386
  264.6 3.1 convolution_convert_fusion.3
  274.2 3.1 fusion.27
  283.7 3.2 fusion.21
  286.9 12.5 %collective-permute-done.34 = bf16[2,4,128,128]{3,2,1,0:T(8,128)(2,1)S(1)} collective-permute-done((bf16[2,4,128,128]{3,2,1,0:T(8,128)(2,1)S(1)}, bf16[2,4,128,128]{3,2,1,0:T(8,128)(2,1)S(1)}, u32[]{:S(2)}, u32[]{:S(2)}) %collective-permute-start.34) | collective-permute-done | bytes 262176 | tf_op jit(solution)/shard_map/ppermute | solution.py:403
  300.2 5.6 %mixer_last_grad.1 = (bf16[1024,512]{1,0:T(8,128)(2,1)}, bf16[1024,512]{1,0:T(8,128)(2,1)}) custom-call(f32[4]{0:T(128)} %get-tuple-element.129.rates, f32[2,2]{1,0:T(2,128)} %pad_maximum_fusion.23.marks, f32[2,512,1]{2,1,0:T(8,128)} %copy.39.seg_c, bf16[1024,512]{1,0:T(8,128)(2,1)} %get-tuple-element.58.k_ref.k, ...), custom_call_target="tpu_custom_call" | custom-call | flops 134217728 | bytes 8388608 | tf_op jit(solution)/shard_map/mixer_last_grad/pallas_call | solution.py:386
  305.8 2.4 fusion.19
  333.6 3.0 fusion.3.rows_ref
  336.6 2.2 divide.2
  347.9 2.2 divide.3
  353.3 6.2 %collective-permute-done.49 = bf16[512,256]{0,1:T(8,128)(2,1)} collective-permute-done((bf16[512,256]{0,1:T(8,128)(2,1)}, bf16[512,256]{0,1:T(8,128)(2,1)}, u32[]{:S(2)}, u32[]{:S(2)}) %collective-permute-start.49) | collective-permute-done | bytes 262176 | tf_op jit(solution)/shard_map/ppermute | solution.py:23
  360.7 15.7 %collective-permute-done.44 = bf16[256,768]{0,1:T(8,128)(2,1)} collective-permute-done((bf16[256,768]{0,1:T(8,128)(2,1)}, bf16[256,768]{0,1:T(8,128)(2,1)}, u32[]{:S(2)}, u32[]{:S(2)}) %collective-permute-start.44) | collective-permute-done | bytes 393248 | tf_op jit(solution)/shard_map/ppermute | solution.py:23
  379.5 16.3 %collective-permute-done.45 = bf16[128,768]{0,1:T(8,128)(2,1)S(1)} collective-permute-done((bf16[128,768]{0,1:T(8,128)(2,1)S(1)}, bf16[128,768]{0,1:T(8,128)(2,1)S(1)}, u32[]{:S(2)}, u32[]{:S(2)}) %collective-permute-start.45) | collective-permute-done | bytes 196640 | tf_op jit(solution)/shard_map/ppermute | solution.py:23
  402.2 4.0 collective-permute-done.51
  (360 shorter events, 116.8 us)
Async XLA Ops:
  7.2 160.0 %all-gather.2.cloned.1.call-start = ((), (), s32[]{:S(2)}) async-start(), calls=%async_computation.2 | async-start | bytes 10305536 | tf_op jit(solution)/shard_map/all_gather | solution.py:416
  9.4 327.3 %reduce-scatter.3.cloned.1.call-start = ((), (), s32[]{:S(2)}) async-start(), calls=%async_computation.3 | async-start | bytes 10813440 | tf_op jit(solution)/shard_map/reduce_scatter | solution.py:443
  10.3 18.6 %collective-permute-start = (bf16[512,256]{1,0:T(8,128)(2,1)S(1)}, bf16[512,256]{1,0:T(8,128)(2,1)S(1)}, u32[]{:S(2)}, u32[]{:S(2)}) collective-permute-start(bf16[512,256]{1,0:T(8,128)(2,1)S(1)} %get-tuple-element.158), channel_id=1, source_target_pairs={{0,2},{2,0},{4,6},{6,4},{1,3},{3,1},{5,7},{7,5},{8,10},{10,8},{12,... | collective-permute-start | bytes 786440 | tf_op jit(solution)/shard_map/ppermute | solution.py:23
  10.8 18.1 %collective-permute-start.1 = (bf16[512,256]{1,0:T(8,128)(2,1)S(1)}, bf16[512,256]{1,0:T(8,128)(2,1)S(1)}, u32[]{:S(2)}, u32[]{:S(2)}) collective-permute-start(bf16[512,256]{1,0:T(8,128)(2,1)S(1)} %get-tuple-element.160), channel_id=1, source_target_pairs={{0,4},{2,6},{4,0},{6,2},{1,5},{3,7},{5,1},{7,3},{8,12},{10,14},{12... | collective-permute-start | bytes 786440 | tf_op jit(solution)/shard_map/ppermute | solution.py:23
  13.2 15.6 %collective-permute-start.2 = (bf16[512,256]{1,0:T(8,128)(2,1)S(1)}, bf16[512,256]{1,0:T(8,128)(2,1)S(1)}, u32[]{:S(2)}, u32[]{:S(2)}) collective-permute-start(bf16[512,256]{1,0:T(8,128)(2,1)S(1)} %get-tuple-element.157), channel_id=1, source_target_pairs={{0,6},{2,4},{4,2},{6,0},{1,7},{3,5},{5,3},{7,1},{8,14},{10,12},{12... | collective-permute-start | bytes 786440 | tf_op jit(solution)/shard_map/ppermute | solution.py:23
  13.4 9.8 %collective-permute-start.6 = (bf16[128,512]{1,0:T(8,128)(2,1)S(1)}, bf16[128,512]{1,0:T(8,128)(2,1)S(1)}, u32[]{:S(2)}, u32[]{:S(2)}) collective-permute-start(bf16[128,512]{1,0:T(8,128)(2,1)S(1)} %fusion.32), channel_id=1, source_target_pairs={{0,16},{8,24},{16,0},{24,8},{1,17},{9,25},{17,1},{25,9},{2,18},{10... | collective-permute-start | bytes 393224 | tf_op jit(solution)/shard_map/ppermute | solution.py:23
  16.5 5.1 %collective-permute-start.4 = (f32[2]{0:T(128)S(1)}, f32[2]{0:T(128)S(1)}, u32[]{:S(2)}, u32[]{:S(2)}) collective-permute-start(f32[2]{0:T(128)S(1)} %get-tuple-element.130), channel_id=1, source_target_pairs={{0,8},{8,16},{16,24},{1,9},{9,17},{17,25},{2,10},{10,18},{18,26},{... | collective-permute-start | bytes 32 | tf_op jit(solution)/shard_map/ppermute | solution.py:587
  21.7 6.4 %collective-permute-start.3 = (f32[2]{0:T(128)S(1)}, f32[2]{0:T(128)S(1)}, u32[]{:S(2)}, u32[]{:S(2)}) collective-permute-start(f32[2]{0:T(128)S(1)} %copy-done.69), channel_id=1, source_target_pairs={{0,4},{2,6},{4,0},{6,2},{1,5},{3,7},{5,1},{7,3},{8,12},{10,14},{12... | collective-permute-start | bytes 32 | tf_op jit(solution)/shard_map/ppermute | solution.py:23
  23.2 19.5 %collective-permute-start.7 = (bf16[256,512]{1,0:T(8,128)(2,1)S(1)}, bf16[256,512]{1,0:T(8,128)(2,1)S(1)}, u32[]{:S(2)}, u32[]{:S(2)}) collective-permute-start(bf16[256,512]{1,0:T(8,128)(2,1)S(1)} %pad_maximum_fusion.19), channel_id=1, source_target_pairs={{0,8},{8,0},{16,24},{24,16},{1,9},{9,1},{17,25},{25,17},{2,10},{10... | collective-permute-start | bytes 786440 | tf_op jit(solution)/shard_map/ppermute | solution.py:23
  33.5 39.7 %collective-permute-start.5 = (bf16[512,1024]{1,0:T(8,128)(2,1)}, bf16[512,1024]{1,0:T(8,128)(2,1)S(1)}, u32[]{:S(2)}, u32[]{:S(2)}) collective-permute-start(bf16[512,1024]{1,0:T(8,128)(2,1)} %get-tuple-element.54), channel_id=1, source_target_pairs={{0,2},{2,0},{4,6},{6,4},{1,3},{3,1},{5,7},{7,5},{8,10},{10,8},{12,... | collective-permute-start | bytes 3145736 | tf_op jit(solution)/shard_map/ppermute | solution.py:23
  42.8 9.2 %collective-permute-start.8 = (bf16[128,512]{1,0:T(8,128)(2,1)S(1)}, bf16[128,512]{1,0:T(8,128)(2,1)S(1)}, u32[]{:S(2)}, u32[]{:S(2)}) collective-permute-start(bf16[128,512]{1,0:T(8,128)(2,1)S(1)} %fusion.31), channel_id=1, source_target_pairs={{0,16},{8,24},{16,0},{24,8},{1,17},{9,25},{17,1},{25,9},{2,18},{10... | collective-permute-start | bytes 393224 | tf_op jit(solution)/shard_map/ppermute | solution.py:23
  44.3 7.8 %collective-permute-start.12 = (bf16[512,256]{1,0:T(8,128)(2,1)S(1)}, bf16[512,256]{1,0:T(8,128)(2,1)S(1)}, u32[]{:S(2)}, u32[]{:S(2)}) collective-permute-start(bf16[512,256]{1,0:T(8,128)(2,1)S(1)} %get-tuple-element.162), channel_id=1, source_target_pairs={{0,4},{2,6},{4,0},{6,2},{1,5},{3,7},{5,1},{7,3},{8,12},{10,14},{12... | collective-permute-start | bytes 786440 | tf_op jit(solution)/shard_map/ppermute | solution.py:23
  46.2 12.1 %collective-permute-start.14 = (bf16[512,256]{1,0:T(8,128)(2,1)S(1)}, bf16[512,256]{1,0:T(8,128)(2,1)S(1)}, u32[]{:S(2)}, u32[]{:S(2)}) collective-permute-start(bf16[512,256]{1,0:T(8,128)(2,1)S(1)} %get-tuple-element.161), channel_id=1, source_target_pairs={{0,1},{1,0},{2,3},{3,2},{4,5},{5,4},{6,7},{7,6},{8,9},{9,8},{10,11... | collective-permute-start | bytes 786440 | tf_op jit(solution)/shard_map/ppermute | solution.py:23
  52.0 20.3 %collective-permute-start.9 = (bf16[256,512]{1,0:T(8,128)(2,1)S(1)}, bf16[256,512]{1,0:T(8,128)(2,1)S(1)}, u32[]{:S(2)}, u32[]{:S(2)}) collective-permute-start(bf16[256,512]{1,0:T(8,128)(2,1)S(1)} %pad_maximum_fusion.20), channel_id=1, source_target_pairs={{0,8},{8,0},{16,24},{24,16},{1,9},{9,1},{17,25},{25,17},{2,10},{10... | collective-permute-start | bytes 786440 | tf_op jit(solution)/shard_map/ppermute | solution.py:23
  52.3 21.0 %collective-permute-start.13 = (bf16[512,512]{1,0:T(8,128)(2,1)S(1)}, bf16[512,512]{1,0:T(8,128)(2,1)S(1)}, u32[]{:S(2)}, u32[]{:S(2)}) collective-permute-start(bf16[512,512]{1,0:T(8,128)(2,1)S(1)} %pad_maximum_fusion.14), channel_id=1, source_target_pairs={{0,1},{1,0},{2,3},{3,2},{4,5},{5,4},{6,7},{7,6},{8,9},{9,8},{10,11... | collective-permute-start | bytes 1572872 | tf_op jit(solution)/shard_map/ppermute | solution.py:23
  58.4 23.9 %collective-permute-start.15 = (bf16[1024,256]{1,0:T(8,128)(2,1)S(1)}, bf16[1024,256]{1,0:T(8,128)(2,1)S(1)}, u32[]{:S(2)}, u32[]{:S(2)}) collective-permute-start(bf16[1024,256]{1,0:T(8,128)(2,1)S(1)} %pad_maximum_fusion.15), channel_id=1, source_target_pairs={{0,4},{2,6},{4,0},{6,2},{1,5},{3,7},{5,1},{7,3},{8,12},{10,14},{12... | collective-permute-start | bytes 1572872 | tf_op jit(solution)/shard_map/ppermute | solution.py:23
  72.5 23.4 %collective-permute-start.10 = (bf16[512,256]{1,0:T(8,128)(2,1)S(1)}, bf16[512,256]{1,0:T(8,128)(2,1)S(1)}, u32[]{:S(2)}, u32[]{:S(2)}) collective-permute-start(bf16[512,256]{1,0:T(8,128)(2,1)S(1)} %get-tuple-element.163), channel_id=1, source_target_pairs={{0,4},{2,6},{4,0},{6,2},{1,5},{3,7},{5,1},{7,3},{8,12},{10,14},{12... | collective-permute-start | bytes 786440 | tf_op jit(solution)/shard_map/ppermute | solution.py:23
  76.7 23.2 %collective-permute-start.19 = (bf16[512,256]{1,0:T(8,128)(2,1)}, bf16[512,256]{1,0:T(8,128)(2,1)S(1)}, u32[]{:S(2)}, u32[]{:S(2)}) collective-permute-start(bf16[512,256]{1,0:T(8,128)(2,1)} %get-tuple-element.155), channel_id=1, source_target_pairs={{0,2},{2,0},{4,6},{6,4},{1,3},{3,1},{5,7},{7,5},{8,10},{10,8},{12,... | collective-permute-start | bytes 786440 | tf_op jit(solution)/shard_map/ppermute | solution.py:23
  76.7 23.7 %collective-permute-start.20 = (bf16[512,256]{1,0:T(8,128)(2,1)S(1)}, bf16[512,256]{1,0:T(8,128)(2,1)S(1)}, u32[]{:S(2)}, u32[]{:S(2)}) collective-permute-start(bf16[512,256]{1,0:T(8,128)(2,1)S(1)} %get-tuple-element.154), channel_id=1, source_target_pairs={{0,4},{2,6},{4,0},{6,2},{1,5},{3,7},{5,1},{7,3},{8,12},{10,14},{12... | collective-permute-start | bytes 786440 | tf_op jit(solution)/shard_map/ppermute | solution.py:23
  78.1 22.3 %collective-permute-start.21 = (bf16[512,256]{1,0:T(8,128)(2,1)S(1)}, bf16[512,256]{1,0:T(8,128)(2,1)S(1)}, u32[]{:S(2)}, u32[]{:S(2)}) collective-permute-start(bf16[512,256]{1,0:T(8,128)(2,1)S(1)} %get-tuple-element.153), channel_id=1, source_target_pairs={{0,6},{2,4},{4,2},{6,0},{1,7},{3,5},{5,3},{7,1},{8,14},{10,12},{12... | collective-permute-start | bytes 786440 | tf_op jit(solution)/shard_map/ppermute | solution.py:23
  90.3 14.5 %collective-permute-start.16 = (bf16[2,4,128,128]{3,2,1,0:T(8,128)(2,1)S(1)}, bf16[2,4,128,128]{3,2,1,0:T(8,128)(2,1)S(1)}, u32[]{:S(2)}, u32[]{:S(2)}) collective-permute-start(bf16[2,4,128,128]{3,2,1,0:T(8,128)(2,1)S(1)} %add_convert_fusion.7), channel_id=1, source_target_pairs={{0,8},{1,9},{2,10},{3,11},{4,12},{5,13},{6,14},{7,15}} | collective-permute-start | bytes 786440 | tf_op jit(solution)/shard_map/ppermute | solution.py:403
  96.6 14.5 %collective-permute-start.24 = (bf16[512,256]{1,0:T(8,128)(2,1)S(1)}, bf16[512,256]{1,0:T(8,128)(2,1)S(1)}, u32[]{:S(2)}, u32[]{:S(2)}) collective-permute-start(bf16[512,256]{1,0:T(8,128)(2,1)S(1)} %get-tuple-element.164), channel_id=1, source_target_pairs={{0,1},{1,0},{2,3},{3,2},{4,5},{5,4},{6,7},{7,6},{8,9},{9,8},{10,11... | collective-permute-start | bytes 786440 | tf_op jit(solution)/shard_map/ppermute | solution.py:23
  99.9 29.8 %collective-permute-start.11 = (bf16[512,512]{1,0:T(8,128)(2,1)}, bf16[512,512]{1,0:T(8,128)(2,1)}, u32[]{:S(2)}, u32[]{:S(2)}) collective-permute-start(bf16[512,512]{1,0:T(8,128)(2,1)} %pad_maximum_fusion.13), channel_id=1, source_target_pairs={{0,1},{1,0},{2,3},{3,2},{4,5},{5,4},{6,7},{7,6},{8,9},{9,8},{10,11... | collective-permute-start | bytes 1572872 | tf_op jit(solution)/shard_map/ppermute | solution.py:23
  104.7 35.1 %collective-permute-start.22 = (bf16[512,1024]{1,0:T(8,128)(2,1)}, bf16[512,1024]{1,0:T(8,128)(2,1)}, u32[]{:S(2)}, u32[]{:S(2)}) collective-permute-start(bf16[512,1024]{1,0:T(8,128)(2,1)} %assemble.3.g0), channel_id=1, source_target_pairs={{0,2},{2,0},{4,6},{6,4},{1,3},{3,1},{5,7},{7,5},{8,10},{10,8},{12,... | collective-permute-start | bytes 3145736 | tf_op jit(solution)/shard_map/ppermute | solution.py:23
  104.9 7.8 %collective-permute-start.17 = (bf16[2,4,128,128]{3,2,1,0:T(8,128)(2,1)S(1)}, bf16[2,4,128,128]{3,2,1,0:T(8,128)(2,1)S(1)}, u32[]{:S(2)}, u32[]{:S(2)}) collective-permute-start(bf16[2,4,128,128]{3,2,1,0:T(8,128)(2,1)S(1)} %add_convert_fusion.6), channel_id=1, source_target_pairs={{8,16},{9,17},{10,18},{11,19},{12,20},{13,21},{14,22},{15,23}} | collective-permute-start | bytes 786440 | tf_op jit(solution)/shard_map/ppermute | solution.py:403
  111.1 34.9 %collective-permute-start.25 = (bf16[1024,256]{1,0:T(8,128)(2,1)S(1)}, bf16[1024,256]{1,0:T(8,128)(2,1)S(1)}, u32[]{:S(2)}, u32[]{:S(2)}) collective-permute-start(bf16[1024,256]{1,0:T(8,128)(2,1)S(1)} %pad_maximum_fusion.16), channel_id=1, source_target_pairs={{0,4},{2,6},{4,0},{6,2},{1,5},{3,7},{5,1},{7,3},{8,12},{10,14},{12... | collective-permute-start | bytes 1572872 | tf_op jit(solution)/shard_map/ppermute | solution.py:23
  113.5 25.5 %collective-permute-start.18 = (bf16[2,4,128,128]{3,2,1,0:T(8,128)(2,1)}, bf16[2,4,128,128]{3,2,1,0:T(8,128)(2,1)S(1)}, u32[]{:S(2)}, u32[]{:S(2)}) collective-permute-start(bf16[2,4,128,128]{3,2,1,0:T(8,128)(2,1)} %get-tuple-element.126), channel_id=1, source_target_pairs={{16,24},{17,25},{18,26},{19,27},{20,28},{21,29},{22,30},{23,31}} | collective-permute-start | bytes 786440 | tf_op jit(solution)/shard_map/ppermute | solution.py:403
  221.1 190.1 %reduce-scatter.5.cloned.1.call-start = ((), (), s32[]{:S(2)}) async-start(), calls=%async_computation.4 | async-start | bytes 2703360 | tf_op jit(solution)/shard_map/reduce_scatter | solution.py:726
  221.4 4.9 %collective-permute-start.28 = (bf16[512,1024]{1,0:T(8,128)(2,1)}, bf16[512,1024]{1,0:T(8,128)(2,1)S(1)}, u32[]{:S(2)}, u32[]{:S(2)}) collective-permute-start(bf16[512,1024]{1,0:T(8,128)(2,1)} %get-tuple-element.70), channel_id=1, source_target_pairs={{0,2},{2,0},{4,6},{6,4},{1,3},{3,1},{5,7},{7,5},{8,10},{10,8},{12,... | collective-permute-start | bytes 3145736 | tf_op jit(solution)/shard_map/ppermute | solution.py:23
  253.1 24.3 %collective-permute-start.32 = (bf16[2,4,128,128]{3,2,1,0:T(8,128)(2,1)}, bf16[2,4,128,128]{3,2,1,0:T(8,128)(2,1)}, u32[]{:S(2)}, u32[]{:S(2)}) collective-permute-start(bf16[2,4,128,128]{3,2,1,0:T(8,128)(2,1)} %add_convert_fusion.4), channel_id=1, source_target_pairs={{24,16},{25,17},{26,18},{27,19},{28,20},{29,21},{30,22},{31,23}} | collective-permute-start | bytes 786440 | tf_op jit(solution)/shard_map/ppermute | solution.py:403
  269.8 49.5 %collective-permute-start.40 = (bf16[1024,384]{0,1:T(8,128)(2,1)}, bf16[1024,384]{0,1:T(8,128)(2,1)}, u32[]{:S(2)}, u32[]{:S(2)}) collective-permute-start(bf16[1024,384]{0,1:T(8,128)(2,1)} %pad_maximum_fusion.10), channel_id=1, source_target_pairs={{0,4},{2,6},{4,0},{6,2},{1,5},{3,7},{5,1},{7,3},{8,12},{10,14},{12... | collective-permute-start | bytes 2359304 | tf_op jit(solution)/shard_map/ppermute | solution.py:23
  272.8 49.4 %collective-permute-start.42 = (bf16[512,768]{0,1:T(8,128)(2,1)}, bf16[512,768]{0,1:T(8,128)(2,1)}, u32[]{:S(2)}, u32[]{:S(2)}) collective-permute-start(bf16[512,768]{0,1:T(8,128)(2,1)} %slice.301), channel_id=1, source_target_pairs={{0,1},{1,0},{2,3},{3,2},{4,5},{5,4},{6,7},{7,6},{8,9},{9,8},{10,11... | collective-permute-start | bytes 2359304 | tf_op jit(solution)/shard_map/ppermute | solution.py:23
  282.4 16.9 %collective-permute-start.34 = (bf16[2,4,128,128]{3,2,1,0:T(8,128)(2,1)S(1)}, bf16[2,4,128,128]{3,2,1,0:T(8,128)(2,1)S(1)}, u32[]{:S(2)}, u32[]{:S(2)}) collective-permute-start(bf16[2,4,128,128]{3,2,1,0:T(8,128)(2,1)S(1)} %get-tuple-element.120), channel_id=1, source_target_pairs={{8,0},{9,1},{10,2},{11,3},{12,4},{13,5},{14,6},{15,7}} | collective-permute-start | bytes 786440 | tf_op jit(solution)/shard_map/ppermute | solution.py:403
  313.6 15.3 %collective-permute-start.35 = (bf16[512,1024]{1,0:T(8,128)(2,1)S(1)}, bf16[512,1024]{1,0:T(8,128)(2,1)S(1)}, u32[]{:S(2)}, u32[]{:S(2)}) collective-permute-start(bf16[512,1024]{1,0:T(8,128)(2,1)S(1)} %add_convert_fusion), channel_id=1, source_target_pairs={{0,2},{2,0},{4,6},{6,4},{1,3},{3,1},{5,7},{7,5},{8,10},{10,8},{12,... | collective-permute-start | bytes 3145736 | tf_op jit(solution)/shard_map/ppermute | solution.py:23
  315.4 23.8 %collective-permute-start.46 = (bf16[1024,256]{0,1:T(8,128)(2,1)}, bf16[1024,256]{0,1:T(8,128)(2,1)}, u32[]{:S(2)}, u32[]{:S(2)}) collective-permute-start(bf16[1024,256]{0,1:T(8,128)(2,1)} %slice.311), channel_id=1, source_target_pairs={{0,4},{2,6},{4,0},{6,2},{1,5},{3,7},{5,1},{7,3},{8,12},{10,14},{12... | collective-permute-start | bytes 1572872 | tf_op jit(solution)/shard_map/ppermute | solution.py:23
  317.9 24.9 %collective-permute-start.48 = (bf16[512,512]{0,1:T(8,128)(2,1)}, bf16[512,512]{0,1:T(8,128)(2,1)}, u32[]{:S(2)}, u32[]{:S(2)}) collective-permute-start(bf16[512,512]{0,1:T(8,128)(2,1)} %slice.315), channel_id=1, source_target_pairs={{0,1},{1,0},{2,3},{3,2},{4,5},{5,4},{6,7},{7,6},{8,9},{9,8},{10,11... | collective-permute-start | bytes 1572872 | tf_op jit(solution)/shard_map/ppermute | solution.py:23
  321.6 24.0 %collective-permute-start.41 = (bf16[512,384]{0,1:T(8,128)(2,1)}, bf16[512,384]{0,1:T(8,128)(2,1)}, u32[]{:S(2)}, u32[]{:S(2)}) collective-permute-start(bf16[512,384]{0,1:T(8,128)(2,1)} %slice.471), channel_id=1, source_target_pairs={{0,1},{1,0},{2,3},{3,2},{4,5},{5,4},{6,7},{7,6},{8,9},{9,8},{10,11... | collective-permute-start | bytes 1179656 | tf_op jit(solution)/shard_map/ppermute | solution.py:23
  325.6 19.9 %collective-permute-start.43 = (bf16[512,384]{0,1:T(8,128)(2,1)}, bf16[512,384]{0,1:T(8,128)(2,1)}, u32[]{:S(2)}, u32[]{:S(2)}) collective-permute-start(bf16[512,384]{0,1:T(8,128)(2,1)} %slice.470), channel_id=1, source_target_pairs={{0,4},{2,6},{4,0},{6,2},{1,5},{3,7},{5,1},{7,3},{8,12},{10,14},{12... | collective-permute-start | bytes 1179656 | tf_op jit(solution)/shard_map/ppermute | solution.py:23
  338.8 38.9 %collective-permute-start.38 = (bf16[512,512]{1,0:T(8,128)(2,1)}, bf16[512,512]{1,0:T(8,128)(2,1)}, u32[]{:S(2)}, u32[]{:S(2)}) collective-permute-start(bf16[512,512]{1,0:T(8,128)(2,1)} %get-tuple-element.82), channel_id=1, source_target_pairs={{0,4},{2,6},{4,0},{6,2},{1,5},{3,7},{5,1},{7,3},{8,12},{10,14},{12... | collective-permute-start | bytes 1572872 | tf_op jit(solution)/shard_map/ppermute | solution.py:23
  341.5 10.8 %collective-permute-start.47 = (bf16[512,256]{0,1:T(8,128)(2,1)}, bf16[512,256]{0,1:T(8,128)(2,1)}, u32[]{:S(2)}, u32[]{:S(2)}) collective-permute-start(bf16[512,256]{0,1:T(8,128)(2,1)} %slice.474), channel_id=1, source_target_pairs={{0,1},{1,0},{2,3},{3,2},{4,5},{5,4},{6,7},{7,6},{8,9},{9,8},{10,11... | collective-permute-start | bytes 786440 | tf_op jit(solution)/shard_map/ppermute | solution.py:23
  344.9 14.7 %collective-permute-start.49 = (bf16[512,256]{0,1:T(8,128)(2,1)}, bf16[512,256]{0,1:T(8,128)(2,1)}, u32[]{:S(2)}, u32[]{:S(2)}) collective-permute-start(bf16[512,256]{0,1:T(8,128)(2,1)} %slice.473), channel_id=1, source_target_pairs={{0,4},{2,6},{4,0},{6,2},{1,5},{3,7},{5,1},{7,3},{8,12},{10,14},{12... | collective-permute-start | bytes 786440 | tf_op jit(solution)/shard_map/ppermute | solution.py:23
  347.8 28.6 %collective-permute-start.44 = (bf16[256,768]{0,1:T(8,128)(2,1)}, bf16[256,768]{0,1:T(8,128)(2,1)}, u32[]{:S(2)}, u32[]{:S(2)}) collective-permute-start(bf16[256,768]{0,1:T(8,128)(2,1)} %fusion.7), channel_id=1, source_target_pairs={{0,8},{8,0},{16,24},{24,16},{1,9},{9,1},{17,25},{25,17},{2,10},{10... | collective-permute-start | bytes 1179656 | tf_op jit(solution)/shard_map/ppermute | solution.py:23
  350.1 28.8 %collective-permute-start.36 = (bf16[512,512]{1,0:T(8,128)(2,1)}, bf16[512,512]{1,0:T(8,128)(2,1)S(1)}, u32[]{:S(2)}, u32[]{:S(2)}) collective-permute-start(bf16[512,512]{1,0:T(8,128)(2,1)} %get-tuple-element.85), channel_id=1, source_target_pairs={{0,4},{2,6},{4,0},{6,2},{1,5},{3,7},{5,1},{7,3},{8,12},{10,14},{12... | collective-permute-start | bytes 1572872 | tf_op jit(solution)/shard_map/ppermute | solution.py:23
  377.6 20.2 %collective-permute-start.50 = (bf16[256,512]{0,1:T(8,128)(2,1)S(1)}, bf16[256,512]{0,1:T(8,128)(2,1)S(1)}, u32[]{:S(2)}, u32[]{:S(2)}) collective-permute-start(bf16[256,512]{0,1:T(8,128)(2,1)S(1)} %slice.472), channel_id=1, source_target_pairs={{0,8},{8,0},{16,24},{24,16},{1,9},{9,1},{17,25},{25,17},{2,10},{10... | collective-permute-start | bytes 786440 | tf_op jit(solution)/shard_map/ppermute | solution.py:23
  377.7 18.1 %collective-permute-start.45 = (bf16[128,768]{0,1:T(8,128)(2,1)S(1)}, bf16[128,768]{0,1:T(8,128)(2,1)S(1)}, u32[]{:S(2)}, u32[]{:S(2)}) collective-permute-start(bf16[128,768]{0,1:T(8,128)(2,1)S(1)} %slice.475), channel_id=1, source_target_pairs={{0,16},{8,24},{16,0},{24,8},{1,17},{9,25},{17,1},{25,9},{2,18},{10... | collective-permute-start | bytes 589832 | tf_op jit(solution)/shard_map/ppermute | solution.py:23
  378.8 29.0 %collective-permute-start.39 = (bf16[512,512]{1,0:T(8,128)(2,1)S(1)}, bf16[512,512]{1,0:T(8,128)(2,1)S(1)}, u32[]{:S(2)}, u32[]{:S(2)}) collective-permute-start(bf16[512,512]{1,0:T(8,128)(2,1)S(1)} %pad_maximum_fusion.18), channel_id=1, source_target_pairs={{0,2},{2,0},{4,6},{6,4},{1,3},{3,1},{5,7},{7,5},{8,10},{10,8},{12,... | collective-permute-start | bytes 1572872 | tf_op jit(solution)/shard_map/ppermute | solution.py:23
  378.9 31.1 %collective-permute-start.37 = (bf16[512,512]{1,0:T(8,128)(2,1)S(1)}, bf16[512,512]{1,0:T(8,128)(2,1)S(1)}, u32[]{:S(2)}, u32[]{:S(2)}) collective-permute-start(bf16[512,512]{1,0:T(8,128)(2,1)S(1)} %pad_maximum_fusion.17), channel_id=1, source_target_pairs={{0,2},{2,0},{4,6},{6,4},{1,3},{3,1},{5,7},{7,5},{8,10},{10,8},{12,... | collective-permute-start | bytes 1572872 | tf_op jit(solution)/shard_map/ppermute | solution.py:23
  398.5 7.6 %collective-permute-start.51 = (bf16[128,512]{0,1:T(8,128)(2,1)}, bf16[128,512]{0,1:T(8,128)(2,1)S(1)}, u32[]{:S(2)}, u32[]{:S(2)}) collective-permute-start(bf16[128,512]{0,1:T(8,128)(2,1)} %slice.476), channel_id=1, source_target_pairs={{0,16},{8,24},{16,0},{24,8},{1,17},{9,25},{17,1},{25,9},{2,18},{10... | collective-permute-start | bytes 393224 | tf_op jit(solution)/shard_map/ppermute | solution.py:23
  (84 other events, 619.4 us)
Sparse Core Ops, SparseCore 0:
  10.7 156.3 all-gather.1
  221.3 96.8 reduce-scatter.2
  339.3 57.6 reduce-scatter.4

commit v7 on v6

--- a/solution.py
+++ b/solution.py
@@ -396,12 +396,13 @@
 
 def chain(local, factor, reverse):
     count = lax.axis_size("row")
-    entry = jnp.zeros(local.shape, BF16)
+    entry, sent = jnp.zeros(local.shape, BF16), []
     for hop in range(count - 1):
         out = (local + factor[:, :, None, None] * entry.astype(F32)).astype(BF16)
+        sent.append(out)
         edge = (count - 1 - hop, count - 2 - hop) if reverse else (hop, hop + 1)
         entry = entry + lax.ppermute(out, "row", [edge])
-    return entry
+    return entry, sent
 
 
 def other_first(value):
@@ -627,7 +628,7 @@
         flops=unit,
         name="mixer_inner",
     )
-    entry = chain(local, factor, False)
+    entry, _ = chain(local, factor, False)
     entry, _, _ = lax.optimization_barrier((entry, g_own, g_pair))
     o, squares = heads_of(
         carry_kernel,
@@ -659,7 +660,6 @@
     )
     dhr = both(dh.astype(BF16))
 
-    grad_out = dot(dhr, y, "td,tc->dc").astype(BF16)
     dy = dot(dhr, wo, "td,cd->tc")
     dn = dy * gate
     dzu = (dy * o * r2 * gate * (1.0 - gate)).astype(BF16)
@@ -675,7 +675,7 @@
         flops=unit // 8,
         name="mixer_entry_grad",
     )
-    d_local = chain(d_entry, factor, True)
+    d_local, sent = chain(d_entry, factor, True)
     dzq, dk, dv = heads_of(
         inner_grad_kernel,
         kinds_in="sscrttttpT",
@@ -684,7 +684,10 @@
         flops=5 * unit // 2,
         name="mixer_inner_grad",
     )
-    grad_u, grad_q = [dot(a, d, "td,tc->dc").astype(BF16) for d in (dzu, dzq)]
+    dzq, dhr, dzu_first, _ = lax.optimization_barrier((dzq, dhr, dzu, sent[1]))
+    grad_out = dot(dhr, y, "td,tc->dc").astype(BF16)
+    grad_u, grad_q = [dot(a, d, "td,tc->dc").astype(BF16) for d in (dzu_first, dzq)]
+    dzq, dzu, _ = lax.optimization_barrier((dzq, dzu, sent[2]))
     cut = wide // 2
     early = [
         jnp.concatenate(

time: 428 us -> 425 us (level)
  starting transfers between devices: 49.2 us -> 54.9 us
  matrix products: 43.9 us -> 39.3 us
    reduce_scatter x1, waiting for transfers between devices: 0.01 us -> 14.6 us  [ff_scatter_xy(): lax.psum_scatter(grads, ('cx', 'dp'), scatter_dimension=0, tiled=True)]
    ppermute x6, waiting for transfers between devices: 12.5 us -> 0.33 us  [chain(): entry = entry + lax.ppermute(out, 'row', [edge])]
    ppermute x45, starting transfers between devices: 35.4 us -> 41.6 us  [swap(): return lax.ppermute(value, axis, [(i, i ^ bits) for i in range(count)])]
    dot_general x18, matrix products: 43.9 us -> 39.3 us  [dot(): return jnp.einsum(form, left, right, preferred_element_type=F32)]
    unnamed x161 -> x177, local copies, waits for them, and re-layouts: 15.2 us -> 12.9 us
  transfers between devices with their start and end apart: 55 -> 55, of which waited for: 20 -> 22; matrix products, arithmetic and copies ran while one was open for 25% -> 24% of each run, Pallas kernels for 10% -> 10%
where the time goes in v7:
time: 425 us; the launch traced here: 418 us
  waiting for transfers between devices  141 us (33%)
  Pallas kernels  88.7 us (21%)
  starting transfers between devices  54.9 us (13%)
  other arithmetic  49.3 us (12%)
  matrix products  39.3 us (9%)
  local copies, waits for them, and re-layouts  28.8 us (7%)
  between operations  15.4 us (4%)
    ppermute x45, waiting for transfers between devices, swap(): return lax.ppermute(value, axis, [(i, i ^ bits) for i in range(count)])  111 us
    ppermute x45, starting transfers between devices, swap(): return lax.ppermute(value, axis, [(i, i ^ bits) for i in range(count)])  41.6 us
    pallas_call x1, Pallas kernels, feed_forward(): pl.pallas_call(ff_kernel, grid=(nx,), in_specs=[pl.BlockSpec(memory_space...  40.2 us
    dot_general x18, matrix products, dot(): return jnp.einsum(form, left, right, preferred_element_type=F32)  39.3 us
    pallas_call x6, Pallas kernels, head_call(): pl.pallas_call(kernel, grid=(2,), in_specs=[specs[k.lower()] for k in kin...  32.1 us
    all_gather x1, waiting for transfers between devices, ff_gather(): blocks = lax.all_gather(shard, CHIPS, axis=0, tiled=True)  15.6 us
    reduce_scatter x1, waiting for transfers between devices, ff_scatter_xy(): lax.psum_scatter(grads, ('cx', 'dp'), scatter_dimension=0, tiled=True)  14.6 us
    unnamed x177, local copies, waits for them, and re-layouts  12.9 us
  transfers between devices with their start and end apart: 55, of which 22 were waited for; matrix products, arithmetic and copies ran while one was open for 24% of the time, Pallas kernels for 10%

profile of v7, /device:TPU:0, one launch (start us, length us, event | category | flops | bytes accessed | tf_op | source)
XLA Modules:
  0.0 417.9 jit_solution(17109787465077546425)
XLA Ops:
  10.8 2.5 collective-permute-start.1
  13.4 2.9 collective-permute-start.6
  16.5 3.5 collective-permute-start.4
  23.2 2.2 collective-permute-start.7
  25.4 2.6 collective-permute-done.3
  29.7 3.8 assemble.2
  33.5 9.3 %collective-permute-done.7 = bf16[256,512]{1,0:T(8,128)(2,1)S(1)} collective-permute-done((bf16[256,512]{1,0:T(8,128)(2,1)S(1)}, bf16[256,512]{1,0:T(8,128)(2,1)S(1)}, u32[]{:S(2)}, u32[]{:S(2)}) %collective-permute-start.7) | collective-permute-done | bytes 262176 | tf_op jit(solution)/shard_map/ppermute | solution.py:23
  47.7 4.3 %collective-permute-done.8 = bf16[128,512]{1,0:T(8,128)(2,1)S(1)} collective-permute-done((bf16[128,512]{1,0:T(8,128)(2,1)S(1)}, bf16[128,512]{1,0:T(8,128)(2,1)S(1)}, u32[]{:S(2)}, u32[]{:S(2)}) %collective-permute-start.8) | collective-permute-done | bytes 131104 | tf_op jit(solution)/shard_map/ppermute | solution.py:23
  53.9 4.5 %collective-permute-done.14 = bf16[512,256]{1,0:T(8,128)(2,1)S(1)} collective-permute-done((bf16[512,256]{1,0:T(8,128)(2,1)S(1)}, bf16[512,256]{1,0:T(8,128)(2,1)S(1)}, u32[]{:S(2)}, u32[]{:S(2)}) %collective-permute-start.14) | collective-permute-done | bytes 262176 | tf_op jit(solution)/shard_map/ppermute | solution.py:23
  58.5 13.9 %collective-permute-done.9 = bf16[256,512]{1,0:T(8,128)(2,1)S(1)} collective-permute-done((bf16[256,512]{1,0:T(8,128)(2,1)S(1)}, bf16[256,512]{1,0:T(8,128)(2,1)S(1)}, u32[]{:S(2)}, u32[]{:S(2)}) %collective-permute-start.9) | collective-permute-done | bytes 262176 | tf_op jit(solution)/shard_map/ppermute | solution.py:23
  73.3 2.6 fusion.48.zk
  78.6 3.7 collective-permute-done.15
  82.3 2.6 fusion.47.zv
  85.0 4.1 mixer_local.1
  90.3 5.0 %collective-permute-start.16 = (bf16[2,4,128,128]{3,2,1,0:T(8,128)(2,1)S(1)}, bf16[2,4,128,128]{3,2,1,0:T(8,128)(2,1)S(1)}, u32[]{:S(2)}, u32[]{:S(2)}) collective-permute-start(bf16[2,4,128,128]{3,2,1,0:T(8,128)(2,1)S(1)} %add_convert_fusion.7), channel_id=1, source_target_pairs={{0,8},{1,9},{2,10},{3,11},{4,12},{5,13},{6,14},{7,15}} | collective-permute-start | bytes 786440 | tf_op jit(solution)/shard_map/ppermute | solution.py:404
  101.2 3.5 assemble.3.g0
  105.7 5.4 %collective-permute-done.24 = bf16[512,256]{1,0:T(8,128)(2,1)S(1)} collective-permute-done((bf16[512,256]{1,0:T(8,128)(2,1)S(1)}, bf16[512,256]{1,0:T(8,128)(2,1)S(1)}, u32[]{:S(2)}, u32[]{:S(2)}) %collective-permute-start.24) | collective-permute-done | bytes 262176 | tf_op jit(solution)/shard_map/ppermute | solution.py:23
  114.7 15.0 %collective-permute-done.11 = bf16[512,512]{1,0:T(8,128)(2,1)} collective-permute-done((bf16[512,512]{1,0:T(8,128)(2,1)}, bf16[512,512]{1,0:T(8,128)(2,1)}, u32[]{:S(2)}, u32[]{:S(2)}) %collective-permute-start.11) | collective-permute-done | bytes 524320 | tf_op jit(solution)/shard_map/ppermute | solution.py:23
  129.7 3.7 fusion.49.zq
  133.4 5.6 %mixer_inner.1 = (bf16[1024,512]{1,0:T(8,128)(2,1)}, f32[1024,512]{1,0:T(8,128)}) custom-call(f32[4]{0:T(128)} %get-tuple-element.139.rates, f32[2,2]{1,0:T(2,128)} %pad_maximum_fusion.21.marks, f32[2,512,1]{2,1,0:T(8,128)} %copy.39.seg_c, f32[2,1,512]{2,1,0:T(1,128)} %copy.38.seg_r, f32[1024,512]{1,0:T(8,128)} %fusion.49.zq, ...), custom_call_target="tpu_custom_call" | custom-call | flops 536870912 | bytes 8388608 | tf_op jit(solution)/shard_map/mixer_inner/pallas_call | solution.py:386
  139.7 3.6 mixer_carry.1
  146.0 5.6 %multiply_convert_fusion.2 = (bf16[1024,512]{1,0:T(8,128)(2,1)}, f32[1024,512]{1,0:T(8,128)}) fusion(f32[1024,512]{1,0:T(8,128)} %get-tuple-element.70, f32[1024]{0:T(1024)S(1)} %bitcast.97, bf16[1024,1024]{1,0:T(8,128)(2,1)} %copy-done.49, bf16[1024,256]{1,0:T(8,128)(2,1)S(1)} %collective-permute-done.25, ...), kind=kOutput, calls=%fused_computation.19 | convolution fusion | flops 1080033280 | bytes 8392704 | tf_op jit(solution)/shard_map/td,dc->tc/dot_general | solution.py:243
  151.6 15.6 %all-gather.2.cloned.1.call-done = bf16[37888,128]{1,0:T(8,128)(2,1)} async-done(((bf16[2368,128]{1,0:T(8,128)(2,1)}), bf16[37888,128]{1,0:T(8,128)(2,1)}) %all-gather.2.cloned.1.call-update) | async-done | bytes 9699344 | tf_op jit(solution)/shard_map/all_gather | solution.py:417
  167.2 4.8 %project_out.1 = (f32[512,1024]{1,0:T(8,128)}, bf16[512,1024]{1,0:T(8,128)(2,1)}, bf16[512,1024]{1,0:T(8,128)(2,1)}) custom-call(s32[2,8]{1,0:T(2,128)} %pad_add_fusion.tables, s32[1]{0:T(128)} %bitcast.9.side_of, bf16[1024,512]{1,0:T(8,128)(2,1)} %get-tuple-element.190.y_ref, bf16[2,8,2368,128]{3,2,1,0:T(8,128)(2,1)} %bitcast.91), custom_call_target="tpu_custom_call" | custom-call | flops 1073741824 | bytes 6291456 | tf_op jit(solution)/shard_map/project_out/pallas_call | solution.py:467
  172.0 2.9 collective-permute-done.26
  177.4 2.7 collective-permute-done.27.b1
  180.0 40.2 %feed_forward.1 = (f32[512,1024]{1,0:T(8,128)}, bf16[512,1024]{1,0:T(8,128)(2,1)}, f32[512,1024]{1,0:T(8,128)}, bf16[512,1024]{1,0:T(8,128)(2,1)}, bf16[2,8,2112,128]{3,2,1,0:T(8,128)(2,1)}) custom-call(s32[2,8]{1,0:T(2,128)} %pad_add_fusion.tables, bf16[512,1024]{1,0:T(8,128)(2,1)} %copy-done.37, bf16[512,1024]{1,0:T(8,128)(2,1)} %collective-permute-done.27.b1, ...), custom_call_target="tpu_custom_call" | custom-call | flops 26575110144 | bytes 37748736 | tf_op jit(solution)/shard_map/feed_forward/pallas_call | solution.py:535
  227.1 2.5 fusion.52
  229.7 2.5 collective-permute-done.30
  232.3 2.7 multiply_reduce_fusion
  236.3 4.0 multiply_convert_fusion
  240.3 3.5 mixer_entry_grad.1
  247.2 10.0 %mixer_inner_grad.1 = (bf16[1024,512]{1,0:T(8,128)(2,1)}, f32[1024,512]{1,0:T(8,128)}, f32[1024,512]{1,0:T(8,128)}) custom-call(f32[4]{0:T(128)} %get-tuple-element.139.rates, f32[2,2]{1,0:T(2,128)} %pad_maximum_fusion.21.marks, f32[2,512,1]{2,1,0:T(8,128)} %copy.39.seg_c, f32[2,1,512]{2,1,0:T(1,128)} %copy.38.seg_r, ...), custom_call_target="tpu_custom_call" | custom-call | flops 1342177280 | bytes 8388608 | tf_op jit(solution)/shard_map/mixer_inner_grad/pallas_call | solution.py:386
  258.0 3.2 convolution_convert_fusion.3
  272.2 3.2 fusion.26
  275.4 3.2 fusion.18
  281.9 5.4 %mixer_last_grad.1 = (bf16[1024,512]{1,0:T(8,128)(2,1)}, bf16[1024,512]{1,0:T(8,128)(2,1)}) custom-call(f32[4]{0:T(128)} %get-tuple-element.139.rates, f32[2,2]{1,0:T(2,128)} %pad_maximum_fusion.21.marks, f32[2,512,1]{2,1,0:T(8,128)} %copy.39.seg_c, bf16[1024,512]{1,0:T(8,128)(2,1)} %get-tuple-element.63.k_ref.k, ...), custom_call_target="tpu_custom_call" | custom-call | flops 134217728 | bytes 8388608 | tf_op jit(solution)/shard_map/mixer_last_grad/pallas_call | solution.py:386
  312.1 3.0 fusion.3.rows_ref
  315.1 14.6 %reduce-scatter.3.cloned.1.call-done = bf16[8448,128]{1,0:T(8,128)(2,1)} async-done(((bf16[33792,128]{1,0:T(8,128)(2,1)}), bf16[8448,128]{1,0:T(8,128)(2,1)}) %reduce-scatter.3.cloned.1.call-update) | async-done | bytes 2162704 | tf_op jit(solution)/shard_map/reduce_scatter | solution.py:444
  329.7 2.2 divide.2
  334.3 2.5 collective-permute-start.47
  343.4 2.2 divide.3
  348.0 4.6 %collective-permute-done.49 = bf16[512,256]{0,1:T(8,128)(2,1)} collective-permute-done((bf16[512,256]{0,1:T(8,128)(2,1)}, bf16[512,256]{0,1:T(8,128)(2,1)}, u32[]{:S(2)}, u32[]{:S(2)}) %collective-permute-start.49) | collective-permute-done | bytes 262176 | tf_op jit(solution)/shard_map/ppermute | solution.py:23
  353.7 17.1 %collective-permute-done.44 = bf16[256,768]{0,1:T(8,128)(2,1)} collective-permute-done((bf16[256,768]{0,1:T(8,128)(2,1)}, bf16[256,768]{0,1:T(8,128)(2,1)}, u32[]{:S(2)}, u32[]{:S(2)}) %collective-permute-start.44) | collective-permute-done | bytes 393248 | tf_op jit(solution)/shard_map/ppermute | solution.py:23
  372.1 6.6 %collective-permute-start.45 = (bf16[128,768]{0,1:T(8,128)(2,1)S(1)}, bf16[128,768]{0,1:T(8,128)(2,1)S(1)}, u32[]{:S(2)}, u32[]{:S(2)}) collective-permute-start(bf16[128,768]{0,1:T(8,128)(2,1)S(1)} %slice.473), channel_id=1, source_target_pairs={{0,16},{8,24},{16,0},{24,8},{1,17},{9,25},{17,1},{25,9},{2,18},{10... | collective-permute-start | bytes 589832 | tf_op jit(solution)/shard_map/ppermute | solution.py:23
  380.4 12.0 %collective-permute-done.45 = bf16[128,768]{0,1:T(8,128)(2,1)S(1)} collective-permute-done((bf16[128,768]{0,1:T(8,128)(2,1)S(1)}, bf16[128,768]{0,1:T(8,128)(2,1)S(1)}, u32[]{:S(2)}, u32[]{:S(2)}) %collective-permute-start.45) | collective-permute-done | bytes 196640 | tf_op jit(solution)/shard_map/ppermute | solution.py:23
  393.1 2.8 collective-permute-done.50
  398.8 4.4 %collective-permute-done.51 = bf16[128,512]{0,1:T(8,128)(2,1)S(1)} collective-permute-done((bf16[128,512]{0,1:T(8,128)(2,1)}, bf16[128,512]{0,1:T(8,128)(2,1)S(1)}, u32[]{:S(2)}, u32[]{:S(2)}) %collective-permute-start.51) | collective-permute-done | bytes 131104 | tf_op jit(solution)/shard_map/ppermute | solution.py:23
  (377 shorter events, 114.6 us)
Async XLA Ops:
  7.2 160.0 %all-gather.2.cloned.1.call-start = ((), (), s32[]{:S(2)}) async-start(), calls=%async_computation.2 | async-start | bytes 10305536 | tf_op jit(solution)/shard_map/all_gather | solution.py:417
  9.4 320.3 %reduce-scatter.3.cloned.1.call-start = ((), (), s32[]{:S(2)}) async-start(), calls=%async_computation.3 | async-start | bytes 10813440 | tf_op jit(solution)/shard_map/reduce_scatter | solution.py:444
  10.3 18.5 %collective-permute-start = (bf16[512,256]{1,0:T(8,128)(2,1)S(1)}, bf16[512,256]{1,0:T(8,128)(2,1)S(1)}, u32[]{:S(2)}, u32[]{:S(2)}) collective-permute-start(bf16[512,256]{1,0:T(8,128)(2,1)S(1)} %get-tuple-element.168), channel_id=1, source_target_pairs={{0,2},{2,0},{4,6},{6,4},{1,3},{3,1},{5,7},{7,5},{8,10},{10,8},{12,... | collective-permute-start | bytes 786440 | tf_op jit(solution)/shard_map/ppermute | solution.py:23
  10.8 18.0 %collective-permute-start.1 = (bf16[512,256]{1,0:T(8,128)(2,1)S(1)}, bf16[512,256]{1,0:T(8,128)(2,1)S(1)}, u32[]{:S(2)}, u32[]{:S(2)}) collective-permute-start(bf16[512,256]{1,0:T(8,128)(2,1)S(1)} %get-tuple-element.170), channel_id=1, source_target_pairs={{0,4},{2,6},{4,0},{6,2},{1,5},{3,7},{5,1},{7,3},{8,12},{10,14},{12... | collective-permute-start | bytes 786440 | tf_op jit(solution)/shard_map/ppermute | solution.py:23
  13.2 15.6 %collective-permute-start.2 = (bf16[512,256]{1,0:T(8,128)(2,1)S(1)}, bf16[512,256]{1,0:T(8,128)(2,1)S(1)}, u32[]{:S(2)}, u32[]{:S(2)}) collective-permute-start(bf16[512,256]{1,0:T(8,128)(2,1)S(1)} %get-tuple-element.167), channel_id=1, source_target_pairs={{0,6},{2,4},{4,2},{6,0},{1,7},{3,5},{5,3},{7,1},{8,14},{10,12},{12... | collective-permute-start | bytes 786440 | tf_op jit(solution)/shard_map/ppermute | solution.py:23
  13.4 9.8 %collective-permute-start.6 = (bf16[128,512]{1,0:T(8,128)(2,1)S(1)}, bf16[128,512]{1,0:T(8,128)(2,1)S(1)}, u32[]{:S(2)}, u32[]{:S(2)}) collective-permute-start(bf16[128,512]{1,0:T(8,128)(2,1)S(1)} %fusion.31), channel_id=1, source_target_pairs={{0,16},{8,24},{16,0},{24,8},{1,17},{9,25},{17,1},{25,9},{2,18},{10... | collective-permute-start | bytes 393224 | tf_op jit(solution)/shard_map/ppermute | solution.py:23
  16.5 5.1 %collective-permute-start.4 = (f32[2]{0:T(128)S(1)}, f32[2]{0:T(128)S(1)}, u32[]{:S(2)}, u32[]{:S(2)}) collective-permute-start(f32[2]{0:T(128)S(1)} %get-tuple-element.140), channel_id=1, source_target_pairs={{0,8},{8,16},{16,24},{1,9},{9,17},{17,25},{2,10},{10,18},{18,26},{... | collective-permute-start | bytes 32 | tf_op jit(solution)/shard_map/ppermute | solution.py:588
  21.7 6.4 %collective-permute-start.3 = (f32[2]{0:T(128)S(1)}, f32[2]{0:T(128)S(1)}, u32[]{:S(2)}, u32[]{:S(2)}) collective-permute-start(f32[2]{0:T(128)S(1)} %copy-done.76), channel_id=1, source_target_pairs={{0,4},{2,6},{4,0},{6,2},{1,5},{3,7},{5,1},{7,3},{8,12},{10,14},{12... | collective-permute-start | bytes 32 | tf_op jit(solution)/shard_map/ppermute | solution.py:23
  23.2 19.5 %collective-permute-start.7 = (bf16[256,512]{1,0:T(8,128)(2,1)S(1)}, bf16[256,512]{1,0:T(8,128)(2,1)S(1)}, u32[]{:S(2)}, u32[]{:S(2)}) collective-permute-start(bf16[256,512]{1,0:T(8,128)(2,1)S(1)} %pad_maximum_fusion.17), channel_id=1, source_target_pairs={{0,8},{8,0},{16,24},{24,16},{1,9},{9,1},{17,25},{25,17},{2,10},{10... | collective-permute-start | bytes 786440 | tf_op jit(solution)/shard_map/ppermute | solution.py:23
  33.4 39.7 %collective-permute-start.5 = (bf16[512,1024]{1,0:T(8,128)(2,1)}, bf16[512,1024]{1,0:T(8,128)(2,1)S(1)}, u32[]{:S(2)}, u32[]{:S(2)}) collective-permute-start(bf16[512,1024]{1,0:T(8,128)(2,1)} %get-tuple-element.59), channel_id=1, source_target_pairs={{0,2},{2,0},{4,6},{6,4},{1,3},{3,1},{5,7},{7,5},{8,10},{10,8},{12,... | collective-permute-start | bytes 3145736 | tf_op jit(solution)/shard_map/ppermute | solution.py:23
  42.8 9.2 %collective-permute-start.8 = (bf16[128,512]{1,0:T(8,128)(2,1)S(1)}, bf16[128,512]{1,0:T(8,128)(2,1)S(1)}, u32[]{:S(2)}, u32[]{:S(2)}) collective-permute-start(bf16[128,512]{1,0:T(8,128)(2,1)S(1)} %fusion.30), channel_id=1, source_target_pairs={{0,16},{8,24},{16,0},{24,8},{1,17},{9,25},{17,1},{25,9},{2,18},{10... | collective-permute-start | bytes 393224 | tf_op jit(solution)/shard_map/ppermute | solution.py:23
  44.3 7.8 %collective-permute-start.12 = (bf16[512,256]{1,0:T(8,128)(2,1)S(1)}, bf16[512,256]{1,0:T(8,128)(2,1)S(1)}, u32[]{:S(2)}, u32[]{:S(2)}) collective-permute-start(bf16[512,256]{1,0:T(8,128)(2,1)S(1)} %get-tuple-element.172), channel_id=1, source_target_pairs={{0,4},{2,6},{4,0},{6,2},{1,5},{3,7},{5,1},{7,3},{8,12},{10,14},{12... | collective-permute-start | bytes 786440 | tf_op jit(solution)/shard_map/ppermute | solution.py:23
  46.2 12.1 %collective-permute-start.14 = (bf16[512,256]{1,0:T(8,128)(2,1)S(1)}, bf16[512,256]{1,0:T(8,128)(2,1)S(1)}, u32[]{:S(2)}, u32[]{:S(2)}) collective-permute-start(bf16[512,256]{1,0:T(8,128)(2,1)S(1)} %get-tuple-element.171), channel_id=1, source_target_pairs={{0,1},{1,0},{2,3},{3,2},{4,5},{5,4},{6,7},{7,6},{8,9},{9,8},{10,11... | collective-permute-start | bytes 786440 | tf_op jit(solution)/shard_map/ppermute | solution.py:23
  52.0 20.3 %collective-permute-start.9 = (bf16[256,512]{1,0:T(8,128)(2,1)S(1)}, bf16[256,512]{1,0:T(8,128)(2,1)S(1)}, u32[]{:S(2)}, u32[]{:S(2)}) collective-permute-start(bf16[256,512]{1,0:T(8,128)(2,1)S(1)} %pad_maximum_fusion.18), channel_id=1, source_target_pairs={{0,8},{8,0},{16,24},{24,16},{1,9},{9,1},{17,25},{25,17},{2,10},{10... | collective-permute-start | bytes 786440 | tf_op jit(solution)/shard_map/ppermute | solution.py:23
  52.2 21.0 %collective-permute-start.13 = (bf16[512,512]{1,0:T(8,128)(2,1)S(1)}, bf16[512,512]{1,0:T(8,128)(2,1)S(1)}, u32[]{:S(2)}, u32[]{:S(2)}) collective-permute-start(bf16[512,512]{1,0:T(8,128)(2,1)S(1)} %pad_maximum_fusion.12), channel_id=1, source_target_pairs={{0,1},{1,0},{2,3},{3,2},{4,5},{5,4},{6,7},{7,6},{8,9},{9,8},{10,11... | collective-permute-start | bytes 1572872 | tf_op jit(solution)/shard_map/ppermute | solution.py:23
  58.4 23.9 %collective-permute-start.15 = (bf16[1024,256]{1,0:T(8,128)(2,1)S(1)}, bf16[1024,256]{1,0:T(8,128)(2,1)S(1)}, u32[]{:S(2)}, u32[]{:S(2)}) collective-permute-start(bf16[1024,256]{1,0:T(8,128)(2,1)S(1)} %pad_maximum_fusion.13), channel_id=1, source_target_pairs={{0,4},{2,6},{4,0},{6,2},{1,5},{3,7},{5,1},{7,3},{8,12},{10,14},{12... | collective-permute-start | bytes 1572872 | tf_op jit(solution)/shard_map/ppermute | solution.py:23
  72.4 23.4 %collective-permute-start.10 = (bf16[512,256]{1,0:T(8,128)(2,1)S(1)}, bf16[512,256]{1,0:T(8,128)(2,1)S(1)}, u32[]{:S(2)}, u32[]{:S(2)}) collective-permute-start(bf16[512,256]{1,0:T(8,128)(2,1)S(1)} %get-tuple-element.173), channel_id=1, source_target_pairs={{0,4},{2,6},{4,0},{6,2},{1,5},{3,7},{5,1},{7,3},{8,12},{10,14},{12... | collective-permute-start | bytes 786440 | tf_op jit(solution)/shard_map/ppermute | solution.py:23
  76.7 23.1 %collective-permute-start.19 = (bf16[512,256]{1,0:T(8,128)(2,1)}, bf16[512,256]{1,0:T(8,128)(2,1)S(1)}, u32[]{:S(2)}, u32[]{:S(2)}) collective-permute-start(bf16[512,256]{1,0:T(8,128)(2,1)} %get-tuple-element.165), channel_id=1, source_target_pairs={{0,2},{2,0},{4,6},{6,4},{1,3},{3,1},{5,7},{7,5},{8,10},{10,8},{12,... | collective-permute-start | bytes 786440 | tf_op jit(solution)/shard_map/ppermute | solution.py:23
  76.7 23.6 %collective-permute-start.20 = (bf16[512,256]{1,0:T(8,128)(2,1)S(1)}, bf16[512,256]{1,0:T(8,128)(2,1)S(1)}, u32[]{:S(2)}, u32[]{:S(2)}) collective-permute-start(bf16[512,256]{1,0:T(8,128)(2,1)S(1)} %get-tuple-element.164), channel_id=1, source_target_pairs={{0,4},{2,6},{4,0},{6,2},{1,5},{3,7},{5,1},{7,3},{8,12},{10,14},{12... | collective-permute-start | bytes 786440 | tf_op jit(solution)/shard_map/ppermute | solution.py:23
  78.1 22.2 %collective-permute-start.21 = (bf16[512,256]{1,0:T(8,128)(2,1)S(1)}, bf16[512,256]{1,0:T(8,128)(2,1)S(1)}, u32[]{:S(2)}, u32[]{:S(2)}) collective-permute-start(bf16[512,256]{1,0:T(8,128)(2,1)S(1)} %get-tuple-element.163), channel_id=1, source_target_pairs={{0,6},{2,4},{4,2},{6,0},{1,7},{3,5},{5,3},{7,1},{8,14},{10,12},{12... | collective-permute-start | bytes 786440 | tf_op jit(solution)/shard_map/ppermute | solution.py:23
  90.3 14.5 %collective-permute-start.16 = (bf16[2,4,128,128]{3,2,1,0:T(8,128)(2,1)S(1)}, bf16[2,4,128,128]{3,2,1,0:T(8,128)(2,1)S(1)}, u32[]{:S(2)}, u32[]{:S(2)}) collective-permute-start(bf16[2,4,128,128]{3,2,1,0:T(8,128)(2,1)S(1)} %add_convert_fusion.7), channel_id=1, source_target_pairs={{0,8},{1,9},{2,10},{3,11},{4,12},{5,13},{6,14},{7,15}} | collective-permute-start | bytes 786440 | tf_op jit(solution)/shard_map/ppermute | solution.py:404
  96.5 14.6 %collective-permute-start.24 = (bf16[512,256]{1,0:T(8,128)(2,1)S(1)}, bf16[512,256]{1,0:T(8,128)(2,1)S(1)}, u32[]{:S(2)}, u32[]{:S(2)}) collective-permute-start(bf16[512,256]{1,0:T(8,128)(2,1)S(1)} %get-tuple-element.174), channel_id=1, source_target_pairs={{0,1},{1,0},{2,3},{3,2},{4,5},{5,4},{6,7},{7,6},{8,9},{9,8},{10,11... | collective-permute-start | bytes 786440 | tf_op jit(solution)/shard_map/ppermute | solution.py:23
  99.8 29.9 %collective-permute-start.11 = (bf16[512,512]{1,0:T(8,128)(2,1)}, bf16[512,512]{1,0:T(8,128)(2,1)}, u32[]{:S(2)}, u32[]{:S(2)}) collective-permute-start(bf16[512,512]{1,0:T(8,128)(2,1)} %pad_maximum_fusion.11), channel_id=1, source_target_pairs={{0,1},{1,0},{2,3},{3,2},{4,5},{5,4},{6,7},{7,6},{8,9},{9,8},{10,11... | collective-permute-start | bytes 1572872 | tf_op jit(solution)/shard_map/ppermute | solution.py:23
  104.6 35.1 %collective-permute-start.22 = (bf16[512,1024]{1,0:T(8,128)(2,1)}, bf16[512,1024]{1,0:T(8,128)(2,1)}, u32[]{:S(2)}, u32[]{:S(2)}) collective-permute-start(bf16[512,1024]{1,0:T(8,128)(2,1)} %assemble.3.g0), channel_id=1, source_target_pairs={{0,2},{2,0},{4,6},{6,4},{1,3},{3,1},{5,7},{7,5},{8,10},{10,8},{12,... | collective-permute-start | bytes 3145736 | tf_op jit(solution)/shard_map/ppermute | solution.py:23
  104.9 7.8 %collective-permute-start.17 = (bf16[2,4,128,128]{3,2,1,0:T(8,128)(2,1)S(1)}, bf16[2,4,128,128]{3,2,1,0:T(8,128)(2,1)S(1)}, u32[]{:S(2)}, u32[]{:S(2)}) collective-permute-start(bf16[2,4,128,128]{3,2,1,0:T(8,128)(2,1)S(1)} %add_convert_fusion.6), channel_id=1, source_target_pairs={{8,16},{9,17},{10,18},{11,19},{12,20},{13,21},{14,22},{15,23}} | collective-permute-start | bytes 786440 | tf_op jit(solution)/shard_map/ppermute | solution.py:404
  111.1 34.8 %collective-permute-start.25 = (bf16[1024,256]{1,0:T(8,128)(2,1)S(1)}, bf16[1024,256]{1,0:T(8,128)(2,1)S(1)}, u32[]{:S(2)}, u32[]{:S(2)}) collective-permute-start(bf16[1024,256]{1,0:T(8,128)(2,1)S(1)} %pad_maximum_fusion.14), channel_id=1, source_target_pairs={{0,4},{2,6},{4,0},{6,2},{1,5},{3,7},{5,1},{7,3},{8,12},{10,14},{12... | collective-permute-start | bytes 1572872 | tf_op jit(solution)/shard_map/ppermute | solution.py:23
  113.5 25.4 %collective-permute-start.18 = (bf16[2,4,128,128]{3,2,1,0:T(8,128)(2,1)}, bf16[2,4,128,128]{3,2,1,0:T(8,128)(2,1)S(1)}, u32[]{:S(2)}, u32[]{:S(2)}) collective-permute-start(bf16[2,4,128,128]{3,2,1,0:T(8,128)(2,1)} %get-tuple-element.136), channel_id=1, source_target_pairs={{16,24},{17,25},{18,26},{19,27},{20,28},{21,29},{22,30},{23,31}} | collective-permute-start | bytes 786440 | tf_op jit(solution)/shard_map/ppermute | solution.py:404
  220.2 188.1 %reduce-scatter.5.cloned.1.call-start = ((), (), s32[]{:S(2)}) async-start(), calls=%async_computation.4 | async-start | bytes 2703360 | tf_op jit(solution)/shard_map/reduce_scatter | solution.py:729
  244.9 12.3 %collective-permute-start.32 = (bf16[2,4,128,128]{3,2,1,0:T(8,128)(2,1)S(1)}, bf16[2,4,128,128]{3,2,1,0:T(8,128)(2,1)S(1)}, u32[]{:S(2)}, u32[]{:S(2)}) collective-permute-start(bf16[2,4,128,128]{3,2,1,0:T(8,128)(2,1)S(1)} %add_convert_fusion.4), channel_id=1, source_target_pairs={{24,16},{25,17},{26,18},{27,19},{28,20},{29,21},{30,22},{31,23}} | collective-permute-start | bytes 786440 | tf_op jit(solution)/shard_map/ppermute | solution.py:404
  257.3 13.2 %collective-permute-start.33 = (bf16[2,4,128,128]{3,2,1,0:T(8,128)(2,1)S(1)}, bf16[2,4,128,128]{3,2,1,0:T(8,128)(2,1)S(1)}, u32[]{:S(2)}, u32[]{:S(2)}) collective-permute-start(bf16[2,4,128,128]{3,2,1,0:T(8,128)(2,1)S(1)} %add_convert_fusion.3), channel_id=1, source_target_pairs={{16,8},{17,9},{18,10},{19,11},{20,12},{21,13},{22,14},{23,15}} | collective-permute-start | bytes 786440 | tf_op jit(solution)/shard_map/ppermute | solution.py:404
  265.3 35.7 %collective-permute-start.40 = (bf16[1024,384]{0,1:T(8,128)(2,1)}, bf16[1024,384]{0,1:T(8,128)(2,1)}, u32[]{:S(2)}, u32[]{:S(2)}) collective-permute-start(bf16[1024,384]{0,1:T(8,128)(2,1)} %pad_maximum_fusion.8), channel_id=1, source_target_pairs={{0,4},{2,6},{4,0},{6,2},{1,5},{3,7},{5,1},{7,3},{8,12},{10,14},{12... | collective-permute-start | bytes 2359304 | tf_op jit(solution)/shard_map/ppermute | solution.py:23
  269.1 35.9 %collective-permute-start.42 = (bf16[512,768]{0,1:T(8,128)(2,1)}, bf16[512,768]{0,1:T(8,128)(2,1)}, u32[]{:S(2)}, u32[]{:S(2)}) collective-permute-start(bf16[512,768]{0,1:T(8,128)(2,1)} %slice.299), channel_id=1, source_target_pairs={{0,1},{1,0},{2,3},{3,2},{4,5},{5,4},{6,7},{7,6},{8,9},{9,8},{10,11... | collective-permute-start | bytes 2359304 | tf_op jit(solution)/shard_map/ppermute | solution.py:23
  270.7 10.4 %collective-permute-start.34 = (bf16[2,4,128,128]{3,2,1,0:T(8,128)(2,1)S(1)}, bf16[2,4,128,128]{3,2,1,0:T(8,128)(2,1)S(1)}, u32[]{:S(2)}, u32[]{:S(2)}) collective-permute-start(bf16[2,4,128,128]{3,2,1,0:T(8,128)(2,1)S(1)} %get-tuple-element.130), channel_id=1, source_target_pairs={{8,0},{9,1},{10,2},{11,3},{12,4},{13,5},{14,6},{15,7}} | collective-permute-start | bytes 786440 | tf_op jit(solution)/shard_map/ppermute | solution.py:404
  292.2 16.5 %collective-permute-start.35 = (bf16[512,1024]{1,0:T(8,128)(2,1)S(1)}, bf16[512,1024]{1,0:T(8,128)(2,1)S(1)}, u32[]{:S(2)}, u32[]{:S(2)}) collective-permute-start(bf16[512,1024]{1,0:T(8,128)(2,1)S(1)} %add_convert_fusion), channel_id=1, source_target_pairs={{0,2},{2,0},{4,6},{6,4},{1,3},{3,1},{5,7},{7,5},{8,10},{10,8},{12,... | collective-permute-start | bytes 3145736 | tf_op jit(solution)/shard_map/ppermute | solution.py:23
  295.8 36.2 %collective-permute-start.46 = (bf16[1024,256]{0,1:T(8,128)(2,1)}, bf16[1024,256]{0,1:T(8,128)(2,1)}, u32[]{:S(2)}, u32[]{:S(2)}) collective-permute-start(bf16[1024,256]{0,1:T(8,128)(2,1)} %slice.309), channel_id=1, source_target_pairs={{0,4},{2,6},{4,0},{6,2},{1,5},{3,7},{5,1},{7,3},{8,12},{10,14},{12... | collective-permute-start | bytes 1572872 | tf_op jit(solution)/shard_map/ppermute | solution.py:23
  298.6 38.2 %collective-permute-start.48 = (bf16[512,512]{0,1:T(8,128)(2,1)}, bf16[512,512]{0,1:T(8,128)(2,1)}, u32[]{:S(2)}, u32[]{:S(2)}) collective-permute-start(bf16[512,512]{0,1:T(8,128)(2,1)} %slice.313), channel_id=1, source_target_pairs={{0,1},{1,0},{2,3},{3,2},{4,5},{5,4},{6,7},{7,6},{8,9},{9,8},{10,11... | collective-permute-start | bytes 1572872 | tf_op jit(solution)/shard_map/ppermute | solution.py:23
  303.8 36.8 %collective-permute-start.41 = (bf16[512,384]{0,1:T(8,128)(2,1)}, bf16[512,384]{0,1:T(8,128)(2,1)}, u32[]{:S(2)}, u32[]{:S(2)}) collective-permute-start(bf16[512,384]{0,1:T(8,128)(2,1)} %slice.469), channel_id=1, source_target_pairs={{0,1},{1,0},{2,3},{3,2},{4,5},{5,4},{6,7},{7,6},{8,9},{9,8},{10,11... | collective-permute-start | bytes 1179656 | tf_op jit(solution)/shard_map/ppermute | solution.py:23
  307.2 33.3 %collective-permute-start.43 = (bf16[512,384]{0,1:T(8,128)(2,1)}, bf16[512,384]{0,1:T(8,128)(2,1)}, u32[]{:S(2)}, u32[]{:S(2)}) collective-permute-start(bf16[512,384]{0,1:T(8,128)(2,1)} %slice.468), channel_id=1, source_target_pairs={{0,4},{2,6},{4,0},{6,2},{1,5},{3,7},{5,1},{7,3},{8,12},{10,14},{12... | collective-permute-start | bytes 1179656 | tf_op jit(solution)/shard_map/ppermute | solution.py:23
  331.9 46.8 %collective-permute-start.38 = (bf16[512,512]{1,0:T(8,128)(2,1)}, bf16[512,512]{1,0:T(8,128)(2,1)}, u32[]{:S(2)}, u32[]{:S(2)}) collective-permute-start(bf16[512,512]{1,0:T(8,128)(2,1)} %get-tuple-element.90), channel_id=1, source_target_pairs={{0,4},{2,6},{4,0},{6,2},{1,5},{3,7},{5,1},{7,3},{8,12},{10,14},{12... | collective-permute-start | bytes 1572872 | tf_op jit(solution)/shard_map/ppermute | solution.py:23
  334.3 12.7 %collective-permute-start.47 = (bf16[512,256]{0,1:T(8,128)(2,1)}, bf16[512,256]{0,1:T(8,128)(2,1)}, u32[]{:S(2)}, u32[]{:S(2)}) collective-permute-start(bf16[512,256]{0,1:T(8,128)(2,1)} %slice.472), channel_id=1, source_target_pairs={{0,1},{1,0},{2,3},{3,2},{4,5},{5,4},{6,7},{7,6},{8,9},{9,8},{10,11... | collective-permute-start | bytes 786440 | tf_op jit(solution)/shard_map/ppermute | solution.py:23
  338.8 13.8 %collective-permute-start.49 = (bf16[512,256]{0,1:T(8,128)(2,1)}, bf16[512,256]{0,1:T(8,128)(2,1)}, u32[]{:S(2)}, u32[]{:S(2)}) collective-permute-start(bf16[512,256]{0,1:T(8,128)(2,1)} %slice.471), channel_id=1, source_target_pairs={{0,4},{2,6},{4,0},{6,2},{1,5},{3,7},{5,1},{7,3},{8,12},{10,14},{12... | collective-permute-start | bytes 786440 | tf_op jit(solution)/shard_map/ppermute | solution.py:23
  342.9 27.9 %collective-permute-start.44 = (bf16[256,768]{0,1:T(8,128)(2,1)}, bf16[256,768]{0,1:T(8,128)(2,1)}, u32[]{:S(2)}, u32[]{:S(2)}) collective-permute-start(bf16[256,768]{0,1:T(8,128)(2,1)} %fusion.6), channel_id=1, source_target_pairs={{0,8},{8,0},{16,24},{24,16},{1,9},{9,1},{17,25},{25,17},{2,10},{10... | collective-permute-start | bytes 1179656 | tf_op jit(solution)/shard_map/ppermute | solution.py:23
  345.6 34.2 %collective-permute-start.36 = (bf16[512,512]{1,0:T(8,128)(2,1)}, bf16[512,512]{1,0:T(8,128)(2,1)S(1)}, u32[]{:S(2)}, u32[]{:S(2)}) collective-permute-start(bf16[512,512]{1,0:T(8,128)(2,1)} %get-tuple-element.93), channel_id=1, source_target_pairs={{0,4},{2,6},{4,0},{6,2},{1,5},{3,7},{5,1},{7,3},{8,12},{10,14},{12... | collective-permute-start | bytes 1572872 | tf_op jit(solution)/shard_map/ppermute | solution.py:23
  372.0 23.9 %collective-permute-start.50 = (bf16[256,512]{0,1:T(8,128)(2,1)S(1)}, bf16[256,512]{0,1:T(8,128)(2,1)S(1)}, u32[]{:S(2)}, u32[]{:S(2)}) collective-permute-start(bf16[256,512]{0,1:T(8,128)(2,1)S(1)} %slice.470), channel_id=1, source_target_pairs={{0,8},{8,0},{16,24},{24,16},{1,9},{9,1},{17,25},{25,17},{2,10},{10... | collective-permute-start | bytes 786440 | tf_op jit(solution)/shard_map/ppermute | solution.py:23
  372.1 20.3 %collective-permute-start.45 = (bf16[128,768]{0,1:T(8,128)(2,1)S(1)}, bf16[128,768]{0,1:T(8,128)(2,1)S(1)}, u32[]{:S(2)}, u32[]{:S(2)}) collective-permute-start(bf16[128,768]{0,1:T(8,128)(2,1)S(1)} %slice.473), channel_id=1, source_target_pairs={{0,16},{8,24},{16,0},{24,8},{1,17},{9,25},{17,1},{25,9},{2,18},{10... | collective-permute-start | bytes 589832 | tf_op jit(solution)/shard_map/ppermute | solution.py:23
  379.7 25.2 %collective-permute-start.39 = (bf16[512,512]{1,0:T(8,128)(2,1)S(1)}, bf16[512,512]{1,0:T(8,128)(2,1)S(1)}, u32[]{:S(2)}, u32[]{:S(2)}) collective-permute-start(bf16[512,512]{1,0:T(8,128)(2,1)S(1)} %pad_maximum_fusion.16), channel_id=1, source_target_pairs={{0,2},{2,0},{4,6},{6,4},{1,3},{3,1},{5,7},{7,5},{8,10},{10,8},{12,... | collective-permute-start | bytes 1572872 | tf_op jit(solution)/shard_map/ppermute | solution.py:23
  379.9 27.2 %collective-permute-start.37 = (bf16[512,512]{1,0:T(8,128)(2,1)S(1)}, bf16[512,512]{1,0:T(8,128)(2,1)S(1)}, u32[]{:S(2)}, u32[]{:S(2)}) collective-permute-start(bf16[512,512]{1,0:T(8,128)(2,1)S(1)} %pad_maximum_fusion.15), channel_id=1, source_target_pairs={{0,2},{2,0},{4,6},{6,4},{1,3},{3,1},{5,7},{7,5},{8,10},{10,8},{12,... | collective-permute-start | bytes 1572872 | tf_op jit(solution)/shard_map/ppermute | solution.py:23
  396.7 6.6 %collective-permute-start.51 = (bf16[128,512]{0,1:T(8,128)(2,1)}, bf16[128,512]{0,1:T(8,128)(2,1)S(1)}, u32[]{:S(2)}, u32[]{:S(2)}) collective-permute-start(bf16[128,512]{0,1:T(8,128)(2,1)} %slice.474), channel_id=1, source_target_pairs={{0,16},{8,24},{16,0},{24,8},{1,17},{9,25},{17,1},{25,9},{2,18},{10... | collective-permute-start | bytes 393224 | tf_op jit(solution)/shard_map/ppermute | solution.py:23
  (92 other events, 653.7 us)
Sparse Core Ops, SparseCore 0:
  10.7 156.3 all-gather.1
  220.3 109.2 reduce-scatter.2
  332.1 65.4 reduce-scatter.4
